TPU v7x, 32 devices: a whole 2x2x4 slice. The times are simulated.
32 devices in a mesh: seq: 4 (over y, core), ctx: 8 (over z, x).
Axes of the slice: x: 2, y: 2, z: 4, core: 2. Of those that a mesh axis runs over, the one named last changes fastest.
Arguments:
- tokens: bfloat16 [8, 2048, 2048], P('seq', 'ctx'), may hold values from -6 to 6
- out_grad: bfloat16 [8, 2048, 2048], P('seq', 'ctx'), may hold values from -6 to 6
- doc_ids: int32 [8, 2048], P('seq', 'ctx'), may hold values from 0 to 5, never falling along the last dimension, each value on 1 to 1024 neighbouring positions
- corpus: int32 [8], P('seq'), may hold values from 0 to 3
- corpus_weight: float32 [4], replicated, may hold values from 0.3 to 3
- attn_gain: bfloat16 [2048], P(('seq', 'ctx')), may hold values from 0.5 to 1.5
- w_query: bfloat16 [2048, 1280], P(('seq', 'ctx')), may hold values from -0.125 to 0.125
- w_key: bfloat16 [2048, 320], P(('seq', 'ctx')), may hold values from -0.125 to 0.125
- w_value: bfloat16 [2048, 320], P(('seq', 'ctx')), may hold values from -0.125 to 0.125
- query_gain: bfloat16 [64], replicated, may hold values from 0.099609375 to 1.8984375
- key_gain: bfloat16 [64], replicated, may hold values from 0.099609375 to 1.8984375
- w_out: bfloat16 [1280, 2048], P(('seq', 'ctx')), may hold values from -1.25 to 1.25
- ffn_gain: bfloat16 [2048], P(('seq', 'ctx')), may hold values from 0.5 to 1.5
- w_gate: bfloat16 [2048, 3584], P(('seq', 'ctx')), may hold values from -0.125 to 0.125
- w_up: bfloat16 [2048, 3584], P(('seq', 'ctx')), may hold values from -0.125 to 0.125
- w_down: bfloat16 [3584, 2048], P(('seq', 'ctx')), may hold values from -0.09375 to 0.09375
Outputs:
- layer_out: bfloat16 [8, 2048, 2048], P('seq', 'ctx')
- tokens_grad: bfloat16 [8, 2048, 2048], P('seq', 'ctx')
- attn_gain_grad: float32 [2048], P(('seq', 'ctx'))
- w_query_grad: float32 [2048, 1280], P(('seq', 'ctx'))
- w_key_grad: float32 [2048, 320], P(('seq', 'ctx'))
- w_value_grad: float32 [2048, 320], P(('seq', 'ctx'))
- query_gain_grad: float32 [64], replicated
- key_gain_grad: float32 [64], replicated
- w_out_grad: float32 [1280, 2048], P(('seq', 'ctx'))
- ffn_gain_grad: float32 [2048], P(('seq', 'ctx'))
- w_gate_grad: float32 [2048, 3584], P(('seq', 'ctx'))
- w_up_grad: float32 [2048, 3584], P(('seq', 'ctx'))
- w_down_grad: float32 [3584, 2048], P(('seq', 'ctx'))
Inputs may be any that keep to these rules, and one draw needn't show every extreme that they name: `doc_ids`: within a sequence ids never fall, and each document spans at most 1024 positions.
All inputs are finite; a program needn't handle non-finite values.
Results may differ from a plain program's by a relative error of at most 0.017.
Values may be sent and summed in bfloat16 or wider, within the bound.
No kernel may reach another device: no remote copies, remote signals or barrier semaphores. Data moves between devices by JAX's collectives and lax.ppermute only.
A program may use at most 512 MiB of HBM per device.

v0:
```python
import math

import jax
import jax.numpy as jnp
import numpy as np
from jax import lax
from jax.sharding import PartitionSpec as P

HEADS = 20
KV_HEADS = 5
HEAD_DIM = 64
QROWS = 512
TAGS = 4
Q_WIDTH = 1280
KV_WIDTH = 320


eps = 1e-06


def matmul(left, right):
    return jnp.dot(left, right, preferred_element_type=jnp.float32)


def dot_rows(left, right):
    return lax.dot_general(
        left, right, (((0,), (0,)), ((), ())), preferred_element_type=jnp.float32
    )


def dot_back(left, right):
    return lax.dot_general(
        left, right, (((1,), (1,)), ((), ())), preferred_element_type=jnp.float32
    )


def rms_scale(values_in, scale_gain):
    return (
        values_in
        * lax.rsqrt(jnp.mean(values_in * values_in, axis=-1, keepdims=True) + eps)
        * scale_gain
    )


def rotary(positions):
    half_dim = HEAD_DIM // 2
    frequency = jnp.exp(
        jnp.arange(half_dim, dtype=jnp.float32) * (-2.0 * math.log(10000.0) / HEAD_DIM)
    )
    angles = positions.astype(jnp.float32)[:, None] * frequency[None, :]
    return (jnp.cos(angles)[:, None, :], jnp.sin(angles)[:, None, :])


def rotate(values_in, cosine, sine):
    half_dim = values_in.shape[-1] // 2
    first_half = values_in[..., :half_dim]
    second_half = values_in[..., half_dim:]
    return jnp.concatenate(
        [first_half * cosine - second_half * sine, second_half * cosine + first_half * sine],
        axis=-1,
    )


def slot_tables(members, head_slots):
    width_slots = members * head_slots
    group_size = HEADS // KV_HEADS
    heads_of = np.full(width_slots, HEADS, dtype=np.int32)
    groups_of = np.full(width_slots, KV_HEADS, dtype=np.int32)
    place = np.zeros(HEADS, dtype=np.int32)
    member = np.zeros((width_slots, KV_HEADS), dtype=np.float32)
    for head_index in range(HEADS):
        position = head_index % members * head_slots + head_index // members
        heads_of[position] = head_index
        groups_of[position] = head_index // group_size
        place[head_index] = position
        member[position, head_index // group_size] = 1.0
    return (heads_of, groups_of, place, member)


def block_scores(query_part, keys, doc_row, block_start, block_end):
    raw_scores = jnp.einsum(
        "qsd,ksd->sqk", query_part, keys[:block_end], preferred_element_type=jnp.float32
    )
    positions = jnp.arange(block_end, dtype=jnp.int32)
    allowed = (positions[None, :] <= positions[block_start:block_end, None]) & (
        doc_row[None, :block_end] == doc_row[block_start:block_end, None]
    )
    return jnp.where(allowed[None], 0.125 * raw_scores, -1e30)


def attend_forward(query, keys, values, doc_row):
    length = query.shape[0]
    block_rows = min(QROWS, length)
    outputs = []
    log_parts = []
    for block_index in range(length // block_rows):
        block_start = block_index * block_rows
        block_end = block_start + block_rows
        masked = block_scores(query[block_start:block_end], keys, doc_row, block_start, block_end)
        row_max = jnp.max(masked, axis=-1, keepdims=True)
        exp_scores = jnp.exp(masked - row_max)
        totals = jnp.sum(exp_scores, axis=-1, keepdims=True)
        attn_probs = (exp_scores / totals).astype(jnp.bfloat16)
        outputs.append(
            jnp.einsum(
                "sqk,ksd->qsd", attn_probs, values[:block_end], preferred_element_type=jnp.float32
            )
        )
        log_parts.append((row_max + jnp.log(totals))[..., 0])
    return (jnp.concatenate(outputs, 0).astype(jnp.bfloat16), jnp.concatenate(log_parts, 1))


def attend_backward(query, keys, values, doc_row, log_sums, grad_mixed):
    length = query.shape[0]
    block_rows = min(QROWS, length)
    grad_keys = jnp.zeros(keys.shape, jnp.float32)
    grad_values = jnp.zeros(values.shape, jnp.float32)
    query_parts = []
    for block_index in range(length // block_rows):
        block_start = block_index * block_rows
        block_end = block_start + block_rows
        query_part = query[block_start:block_end]
        masked = block_scores(query_part, keys, doc_row, block_start, block_end)
        attn_probs = jnp.exp(masked - log_sums[:, block_start:block_end, None])
        grad_part = grad_mixed[block_start:block_end]
        grad_values = grad_values.at[:block_end].add(
            jnp.einsum(
                "sqk,qsd->ksd",
                attn_probs.astype(jnp.bfloat16),
                grad_part,
                preferred_element_type=jnp.float32,
            )
        )
        grad_probs = jnp.einsum(
            "qsd,ksd->sqk", grad_part, values[:block_end], preferred_element_type=jnp.float32
        )
        centre = jnp.sum(attn_probs * grad_probs, axis=-1, keepdims=True)
        grad_scores = (0.125 * attn_probs * (grad_probs - centre)).astype(jnp.bfloat16)
        query_parts.append(
            jnp.einsum(
                "sqk,ksd->qsd", grad_scores, keys[:block_end], preferred_element_type=jnp.float32
            )
        )
        grad_keys = grad_keys.at[:block_end].add(
            jnp.einsum("sqk,qsd->ksd", grad_scores, query_part, preferred_element_type=jnp.float32)
        )
    grad_query = jnp.concatenate(query_parts, 0)
    return (
        grad_query.astype(jnp.bfloat16),
        grad_keys.astype(jnp.bfloat16),
        grad_values.astype(jnp.bfloat16),
    )


def per_device(
    tokens,
    out_grad,
    doc_ids,
    corpus,
    corpus_weight,
    attn_gain,
    w_query,
    w_key,
    w_value,
    query_gain,
    key_gain,
    w_out,
    ffn_gain,
    w_gate,
    w_up,
    w_down,
):
    members = lax.axis_size("ctx")
    head_slots = (HEADS + members - 1) // members
    heads_of, groups_of, place, member = slot_tables(members, head_slots)
    batches, local_len, model_width = tokens.shape
    length = local_len * members
    cosine, sine = rotary(
        lax.axis_index("ctx") * local_len + jnp.arange(local_len, dtype=jnp.int32)
    )
    full_ids = lax.all_gather(doc_ids, "ctx", axis=1, tiled=True)
    query_gain_f = query_gain.astype(jnp.float32)
    key_gain_f = key_gain.astype(jnp.float32)
    tag_range = jnp.arange(TAGS, dtype=jnp.int32)
    slot_shape = (length, head_slots, HEAD_DIM)
    zero_head = jnp.zeros((local_len, 1, HEAD_DIM), jnp.bfloat16)
    shards = (attn_gain, w_query, w_key, w_value, w_out, ffn_gain, w_gate, w_up, w_down)

    def query_path(lin_values, scale_gain):
        return rotate(
            rms_scale(lin_values.reshape(local_len, HEADS, HEAD_DIM), scale_gain), cosine, sine
        )

    def key_path(lin_values, scale_gain):
        return rotate(
            rms_scale(lin_values.reshape(local_len, KV_HEADS, HEAD_DIM), scale_gain), cosine, sine
        )

    def to_slots(per_head, table):
        return jnp.concatenate([per_head, zero_head], 1)[:, table].reshape(
            local_len, members * head_slots * HEAD_DIM
        )

    def micro(micro_index, weights):
        gain_attn, wq_full, wk_full, wv_full, wo_full, gain_ffn, wg_full, wu_full, wd_full = weights
        inputs_f = lax.dynamic_index_in_dim(tokens, micro_index, 0, keepdims=False).astype(
            jnp.float32
        )
        doc_row = lax.dynamic_index_in_dim(full_ids, micro_index, 0, keepdims=False)
        corpus_tag = lax.dynamic_index_in_dim(corpus, micro_index, 0, keepdims=False)
        normed, norm_back = jax.vjp(rms_scale, inputs_f, gain_attn.astype(jnp.float32))
        normed_low = normed.astype(jnp.bfloat16)
        query_lin = matmul(normed_low, wq_full)
        key_lin = matmul(normed_low, wk_full)
        value_lin = matmul(normed_low, wv_full)
        query_rot, query_back = jax.vjp(query_path, query_lin, query_gain_f)
        key_rot, key_back = jax.vjp(key_path, key_lin, key_gain_f)
        query_low = query_rot.astype(jnp.bfloat16)
        key_low = key_rot.astype(jnp.bfloat16)
        value_low = value_lin.astype(jnp.bfloat16).reshape(local_len, KV_HEADS, HEAD_DIM)
        query_heads, key_heads, value_heads = (
            lax.all_to_all(
                to_slots(query_low, heads_of), "ctx", split_axis=1, concat_axis=0, tiled=True
            ),
            lax.all_to_all(
                to_slots(key_low, groups_of), "ctx", split_axis=1, concat_axis=0, tiled=True
            ),
            lax.all_to_all(
                to_slots(value_low, groups_of), "ctx", split_axis=1, concat_axis=0, tiled=True
            ),
        )
        query_heads = query_heads.reshape(slot_shape)
        key_heads = key_heads.reshape(slot_shape)
        value_heads = value_heads.reshape(slot_shape)
        mixed_heads, log_sums = attend_forward(query_heads, key_heads, value_heads, doc_row)
        mixed_back = lax.all_to_all(
            mixed_heads.reshape(length, head_slots * HEAD_DIM),
            "ctx",
            split_axis=0,
            concat_axis=1,
            tiled=True,
        )
        mixed = mixed_back.reshape(local_len, members * head_slots, HEAD_DIM)[:, place].reshape(
            local_len, Q_WIDTH
        )
        resid = inputs_f + matmul(mixed, wo_full)
        normed_ffn, ffn_back = jax.vjp(rms_scale, resid, gain_ffn.astype(jnp.float32))
        ffn_low = normed_ffn.astype(jnp.bfloat16)
        gate_lin = matmul(ffn_low, wg_full)
        up_lin = matmul(ffn_low, wu_full)

        def swiglu(gate_in, up_in):
            return jax.nn.silu(gate_in) * up_in

        hidden, swiglu_back = jax.vjp(swiglu, gate_lin, up_lin)
        hidden_low = hidden.astype(jnp.bfloat16)
        result = resid + matmul(hidden_low, wd_full)
        scale = jnp.sum(
            jnp.where(tag_range == corpus_tag, corpus_weight, jnp.zeros_like(corpus_weight))
        )
        grad_res = scale * lax.dynamic_index_in_dim(
            out_grad, micro_index, 0, keepdims=False
        ).astype(jnp.float32)
        grad_res_low = grad_res.astype(jnp.bfloat16)
        grad_wdown = dot_rows(hidden_low, grad_res_low)
        grad_hidden = dot_back(grad_res_low, wd_full)
        grad_gate, grad_up = swiglu_back(grad_hidden)
        gate_low = grad_gate.astype(jnp.bfloat16)
        up_low = grad_up.astype(jnp.bfloat16)
        grad_wgate = dot_rows(ffn_low, gate_low)
        grad_wup = dot_rows(ffn_low, up_low)
        grad_normed_ffn = dot_back(gate_low, wg_full) + dot_back(up_low, wu_full)
        grad_resid_part, grad_gain_ffn = ffn_back(grad_normed_ffn)
        grad_resid = grad_res + grad_resid_part
        resid_low = grad_resid.astype(jnp.bfloat16)
        grad_wout = dot_rows(mixed, resid_low)
        grad_mixed = (
            dot_back(resid_low, wo_full).astype(jnp.bfloat16).reshape(local_len, HEADS, HEAD_DIM)
        )
        grad_mixed_heads = lax.all_to_all(
            to_slots(grad_mixed, heads_of), "ctx", split_axis=1, concat_axis=0, tiled=True
        ).reshape(slot_shape)
        grad_query_h, grad_key_h, grad_value_h = attend_backward(
            query_heads, key_heads, value_heads, doc_row, log_sums, grad_mixed_heads
        )
        flat_shape = (length, head_slots * HEAD_DIM)
        grad_query_t, grad_key_t, grad_value_t = (
            lax.all_to_all(
                grad_query_h.reshape(flat_shape), "ctx", split_axis=0, concat_axis=1, tiled=True
            ),
            lax.all_to_all(
                grad_key_h.reshape(flat_shape), "ctx", split_axis=0, concat_axis=1, tiled=True
            ),
            lax.all_to_all(
                grad_value_h.reshape(flat_shape), "ctx", split_axis=0, concat_axis=1, tiled=True
            ),
        )
        tok_shape = (local_len, members * head_slots, HEAD_DIM)
        grad_query_rot = grad_query_t.reshape(tok_shape)[:, place].astype(jnp.float32)
        grad_key_rot = jnp.einsum(
            "lpd,pg->lgd", grad_key_t.reshape(tok_shape).astype(jnp.float32), member
        )
        grad_value_sum = jnp.einsum(
            "lpd,pg->lgd", grad_value_t.reshape(tok_shape).astype(jnp.float32), member
        )
        grad_query_lin, grad_query_gain = query_back(grad_query_rot)
        grad_key_lin, grad_key_gain = key_back(grad_key_rot)
        query_lin_low = grad_query_lin.astype(jnp.bfloat16)
        key_lin_low = grad_key_lin.astype(jnp.bfloat16)
        value_lin_low = grad_value_sum.reshape(local_len, KV_WIDTH).astype(jnp.bfloat16)
        grad_wquery = dot_rows(normed_low, query_lin_low)
        grad_wkey = dot_rows(normed_low, key_lin_low)
        grad_wvalue = dot_rows(normed_low, value_lin_low)
        grad_normed = (
            dot_back(query_lin_low, wq_full)
            + dot_back(key_lin_low, wk_full)
            + dot_back(value_lin_low, wv_full)
        )
        grad_input_part, grad_gain_attn = norm_back(grad_normed)
        grad_inputs = grad_resid + grad_input_part
        gradients = (
            grad_gain_attn,
            grad_wquery,
            grad_wkey,
            grad_wvalue,
            grad_wout,
            grad_gain_ffn,
            grad_wgate,
            grad_wup,
            grad_wdown,
        )
        return (
            result.astype(jnp.bfloat16),
            grad_inputs.astype(jnp.bfloat16),
            gradients,
            (grad_query_gain, grad_key_gain),
        )

    row_factor = lax.axis_size(("seq", "ctx"))

    def advance(micro_index, carried):
        outputs, input_grads, totals, small_totals = carried
        weights = (
            lax.all_gather(attn_gain, ("seq", "ctx"), axis=0, tiled=True),
            lax.all_gather(w_query, ("seq", "ctx"), axis=0, tiled=True),
            lax.all_gather(w_key, ("seq", "ctx"), axis=0, tiled=True),
            lax.all_gather(w_value, ("seq", "ctx"), axis=0, tiled=True),
            lax.all_gather(w_out, ("seq", "ctx"), axis=0, tiled=True),
            lax.all_gather(ffn_gain, ("seq", "ctx"), axis=0, tiled=True),
            lax.all_gather(w_gate, ("seq", "ctx"), axis=0, tiled=True),
            lax.all_gather(w_up, ("seq", "ctx"), axis=0, tiled=True),
            lax.all_gather(w_down, ("seq", "ctx"), axis=0, tiled=True),
        )
        result, grad_inputs, gradients, small_grads = micro(micro_index, weights)
        outputs = lax.dynamic_update_index_in_dim(outputs, result, micro_index, 0)
        input_grads = lax.dynamic_update_index_in_dim(input_grads, grad_inputs, micro_index, 0)
        totals = tuple((older + newer for older, newer in zip(totals, gradients)))
        small_totals = tuple((older + newer for older, newer in zip(small_totals, small_grads)))
        return (outputs, input_grads, totals, small_totals)

    initial_totals = tuple(
        (
            jnp.zeros((shard.shape[0] * row_factor,) + shard.shape[1:], jnp.float32)
            for shard in shards
        )
    )
    initial_small = (jnp.zeros((HEAD_DIM,), jnp.float32), jnp.zeros((HEAD_DIM,), jnp.float32))
    initial = (
        jnp.zeros(tokens.shape, jnp.bfloat16),
        jnp.zeros(tokens.shape, jnp.bfloat16),
        initial_totals,
        initial_small,
    )
    outputs, input_grads, totals, small_totals = lax.fori_loop(0, batches, advance, initial)
    totals = lax.psum_scatter(totals, ("seq", "ctx"), scatter_dimension=0, tiled=True)
    query_gain_grad, key_gain_grad = lax.psum((small_totals[0], small_totals[1]), ("seq", "ctx"))
    return (
        outputs,
        input_grads,
        totals[0],
        totals[1],
        totals[2],
        totals[3],
        query_gain_grad,
        key_gain_grad,
        totals[4],
        totals[5],
        totals[6],
        totals[7],
        totals[8],
    )


def solution(mesh):
    in_specs = (
        P("seq", "ctx", None),
        P("seq", "ctx", None),
        P("seq", "ctx"),
        P("seq"),
        P(),
        P(("seq", "ctx")),
        P(("seq", "ctx"), None),
        P(("seq", "ctx"), None),
        P(("seq", "ctx"), None),
        P(),
        P(),
        P(("seq", "ctx"), None),
        P(("seq", "ctx")),
        P(("seq", "ctx"), None),
        P(("seq", "ctx"), None),
        P(("seq", "ctx"), None),
    )
    out_specs = (
        P("seq", "ctx", None),
        P("seq", "ctx", None),
        P(("seq", "ctx")),
        P(("seq", "ctx"), None),
        P(("seq", "ctx"), None),
        P(("seq", "ctx"), None),
        P(),
        P(),
        P(("seq", "ctx"), None),
        P(("seq", "ctx")),
        P(("seq", "ctx"), None),
        P(("seq", "ctx"), None),
        P(("seq", "ctx"), None),
    )
    return jax.shard_map(
        per_device, mesh=mesh, in_specs=in_specs, out_specs=out_specs, check_vma=False
    )
```

profile of v0, /device:TPU:0, one launch (start us, length us, event | category | flops | bytes accessed | tf_op | source)
XLA Modules:
  0.0 4293.7 jit_solution(16186195369262377414)
XLA Ops:
  8.7 28.1 all_gather.93
  38.6 1709.9 %while.68 = (s32[]{:T(128)}, bf16[2,256,2048]{2,1,0:T(8,128)(2,1)}, bf16[2,256,2048]{2,1,0:T(8,128)(2,1)}, f32[2048]{0:T(1024)}, f32[2048,1280]{1,0:T(8,128)}, /...) while((s32[]{:T(128)}, bf16[2,256,2048]{2,1,0:T(8,128)(2,1)}, ...), condition=%wide.region_26.27_spmd.clone.clone.clone.clone.clone, body=%wide.region_0.26_spmd.sunk.clone.clone.clone.clone.clone.sunk | while | flops 50221916160 | bytes 1582742272 | solution.py:374
  45.1 39.0 all-reduce.23
  86.5 10.3 all-gather.12.cloned.1.call-done
  106.9 50.7 %all-gather.8.cloned.1.call-done = bf16[2048,320]{1,0:T(8,128)(2,1)} async-done(((bf16[64,320]{1,0:T(8,128)(2,1)}), bf16[2048,320]{1,0:T(8,128)(2,1)}) %all-gather.8.cloned.1.call-update) | async-done | bytes 1310736 | tf_op jit(solution)/shard_map/while/body/eval_jaxpr/all_gather | solution.py:347
  161.3 63.4 %all-gather.10.cloned.1.call-done = bf16[2048,1280]{1,0:T(8,128)(2,1)} async-done(((bf16[64,1280]{1,0:T(8,128)(2,1)}), bf16[2048,1280]{1,0:T(8,128)(2,1)}) %all-gather.10.cloned.1.call-update) | async-done | bytes 5242896 | tf_op jit(solution)/shard_map/while/body/eval_jaxpr/all_gather | solution.py:345
  224.7 7.9 copy.196
  246.2 14.9 all-to-all-done
  338.6 6.3 fusion.466
  345.0 5.6 fusion.462
  354.8 5.9 all-to-all-start.3
  365.2 34.5 all-to-all-done.3
  406.4 15.3 all-gather.16.cloned.1.call-done
  421.7 9.0 fusion.472
  430.7 97.4 %all-gather.18.cloned.1.call-done = bf16[2048,3584]{1,0:T(8,128)(2,1)} async-done(((bf16[64,3584]{1,0:T(8,128)(2,1)}), bf16[2048,3584]{1,0:T(8,128)(2,1)}) %all-gather.18.cloned.1.call-update) | async-done | bytes 14680080 | tf_op jit(solution)/shard_map/while/body/eval_jaxpr/all_gather | solution.py:351
  528.2 9.0 fusion.473
  537.2 97.0 %all-gather.20.cloned.1.call-done = bf16[3584,2048]{1,0:T(8,128)(2,1)} async-done(((bf16[112,2048]{1,0:T(8,128)(2,1)}), bf16[3584,2048]{1,0:T(8,128)(2,1)}) %all-gather.20.cloned.1.call-update) | async-done | bytes 14680080 | tf_op jit(solution)/shard_map/while/body/eval_jaxpr/all_gather | solution.py:352
  634.2 12.0 multiply_convert_fusion.14
  646.2 9.5 fusion.476
  655.7 12.3 multiply_reduce_fusion.26
  682.9 13.4 select_add_fusion.16
  696.3 13.6 select_add_fusion.18
  709.9 13.4 select_add_fusion.17
  723.3 11.4 fusion.475
  757.5 5.9 multiply_convert_fusion.16
  780.4 5.9 all-to-all-start.6
  798.1 8.5 all-to-all-done.6
  819.6 6.7 fusion.489
  844.7 9.9 all-to-all-done.7
  888.9 38.1 all-reduce.23
  929.4 10.8 all-gather.12.cloned.1.call-done
  950.4 50.6 %all-gather.8.cloned.1.call-done = bf16[2048,320]{1,0:T(8,128)(2,1)} async-done(((bf16[64,320]{1,0:T(8,128)(2,1)}), bf16[2048,320]{1,0:T(8,128)(2,1)}) %all-gather.8.cloned.1.call-update) | async-done | bytes 1310736 | tf_op jit(solution)/shard_map/while/body/eval_jaxpr/all_gather | solution.py:347
  1004.7 63.2 %all-gather.10.cloned.1.call-done = bf16[2048,1280]{1,0:T(8,128)(2,1)} async-done(((bf16[64,1280]{1,0:T(8,128)(2,1)}), bf16[2048,1280]{1,0:T(8,128)(2,1)}) %all-gather.10.cloned.1.call-update) | async-done | bytes 5242896 | tf_op jit(solution)/shard_map/while/body/eval_jaxpr/all_gather | solution.py:345
  1067.9 7.9 copy.196
  1089.4 15.5 all-to-all-done
  1181.9 6.3 fusion.466
  1198.1 6.0 all-to-all-start.3
  1208.6 36.4 all-to-all-done.3
  1251.8 13.6 all-gather.16.cloned.1.call-done
  1265.4 9.0 fusion.472
  1274.4 97.6 %all-gather.18.cloned.1.call-done = bf16[2048,3584]{1,0:T(8,128)(2,1)} async-done(((bf16[64,3584]{1,0:T(8,128)(2,1)}), bf16[2048,3584]{1,0:T(8,128)(2,1)}) %all-gather.18.cloned.1.call-update) | async-done | bytes 14680080 | tf_op jit(solution)/shard_map/while/body/eval_jaxpr/all_gather | solution.py:351
  1372.0 9.0 fusion.473
  1381.0 96.9 %all-gather.20.cloned.1.call-done = bf16[3584,2048]{1,0:T(8,128)(2,1)} async-done(((bf16[112,2048]{1,0:T(8,128)(2,1)}), bf16[3584,2048]{1,0:T(8,128)(2,1)}) %all-gather.20.cloned.1.call-update) | async-done | bytes 14680080 | tf_op jit(solution)/shard_map/while/body/eval_jaxpr/all_gather | solution.py:352
  1477.8 12.0 multiply_convert_fusion.14
  1489.8 9.5 fusion.476
  1499.4 12.3 multiply_reduce_fusion.26
  1526.5 20.0 select_add_fusion.16
  1546.6 20.5 select_add_fusion.18
  1567.0 20.1 select_add_fusion.17
  1587.1 11.4 fusion.475
  1621.4 5.9 multiply_convert_fusion.16
  1644.2 5.9 all-to-all-start.6
  1661.9 8.5 all-to-all-done.6
  1683.4 6.7 fusion.489
  1698.8 9.4 select_add_fusion.15
  1712.5 5.9 all-to-all-done.7
  1759.7 38.3 all-reduce.21
  1799.2 56.9 %reduce-scatter.10.cloned.1.call-done = f32[64,320]{1,0:T(8,128)} async-done(((f32[2048,320]{1,0:T(8,128)}), f32[64,320]{1,0:T(8,128)}) %reduce-scatter.10.cloned.1.call-update) | async-done | bytes 81936 | tf_op jit(solution)/shard_map/reduce_scatter | solution.py:375
  1856.1 107.0 %reduce-scatter.12.cloned.1.call-done = f32[64,320]{1,0:T(8,128)} async-done(((f32[2048,320]{1,0:T(8,128)}), f32[64,320]{1,0:T(8,128)}) %reduce-scatter.12.cloned.1.call-update) | async-done | bytes 81936 | tf_op jit(solution)/shard_map/reduce_scatter | solution.py:375
  1963.1 230.2 %reduce-scatter.14.cloned.1.call-done = f32[40,2048]{1,0:T(8,128)} async-done(((f32[1280,2048]{1,0:T(8,128)}), f32[40,2048]{1,0:T(8,128)}) %reduce-scatter.14.cloned.1.call-update) | async-done | bytes 327696 | tf_op jit(solution)/shard_map/reduce_scatter | solution.py:375
  2193.3 229.4 %reduce-scatter.8.cloned.1.call-done = f32[64,1280]{1,0:T(8,128)} async-done(((f32[2048,1280]{1,0:T(8,128)}), f32[64,1280]{1,0:T(8,128)}) %reduce-scatter.8.cloned.1.call-update) | async-done | bytes 327696 | tf_op jit(solution)/shard_map/reduce_scatter | solution.py:375
  2422.7 620.5 %reduce-scatter.16.cloned.1.call-done = f32[64,3584]{1,0:T(8,128)} async-done(((f32[2048,3584]{1,0:T(8,128)}), f32[64,3584]{1,0:T(8,128)}) %reduce-scatter.16.cloned.1.call-update) | async-done | bytes 917520 | tf_op jit(solution)/shard_map/reduce_scatter | solution.py:375
  3043.1 621.6 %reduce-scatter.18.cloned.1.call-done = f32[64,3584]{1,0:T(8,128)} async-done(((f32[2048,3584]{1,0:T(8,128)}), f32[64,3584]{1,0:T(8,128)}) %reduce-scatter.18.cloned.1.call-update) | async-done | bytes 917520 | tf_op jit(solution)/shard_map/reduce_scatter | solution.py:375
  3664.8 621.5 %reduce-scatter.20.cloned.1.call-done = f32[112,2048]{1,0:T(8,128)} async-done(((f32[3584,2048]{1,0:T(8,128)}), f32[112,2048]{1,0:T(8,128)}) %reduce-scatter.20.cloned.1.call-update) | async-done | bytes 917520 | tf_op jit(solution)/shard_map/reduce_scatter | solution.py:375
  (939 shorter events, 518.8 us)
Async XLA Ops:
  38.6 60.6 %copy-start.109 = (f32[64]{0:T(128)}, f32[64]{0:T(128)S(1)}, u32[]{:S(2)}) copy-start(f32[64]{0:T(128)S(1)} %get-tuple-element.2352) | copy-start | bytes 772 | tf_op jit(solution)/shard_map/while
  38.6 202.5 %copy-start.111 = (f32[64]{0:T(128)}, f32[64]{0:T(128)S(1)}, u32[]{:S(2)}) copy-start(f32[64]{0:T(128)S(1)} %get-tuple-element.2350) | copy-start | bytes 772 | tf_op jit(solution)/shard_map/while
  38.6 227.4 %copy-start.82 = (s32[2,2048]{1,0:T(2,128)}, s32[2,2048]{1,0:T(2,128)S(1)}, u32[]{:S(2)}) copy-start(s32[2,2048]{1,0:T(2,128)S(1)} %get-tuple-element.2348) | copy-start | bytes 49156 | tf_op jit(solution)/shard_map/while
  38.6 47.0 %copy-start.120 = (s32[24]{0:T(128)S(1)}, s32[24]{0:T(128)}, u32[]{:S(2)}) copy-start(s32[24]{0:T(128)} %get-tuple-element.2367) | copy-start | bytes 292 | tf_op jit(solution)/shard_map/while
  38.6 58.2 %all-gather.12.cloned.1.call-start = ((), (), s32[]{:S(2)}) async-start(), calls=%async_computation.24 | async-start | bytes 1622016 | tf_op jit(solution)/shard_map/while/body/eval_jaxpr/all_gather | solution.py:346
  39.4 118.3 %all-gather.8.cloned.1.call-start = ((), (), s32[]{:S(2)}) async-start(), calls=%async_computation.22 | async-start | bytes 1622016 | tf_op jit(solution)/shard_map/while/body/eval_jaxpr/all_gather | solution.py:347
  40.1 184.6 %all-gather.10.cloned.1.call-start = ((), (), s32[]{:S(2)}) async-start(), calls=%async_computation.23 | async-start | bytes 5406720 | tf_op jit(solution)/shard_map/while/body/eval_jaxpr/all_gather | solution.py:345
  40.8 359.6 %all-gather.14.cloned.1.call-start = ((), (), s32[]{:S(2)}) async-start(), calls=%async_computation.25 | async-start | bytes 5406720 | tf_op jit(solution)/shard_map/while/body/eval_jaxpr/all_gather | solution.py:348
  41.4 380.3 %all-gather.16.cloned.1.call-start = ((), (), s32[]{:S(2)}) async-start(), calls=%async_computation.26 | async-start | bytes 15138816 | tf_op jit(solution)/shard_map/while/body/eval_jaxpr/all_gather | solution.py:350
  41.5 57.1 %copy-start.8 = (bf16[2,256,2048]{2,1,0:T(8,128)(2,1)S(1)}, bf16[2,256,2048]{2,1,0:T(8,128)(2,1)}, u32[]{:S(2)}) copy-start(bf16[2,256,2048]{2,1,0:T(8,128)(2,1)} %get-tuple-element.2345) | copy-start | bytes 6291460 | tf_op jit(solution)/shard_map/while
  42.0 486.2 %all-gather.18.cloned.1.call-start = ((), (), s32[]{:S(2)}) async-start(), calls=%async_computation.27 | async-start | bytes 15138816 | tf_op jit(solution)/shard_map/while/body/eval_jaxpr/all_gather | solution.py:351
  42.6 591.6 %all-gather.20.cloned.1.call-start = ((), (), s32[]{:S(2)}) async-start(), calls=%async_computation.28 | async-start | bytes 15138816 | tf_op jit(solution)/shard_map/while/body/eval_jaxpr/all_gather | solution.py:352
  84.0 152.8 %copy-start.67 = (f32[2048]{0:T(1024)}, f32[2048]{0:T(1024)S(1)}, u32[]{:S(2)}) copy-start(f32[2048]{0:T(1024)S(1)} %convert_element_type.995) | copy-start | bytes 24580 | tf_op jit(solution)/shard_map/while
  85.6 151.3 %copy-start.84 = (f32[256]{0:T(256)}, f32[256]{0:T(256)S(1)}, u32[]{:S(2)}) copy-start(f32[256]{0:T(256)S(1)} %fusion.448) | copy-start | bytes 3076 | tf_op jit(solution)/shard_map/while
  86.5 156.0 %copy-start.55 = (f32[256,32]{0,1:T(8,128)}, f32[256,32]{0,1:T(8,128)S(1)}, u32[]{:S(2)}) copy-start(f32[256,32]{0,1:T(8,128)S(1)} %get-tuple-element.2182) | copy-start | bytes 98308 | tf_op jit(solution)/shard_map/while
  86.5 156.0 %copy-start.57 = (f32[256,32]{0,1:T(8,128)}, f32[256,32]{0,1:T(8,128)S(1)}, u32[]{:S(2)}) copy-start(f32[256,32]{0,1:T(8,128)S(1)} %get-tuple-element.2181) | copy-start | bytes 98308 | tf_op jit(solution)/shard_map/while
  101.4 131.2 %all-to-all-start.2 = ((bf16[256,8,192]{0,2,1:T(8,128)(2,1)}), bf16[256,8,192]{0,2,1:T(8,128)(2,1)S(1)}, u32[]{:S(2)}, u32[]{:S(2)}) async-start(bf16[256,8,192]{0,2,1:T(8,128)(2,1)} %bitcast.616), calls=%async_computation.2 | async-start | bytes 1572864 | tf_op jit(solution)/shard_map/while/body/eval_jaxpr/all_to_all | solution.py:225
  105.9 137.7 %copy-start.108 = (s32[1024]{0:T(1024)}, s32[1024]{0:T(1024)S(1)}, u32[]{:S(2)}) copy-start(s32[1024]{0:T(1024)S(1)} %pad_clamp_fusion.7) | copy-start | bytes 12292 | tf_op jit(solution)/shard_map/while
  232.7 28.5 all-to-all-start
  261.2 41.6 all-to-all-start.1
  302.7 47.8 %copy-start.21 = (bf16[2048,3,64]{0,2,1:T(8,128)(2,1)}, bf16[2048,3,64]{0,2,1:T(8,128)(2,1)S(1)}, u32[]{:S(2)}) copy-start(bf16[2048,3,64]{0,2,1:T(8,128)(2,1)S(1)} %reshape.1788) | copy-start | bytes 2359300 | tf_op jit(solution)/shard_map/while
  354.8 44.8 %all-to-all-start.3 = ((bf16[8,256,192]{1,2,0:T(8,128)(2,1)}), bf16[8,256,192]{1,2,0:T(8,128)(2,1)S(1)}, u32[]{:S(2)}, u32[]{:S(2)}) async-start(bf16[8,256,192]{1,2,0:T(8,128)(2,1)} %bitcast.627), calls=%async_computation.3 | async-start | bytes 1572864 | tf_op jit(solution)/shard_map/while/body/eval_jaxpr/all_to_all | solution.py:236
  364.5 382.6 %copy-start.74 = (f32[3,512]{1,0:T(4,128)}, f32[3,512]{1,0:T(4,128)S(1)}, u32[]{:S(2)}) copy-start(f32[3,512]{1,0:T(4,128)S(1)} %log_add_fusion.10) | copy-start | bytes 18436 | tf_op jit(solution)/shard_map/while
  430.7 203.5 %copy-start.43 = (bf16[2,256,2048]{2,1,0:T(8,128)(2,1)S(1)}, bf16[2,256,2048]{2,1,0:T(8,128)(2,1)}, u32[]{:S(2)}) copy-start(bf16[2,256,2048]{2,1,0:T(8,128)(2,1)} %get-tuple-element.2360) | copy-start | bytes 6291460 | tf_op jit(solution)/shard_map/while
  678.7 56.0 %all-to-all-start.4 = ((bf16[256,8,192]{0,2,1:T(8,128)(2,1)}), bf16[256,8,192]{0,2,1:T(8,128)(2,1)}, u32[]{:S(2)}, u32[]{:S(2)}) async-start(bf16[256,8,192]{0,2,1:T(8,128)(2,1)} %bitcast.584), calls=%async_computation.4 | async-start | bytes 1572864 | tf_op jit(solution)/shard_map/while/body/eval_jaxpr/all_to_all | solution.py:280
  780.4 26.2 all-to-all-start.6
  806.6 23.9 all-to-all-start.5
  830.5 24.1 all-to-all-start.7
  882.4 60.2 %copy-start.109 = (f32[64]{0:T(128)}, f32[64]{0:T(128)S(1)}, u32[]{:S(2)}) copy-start(f32[64]{0:T(128)S(1)} %get-tuple-element.2352) | copy-start | bytes 772 | tf_op jit(solution)/shard_map/while
  882.4 201.9 %copy-start.111 = (f32[64]{0:T(128)}, f32[64]{0:T(128)S(1)}, u32[]{:S(2)}) copy-start(f32[64]{0:T(128)S(1)} %get-tuple-element.2350) | copy-start | bytes 772 | tf_op jit(solution)/shard_map/while
  882.4 227.1 %copy-start.82 = (s32[2,2048]{1,0:T(2,128)}, s32[2,2048]{1,0:T(2,128)S(1)}, u32[]{:S(2)}) copy-start(s32[2,2048]{1,0:T(2,128)S(1)} %get-tuple-element.2348) | copy-start | bytes 49156 | tf_op jit(solution)/shard_map/while
  882.4 46.0 %copy-start.120 = (s32[24]{0:T(128)S(1)}, s32[24]{0:T(128)}, u32[]{:S(2)}) copy-start(s32[24]{0:T(128)} %get-tuple-element.2367) | copy-start | bytes 292 | tf_op jit(solution)/shard_map/while
  882.4 57.8 %all-gather.12.cloned.1.call-start = ((), (), s32[]{:S(2)}) async-start(), calls=%async_computation.24 | async-start | bytes 1622016 | tf_op jit(solution)/shard_map/while/body/eval_jaxpr/all_gather | solution.py:346
  883.2 117.8 %all-gather.8.cloned.1.call-start = ((), (), s32[]{:S(2)}) async-start(), calls=%async_computation.22 | async-start | bytes 1622016 | tf_op jit(solution)/shard_map/while/body/eval_jaxpr/all_gather | solution.py:347
  883.9 184.0 %all-gather.10.cloned.1.call-start = ((), (), s32[]{:S(2)}) async-start(), calls=%async_computation.23 | async-start | bytes 5406720 | tf_op jit(solution)/shard_map/while/body/eval_jaxpr/all_gather | solution.py:345
  884.5 361.2 %all-gather.14.cloned.1.call-start = ((), (), s32[]{:S(2)}) async-start(), calls=%async_computation.25 | async-start | bytes 5406720 | tf_op jit(solution)/shard_map/while/body/eval_jaxpr/all_gather | solution.py:348
  885.2 380.1 %all-gather.16.cloned.1.call-start = ((), (), s32[]{:S(2)}) async-start(), calls=%async_computation.26 | async-start | bytes 15138816 | tf_op jit(solution)/shard_map/while/body/eval_jaxpr/all_gather | solution.py:350
  885.3 56.6 %copy-start.8 = (bf16[2,256,2048]{2,1,0:T(8,128)(2,1)S(1)}, bf16[2,256,2048]{2,1,0:T(8,128)(2,1)}, u32[]{:S(2)}) copy-start(bf16[2,256,2048]{2,1,0:T(8,128)(2,1)} %get-tuple-element.2345) | copy-start | bytes 6291460 | tf_op jit(solution)/shard_map/while
  885.8 486.2 %all-gather.18.cloned.1.call-start = ((), (), s32[]{:S(2)}) async-start(), calls=%async_computation.27 | async-start | bytes 15138816 | tf_op jit(solution)/shard_map/while/body/eval_jaxpr/all_gather | solution.py:351
  886.6 591.3 %all-gather.20.cloned.1.call-start = ((), (), s32[]{:S(2)}) async-start(), calls=%async_computation.28 | async-start | bytes 15138816 | tf_op jit(solution)/shard_map/while/body/eval_jaxpr/all_gather | solution.py:352
  926.9 153.2 %copy-start.67 = (f32[2048]{0:T(1024)}, f32[2048]{0:T(1024)S(1)}, u32[]{:S(2)}) copy-start(f32[2048]{0:T(1024)S(1)} %convert_element_type.995) | copy-start | bytes 24580 | tf_op jit(solution)/shard_map/while
  928.5 151.6 %copy-start.84 = (f32[256]{0:T(256)}, f32[256]{0:T(256)S(1)}, u32[]{:S(2)}) copy-start(f32[256]{0:T(256)S(1)} %fusion.448) | copy-start | bytes 3076 | tf_op jit(solution)/shard_map/while
  929.4 156.3 %copy-start.55 = (f32[256,32]{0,1:T(8,128)}, f32[256,32]{0,1:T(8,128)S(1)}, u32[]{:S(2)}) copy-start(f32[256,32]{0,1:T(8,128)S(1)} %get-tuple-element.2182) | copy-start | bytes 98308 | tf_op jit(solution)/shard_map/while
  929.4 156.3 %copy-start.57 = (f32[256,32]{0,1:T(8,128)}, f32[256,32]{0,1:T(8,128)S(1)}, u32[]{:S(2)}) copy-start(f32[256,32]{0,1:T(8,128)S(1)} %get-tuple-element.2181) | copy-start | bytes 98308 | tf_op jit(solution)/shard_map/while
  944.8 131.0 %all-to-all-start.2 = ((bf16[256,8,192]{0,2,1:T(8,128)(2,1)}), bf16[256,8,192]{0,2,1:T(8,128)(2,1)S(1)}, u32[]{:S(2)}, u32[]{:S(2)}) async-start(bf16[256,8,192]{0,2,1:T(8,128)(2,1)} %bitcast.616), calls=%async_computation.2 | async-start | bytes 1572864 | tf_op jit(solution)/shard_map/while/body/eval_jaxpr/all_to_all | solution.py:225
  949.4 137.4 %copy-start.108 = (s32[1024]{0:T(1024)}, s32[1024]{0:T(1024)S(1)}, u32[]{:S(2)}) copy-start(s32[1024]{0:T(1024)S(1)} %pad_clamp_fusion.7) | copy-start | bytes 12292 | tf_op jit(solution)/shard_map/while
  1075.9 29.0 all-to-all-start
  1104.9 41.3 all-to-all-start.1
  1138.3 29.0 copy-start.19
  1146.2 47.7 %copy-start.21 = (bf16[2048,3,64]{0,2,1:T(8,128)(2,1)}, bf16[2048,3,64]{0,2,1:T(8,128)(2,1)S(1)}, u32[]{:S(2)}) copy-start(bf16[2048,3,64]{0,2,1:T(8,128)(2,1)S(1)} %reshape.1788) | copy-start | bytes 2359300 | tf_op jit(solution)/shard_map/while
  1198.1 46.8 %all-to-all-start.3 = ((bf16[8,256,192]{1,2,0:T(8,128)(2,1)}), bf16[8,256,192]{1,2,0:T(8,128)(2,1)S(1)}, u32[]{:S(2)}, u32[]{:S(2)}) async-start(bf16[8,256,192]{1,2,0:T(8,128)(2,1)} %bitcast.627), calls=%async_computation.3 | async-start | bytes 1572864 | tf_op jit(solution)/shard_map/while/body/eval_jaxpr/all_to_all | solution.py:236
  1207.9 403.0 %copy-start.74 = (f32[3,512]{1,0:T(4,128)}, f32[3,512]{1,0:T(4,128)S(1)}, u32[]{:S(2)}) copy-start(f32[3,512]{1,0:T(4,128)S(1)} %log_add_fusion.10) | copy-start | bytes 18436 | tf_op jit(solution)/shard_map/while
  1274.4 203.5 %copy-start.43 = (bf16[2,256,2048]{2,1,0:T(8,128)(2,1)S(1)}, bf16[2,256,2048]{2,1,0:T(8,128)(2,1)}, u32[]{:S(2)}) copy-start(bf16[2,256,2048]{2,1,0:T(8,128)(2,1)} %get-tuple-element.2360) | copy-start | bytes 6291460 | tf_op jit(solution)/shard_map/while
  1522.3 76.2 %all-to-all-start.4 = ((bf16[256,8,192]{0,2,1:T(8,128)(2,1)}), bf16[256,8,192]{0,2,1:T(8,128)(2,1)}, u32[]{:S(2)}, u32[]{:S(2)}) async-start(bf16[256,8,192]{0,2,1:T(8,128)(2,1)} %bitcast.584), calls=%async_computation.4 | async-start | bytes 1572864 | tf_op jit(solution)/shard_map/while/body/eval_jaxpr/all_to_all | solution.py:280
  1644.2 26.2 all-to-all-start.6
  1670.4 23.9 all-to-all-start.5
  1694.3 24.1 all-to-all-start.7
  1748.5 107.6 %reduce-scatter.10.cloned.1.call-start = ((), (), s32[]{:S(2)}) async-start(), calls=%async_computation.16 | async-start | bytes 3244032 | tf_op jit(solution)/shard_map/reduce_scatter | solution.py:375
  1752.1 211.0 %reduce-scatter.12.cloned.1.call-start = ((), (), s32[]{:S(2)}) async-start(), calls=%async_computation.17 | async-start | bytes 3244032 | tf_op jit(solution)/shard_map/reduce_scatter | solution.py:375
  1756.1 437.2 %reduce-scatter.14.cloned.1.call-start = ((), (), s32[]{:S(2)}) async-start(), calls=%async_computation.18 | async-start | bytes 10813440 | tf_op jit(solution)/shard_map/reduce_scatter | solution.py:375
  1756.7 666.0 %reduce-scatter.8.cloned.1.call-start = ((), (), s32[]{:S(2)}) async-start(), calls=%async_computation.15 | async-start | bytes 10813440 | tf_op jit(solution)/shard_map/reduce_scatter | solution.py:375
  1757.5 1285.7 %reduce-scatter.16.cloned.1.call-start = ((), (), s32[]{:S(2)}) async-start(), calls=%async_computation.19 | async-start | bytes 30277632 | tf_op jit(solution)/shard_map/reduce_scatter | solution.py:375
  1758.2 1906.6 %reduce-scatter.18.cloned.1.call-start = ((), (), s32[]{:S(2)}) async-start(), calls=%async_computation.20 | async-start | bytes 30277632 | tf_op jit(solution)/shard_map/reduce_scatter | solution.py:375
  1758.9 2527.3 %reduce-scatter.20.cloned.1.call-start = ((), (), s32[]{:S(2)}) async-start(), calls=%async_computation.21 | async-start | bytes 30277632 | tf_op jit(solution)/shard_map/reduce_scatter | solution.py:375
  (238 other events, 1345.1 us)
Sparse Core Ops, SparseCore 0:
  42.4 54.3 all-gather.11
  99.8 57.7 all-gather.7
  160.5 64.2 all-gather.9
  227.4 75.1 all-gather.13
  305.4 116.3 all-gather.15
  424.4 103.7 all-gather.17
  531.0 103.1 all-gather.19
  886.2 53.9 all-gather.11
  943.2 57.7 all-gather.7
  1003.7 64.2 all-gather.9
  1070.8 75.0 all-gather.13
  1148.5 116.7 all-gather.15
  1268.2 103.7 all-gather.17
  1374.7 103.1 all-gather.19
Sparse Core Ops, SparseCore 1:
  1755.0 101.0 reduce-scatter.9
  1861.9 101.1 reduce-scatter.11
  1965.8 227.4 reduce-scatter.13
  2196.2 226.4 reduce-scatter.7
  2425.6 617.5 reduce-scatter.15
  3046.0 618.7 reduce-scatter.17
  3667.5 618.7 reduce-scatter.19
where the time goes:
time: 4300 us; the launch traced here: 4290 us
  waiting for transfers between devices  3310 us (77%)
  matrix products  450 us (10%)
  local copies, waits for them, and re-layouts  207 us (5%)
  blocking collectives  143 us (3%)
  other arithmetic  88.5 us (2%)
  starting transfers between devices  75.6 us (2%)
    reduce_scatter x7, waiting for transfers between devices, per_device(): lax.psum_scatter(totals, ('seq', 'ctx'), scatter_dimension=0, tiled=True)  2490 us
    all_gather x2, waiting for transfers between devices, advance(): lax.all_gather(w_up, ('seq', 'ctx'), axis=0, tiled=True)  195 us
    all_gather x2, waiting for transfers between devices, advance(): lax.all_gather(w_down, ('seq', 'ctx'), axis=0, tiled=True)  194 us
    dot_general x14, matrix products, dot_rows(): lax.dot_general(left, right, (((0,), (0,)), ((), ())), preferred_element_...  129 us
    all_gather x2, waiting for transfers between devices, advance(): lax.all_gather(w_query, ('seq', 'ctx'), axis=0, tiled=True)  127 us
    all_gather x2, waiting for transfers between devices, advance(): lax.all_gather(w_value, ('seq', 'ctx'), axis=0, tiled=True)  101 us
    dot_general x14, matrix products, dot_back(): lax.dot_general(left, right, (((1,), (1,)), ((), ())), preferred_element_...  88.2 us
  transfers between devices with their start and end apart: 37, of which 29 were waited for; matrix products, arithmetic and copies ran while one was open for 11% of the time, Pallas kernels for 0%

commit v1 on v0

v1 whole, which is shorter than its diff:
```python
import functools
import math

import jax
import jax.numpy as jnp
import numpy as np
from jax import lax
from jax.experimental import pallas as pl
from jax.experimental.pallas import tpu as pltpu
from jax.sharding import Mesh
from jax.sharding import PartitionSpec as P

HEADS = 20
KV_HEADS = 5
GROUP = HEADS // KV_HEADS
HEAD_DIM = 64
TAGS = 4
Q_WIDTH = HEADS * HEAD_DIM
KV_WIDTH = KV_HEADS * HEAD_DIM
DOC_MOST = 1024
Z_CHIPS = 4
EPS = 1e-06
SCORE_SCALE = 0.125
LOG2E = math.log2(math.e)
MASKED = -1e30
KEY_BLOCK = 256

bf16 = jnp.bfloat16
f32 = jnp.float32


def dot(left, right, left_dim, right_dim):
    return lax.dot_general(
        left, right, (((left_dim,), (right_dim,)), ((), ())), preferred_element_type=f32
    )


def matmul(left, right):
    return dot(left, right, 1, 0)


def forward_kernel(meta, start_ref, q_ref, k_ref, v_ref, o_ref, lse_ref, bias_ref, q_rows, v_rows, acc):
    rows = q_ref.shape[1]
    window = k_ref.shape[1]
    low, high, q_start = meta[0], meta[1], meta[2]

    @pl.when(pl.program_id(0) == 0)
    def _():
        q_pos = q_start + lax.broadcasted_iota(jnp.int32, (rows, KEY_BLOCK), 0)
        lanes = lax.broadcasted_iota(jnp.int32, (rows, KEY_BLOCK), 1)

        def fill(block, carry):
            key_pos = block * KEY_BLOCK + lanes
            allowed = (key_pos >= start_ref[...]) & (key_pos <= q_pos)
            bias_ref[block] = jnp.where(allowed, 0.0, MASKED)
            return carry

        lax.fori_loop(low, high, fill, 0)

    q_cols = q_ref[...].T
    for head in range(GROUP):
        q_rows[head] = q_cols[:, head * HEAD_DIM : (head + 1) * HEAD_DIM]
    sub = lax.broadcasted_iota(jnp.int32, (HEAD_DIM, window), 0)
    ones = jnp.where(sub == 0, 1.0, 0.0).astype(bf16)
    v_rows[...] = jnp.concatenate([v_ref[...], ones], axis=0).T
    acc[...] = jnp.zeros_like(acc)

    def body(block, carry):
        at = pl.multiple_of(block * KEY_BLOCK, KEY_BLOCK)
        key_cols = k_ref[:, pl.ds(at, KEY_BLOCK)]
        value_rows = v_rows[pl.ds(at, KEY_BLOCK), :]
        bias = bias_ref[block]
        for head in range(GROUP):
            raw = jnp.dot(q_rows[head], key_cols, preferred_element_type=f32)
            probs = jnp.exp2(raw * (SCORE_SCALE * LOG2E) + bias).astype(bf16)
            acc[head] += jnp.dot(probs, value_rows, preferred_element_type=f32)
        return carry

    lax.fori_loop(low, high, body, 0)
    for head in range(GROUP):
        turned = acc[head].T
        total = turned[HEAD_DIM : HEAD_DIM + 1, :]
        o_ref[head * HEAD_DIM : (head + 1) * HEAD_DIM, :] = (turned[:HEAD_DIM] / total).astype(bf16)
        lse_ref[0, head : head + 1, :] = jnp.log2(total)


def backward_kernel(
    meta, start_ref, q_ref, k_ref, v_ref, go_ref, o_ref, lse_ref,
    dq_ref, dk_ref, dv_ref, bias_ref, q_rows, go_rows, k_rows, v_rows, dq_acc, delta_ref,
):
    rows = q_ref.shape[1]
    low, high, q_start = meta[0], meta[1], meta[2]

    @pl.when(pl.program_id(0) == 0)
    def _():
        q_pos = q_start + lax.broadcasted_iota(jnp.int32, (KEY_BLOCK, rows), 1)
        subs = lax.broadcasted_iota(jnp.int32, (KEY_BLOCK, rows), 0)

        def fill(block, carry):
            key_pos = block * KEY_BLOCK + subs
            allowed = (key_pos >= start_ref[...]) & (key_pos <= q_pos)
            bias_ref[block] = jnp.where(allowed, 0.0, MASKED)
            return carry

        lax.fori_loop(low, high, fill, 0)

    q_cols = q_ref[...].T
    go_cols = go_ref[...].T
    for head in range(GROUP):
        part = slice(head * HEAD_DIM, (head + 1) * HEAD_DIM)
        q_rows[head] = q_cols[:, part]
        go_rows[head] = go_cols[:, part]
        delta_ref[head : head + 1, :] = jnp.sum(
            go_ref[part, :].astype(f32) * o_ref[part, :].astype(f32), axis=0, keepdims=True
        )
    k_rows[...] = k_ref[...].T
    v_rows[...] = v_ref[...].T
    dk_ref[...] = jnp.zeros_like(dk_ref)
    dv_ref[...] = jnp.zeros_like(dv_ref)
    dq_acc[...] = jnp.zeros_like(dq_acc)

    def body(block, carry):
        at = pl.multiple_of(block * KEY_BLOCK, KEY_BLOCK)
        key_cols = k_ref[:, pl.ds(at, KEY_BLOCK)]
        key_rows = k_rows[pl.ds(at, KEY_BLOCK), :]
        value_rows = v_rows[pl.ds(at, KEY_BLOCK), :]
        bias = bias_ref[block]
        dk = jnp.zeros((KEY_BLOCK, HEAD_DIM), f32)
        dv = jnp.zeros((KEY_BLOCK, HEAD_DIM), f32)
        for head in range(GROUP):
            part = slice(head * HEAD_DIM, (head + 1) * HEAD_DIM)
            raw = jnp.dot(key_rows, q_ref[part, :], preferred_element_type=f32)
            probs = jnp.exp2(
                raw * (SCORE_SCALE * LOG2E) + (bias - lse_ref[0, head : head + 1, :])
            )
            grad_probs = jnp.dot(value_rows, go_ref[part, :], preferred_element_type=f32)
            grad_scores = (probs * (grad_probs - delta_ref[head : head + 1, :])).astype(bf16)
            dv += jnp.dot(probs.astype(bf16), go_rows[head], preferred_element_type=f32)
            dk += jnp.dot(grad_scores, q_rows[head], preferred_element_type=f32)
            dq_acc[part, :] += jnp.dot(key_cols, grad_scores, preferred_element_type=f32)
        dk_ref[:, pl.ds(at, KEY_BLOCK)] = (SCORE_SCALE * dk).T.astype(bf16)
        dv_ref[:, pl.ds(at, KEY_BLOCK)] = dv.T.astype(bf16)
        return carry

    lax.fori_loop(low, high, body, 0)
    dq_ref[...] = (SCORE_SCALE * dq_acc[...]).astype(bf16)


def attend_forward(meta, start_col, q_t, kv_t):
    rows, window = q_t.shape[1], kv_t.shape[1]
    wide = GROUP * HEAD_DIM
    return pl.pallas_call(
        forward_kernel,
        name="attend_forward",
        grid_spec=pltpu.PrefetchScalarGridSpec(
            num_scalar_prefetch=1,
            grid=(KV_HEADS,),
            in_specs=[
                pl.BlockSpec((rows, 1), lambda g, m: (0, 0)),
                pl.BlockSpec((wide, rows), lambda g, m: (g, 0)),
                pl.BlockSpec((HEAD_DIM, window), lambda g, m: (g, 0)),
                pl.BlockSpec((HEAD_DIM, window), lambda g, m: (KV_HEADS + g, 0)),
            ],
            out_specs=[
                pl.BlockSpec((wide, rows), lambda g, m: (g, 0)),
                pl.BlockSpec((1, GROUP, rows), lambda g, m: (g, 0, 0)),
            ],
            scratch_shapes=[
                pltpu.VMEM((window // KEY_BLOCK, rows, KEY_BLOCK), f32),
                pltpu.VMEM((GROUP, rows, HEAD_DIM), bf16),
                pltpu.VMEM((window, 2 * HEAD_DIM), bf16),
                pltpu.VMEM((GROUP, rows, 2 * HEAD_DIM), f32),
            ],
        ),
        out_shape=[
            jax.ShapeDtypeStruct((Q_WIDTH, rows), bf16),
            jax.ShapeDtypeStruct((KV_HEADS, GROUP, rows), f32),
        ],
        cost_estimate=pl.CostEstimate(
            flops=4 * HEADS * rows * window * 128, bytes_accessed=4 * 1024 * 1024,
            transcendentals=HEADS * rows * window,
        ),
    )(meta, start_col, q_t, kv_t, kv_t)


def attend_backward(meta, start_row, q_t, kv_t, go_t, o_t, lse):
    rows, window = q_t.shape[1], kv_t.shape[1]
    wide = GROUP * HEAD_DIM
    return pl.pallas_call(
        backward_kernel,
        name="attend_backward",
        grid_spec=pltpu.PrefetchScalarGridSpec(
            num_scalar_prefetch=1,
            grid=(KV_HEADS,),
            in_specs=[
                pl.BlockSpec((1, rows), lambda g, m: (0, 0)),
                pl.BlockSpec((wide, rows), lambda g, m: (g, 0)),
                pl.BlockSpec((HEAD_DIM, window), lambda g, m: (g, 0)),
                pl.BlockSpec((HEAD_DIM, window), lambda g, m: (KV_HEADS + g, 0)),
                pl.BlockSpec((wide, rows), lambda g, m: (g, 0)),
                pl.BlockSpec((wide, rows), lambda g, m: (g, 0)),
                pl.BlockSpec((1, GROUP, rows), lambda g, m: (g, 0, 0)),
            ],
            out_specs=[
                pl.BlockSpec((wide, rows), lambda g, m: (g, 0)),
                pl.BlockSpec((HEAD_DIM, window), lambda g, m: (g, 0)),
                pl.BlockSpec((HEAD_DIM, window), lambda g, m: (g, 0)),
            ],
            scratch_shapes=[
                pltpu.VMEM((window // KEY_BLOCK, KEY_BLOCK, rows), f32),
                pltpu.VMEM((GROUP, rows, HEAD_DIM), bf16),
                pltpu.VMEM((GROUP, rows, HEAD_DIM), bf16),
                pltpu.VMEM((window, HEAD_DIM), bf16),
                pltpu.VMEM((window, HEAD_DIM), bf16),
                pltpu.VMEM((wide, rows), f32),
                pltpu.VMEM((8, rows), f32),
            ],
        ),
        out_shape=[
            jax.ShapeDtypeStruct((Q_WIDTH, rows), bf16),
            jax.ShapeDtypeStruct((KV_WIDTH, window), bf16),
            jax.ShapeDtypeStruct((KV_WIDTH, window), bf16),
        ],
        cost_estimate=pl.CostEstimate(
            flops=10 * HEADS * rows * window * 128, bytes_accessed=8 * 1024 * 1024,
            transcendentals=HEADS * rows * window,
        ),
    )(meta, start_row, q_t, kv_t, kv_t, go_t, o_t, lse)


class Transfers:
    def __init__(self, sizes):
        self.sizes = sizes

    def shift(self, value, axis, step):
        size = self.sizes[axis]
        return lax.ppermute(value, axis, [(i, (i + step) % size) for i in range(size)])

    def place(self, pieces, axis, dim):
        size = self.sizes[axis]
        if size == 1:
            return jnp.expand_dims(pieces[0], dim)
        shape = pieces[0].shape
        rank = len(shape) + 1
        index = lax.broadcasted_iota(
            jnp.int32, tuple(size if d == dim else 1 for d in range(rank)), dim
        )
        back = jnp.mod(lax.axis_index(axis) - index, size)
        whole = jnp.broadcast_to(
            jnp.expand_dims(pieces[0], dim), shape[:dim] + (size,) + shape[dim:]
        )
        for k in range(1, size):
            whole = jnp.where(back == k, jnp.expand_dims(pieces[k], dim), whole)
        return whole

    def ring(self, value, axis):
        pieces = [value]
        for _ in range(1, self.sizes[axis]):
            pieces.append(self.shift(pieces[-1], axis, 1))
        return pieces

    def gather(self, value, axis, dim):
        return self.place(self.ring(value, axis), axis, dim)

    def take(self, value, axis, dim, step):
        size = self.sizes[axis]
        index = jnp.mod(lax.axis_index(axis) + step, size)
        return lax.dynamic_index_in_dim(value, index, dim, keepdims=False)

    def scatter(self, value, axis, dim):
        total = self.take(value, axis, dim, 0).astype(f32)
        for k in range(1, self.sizes[axis]):
            sent = self.take(value, axis, dim, k).astype(bf16)
            total = total + self.shift(sent, axis, k).astype(f32)
        return total

    def exchange(self, value, axis, dim, out_dim):
        pieces = [self.take(value, axis, dim, 0)]
        for k in range(1, self.sizes[axis]):
            pieces.append(self.shift(self.take(value, axis, dim, k), axis, k))
        return self.place(pieces, axis, out_dim)

    def gather_chips(self, value, order):
        have = []
        for axis in order:
            dim = sum(1 for a in have if "ycz x".index(a) < "ycz x".index(axis))
            value = self.gather(value, axis, dim)
            have.append(axis)
        return value

    def scatter_chips(self, value, order):
        have = ["y", "c", "z", "x"]
        for number, axis in enumerate(order):
            value = self.scatter(value, axis, have.index(axis))
            if number < len(order) - 1:
                value = value.astype(bf16)
            have.remove(axis)
        return value


def head_forward(lin, gain, cosine, sine):
    scale = lax.rsqrt(jnp.mean(lin * lin, axis=1, keepdims=True) + EPS)
    normal = lin * scale * gain[None, :, None]
    half = HEAD_DIM // 2
    first, second = normal[:, :half], normal[:, half:]
    turned = jnp.concatenate(
        [first * cosine - second * sine, second * cosine + first * sine], axis=1
    )
    return turned, scale


def head_backward(grad, lin, scale, gain, cosine, sine):
    half = HEAD_DIM // 2
    first, second = grad[:, :half], grad[:, half:]
    back = jnp.concatenate(
        [first * cosine + second * sine, second * cosine - first * sine], axis=1
    )
    gain_grad = jnp.sum(back * lin * scale, axis=(0, 2))
    scaled = back * gain[None, :, None]
    lin_grad = scale * scaled - lin * (scale**3) * jnp.mean(scaled * lin, axis=1, keepdims=True)
    return lin_grad, gain_grad


def row_scale(values):
    return lax.rsqrt(jnp.mean(values * values, axis=-1, keepdims=True) + EPS)


def norm_backward(grad, values, scale):
    return scale * grad - values * (scale**3) * jnp.mean(grad * values, axis=-1, keepdims=True)


def per_device(
    sizes, tokens, out_grad, doc_ids, corpus, corpus_weight, attn_gain, w_query, w_key, w_value,
    query_gain, key_gain, w_out, ffn_gain, w_gate, w_up, w_down,
):
    move = Transfers(sizes)
    ys, cs, zs, xs = (sizes[a] for a in "yczx")
    batches, local, width = tokens.shape
    span = xs * local
    back_groups = -(-(DOC_MOST - 1) // span)
    window = (back_groups + 1) * span
    at_z, at_x = lax.axis_index("z"), lax.axis_index("x")
    ffn_part = w_gate.shape[1] // (ys * cs)
    d_rows = w_gate.shape[0]

    gain_a = attn_gain.astype(f32)[:, None]
    gain_f = ffn_gain.astype(f32)[:, None]
    w_qkv = jnp.concatenate([w_key, w_value, w_query], axis=1)
    w_qkv_low = (w_qkv.astype(f32) * gain_a).astype(bf16)

    def gather_weight(shard):
        half = shard.shape[1] // 2
        near = move.gather(shard, "z", 0)
        first, second = near[..., :half], near[..., half:]
        first = move.gather(move.gather(first, "y", 0), "x", 2)
        second = move.gather(move.gather(second, "x", 1), "y", 0)
        return tuple(
            move.gather(part, "c", 1).reshape(-1, half) for part in (first, second)
        )

    w_qkv_a, w_qkv_b = gather_weight(w_qkv_low)
    w_out_a, w_out_b = gather_weight(w_out)

    w_gate_low = (w_gate.astype(f32) * gain_f).astype(bf16).reshape(d_rows, ys, cs, 1, ffn_part)
    w_up_low = (w_up.astype(f32) * gain_f).astype(bf16).reshape(d_rows, ys, cs, 1, ffn_part)
    both = jnp.concatenate([w_gate_low, w_up_low], axis=3).reshape(d_rows, ys, cs, 2 * ffn_part)
    both = move.exchange(both, "c", 2, 0)
    both = move.exchange(both, "y", 2, 0)
    both = move.gather(both, "z", 2)
    w_both = move.gather(both, "x", 3).reshape(width, 2 * ffn_part)
    w_down_all = move.gather(move.gather(w_down, "x", 0), "z", 0).reshape(ffn_part, width)

    group_docs = move.gather(doc_ids, "x", 1).reshape(batches, span)
    doc_groups = [group_docs]
    for k in range(1, back_groups + 1):
        earlier = move.shift(doc_groups[-1], "z", 1)
        doc_groups.append(earlier)
    doc_window = jnp.concatenate(
        [
            jnp.where(at_z >= k, doc_groups[k], -1)
            for k in range(back_groups, -1, -1)
        ],
        axis=1,
    )
    starts = jnp.sum(
        (doc_window[:, None, :] < doc_ids[:, :, None]).astype(jnp.int32), axis=-1
    )
    q_start = back_groups * span + at_x * local
    high = (q_start + local + KEY_BLOCK - 1) // KEY_BLOCK

    half_dim = HEAD_DIM // 2
    frequency = jnp.exp(
        jnp.arange(half_dim, dtype=f32) * (-2.0 * math.log(10000.0) / HEAD_DIM)
    )
    positions = (at_z * xs + at_x) * local + jnp.arange(local, dtype=jnp.int32)
    angles = frequency[:, None] * positions.astype(f32)[None, :]
    cosine, sine = jnp.cos(angles)[None], jnp.sin(angles)[None]
    gain_q, gain_k = query_gain.astype(f32), key_gain.astype(f32)

    tag_range = jnp.arange(TAGS, dtype=jnp.int32)
    inputs = [tokens[b].astype(f32) for b in range(batches)]
    grads_out = [
        jnp.sum(jnp.where(tag_range == corpus[b], corpus_weight, 0.0)) * out_grad[b].astype(f32)
        for b in range(batches)
    ]

    def seq_gather(rows):
        chips = jnp.concatenate(move.ring(rows, "y"), axis=0)
        return jnp.concatenate(move.ring(chips, "c"), axis=0)

    def seq_scatter(partial):
        blocks = partial.reshape(cs, ys, local, width)
        total = blocks[0].astype(f32)
        for k in range(1, cs):
            total = total + move.shift(blocks[k], "c", -k).astype(f32)
        result = total[0]
        for k in range(1, ys):
            result = result + move.shift(total[k].astype(bf16), "y", -k).astype(f32)
        return result

    grads_all = [seq_gather(g.astype(bf16)) for g in grads_out]

    state = []
    for b in range(batches):
        scale_in = row_scale(inputs[b])
        normed = (inputs[b] * scale_in).astype(bf16)
        lin_a = dot(w_qkv_a, normed, 0, 1)
        lin_b = dot(w_qkv_b, normed, 0, 1)
        key_lin = lin_a[:KV_WIDTH].reshape(KV_HEADS, HEAD_DIM, local)
        value_t = lin_a[KV_WIDTH : 2 * KV_WIDTH].astype(bf16)
        query_lin = jnp.concatenate([lin_a[2 * KV_WIDTH :], lin_b], axis=0).reshape(
            HEADS, HEAD_DIM, local
        )
        key_rot, key_scale = head_forward(key_lin, gain_k, cosine, sine)
        query_rot, query_scale = head_forward(query_lin, gain_q, cosine, sine)
        query_t = query_rot.astype(bf16).reshape(Q_WIDTH, local)
        kv = jnp.concatenate([key_rot.astype(bf16).reshape(KV_WIDTH, local), value_t], axis=0)
        kv_groups = [move.gather(kv, "x", 1).reshape(2 * KV_WIDTH, span)]
        for k in range(back_groups):
            kv_groups.append(move.shift(kv_groups[-1], "z", 1))
        kv_t = jnp.concatenate(kv_groups[::-1], axis=1)
        meta = jnp.stack([starts[b, 0] // KEY_BLOCK, high, q_start]).astype(jnp.int32)
        mixed_t, lse = attend_forward(meta, starts[b][:, None], query_t, kv_t)
        resid = inputs[b] + jnp.concatenate(
            [dot(mixed_t, w_out_a, 0, 0), dot(mixed_t, w_out_b, 0, 0)], axis=1
        )
        scale_mid = row_scale(resid)
        normed2_all = seq_gather((resid * scale_mid).astype(bf16))
        state.append(
            dict(
                scale_in=scale_in, normed=normed, key_lin=key_lin, query_lin=query_lin,
                key_scale=key_scale, query_scale=query_scale, query_t=query_t, kv_t=kv_t,
                meta=meta, mixed_t=mixed_t, lse=lse, resid=resid, scale_mid=scale_mid,
                normed2_all=normed2_all,
            )
        )

    outputs = []
    grad_both_wide = None
    grad_down_wide = None
    for b in range(batches):
        s = state[b]
        wide = matmul(s["normed2_all"], w_both)
        gate, up = wide[:, :ffn_part], wide[:, ffn_part:]
        sig = jax.nn.sigmoid(gate)
        silu = gate * sig
        hidden = (silu * up).astype(bf16)
        grad_hidden = dot(grads_all[b], w_down_all, 1, 1)
        grad_gate = (grad_hidden * up * (sig * (1.0 + gate * (1.0 - sig)))).astype(bf16)
        grad_up = (grad_hidden * silu).astype(bf16)
        grad_wide = jnp.concatenate([grad_gate, grad_up], axis=1)
        grad_normed2 = seq_scatter(dot(grad_wide, w_both, 1, 1).astype(bf16))
        grad_resid = grads_out[b] + norm_backward(grad_normed2, s["resid"], s["scale_mid"])
        s["grad_resid"] = grad_resid
        s["grad_resid_low"] = grad_resid.astype(bf16)
        down = dot(hidden, grads_all[b], 0, 0)
        grad_down_wide = down if b == 0 else grad_down_wide + down
        part = dot(s["normed2_all"], grad_wide, 0, 0)
        grad_both_wide = part if b == 0 else grad_both_wide + part
        outputs.append(
            (s["resid"] + seq_scatter(matmul(hidden, w_down_all).astype(bf16))).astype(bf16)
        )

    down_parts = grad_down_wide.astype(bf16).reshape(zs, xs, -1, width)
    grad_down = move.scatter(move.scatter(down_parts, "x", 1).astype(bf16), "z", 0)
    both_parts = grad_both_wide.astype(bf16).reshape(ys, cs, zs, xs, d_rows, 2 * ffn_part)
    both_sum = move.scatter(move.scatter(both_parts, "x", 3).astype(bf16), "z", 2).astype(bf16)
    both_sum = move.exchange(both_sum, "y", 0, 2)
    both_sum = move.exchange(both_sum, "c", 0, 2).astype(f32)
    grad_gate_w = both_sum[..., :ffn_part].reshape(d_rows, -1)
    grad_up_w = both_sum[..., ffn_part:].reshape(d_rows, -1)

    gq_parts, gq_gain, gk_gain, token_grads = [], 0.0, 0.0, []
    qkv_grads = []
    for b in range(batches):
        s = state[b]
        low_grad = s["grad_resid_low"]
        grad_mixed_t = jnp.concatenate(
            [dot(w_out_a, low_grad[:, : width // 2], 1, 1)], axis=0
        ) + dot(w_out_b, low_grad[:, width // 2 :], 1, 1)
        grad_mixed_t = grad_mixed_t.astype(bf16)
        dq_t, dk_t, dv_t = attend_backward(
            s["meta"], starts[b][None, :], s["query_t"], s["kv_t"], grad_mixed_t, s["mixed_t"],
            s["lse"],
        )
        dkv = jnp.concatenate([dk_t, dv_t], axis=0).reshape(
            2 * KV_WIDTH, back_groups + 1, span
        )
        carried = dkv[:, 0]
        for k in range(1, back_groups + 1):
            carried = (
                move.shift(carried.astype(bf16), "z", -1).astype(f32) + dkv[:, k].astype(f32)
            )
        carried = carried.astype(bf16).reshape(2 * KV_WIDTH, xs, local)
        dkv_sum = move.scatter(carried, "x", 1)
        key_grad, key_gain_part = head_backward(
            dkv_sum[:KV_WIDTH].reshape(KV_HEADS, HEAD_DIM, local), s["key_lin"], s["key_scale"],
            gain_k, cosine, sine,
        )
        query_grad, query_gain_part = head_backward(
            dq_t.astype(f32).reshape(HEADS, HEAD_DIM, local), s["query_lin"], s["query_scale"],
            gain_q, cosine, sine,
        )
        gq_gain = gq_gain + query_gain_part
        gk_gain = gk_gain + key_gain_part
        query_grad = query_grad.astype(bf16).reshape(Q_WIDTH, local)
        grad_a = jnp.concatenate(
            [
                key_grad.astype(bf16).reshape(KV_WIDTH, local),
                dkv_sum[KV_WIDTH:].astype(bf16),
                query_grad[:KV_WIDTH],
            ],
            axis=0,
        )
        grad_b = query_grad[KV_WIDTH:]
        qkv_grads.append((grad_a, grad_b))
        grad_normed = dot(grad_a, w_qkv_a, 0, 1) + dot(grad_b, w_qkv_b, 0, 1)
        token_grads.append(
            (s["grad_resid"] + norm_backward(grad_normed, inputs[b], s["scale_in"])).astype(bf16)
        )

    def scatter_weight(first, second, rows):
        parts = []
        for part, order in ((first, "cxyz"), (second, "cyxz")):
            shaped = part.astype(bf16).reshape(ys, cs, zs, xs, rows, -1)
            parts.append(move.scatter_chips(shaped, order))
        return jnp.concatenate(parts, axis=1)

    normed_all = jnp.concatenate([s["normed"] for s in state], axis=0)
    mixed_all = jnp.concatenate([s["mixed_t"] for s in state], axis=1)
    low_all = jnp.concatenate([s["grad_resid_low"] for s in state], axis=0)
    grad_out_w = scatter_weight(
        matmul(mixed_all, low_all[:, : width // 2]),
        matmul(mixed_all, low_all[:, width // 2 :]),
        w_out.shape[0],
    )
    grad_qkv = scatter_weight(
        dot(normed_all, jnp.concatenate([g[0] for g in qkv_grads], axis=1), 0, 1),
        dot(normed_all, jnp.concatenate([g[1] for g in qkv_grads], axis=1), 0, 1),
        d_rows,
    )

    attn_gain_grad = jnp.sum(grad_qkv * w_qkv.astype(f32), axis=1)
    ffn_gain_grad = jnp.sum(
        grad_gate_w * w_gate.astype(f32) + grad_up_w * w_up.astype(f32), axis=1
    )
    grad_qkv = grad_qkv * gain_a
    small = jnp.concatenate([gq_gain, gk_gain])[None, :]
    for axis in "cyxz":
        small = jnp.sum(move.gather(small, axis, 0), axis=0)

    return (
        jnp.stack(outputs),
        jnp.stack(token_grads),
        attn_gain_grad,
        grad_qkv[:, 2 * KV_WIDTH :],
        grad_qkv[:, :KV_WIDTH],
        grad_qkv[:, KV_WIDTH : 2 * KV_WIDTH],
        small[0, :HEAD_DIM],
        small[0, HEAD_DIM:],
        grad_out_w,
        ffn_gain_grad,
        grad_gate_w * gain_f,
        grad_up_w * gain_f,
        grad_down,
    )


def solution(mesh):
    sizes = {"c": 2, "z": Z_CHIPS}
    sizes["y"] = mesh.shape["seq"] // sizes["c"]
    sizes["x"] = mesh.shape["ctx"] // sizes["z"]
    grid = Mesh(mesh.devices.reshape([sizes[a] for a in "yczx"]), ("y", "c", "z", "x"))
    seq, ctx, every = ("y", "c"), ("z", "x"), ("y", "c", "z", "x")
    acts, vector, matrix = P(seq, ctx, None), P(every), P(every, None)
    in_specs = (
        acts, acts, P(seq, ctx), P(seq), P(), vector, matrix, matrix, matrix, P(), P(), matrix,
        vector, matrix, matrix, matrix,
    )
    out_specs = (
        acts, acts, vector, matrix, matrix, matrix, P(), P(), matrix, vector, matrix, matrix,
        matrix,
    )
    return jax.shard_map(
        functools.partial(per_device, sizes), mesh=grid, in_specs=in_specs, out_specs=out_specs,
        check_vma=False,
    )
```

time: 4300 us -> 1110 us (0.26)
  waiting for transfers between devices: 3310 us -> 476 us
  matrix products: 450 us -> 164 us
  blocking collectives: 143 us -> 0 us
  local copies, waits for them, and re-layouts: 207 us -> 99.9 us
  starting transfers between devices: 75.6 us -> 162 us
  other arithmetic: 88.5 us -> 145 us
    reduce_scatter x7 -> x0, waiting for transfers between devices: 2490 us -> none  [per_device(): lax.psum_scatter(totals, ('seq', 'ctx'), scatter_dimension=0, tiled=True)]
    all_gather x14 -> x0, waiting for transfers between devices: 667 us -> none  [the longest x2 195 us: advance(): lax.all_gather(w_up, ('seq', 'ctx'), axis=0, tiled=True)]
    ppermute x0 -> x99, waiting for transfers between devices: none -> 476 us  [shift(): lax.ppermute(value, axis, [(i, (i + step) % size) for i in range(size)])]
    dot_general x94 -> x32, matrix products: 450 us -> 164 us  [dot(): lax.dot_general(left, right, (((left_dim,), (right_dim,)), ((), ())), pre...]
    ppermute x0 -> x99, starting transfers between devices: none -> 162 us  [shift(): lax.ppermute(value, axis, [(i, (i + step) % size) for i in range(size)])]
    all_to_all x16 -> x0, waiting for transfers between devices: 140 us -> none  [the longest x2 70.9 us: micro(): lax.all_to_all(mixed_heads.reshape(length, head_slots * HEAD_DIM), 'ctx',...]
    while x2 -> x0, blocking collectives: 77 us -> none
    slice x80 -> x24, local copies, waits for them, and re-layouts: 90.9 us -> 14.9 us  [the longest x4 7.26 us: seq_scatter(): total = total + move.shift(blocks[k], 'c', -k).astype(f32)]
  transfers between devices with their start and end apart: 37 -> 99, of which waited for: 29 -> 42; matrix products, arithmetic and copies ran while one was open for 11% -> 32% of each run, Pallas kernels for 0% -> 4%
where the time goes in v1:
time: 1110 us; the launch traced here: 1090 us
  waiting for transfers between devices  476 us (43%)
  matrix products  164 us (15%)
  starting transfers between devices  162 us (15%)
  other arithmetic  145 us (13%)
  local copies, waits for them, and re-layouts  99.9 us (9%)
  Pallas kernels  38.5 us (3%)
    ppermute x99, waiting for transfers between devices, shift(): lax.ppermute(value, axis, [(i, (i + step) % size) for i in range(size)])  476 us
    dot_general x32, matrix products, dot(): lax.dot_general(left, right, (((left_dim,), (right_dim,)), ((), ())), pre...  164 us
    ppermute x99, starting transfers between devices, shift(): lax.ppermute(value, axis, [(i, (i + step) % size) for i in range(size)])  162 us
    select_n x22, other arithmetic, place(): whole = jnp.where(back == k, jnp.expand_dims(pieces[k], dim), whole)  38.3 us
    pallas_call x2, Pallas kernels, attend_backward(): pl.pallas_call(backward_kernel, name='attend_backward', grid_spec=pltpu.P...  22.2 us
  transfers between devices with their start and end apart: 99, of which 42 were waited for; matrix products, arithmetic and copies ran while one was open for 32% of the time, Pallas kernels for 4%

profile of v1, /device:TPU:0, one launch (start us, length us, event | category | flops | bytes accessed | tf_op | source)
XLA Modules:
  0.0 1093.5 jit_solution(6853363437076690374)
XLA Ops:
  23.5 4.8 bitcast_convert_fusion
  32.0 5.4 collective-permute-done.1
  46.4 5.3 collective-permute-done.17
  54.7 20.8 %collective-permute-done.5 = bf16[64,1920]{1,0:T(8,128)(2,1)S(1)} collective-permute-done((bf16[64,1920]{1,0:T(8,128)(2,1)S(1)}, bf16[64,1920]{1,0:T(8,128)(2,1)S(1)}, u32[]{:S(2)}, u32[]{:S(2)}) %collective-permute-start.5) | collective-permute-done | bytes 245792 | tf_op jit(solution)/shard_map/ppermute | solution.py:237
  78.5 5.5 collective-permute-done.21
  88.0 9.7 collective-permute-done.9
  102.0 10.7 collective-permute-done.22
  120.0 15.3 %collective-permute-done.10 = bf16[4,2,64,960]{3,2,1,0:T(8,128)(2,1)S(1)} collective-permute-done((bf16[4,2,64,960]{3,2,1,0:T(8,128)(2,1)S(1)}, bf16[4,2,64,960]{3,2,1,0:T(8,128)(2,1)S(1)}, u32[]{:S(2)}, u32[]{:S(2)}) %collective-permute-start.10) | collective-permute-done | bytes 983072 | tf_op jit(solution)/shard_map/ppermute | solution.py:237
  140.1 17.7 %collective-permute-done.52 = bf16[256,2048]{1,0:T(8,128)(2,1)} collective-permute-done((bf16[256,2048]{1,0:T(8,128)(2,1)}, bf16[256,2048]{1,0:T(8,128)(2,1)}, u32[]{:S(2)}, u32[]{:S(2)}) %collective-permute-start.52) | collective-permute-done | bytes 1048608 | tf_op jit(solution)/shard_map/ppermute | solution.py:237
  157.8 19.5 %collective-permute-done.45 = bf16[256,2048]{1,0:T(8,128)(2,1)} collective-permute-done((bf16[256,2048]{1,0:T(8,128)(2,1)}, bf16[256,2048]{1,0:T(8,128)(2,1)}, u32[]{:S(2)}, u32[]{:S(2)}) %collective-permute-start.45) | collective-permute-done | bytes 1048608 | tf_op jit(solution)/shard_map/ppermute | solution.py:237
  194.9 5.1 bitcast_select_fusion.4
  200.0 10.4 collective-permute-done.35
  210.4 4.1 fusion.5
  214.6 14.5 %collective-permute-done.30 = bf16[2,2,64,1792]{3,2,1,0:T(8,128)(2,1)} collective-permute-done((bf16[2,2,64,1792]{3,2,1,0:T(8,128)(2,1)}, bf16[2,2,64,1792]{3,2,1,0:T(8,128)(2,1)}, u32[]{:S(2)}, u32[]{:S(2)}) %collective-permute-start.30) | collective-permute-done | bytes 917536 | tf_op jit(solution)/shard_map/ppermute | solution.py:237
  229.1 4.3 select_select_fusion
  249.1 71.9 %collective-permute-done.12 = bf16[640,256]{1,0:T(8,128)(2,1)S(1)} collective-permute-done((bf16[640,256]{1,0:T(8,128)(2,1)S(1)}, bf16[640,256]{1,0:T(8,128)(2,1)S(1)}, u32[]{:S(2)}, u32[]{:S(2)}) %collective-permute-start.12) | collective-permute-done | bytes 327712 | tf_op jit(solution)/shard_map/ppermute | solution.py:237
  321.9 16.5 %collective-permute-done.13 = bf16[640,512]{1,0:T(8,128)(2,1)S(1)} collective-permute-done((bf16[640,512]{1,0:T(8,128)(2,1)S(1)}, bf16[640,512]{1,0:T(8,128)(2,1)S(1)}, u32[]{:S(2)}, u32[]{:S(2)}) %collective-permute-start.13) | collective-permute-done | bytes 655392 | tf_op jit(solution)/shard_map/ppermute | solution.py:237
  339.9 14.5 %collective-permute-done.14 = bf16[640,512]{1,0:T(8,128)(2,1)S(1)} collective-permute-done((bf16[640,512]{1,0:T(8,128)(2,1)S(1)}, bf16[640,512]{1,0:T(8,128)(2,1)S(1)}, u32[]{:S(2)}, u32[]{:S(2)}) %collective-permute-start.14) | collective-permute-done | bytes 655392 | tf_op jit(solution)/shard_map/ppermute | solution.py:237
  355.8 8.1 attend_forward.2
  375.6 4.3 collective-permute-start.38
  380.4 14.1 %collective-permute-done.24 = bf16[256,2048]{1,0:T(8,128)(2,1)S(1)} collective-permute-done((bf16[256,2048]{1,0:T(8,128)(2,1)S(1)}, bf16[256,2048]{1,0:T(8,128)(2,1)S(1)}, u32[]{:S(2)}, u32[]{:S(2)}) %collective-permute-start.24) | collective-permute-done | bytes 1048608 | tf_op jit(solution)/shard_map/ppermute | solution.py:237
  401.6 15.3 %collective-permute-done.39 = bf16[640,512]{1,0:T(8,128)(2,1)} collective-permute-done((bf16[640,512]{1,0:T(8,128)(2,1)S(1)}, bf16[640,512]{1,0:T(8,128)(2,1)}, u32[]{:S(2)}, u32[]{:S(2)}) %collective-permute-start.39) | collective-permute-done | bytes 655392 | tf_op jit(solution)/shard_map/ppermute | solution.py:237
  418.6 4.4 bitcast_select_fusion
  423.1 12.1 %fusion.56 = f32[1024,1792]{1,0:T(8,128)} fusion(bf16[2048,1792]{1,0:T(8,128)(2,1)S(1)} %bitcast_select_fusion, bf16[512,2048]{1,0:T(8,128)(2,1)S(1)} %collective-permute-done.25, bf16[256,2048]{1,0:T(8,128)(2,1)S(1)} %collective-permute-done.24, bf16[256,2048]{1,0:T(8,128)(2,1)S(1)} %multiply_convert_fusion.7), kind=kOutput, calls=%fused_computation.152 | convolution fusion | flops 7528775680 | bytes 18874368 | tf_op jit(solution)/shard_map/dot_general | solution.py:33
  435.3 12.4 %multiply_convert_fusion.3 = (bf16[1024,896]{1,0:T(8,128)(2,1)}, bf16[1024,896]{1,0:T(8,128)(2,1)}, bf16[1024,896]{1,0:T(8,128)(2,1)}) fusion(f32[1024,1792]{1,0:T(8,128)} %fusion.56, bf16[896,2048]{1,0:T(8,128)(2,1)S(1)} %copy-done.41, bf16[512,2048]{1,0:T(8,128)(2,1)} %collective-permute-done.46, bf16[256,2048]{1,0:T(8,128)(2,1)} %collective-permute-done.45, ...), kind=kOutput, calls=%fused_computation.39 | convolution fusion | flops 3784441856 | bytes 20709376 | tf_op jit(solution)/shard_map/dot_general | solution.py:33
  447.7 10.0 convolution_convert_fusion.3
  460.3 4.7 convolution_convert_fusion.5
  470.6 8.1 attend_forward.3
  491.1 19.5 %collective-permute-done.48 = bf16[256,2048]{1,0:T(8,128)(2,1)S(1)} collective-permute-done((bf16[256,2048]{1,0:T(8,128)(2,1)S(1)}, bf16[256,2048]{1,0:T(8,128)(2,1)S(1)}, u32[]{:S(2)}, u32[]{:S(2)}) %collective-permute-start.48) | collective-permute-done | bytes 1048608 | tf_op jit(solution)/shard_map/ppermute | solution.py:237
  512.1 20.1 %collective-permute-done.37 = bf16[256,2048]{1,0:T(8,128)(2,1)S(1)} collective-permute-done((bf16[256,2048]{1,0:T(8,128)(2,1)S(1)}, bf16[256,2048]{1,0:T(8,128)(2,1)S(1)}, u32[]{:S(2)}, u32[]{:S(2)}) %collective-permute-start.37) | collective-permute-done | bytes 1048608 | tf_op jit(solution)/shard_map/ppermute | solution.py:237
  540.1 11.1 %attend_backward.2 = (bf16[1280,256]{1,0:T(8,128)(2,1)}, bf16[320,1536]{1,0:T(8,128)(2,1)}, bf16[320,1536]{1,0:T(8,128)(2,1)}) custom-call(s32[3]{0:T(128)} %add_add_fusion.meta, s32[1,256]{1,0:T(1,128)} %get-tuple-element.164.start_ref, bf16[1280,256]{1,0:T(8,128)(2,1)} %bitcast.584, bf16[640,1536]{1,0:T(8,128)(2,1)} %pad_maximum_fusion.17.k_ref.v_ref, ...), custom_call_target="tpu_custom_call" | custom-call | flops 10066329600 | bytes 8388608 | tf_op jit(solution)/shard_map/attend_backward/pallas_call | solution.py:189
  557.0 32.5 %collective-permute-start.49 = (bf16[640,512]{0,1:T(8,128)(2,1)S(1)}, bf16[640,512]{0,1:T(8,128)(2,1)S(1)}, u32[]{:S(2)}, u32[]{:S(2)}) collective-permute-start(bf16[640,512]{0,1:T(8,128)(2,1)S(1)} %slice_bitcast_fusion.9), channel_id=1, source_target_pairs={{0,6},{2,0},{4,2},{6,4},{1,7},{3,1},{5,3},{7,5},{8,14},{10,8},{12,... | collective-permute-start | bytes 1966088 | tf_op jit(solution)/shard_map/ppermute | solution.py:237
  592.9 6.5 collective-permute-done.49
  599.5 5.0 collective-permute-start.50
  614.6 4.8 fusion.186
  625.8 14.7 %fusion.55 = f32[1024,1792]{1,0:T(8,128)} fusion(bf16[2048,1792]{1,0:T(8,128)(2,1)} %copy-done.22, bf16[512,2048]{1,0:T(8,128)(2,1)} %collective-permute-done.42, bf16[256,2048]{1,0:T(8,128)(2,1)} %collective-permute-done.41, bf16[256,2048]{1,0:T(8,128)(2,1)} %get-tuple-element.84), kind=kOutput, calls=%fused_computation.151 | convolution fusion | flops 7528775680 | bytes 18874368 | tf_op jit(solution)/shard_map/dot_general | solution.py:33
  640.5 10.1 multiply_convert_fusion.1
  651.9 8.0 convolution_convert_fusion.2
  661.6 5.1 convolution_convert_fusion.4
  667.1 6.0 fusion.52
  673.2 6.5 add_convert_fusion.1
  683.7 12.7 %fusion.22 = f32[2048,1792]{1,0:T(8,128)} fusion(bf16[1024,896]{1,0:T(8,128)(2,1)S(1)} %copy-done.152, bf16[1024,896]{1,0:T(8,128)(2,1)S(1)} %copy-done.150, bf16[512,2048]{1,0:T(8,128)(2,1)} %collective-permute-done.42, bf16[256,2048]{1,0:T(8,128)(2,1)} %collective-permute-done.41, bf16[256,2048]{1,0:T(8,128)(2,1)} %get-tuple-element.84), kind=kOutput, calls=%fused_computation.74 | convolution fusion | flops 7536115712 | bytes 22544384 | tf_op jit(solution)/shard_map/dot_general | solution.py:33
  696.4 14.8 %add_convert_fusion = bf16[2048,1792]{1,0:T(8,128)(2,1)} fusion(f32[2048,1792]{1,0:T(8,128)} %fusion.22, bf16[1024,896]{1,0:T(8,128)(2,1)} %get-tuple-element.54, bf16[1024,896]{1,0:T(8,128)(2,1)} %get-tuple-element.53, bf16[512,2048]{1,0:T(8,128)(2,1)} %copy-done.145, bf16[256,2048]{1,0:T(8,128)(2,1)} %copy-done.73, bf16[256,2048]{1,0:T(8,128)(2,1)S(1)} %copy-done.36), kind=kOutput, calls=%fused_computation | convolution fusion | flops 7543455744 | bytes 29884416 | tf_op jit(solution)/shard_map/dot_general | solution.py:33
  711.2 4.4 dynamic-slice_bitcast_fusion
  717.0 7.4 collective-permute-done.95
  737.9 4.8 collective-permute-done.96
  742.6 7.2 collective-permute-done.98
  749.8 19.9 %collective-permute-done.97 = bf16[112,2048]{1,0:T(8,128)(2,1)S(1)} collective-permute-done((bf16[112,2048]{1,0:T(8,128)(2,1)S(1)}, bf16[112,2048]{1,0:T(8,128)(2,1)S(1)}, u32[]{:S(2)}, u32[]{:S(2)}) %collective-permute-start.97) | collective-permute-done | bytes 458784 | tf_op jit(solution)/shard_map/ppermute | solution.py:237
  774.3 5.8 collective-permute-done.44
  787.7 11.1 %attend_backward.3 = (bf16[1280,256]{1,0:T(8,128)(2,1)}, bf16[320,1536]{1,0:T(8,128)(2,1)}, bf16[320,1536]{1,0:T(8,128)(2,1)}) custom-call(s32[3]{0:T(128)} %add_add_fusion.1.meta, s32[1,256]{1,0:T(1,128)} %get-tuple-element.161.start_ref, bf16[1280,256]{1,0:T(8,128)(2,1)} %bitcast.582, bf16[640,1536]{1,0:T(8,128)(2,1)} %pad_maximum_fusion.18.k_ref.v_ref, ...), custom_call_target="tpu_custom_call" | custom-call | flops 10066329600 | bytes 8388608 | tf_op jit(solution)/shard_map/attend_backward/pallas_call | solution.py:189
  807.0 23.1 %collective-permute-start.56 = (bf16[640,512]{0,1:T(8,128)(2,1)S(1)}, bf16[640,512]{0,1:T(8,128)(2,1)S(1)}, u32[]{:S(2)}, u32[]{:S(2)}) collective-permute-start(bf16[640,512]{0,1:T(8,128)(2,1)S(1)} %slice_bitcast_fusion.6), channel_id=1, source_target_pairs={{0,6},{2,0},{4,2},{6,4},{1,7},{3,1},{5,3},{7,5},{8,14},{10,8},{12,... | collective-permute-start | bytes 1966088 | tf_op jit(solution)/shard_map/ppermute | solution.py:237
  860.1 27.1 %collective-permute-done.57 = bf16[640,512]{0,1:T(8,128)(2,1)S(1)} collective-permute-done((bf16[640,512]{0,1:T(8,128)(2,1)S(1)}, bf16[640,512]{0,1:T(8,128)(2,1)S(1)}, u32[]{:S(2)}, u32[]{:S(2)}) %collective-permute-start.57) | collective-permute-done | bytes 655392 | tf_op jit(solution)/shard_map/ppermute | solution.py:237
  900.1 9.7 collective-permute-done.92
  909.8 28.4 %collective-permute-done.91 = bf16[2,2,64,1792]{3,2,1,0:T(8,128)(2,1)} collective-permute-done((bf16[2,2,64,1792]{3,2,1,0:T(8,128)(2,1)}, bf16[2,2,64,1792]{3,2,1,0:T(8,128)(2,1)}, u32[]{:S(2)}, u32[]{:S(2)}) %collective-permute-start.91) | collective-permute-done | bytes 917536 | tf_op jit(solution)/shard_map/ppermute | solution.py:237
  945.0 4.7 fusion.36
  954.7 4.2 convolution_convert_fusion.7
  964.6 6.3 copy.83
  981.0 6.3 copy.84
  1003.9 6.4 collective-permute-done.85
  1045.8 5.2 collective-permute-done.60
  1052.7 5.0 collective-permute-done.66
  1059.2 7.1 collective-permute-done.61
  1075.4 6.3 collective-permute-start.69
  1081.7 5.2 collective-permute-done.63
  (756 shorter events, 352.2 us)
Async XLA Ops:
  0.6 27.9 %collective-permute-start = (s32[2,256]{1,0:T(2,128)}, s32[2,256]{1,0:T(2,128)S(1)}, u32[]{:S(2)}, u32[]{:S(2)}) collective-permute-start(s32[2,256]{1,0:T(2,128)} %param.18), channel_id=1, source_target_pairs={{0,1},{1,0},{2,3},{3,2},{4,5},{5,4},{6,7},{7,6},{8,9},{9,8},{10,11... | collective-permute-start | bytes 6152 | tf_op jit(solution)/shard_map/ppermute | solution.py:237
  3.7 24.9 %collective-permute-start.15 = (bf16[40,2048]{1,0:T(8,128)(2,1)}, bf16[40,2048]{1,0:T(8,128)(2,1)}, u32[]{:S(2)}, u32[]{:S(2)}) collective-permute-start(bf16[40,2048]{1,0:T(8,128)(2,1)} %param.27), channel_id=1, source_target_pairs={{0,2},{2,4},{4,6},{6,0},{1,3},{3,5},{5,7},{7,1},{8,10},{10,12},{12... | collective-permute-start | bytes 491528 | tf_op jit(solution)/shard_map/ppermute | solution.py:237
  7.1 30.3 %collective-permute-start.3 = (bf16[64,1920]{1,0:T(8,128)(2,1)S(1)}, bf16[64,1920]{1,0:T(8,128)(2,1)}, u32[]{:S(2)}, u32[]{:S(2)}) collective-permute-start(bf16[64,1920]{1,0:T(8,128)(2,1)S(1)} %fusion.107), channel_id=1, source_target_pairs={{0,2},{2,4},{4,6},{6,0},{1,3},{3,5},{5,7},{7,1},{8,10},{10,12},{12... | collective-permute-start | bytes 737288 | tf_op jit(solution)/shard_map/ppermute | solution.py:237
  8.8 33.1 %collective-permute-start.32 = (bf16[112,2048]{1,0:T(8,128)(2,1)}, bf16[112,2048]{1,0:T(8,128)(2,1)}, u32[]{:S(2)}, u32[]{:S(2)}) collective-permute-start(bf16[112,2048]{1,0:T(8,128)(2,1)} %param.31), channel_id=1, source_target_pairs={{0,1},{1,0},{2,3},{3,2},{4,5},{5,4},{6,7},{7,6},{8,9},{9,8},{10,11... | collective-permute-start | bytes 1376264 | tf_op jit(solution)/shard_map/ppermute | solution.py:237
  19.7 19.3 %collective-permute-start.26 = (bf16[64,2,1792]{2,0,1:T(8,128)(2,1)}, bf16[64,2,1792]{2,0,1:T(8,128)(2,1)}, u32[]{:S(2)}, u32[]{:S(2)}) collective-permute-start(bf16[64,2,1792]{2,0,1:T(8,128)(2,1)} %get-tuple-element.117), channel_id=1, source_target_pairs={{0,8},{8,0},{1,9},{9,1},{2,10},{10,2},{3,11},{11,3},{4,12},{12,4},... | collective-permute-start | bytes 1376264 | tf_op jit(solution)/shard_map/ppermute | solution.py:237
  37.4 62.0 %collective-permute-start.2 = (s32[2,512]{1,0:T(2,128)S(1)}, s32[2,512]{1,0:T(2,128)S(1)}, u32[]{:S(2)}, u32[]{:S(2)}) collective-permute-start(s32[2,512]{1,0:T(2,128)S(1)} %collective-permute-done.1), channel_id=1, source_target_pairs={{0,2},{2,4},{4,6},{6,0},{1,3},{3,5},{5,7},{7,1},{8,10},{10,12},{12... | collective-permute-start | bytes 12296 | tf_op jit(solution)/shard_map/ppermute | solution.py:237
  40.2 47.1 %collective-permute-start.27 = (bf16[2,64,1792]{2,1,0:T(8,128)(2,1)S(1)}, bf16[2,64,1792]{2,1,0:T(8,128)(2,1)S(1)}, u32[]{:S(2)}, u32[]{:S(2)}) collective-permute-start(bf16[2,64,1792]{2,1,0:T(8,128)(2,1)S(1)} %get-tuple-element.115), channel_id=1, source_target_pairs={{0,16},{16,0},{1,17},{17,1},{2,18},{18,2},{3,19},{19,3},{4,20},{20... | collective-permute-start | bytes 1376264 | tf_op jit(solution)/shard_map/ppermute | solution.py:237
  43.0 57.4 %collective-permute-start.33 = (bf16[2,112,2048]{2,1,0:T(8,128)(2,1)S(1)}, bf16[2,112,2048]{2,1,0:T(8,128)(2,1)S(1)}, u32[]{:S(2)}, u32[]{:S(2)}) collective-permute-start(bf16[2,112,2048]{2,1,0:T(8,128)(2,1)S(1)} %broadcast_select_fusion.10), channel_id=1, source_target_pairs={{0,2},{2,4},{4,6},{6,0},{1,3},{3,5},{5,7},{7,1},{8,10},{10,12},{12... | collective-permute-start | bytes 2752520 | tf_op jit(solution)/shard_map/ppermute | solution.py:237
  53.0 22.5 %collective-permute-start.5 = (bf16[64,1920]{1,0:T(8,128)(2,1)S(1)}, bf16[64,1920]{1,0:T(8,128)(2,1)S(1)}, u32[]{:S(2)}, u32[]{:S(2)}) collective-permute-start(bf16[64,1920]{1,0:T(8,128)(2,1)S(1)} %collective-permute-done.4), channel_id=1, source_target_pairs={{0,2},{2,4},{4,6},{6,0},{1,3},{3,5},{5,7},{7,1},{8,10},{10,12},{12... | collective-permute-start | bytes 737288 | tf_op jit(solution)/shard_map/ppermute | solution.py:237
  53.1 32.5 %collective-permute-start.18 = (bf16[4,40,1024]{2,1,0:T(8,128)(2,1)S(1)}, bf16[4,40,1024]{2,1,0:T(8,128)(2,1)S(1)}, u32[]{:S(2)}, u32[]{:S(2)}) collective-permute-start(bf16[4,40,1024]{2,1,0:T(8,128)(2,1)S(1)} %get-tuple-element.123), channel_id=1, source_target_pairs={{0,16},{16,0},{1,17},{17,1},{2,18},{18,2},{3,19},{19,3},{4,20},{20... | collective-permute-start | bytes 983048 | tf_op jit(solution)/shard_map/ppermute | solution.py:237
  87.3 25.5 %collective-permute-start.22 = (bf16[4,2,40,1024]{3,2,1,0:T(8,128)(2,1)S(1)}, bf16[4,2,40,1024]{3,2,1,0:T(8,128)(2,1)S(1)}, u32[]{:S(2)}, u32[]{:S(2)}) collective-permute-start(bf16[4,2,40,1024]{3,2,1,0:T(8,128)(2,1)S(1)} %broadcast_select_fusion.13), channel_id=1, source_target_pairs={{0,16},{16,0},{1,17},{17,1},{2,18},{18,2},{3,19},{19,3},{4,20},{20... | collective-permute-start | bytes 1966088 | tf_op jit(solution)/shard_map/ppermute | solution.py:237
  99.4 20.6 %collective-permute-start.28 = (bf16[2,2,64,1792]{3,2,1,0:T(8,128)(2,1)S(1)}, bf16[2,2,64,1792]{3,2,1,0:T(8,128)(2,1)}, u32[]{:S(2)}, u32[]{:S(2)}) collective-permute-start(bf16[2,2,64,1792]{3,2,1,0:T(8,128)(2,1)S(1)} %broadcast_select_fusion.12), channel_id=1, source_target_pairs={{0,2},{2,4},{4,6},{6,0},{1,3},{3,5},{5,7},{7,1},{8,10},{10,12},{12... | collective-permute-start | bytes 2752520 | tf_op jit(solution)/shard_map/ppermute | solution.py:237
  99.5 35.8 %collective-permute-start.10 = (bf16[4,2,64,960]{3,2,1,0:T(8,128)(2,1)S(1)}, bf16[4,2,64,960]{3,2,1,0:T(8,128)(2,1)S(1)}, u32[]{:S(2)}, u32[]{:S(2)}) collective-permute-start(bf16[4,2,64,960]{3,2,1,0:T(8,128)(2,1)S(1)} %broadcast_select_fusion.8), channel_id=1, source_target_pairs={{0,16},{16,0},{1,17},{17,1},{2,18},{18,2},{3,19},{19,3},{4,20},{20... | collective-permute-start | bytes 2949128 | tf_op jit(solution)/shard_map/ppermute | solution.py:237
  100.4 36.1 %collective-permute-start.7 = (bf16[2,4,64,960]{3,2,1,0:T(8,128)(2,1)S(1)}, bf16[2,4,64,960]{3,2,1,0:T(8,128)(2,1)S(1)}, u32[]{:S(2)}, u32[]{:S(2)}) collective-permute-start(bf16[2,4,64,960]{3,2,1,0:T(8,128)(2,1)S(1)} %broadcast_select_fusion.9), channel_id=1, source_target_pairs={{0,1},{1,0},{2,3},{3,2},{4,5},{5,4},{6,7},{7,6},{8,9},{9,8},{10,11... | collective-permute-start | bytes 2949128 | tf_op jit(solution)/shard_map/ppermute | solution.py:237
  112.8 45.0 %collective-permute-start.52 = (bf16[256,2048]{1,0:T(8,128)(2,1)}, bf16[256,2048]{1,0:T(8,128)(2,1)}, u32[]{:S(2)}, u32[]{:S(2)}) collective-permute-start(bf16[256,2048]{1,0:T(8,128)(2,1)} %get-tuple-element.82), channel_id=1, source_target_pairs={{0,16},{16,0},{1,17},{17,1},{2,18},{18,2},{3,19},{19,3},{4,20},{20... | collective-permute-start | bytes 3145736 | tf_op jit(solution)/shard_map/ppermute | solution.py:237
  115.3 62.0 %collective-permute-start.45 = (bf16[256,2048]{1,0:T(8,128)(2,1)}, bf16[256,2048]{1,0:T(8,128)(2,1)}, u32[]{:S(2)}, u32[]{:S(2)}) collective-permute-start(bf16[256,2048]{1,0:T(8,128)(2,1)} %get-tuple-element.83), channel_id=1, source_target_pairs={{0,16},{16,0},{1,17},{17,1},{2,18},{18,2},{3,19},{19,3},{4,20},{20... | collective-permute-start | bytes 3145736 | tf_op jit(solution)/shard_map/ppermute | solution.py:237
  120.0 57.4 %collective-permute-start.34 = (bf16[2,112,2048]{2,1,0:T(8,128)(2,1)S(1)}, bf16[2,112,2048]{2,1,0:T(8,128)(2,1)S(1)}, u32[]{:S(2)}, u32[]{:S(2)}) collective-permute-start(bf16[2,112,2048]{2,1,0:T(8,128)(2,1)S(1)} %collective-permute-done.33), channel_id=1, source_target_pairs={{0,2},{2,4},{4,6},{6,0},{1,3},{3,5},{5,7},{7,1},{8,10},{10,12},{12... | collective-permute-start | bytes 2752520 | tf_op jit(solution)/shard_map/ppermute | solution.py:237
  135.2 49.9 %collective-permute-start.20 = (bf16[2,4,2,40,1024]{4,3,2,1,0:T(8,128)(2,1)S(1)}, bf16[2,4,2,40,1024]{4,3,2,1,0:T(8,128)(2,1)}, u32[]{:S(2)}, u32[]{:S(2)}) collective-permute-start(bf16[2,4,2,40,1024]{4,3,2,1,0:T(8,128)(2,1)S(1)} %broadcast_select_fusion.7), channel_id=1, source_target_pairs={{0,8},{8,0},{1,9},{9,1},{2,10},{10,2},{3,11},{11,3},{4,12},{12,4},... | collective-permute-start | bytes 3932168 | tf_op jit(solution)/shard_map/ppermute | solution.py:237
  136.5 48.5 %collective-permute-start.29 = (bf16[2,2,64,1792]{3,2,1,0:T(8,128)(2,1)}, bf16[2,2,64,1792]{3,2,1,0:T(8,128)(2,1)}, u32[]{:S(2)}, u32[]{:S(2)}) collective-permute-start(bf16[2,2,64,1792]{3,2,1,0:T(8,128)(2,1)} %collective-permute-done.28), channel_id=1, source_target_pairs={{0,2},{2,4},{4,6},{6,0},{1,3},{3,5},{5,7},{7,1},{8,10},{10,12},{12... | collective-permute-start | bytes 2752520 | tf_op jit(solution)/shard_map/ppermute | solution.py:237
  157.8 37.0 %collective-permute-start.23 = (bf16[2,4,2,40,1024]{4,3,2,1,0:T(8,128)(2,1)}, bf16[2,4,2,40,1024]{4,3,2,1,0:T(8,128)(2,1)}, u32[]{:S(2)}, u32[]{:S(2)}) collective-permute-start(bf16[2,4,2,40,1024]{4,3,2,1,0:T(8,128)(2,1)} %broadcast_select_fusion.6), channel_id=1, source_target_pairs={{0,8},{8,0},{1,9},{9,1},{2,10},{10,2},{3,11},{11,3},{4,12},{12,4},... | collective-permute-start | bytes 3932168 | tf_op jit(solution)/shard_map/ppermute | solution.py:237
  177.3 57.5 %collective-permute-start.8 = (bf16[2,4,2,64,960]{4,3,2,1,0:T(8,128)(2,1)}, bf16[2,4,2,64,960]{4,3,2,1,0:T(8,128)(2,1)}, u32[]{:S(2)}, u32[]{:S(2)}) collective-permute-start(bf16[2,4,2,64,960]{4,3,2,1,0:T(8,128)(2,1)} %broadcast_select_fusion.3), channel_id=1, source_target_pairs={{0,8},{8,0},{1,9},{9,1},{2,10},{10,2},{3,11},{11,3},{4,12},{12,4},... | collective-permute-start | bytes 5898248 | tf_op jit(solution)/shard_map/ppermute | solution.py:237
  178.3 56.6 %collective-permute-start.11 = (bf16[2,4,2,64,960]{4,3,2,1,0:T(8,128)(2,1)}, bf16[2,4,2,64,960]{4,3,2,1,0:T(8,128)(2,1)}, u32[]{:S(2)}, u32[]{:S(2)}) collective-permute-start(bf16[2,4,2,64,960]{4,3,2,1,0:T(8,128)(2,1)} %broadcast_select_fusion.2), channel_id=1, source_target_pairs={{0,8},{8,0},{1,9},{9,1},{2,10},{10,2},{3,11},{11,3},{4,12},{12,4},... | collective-permute-start | bytes 5898248 | tf_op jit(solution)/shard_map/ppermute | solution.py:237
  185.0 25.4 %collective-permute-start.35 = (bf16[2,112,2048]{2,1,0:T(8,128)(2,1)}, bf16[2,112,2048]{2,1,0:T(8,128)(2,1)}, u32[]{:S(2)}, u32[]{:S(2)}) collective-permute-start(bf16[2,112,2048]{2,1,0:T(8,128)(2,1)} %copy-done.76), channel_id=1, source_target_pairs={{0,2},{2,4},{4,6},{6,0},{1,3},{3,5},{5,7},{7,1},{8,10},{10,12},{12... | collective-permute-start | bytes 2752520 | tf_op jit(solution)/shard_map/ppermute | solution.py:237
  185.1 44.0 %collective-permute-start.30 = (bf16[2,2,64,1792]{3,2,1,0:T(8,128)(2,1)}, bf16[2,2,64,1792]{3,2,1,0:T(8,128)(2,1)}, u32[]{:S(2)}, u32[]{:S(2)}) collective-permute-start(bf16[2,2,64,1792]{3,2,1,0:T(8,128)(2,1)} %collective-permute-done.29), channel_id=1, source_target_pairs={{0,2},{2,4},{4,6},{6,0},{1,3},{3,5},{5,7},{7,1},{8,10},{10,12},{12... | collective-permute-start | bytes 2752520 | tf_op jit(solution)/shard_map/ppermute | solution.py:237
  194.8 445.6 %collective-permute-start.53 = (bf16[512,2048]{1,0:T(8,128)(2,1)}, bf16[512,2048]{1,0:T(8,128)(2,1)}, u32[]{:S(2)}, u32[]{:S(2)}) collective-permute-start(bf16[512,2048]{1,0:T(8,128)(2,1)} %pad_maximum_fusion.14), channel_id=1, source_target_pairs={{0,8},{8,0},{1,9},{9,1},{2,10},{10,2},{3,11},{11,3},{4,12},{12,4},... | collective-permute-start | bytes 6291464 | tf_op jit(solution)/shard_map/ppermute | solution.py:237
  210.4 224.9 %collective-permute-start.46 = (bf16[512,2048]{1,0:T(8,128)(2,1)}, bf16[512,2048]{1,0:T(8,128)(2,1)}, u32[]{:S(2)}, u32[]{:S(2)}) collective-permute-start(bf16[512,2048]{1,0:T(8,128)(2,1)} %pad_maximum_fusion.13), channel_id=1, source_target_pairs={{0,8},{8,0},{1,9},{9,1},{2,10},{10,2},{3,11},{11,3},{4,12},{12,4},... | collective-permute-start | bytes 6291464 | tf_op jit(solution)/shard_map/ppermute | solution.py:237
  233.4 185.3 %collective-permute-start.31 = (bf16[2,2,4,64,1792]{4,3,2,1,0:T(8,128)(2,1)}, bf16[2,2,4,64,1792]{4,3,2,1,0:T(8,128)(2,1)}, u32[]{:S(2)}, u32[]{:S(2)}) collective-permute-start(bf16[2,2,4,64,1792]{4,3,2,1,0:T(8,128)(2,1)} %select_select_fusion), channel_id=1, source_target_pairs={{0,1},{1,0},{2,3},{3,2},{4,5},{5,4},{6,7},{7,6},{8,9},{9,8},{10,11... | collective-permute-start | bytes 11010056 | tf_op jit(solution)/shard_map/ppermute | solution.py:237
  242.7 78.3 %collective-permute-start.12 = (bf16[640,256]{1,0:T(8,128)(2,1)S(1)}, bf16[640,256]{1,0:T(8,128)(2,1)S(1)}, u32[]{:S(2)}, u32[]{:S(2)}) collective-permute-start(bf16[640,256]{1,0:T(8,128)(2,1)S(1)} %pad_maximum_fusion.41), channel_id=1, source_target_pairs={{0,1},{1,0},{2,3},{3,2},{4,5},{5,4},{6,7},{7,6},{8,9},{9,8},{10,11... | collective-permute-start | bytes 983048 | tf_op jit(solution)/shard_map/ppermute | solution.py:237
  372.8 21.7 %collective-permute-start.24 = (bf16[256,2048]{1,0:T(8,128)(2,1)S(1)}, bf16[256,2048]{1,0:T(8,128)(2,1)S(1)}, u32[]{:S(2)}, u32[]{:S(2)}) collective-permute-start(bf16[256,2048]{1,0:T(8,128)(2,1)S(1)} %multiply_convert_fusion.7), channel_id=1, source_target_pairs={{0,16},{16,0},{1,17},{17,1},{2,18},{18,2},{3,19},{19,3},{4,20},{20... | collective-permute-start | bytes 3145736 | tf_op jit(solution)/shard_map/ppermute | solution.py:237
  375.6 21.6 %collective-permute-start.38 = (bf16[640,256]{1,0:T(8,128)(2,1)S(1)}, bf16[640,256]{1,0:T(8,128)(2,1)S(1)}, u32[]{:S(2)}, u32[]{:S(2)}) collective-permute-start(bf16[640,256]{1,0:T(8,128)(2,1)S(1)} %pad_maximum_fusion.42), channel_id=1, source_target_pairs={{0,1},{1,0},{2,3},{3,2},{4,5},{5,4},{6,7},{7,6},{8,9},{9,8},{10,11... | collective-permute-start | bytes 983048 | tf_op jit(solution)/shard_map/ppermute | solution.py:237
  394.7 28.4 %collective-permute-start.25 = (bf16[512,2048]{1,0:T(8,128)(2,1)S(1)}, bf16[512,2048]{1,0:T(8,128)(2,1)S(1)}, u32[]{:S(2)}, u32[]{:S(2)}) collective-permute-start(bf16[512,2048]{1,0:T(8,128)(2,1)S(1)} %pad_maximum_fusion.10), channel_id=1, source_target_pairs={{0,8},{8,0},{1,9},{9,1},{2,10},{10,2},{3,11},{11,3},{4,12},{12,4},... | collective-permute-start | bytes 6291464 | tf_op jit(solution)/shard_map/ppermute | solution.py:237
  397.7 19.2 %collective-permute-start.39 = (bf16[640,512]{1,0:T(8,128)(2,1)S(1)}, bf16[640,512]{1,0:T(8,128)(2,1)}, u32[]{:S(2)}, u32[]{:S(2)}) collective-permute-start(bf16[640,512]{1,0:T(8,128)(2,1)S(1)} %broadcast_select_fusion.15), channel_id=1, source_target_pairs={{0,2},{2,4},{4,6},{6,0},{1,3},{3,5},{5,7},{7,1},{8,10},{10,12},{12... | collective-permute-start | bytes 1966088 | tf_op jit(solution)/shard_map/ppermute | solution.py:237
  416.9 51.2 %collective-permute-start.40 = (bf16[640,512]{1,0:T(8,128)(2,1)}, bf16[640,512]{1,0:T(8,128)(2,1)S(1)}, u32[]{:S(2)}, u32[]{:S(2)}) collective-permute-start(bf16[640,512]{1,0:T(8,128)(2,1)} %collective-permute-done.39), channel_id=1, source_target_pairs={{0,2},{2,4},{4,6},{6,0},{1,3},{3,5},{5,7},{7,1},{8,10},{10,12},{12... | collective-permute-start | bytes 1966088 | tf_op jit(solution)/shard_map/ppermute | solution.py:237
  460.3 21.4 %collective-permute-start.47 = (bf16[2,256,2048]{2,1,0:T(8,128)(2,1)}, bf16[2,256,2048]{2,1,0:T(8,128)(2,1)}, u32[]{:S(2)}, u32[]{:S(2)}) collective-permute-start(bf16[2,256,2048]{2,1,0:T(8,128)(2,1)} %bitcast.49), channel_id=1, source_target_pairs={{0,8},{8,0},{1,9},{9,1},{2,10},{10,2},{3,11},{11,3},{4,12},{12,4},... | collective-permute-start | bytes 6291464 | tf_op jit(solution)/shard_map/ppermute | solution.py:237
  484.6 26.1 %collective-permute-start.48 = (bf16[256,2048]{1,0:T(8,128)(2,1)S(1)}, bf16[256,2048]{1,0:T(8,128)(2,1)S(1)}, u32[]{:S(2)}, u32[]{:S(2)}) collective-permute-start(bf16[256,2048]{1,0:T(8,128)(2,1)S(1)} %fusion.69), channel_id=1, source_target_pairs={{0,16},{16,0},{1,17},{17,1},{2,18},{18,2},{3,19},{19,3},{4,20},{20... | collective-permute-start | bytes 3145736 | tf_op jit(solution)/shard_map/ppermute | solution.py:237
  488.8 43.3 %collective-permute-start.37 = (bf16[256,2048]{1,0:T(8,128)(2,1)S(1)}, bf16[256,2048]{1,0:T(8,128)(2,1)S(1)}, u32[]{:S(2)}, u32[]{:S(2)}) collective-permute-start(bf16[256,2048]{1,0:T(8,128)(2,1)S(1)} %fusion.66), channel_id=1, source_target_pairs={{0,16},{16,0},{1,17},{17,1},{2,18},{18,2},{3,19},{19,3},{4,20},{20... | collective-permute-start | bytes 3145736 | tf_op jit(solution)/shard_map/ppermute | solution.py:237
  535.9 68.6 %collective-permute-start.41 = (bf16[256,2048]{1,0:T(8,128)(2,1)}, bf16[256,2048]{1,0:T(8,128)(2,1)}, u32[]{:S(2)}, u32[]{:S(2)}) collective-permute-start(bf16[256,2048]{1,0:T(8,128)(2,1)} %get-tuple-element.84), channel_id=1, source_target_pairs={{0,16},{16,0},{1,17},{17,1},{2,18},{18,2},{3,19},{19,3},{4,20},{20... | collective-permute-start | bytes 3145736 | tf_op jit(solution)/shard_map/ppermute | solution.py:237
  557.0 42.4 %collective-permute-start.49 = (bf16[640,512]{0,1:T(8,128)(2,1)S(1)}, bf16[640,512]{0,1:T(8,128)(2,1)S(1)}, u32[]{:S(2)}, u32[]{:S(2)}) collective-permute-start(bf16[640,512]{0,1:T(8,128)(2,1)S(1)} %slice_bitcast_fusion.9), channel_id=1, source_target_pairs={{0,6},{2,0},{4,2},{6,4},{1,7},{3,1},{5,3},{7,5},{8,14},{10,8},{12,... | collective-permute-start | bytes 1966088 | tf_op jit(solution)/shard_map/ppermute | solution.py:237
  681.2 43.2 %collective-permute-start.95 = (bf16[4,112,2048]{2,1,0:T(8,128)(2,1)}, bf16[4,112,2048]{2,1,0:T(8,128)(2,1)}, u32[]{:S(2)}, u32[]{:S(2)}) collective-permute-start(bf16[4,112,2048]{2,1,0:T(8,128)(2,1)} %dynamic-slice_bitcast_fusion.2), channel_id=1, source_target_pairs={{0,1},{1,0},{2,3},{3,2},{4,5},{5,4},{6,7},{7,6},{8,9},{9,8},{10,11... | collective-permute-start | bytes 5505032 | tf_op jit(solution)/shard_map/ppermute | solution.py:237
  682.6 52.4 %collective-permute-start.43 = (bf16[2,256,2048]{2,1,0:T(8,128)(2,1)S(1)}, bf16[2,256,2048]{2,1,0:T(8,128)(2,1)}, u32[]{:S(2)}, u32[]{:S(2)}) collective-permute-start(bf16[2,256,2048]{2,1,0:T(8,128)(2,1)S(1)} %bitcast.571), channel_id=1, source_target_pairs={{0,8},{8,0},{1,9},{9,1},{2,10},{10,2},{3,11},{11,3},{4,12},{12,4},... | collective-permute-start | bytes 6291464 | tf_op jit(solution)/shard_map/ppermute | solution.py:237
  682.6 48.7 %collective-permute-start.54 = (bf16[2,256,2048]{2,1,0:T(8,128)(2,1)}, bf16[2,256,2048]{2,1,0:T(8,128)(2,1)}, u32[]{:S(2)}, u32[]{:S(2)}) collective-permute-start(bf16[2,256,2048]{2,1,0:T(8,128)(2,1)} %bitcast.74), channel_id=1, source_target_pairs={{0,8},{8,0},{1,9},{9,1},{2,10},{10,2},{3,11},{11,3},{4,12},{12,4},... | collective-permute-start | bytes 6291464 | tf_op jit(solution)/shard_map/ppermute | solution.py:237
  715.7 134.3 %collective-permute-start.89 = (bf16[2,2,4,64,1792]{4,3,2,1,0:T(8,128)(2,1)}, bf16[2,2,4,64,1792]{4,3,2,1,0:T(8,128)(2,1)}, u32[]{:S(2)}, u32[]{:S(2)}) collective-permute-start(bf16[2,2,4,64,1792]{4,3,2,1,0:T(8,128)(2,1)} %dynamic-slice_bitcast_fusion), channel_id=1, source_target_pairs={{0,1},{1,0},{2,3},{3,2},{4,5},{5,4},{6,7},{7,6},{8,9},{9,8},{10,11... | collective-permute-start | bytes 11010056 | tf_op jit(solution)/shard_map/ppermute | solution.py:237
  729.0 20.8 %collective-permute-start.98 = (bf16[112,2048]{1,0:T(8,128)(2,1)S(1)}, bf16[112,2048]{1,0:T(8,128)(2,1)S(1)}, u32[]{:S(2)}, u32[]{:S(2)}) collective-permute-start(bf16[112,2048]{1,0:T(8,128)(2,1)S(1)} %get-tuple-element.86), channel_id=1, source_target_pairs={{0,6},{2,0},{4,2},{6,4},{1,7},{3,1},{5,3},{7,5},{8,14},{10,8},{12,... | collective-permute-start | bytes 1376264 | tf_op jit(solution)/shard_map/ppermute | solution.py:237
  731.3 38.4 %collective-permute-start.97 = (bf16[112,2048]{1,0:T(8,128)(2,1)S(1)}, bf16[112,2048]{1,0:T(8,128)(2,1)S(1)}, u32[]{:S(2)}, u32[]{:S(2)}) collective-permute-start(bf16[112,2048]{1,0:T(8,128)(2,1)S(1)} %get-tuple-element.87), channel_id=1, source_target_pairs={{0,4},{2,6},{4,0},{6,2},{1,5},{3,7},{5,1},{7,3},{8,12},{10,14},{12... | collective-permute-start | bytes 1376264 | tf_op jit(solution)/shard_map/ppermute | solution.py:237
  735.0 35.9 %collective-permute-start.55 = (bf16[256,2048]{1,0:T(8,128)(2,1)S(1)}, bf16[256,2048]{1,0:T(8,128)(2,1)S(1)}, u32[]{:S(2)}, u32[]{:S(2)}) collective-permute-start(bf16[256,2048]{1,0:T(8,128)(2,1)S(1)} %fusion.70), channel_id=1, source_target_pairs={{0,16},{16,0},{1,17},{17,1},{2,18},{18,2},{3,19},{19,3},{4,20},{20... | collective-permute-start | bytes 3145736 | tf_op jit(solution)/shard_map/ppermute | solution.py:237
  742.6 37.4 %collective-permute-start.44 = (bf16[256,2048]{1,0:T(8,128)(2,1)S(1)}, bf16[256,2048]{1,0:T(8,128)(2,1)S(1)}, u32[]{:S(2)}, u32[]{:S(2)}) collective-permute-start(bf16[256,2048]{1,0:T(8,128)(2,1)S(1)} %fusion.68), channel_id=1, source_target_pairs={{0,16},{16,0},{1,17},{17,1},{2,18},{18,2},{3,19},{19,3},{4,20},{20... | collective-permute-start | bytes 3145736 | tf_op jit(solution)/shard_map/ppermute | solution.py:237
  807.0 42.7 %collective-permute-start.56 = (bf16[640,512]{0,1:T(8,128)(2,1)S(1)}, bf16[640,512]{0,1:T(8,128)(2,1)S(1)}, u32[]{:S(2)}, u32[]{:S(2)}) collective-permute-start(bf16[640,512]{0,1:T(8,128)(2,1)S(1)} %slice_bitcast_fusion.6), channel_id=1, source_target_pairs={{0,6},{2,0},{4,2},{6,4},{1,7},{3,1},{5,3},{7,5},{8,14},{10,8},{12,... | collective-permute-start | bytes 1966088 | tf_op jit(solution)/shard_map/ppermute | solution.py:237
  845.5 46.5 %collective-permute-start.83 = (bf16[2,4,2,40,1024]{4,3,1,2,0:T(8,128)(2,1)S(1)}, bf16[2,4,2,40,1024]{4,3,1,2,0:T(8,128)(2,1)}, u32[]{:S(2)}, u32[]{:S(2)}) collective-permute-start(bf16[2,4,2,40,1024]{4,3,1,2,0:T(8,128)(2,1)S(1)} %bitcast.572), channel_id=1, source_target_pairs={{0,8},{8,0},{1,9},{9,1},{2,10},{10,2},{3,11},{11,3},{4,12},{12,4},... | collective-permute-start | bytes 3932168 | tf_op jit(solution)/shard_map/ppermute | solution.py:237
  845.6 49.7 %collective-permute-start.77 = (bf16[2,4,2,40,1024]{4,3,1,0,2:T(8,128)(2,1)}, bf16[2,4,2,40,1024]{4,3,1,0,2:T(8,128)(2,1)}, u32[]{:S(2)}, u32[]{:S(2)}) collective-permute-start(bf16[2,4,2,40,1024]{4,3,1,0,2:T(8,128)(2,1)} %bitcast.517), channel_id=1, source_target_pairs={{0,8},{8,0},{1,9},{9,1},{2,10},{10,2},{3,11},{11,3},{4,12},{12,4},... | collective-permute-start | bytes 3932168 | tf_op jit(solution)/shard_map/ppermute | solution.py:237
  849.9 37.3 %collective-permute-start.57 = (bf16[640,512]{0,1:T(8,128)(2,1)S(1)}, bf16[640,512]{0,1:T(8,128)(2,1)S(1)}, u32[]{:S(2)}, u32[]{:S(2)}) collective-permute-start(bf16[640,512]{0,1:T(8,128)(2,1)S(1)} %fusion.60), channel_id=1, source_target_pairs={{0,6},{2,0},{4,2},{6,4},{1,7},{3,1},{5,3},{7,5},{8,14},{10,8},{12,... | collective-permute-start | bytes 1966088 | tf_op jit(solution)/shard_map/ppermute | solution.py:237
  855.8 44.1 %collective-permute-start.90 = (bf16[2,2,64,1792]{3,2,1,0:T(8,128)(2,1)}, bf16[2,2,64,1792]{3,2,1,0:T(8,128)(2,1)}, u32[]{:S(2)}, u32[]{:S(2)}) collective-permute-start(bf16[2,2,64,1792]{3,2,1,0:T(8,128)(2,1)} %get-tuple-element.69), channel_id=1, source_target_pairs={{0,2},{2,4},{4,6},{6,0},{1,3},{3,5},{5,7},{7,1},{8,10},{10,12},{12... | collective-permute-start | bytes 2752520 | tf_op jit(solution)/shard_map/ppermute | solution.py:237
  858.2 51.6 %collective-permute-start.92 = (bf16[2,2,64,1792]{3,2,1,0:T(8,128)(2,1)}, bf16[2,2,64,1792]{3,2,1,0:T(8,128)(2,1)}, u32[]{:S(2)}, u32[]{:S(2)}) collective-permute-start(bf16[2,2,64,1792]{3,2,1,0:T(8,128)(2,1)} %get-tuple-element.70), channel_id=1, source_target_pairs={{0,6},{2,0},{4,2},{6,4},{1,7},{3,1},{5,3},{7,5},{8,14},{10,8},{12,... | collective-permute-start | bytes 2752520 | tf_op jit(solution)/shard_map/ppermute | solution.py:237
  887.2 51.0 %collective-permute-start.91 = (bf16[2,2,64,1792]{3,2,1,0:T(8,128)(2,1)}, bf16[2,2,64,1792]{3,2,1,0:T(8,128)(2,1)}, u32[]{:S(2)}, u32[]{:S(2)}) collective-permute-start(bf16[2,2,64,1792]{3,2,1,0:T(8,128)(2,1)} %get-tuple-element.71), channel_id=1, source_target_pairs={{0,4},{2,6},{4,0},{6,2},{1,5},{3,7},{5,1},{7,3},{8,12},{10,14},{12... | collective-permute-start | bytes 2752520 | tf_op jit(solution)/shard_map/ppermute | solution.py:237
  892.0 49.7 %collective-permute-start.58 = (bf16[640,256]{1,0:T(8,128)(2,1)}, bf16[640,256]{1,0:T(8,128)(2,1)S(1)}, u32[]{:S(2)}, u32[]{:S(2)}) collective-permute-start(bf16[640,256]{1,0:T(8,128)(2,1)} %bitcast.593), channel_id=1, source_target_pairs={{0,1},{1,0},{2,3},{3,2},{4,5},{5,4},{6,7},{7,6},{8,9},{9,8},{10,11... | collective-permute-start | bytes 983048 | tf_op jit(solution)/shard_map/ppermute | solution.py:237
  895.3 103.7 %collective-permute-start.84 = (bf16[4,2,40,1024]{3,2,0,1:T(8,128)(2,1)}, bf16[4,2,40,1024]{3,2,0,1:T(8,128)(2,1)}, u32[]{:S(2)}, u32[]{:S(2)}) collective-permute-start(bf16[4,2,40,1024]{3,2,0,1:T(8,128)(2,1)} %dynamic-slice_bitcast_fusion.8), channel_id=1, source_target_pairs={{0,16},{16,0},{1,17},{17,1},{2,18},{18,2},{3,19},{19,3},{4,20},{20... | collective-permute-start | bytes 1966088 | tf_op jit(solution)/shard_map/ppermute | solution.py:237
  899.9 102.5 %collective-permute-start.78 = (bf16[2,4,40,1024]{3,2,1,0:T(8,128)(2,1)}, bf16[2,4,40,1024]{3,2,1,0:T(8,128)(2,1)}, u32[]{:S(2)}, u32[]{:S(2)}) collective-permute-start(bf16[2,4,40,1024]{3,2,1,0:T(8,128)(2,1)} %dynamic-slice_bitcast_fusion.9), channel_id=1, source_target_pairs={{0,1},{1,0},{2,3},{3,2},{4,5},{5,4},{6,7},{7,6},{8,9},{9,8},{10,11... | collective-permute-start | bytes 1966088 | tf_op jit(solution)/shard_map/ppermute | solution.py:237
  941.7 53.7 %collective-permute-start.93 = (bf16[2,64,1792]{2,1,0:T(8,128)(2,1)}, bf16[2,64,1792]{2,1,0:T(8,128)(2,1)}, u32[]{:S(2)}, u32[]{:S(2)}) collective-permute-start(bf16[2,64,1792]{2,1,0:T(8,128)(2,1)} %get-tuple-element.113), channel_id=1, source_target_pairs={{0,16},{16,0},{1,17},{17,1},{2,18},{18,2},{3,19},{19,3},{4,20},{20... | collective-permute-start | bytes 1376264 | tf_op jit(solution)/shard_map/ppermute | solution.py:237
  978.4 45.1 %collective-permute-start.59 = (bf16[2,4,2,64,960]{4,3,2,1,0:T(8,128)(2,1)}, bf16[2,4,2,64,960]{4,3,2,1,0:T(8,128)(2,1)}, u32[]{:S(2)}, u32[]{:S(2)}) collective-permute-start(bf16[2,4,2,64,960]{4,3,2,1,0:T(8,128)(2,1)} %dynamic-slice_bitcast_fusion.1), channel_id=1, source_target_pairs={{0,8},{8,0},{1,9},{9,1},{2,10},{10,2},{3,11},{11,3},{4,12},{12,4},... | collective-permute-start | bytes 5898248 | tf_op jit(solution)/shard_map/ppermute | solution.py:237
  994.7 34.0 %collective-permute-start.65 = (bf16[2,4,2,64,960]{4,3,1,2,0:T(8,128)(2,1)}, bf16[2,4,2,64,960]{4,3,1,2,0:T(8,128)(2,1)}, u32[]{:S(2)}, u32[]{:S(2)}) collective-permute-start(bf16[2,4,2,64,960]{4,3,1,2,0:T(8,128)(2,1)} %bitcast.515), channel_id=1, source_target_pairs={{0,8},{8,0},{1,9},{9,1},{2,10},{10,2},{3,11},{11,3},{4,12},{12,4},... | collective-permute-start | bytes 5898248 | tf_op jit(solution)/shard_map/ppermute | solution.py:237
  1011.1 23.9 %collective-permute-start.86 = (bf16[40,1024]{1,0:T(8,128)(2,1)}, bf16[40,1024]{1,0:T(8,128)(2,1)S(1)}, u32[]{:S(2)}, u32[]{:S(2)}) collective-permute-start(bf16[40,1024]{1,0:T(8,128)(2,1)} %get-tuple-element.146), channel_id=1, source_target_pairs={{0,2},{2,4},{4,6},{6,0},{1,3},{3,5},{5,7},{7,1},{8,10},{10,12},{12... | collective-permute-start | bytes 245768 | tf_op jit(solution)/shard_map/ppermute | solution.py:237
  1013.2 22.5 %collective-permute-start.88 = (bf16[40,1024]{1,0:T(8,128)(2,1)}, bf16[40,1024]{1,0:T(8,128)(2,1)}, u32[]{:S(2)}, u32[]{:S(2)}) collective-permute-start(bf16[40,1024]{1,0:T(8,128)(2,1)} %get-tuple-element.147), channel_id=1, source_target_pairs={{0,6},{2,0},{4,2},{6,4},{1,7},{3,1},{5,3},{7,5},{8,14},{10,8},{12,... | collective-permute-start | bytes 245768 | tf_op jit(solution)/shard_map/ppermute | solution.py:237
  1015.8 23.0 %collective-permute-start.87 = (bf16[40,1024]{1,0:T(8,128)(2,1)}, bf16[40,1024]{1,0:T(8,128)(2,1)}, u32[]{:S(2)}, u32[]{:S(2)}) collective-permute-start(bf16[40,1024]{1,0:T(8,128)(2,1)} %get-tuple-element.148), channel_id=1, source_target_pairs={{0,4},{2,6},{4,0},{6,2},{1,5},{3,7},{5,1},{7,3},{8,12},{10,14},{12... | collective-permute-start | bytes 245768 | tf_op jit(solution)/shard_map/ppermute | solution.py:237
  1027.0 24.0 %collective-permute-start.60 = (bf16[2,4,64,960]{3,2,1,0:T(8,128)(2,1)S(1)}, bf16[2,4,64,960]{3,2,1,0:T(8,128)(2,1)S(1)}, u32[]{:S(2)}, u32[]{:S(2)}) collective-permute-start(bf16[2,4,64,960]{3,2,1,0:T(8,128)(2,1)S(1)} %dynamic-slice_bitcast_fusion.4), channel_id=1, source_target_pairs={{0,1},{1,0},{2,3},{3,2},{4,5},{5,4},{6,7},{7,6},{8,9},{9,8},{10,11... | collective-permute-start | bytes 2949128 | tf_op jit(solution)/shard_map/ppermute | solution.py:237
  1031.6 26.1 %collective-permute-start.66 = (bf16[4,2,64,960]{3,2,0,1:T(8,128)(2,1)S(1)}, bf16[4,2,64,960]{3,2,0,1:T(8,128)(2,1)S(1)}, u32[]{:S(2)}, u32[]{:S(2)}) collective-permute-start(bf16[4,2,64,960]{3,2,0,1:T(8,128)(2,1)S(1)} %dynamic-slice_bitcast_fusion.3), channel_id=1, source_target_pairs={{0,16},{16,0},{1,17},{17,1},{2,18},{18,2},{3,19},{19,3},{4,20},{20... | collective-permute-start | bytes 2949128 | tf_op jit(solution)/shard_map/ppermute | solution.py:237
  (192 other events, 5833.0 us)

commit v2 on v1

v2 whole, which is shorter than its diff:
```python
import functools
import math

import jax
import jax.numpy as jnp
import numpy as np
from jax import lax
from jax.experimental import pallas as pl
from jax.experimental.pallas import tpu as pltpu
from jax.sharding import Mesh
from jax.sharding import PartitionSpec as P

HEADS = 20
KV_HEADS = 5
GROUP = HEADS // KV_HEADS
HEAD_DIM = 64
TAGS = 4
Q_WIDTH = HEADS * HEAD_DIM
KV_WIDTH = KV_HEADS * HEAD_DIM
DOC_MOST = 1024
Z_CHIPS = 4
EPS = 1e-06
SCORE_SCALE = 0.125
LOG2E = math.log2(math.e)
MASKED = -1e30

bf16 = jnp.bfloat16
f32 = jnp.float32


def dot(left, right, left_dim, right_dim):
    return lax.dot_general(
        left, right, (((left_dim,), (right_dim,)), ((), ())), preferred_element_type=f32
    )


def matmul(left, right):
    return dot(left, right, 1, 0)


def block_slot(block, at_x, xs):
    return (block // xs) * xs + lax.rem(at_x - lax.rem(block, xs) + xs, xs)


def forward_kernel(xs, meta, start_ref, q_ref, k_ref, v_ref, o_ref, lse_ref, bias_ref, q_rows, acc):
    rows = q_ref.shape[1]
    size = k_ref.shape[2]
    low, high, q_start, at_x = meta[0], meta[1], meta[2], meta[3]

    @pl.when(pl.program_id(0) == 0)
    def _():
        q_pos = q_start + lax.broadcasted_iota(jnp.int32, (rows, size), 0)
        lanes = lax.broadcasted_iota(jnp.int32, (rows, size), 1)

        def fill(block, carry):
            key_pos = block * size + lanes
            allowed = (key_pos >= start_ref[...]) & (key_pos <= q_pos)
            bias_ref[block] = jnp.where(allowed, 0.0, MASKED)
            return carry

        lax.fori_loop(low, high, fill, 0)

    q_cols = q_ref[...].T
    for head in range(GROUP):
        q_rows[head] = q_cols[:, head * HEAD_DIM : (head + 1) * HEAD_DIM]
    sub = lax.broadcasted_iota(jnp.int32, (HEAD_DIM, size), 0)
    ones = jnp.where(sub == 0, 1.0, 0.0).astype(bf16)
    acc[...] = jnp.zeros_like(acc)

    def body(block, carry):
        slot = block_slot(block, at_x, xs)
        key_cols = k_ref[slot]
        value_rows = jnp.concatenate([v_ref[slot], ones], axis=0).T
        bias = bias_ref[block]
        for head in range(GROUP):
            raw = jnp.dot(q_rows[head], key_cols, preferred_element_type=f32)
            probs = jnp.exp2(raw * (SCORE_SCALE * LOG2E) + bias).astype(bf16)
            acc[head] += jnp.dot(probs, value_rows, preferred_element_type=f32)
        return carry

    lax.fori_loop(low, high, body, 0)
    for head in range(GROUP):
        turned = acc[head].T
        total = turned[HEAD_DIM : HEAD_DIM + 1, :]
        o_ref[head * HEAD_DIM : (head + 1) * HEAD_DIM, :] = (turned[:HEAD_DIM] / total).astype(bf16)
        lse_ref[0, head : head + 1, :] = jnp.log2(total)


def backward_kernel(
    xs, meta, start_ref, q_ref, k_ref, v_ref, go_ref, o_ref, lse_ref,
    dq_ref, dkv_ref, bias_ref, q_rows, go_rows, dq_acc, delta_ref,
):
    rows = q_ref.shape[1]
    size = k_ref.shape[2]
    low, high, q_start, at_x = meta[0], meta[1], meta[2], meta[3]

    @pl.when(pl.program_id(0) == 0)
    def _():
        q_pos = q_start + lax.broadcasted_iota(jnp.int32, (size, rows), 1)
        subs = lax.broadcasted_iota(jnp.int32, (size, rows), 0)

        def fill(block, carry):
            key_pos = block * size + subs
            allowed = (key_pos >= start_ref[...]) & (key_pos <= q_pos)
            bias_ref[block] = jnp.where(allowed, 0.0, MASKED)
            return carry

        lax.fori_loop(low, high, fill, 0)

    q_cols = q_ref[...].T
    go_cols = go_ref[...].T
    for head in range(GROUP):
        part = slice(head * HEAD_DIM, (head + 1) * HEAD_DIM)
        q_rows[head] = q_cols[:, part]
        go_rows[head] = go_cols[:, part]
        delta_ref[head : head + 1, :] = jnp.sum(
            go_ref[part, :].astype(f32) * o_ref[part, :].astype(f32), axis=0, keepdims=True
        )
    dkv_ref[...] = jnp.zeros_like(dkv_ref)
    dq_acc[...] = jnp.zeros_like(dq_acc)

    def body(block, carry):
        slot = block_slot(block, at_x, xs)
        key_cols = k_ref[slot]
        key_rows = key_cols.T
        value_rows = v_ref[slot].T
        bias = bias_ref[block]
        dk = jnp.zeros((size, HEAD_DIM), f32)
        dv = jnp.zeros((size, HEAD_DIM), f32)
        for head in range(GROUP):
            part = slice(head * HEAD_DIM, (head + 1) * HEAD_DIM)
            raw = jnp.dot(key_rows, q_ref[part, :], preferred_element_type=f32)
            probs = jnp.exp2(
                raw * (SCORE_SCALE * LOG2E) + (bias - lse_ref[0, head : head + 1, :])
            )
            grad_probs = jnp.dot(value_rows, go_ref[part, :], preferred_element_type=f32)
            grad_scores = (probs * (grad_probs - delta_ref[head : head + 1, :])).astype(bf16)
            dv += jnp.dot(probs.astype(bf16), go_rows[head], preferred_element_type=f32)
            dk += jnp.dot(grad_scores, q_rows[head], preferred_element_type=f32)
            dq_acc[part, :] += jnp.dot(key_cols, grad_scores, preferred_element_type=f32)
        dkv_ref[slot, 0] = (SCORE_SCALE * dk).T.astype(bf16)
        dkv_ref[slot, 1] = dv.T.astype(bf16)
        return carry

    lax.fori_loop(low, high, body, 0)
    dq_ref[...] = (SCORE_SCALE * dq_acc[...]).astype(bf16)


def attend_forward(xs, meta, start_col, q_t, batch, window):
    rows = start_col.shape[0]
    blocks, _, size = window.shape
    wide = GROUP * HEAD_DIM
    return pl.pallas_call(
        functools.partial(forward_kernel, xs),
        name="attend_forward",
        grid_spec=pltpu.PrefetchScalarGridSpec(
            num_scalar_prefetch=1,
            grid=(KV_HEADS,),
            in_specs=[
                pl.BlockSpec((rows, 1), lambda g, m: (0, 0)),
                pl.BlockSpec((wide, rows), lambda g, m: (g, batch)),
                pl.BlockSpec((blocks, HEAD_DIM, size), lambda g, m: (0, g, 0)),
                pl.BlockSpec((blocks, HEAD_DIM, size), lambda g, m: (0, KV_HEADS + g, 0)),
            ],
            out_specs=[
                pl.BlockSpec((wide, rows), lambda g, m: (g, 0)),
                pl.BlockSpec((1, GROUP, rows), lambda g, m: (g, 0, 0)),
            ],
            scratch_shapes=[
                pltpu.VMEM((blocks, rows, size), f32),
                pltpu.VMEM((GROUP, rows, HEAD_DIM), bf16),
                pltpu.VMEM((GROUP, rows, 2 * HEAD_DIM), f32),
            ],
        ),
        out_shape=[
            jax.ShapeDtypeStruct((Q_WIDTH, rows), bf16),
            jax.ShapeDtypeStruct((KV_HEADS, GROUP, rows), f32),
        ],
        cost_estimate=pl.CostEstimate(
            flops=4 * HEADS * rows * blocks * size * 128, bytes_accessed=4 * 1024 * 1024,
            transcendentals=HEADS * rows * blocks * size,
        ),
    )(meta, start_col, q_t, window, window)


def attend_backward(xs, meta, start_row, q_t, batch, window, go_t, o_t, lse):
    rows = start_row.shape[1]
    blocks, _, size = window.shape
    wide = GROUP * HEAD_DIM
    return pl.pallas_call(
        functools.partial(backward_kernel, xs),
        name="attend_backward",
        grid_spec=pltpu.PrefetchScalarGridSpec(
            num_scalar_prefetch=1,
            grid=(KV_HEADS,),
            in_specs=[
                pl.BlockSpec((1, rows), lambda g, m: (0, 0)),
                pl.BlockSpec((wide, rows), lambda g, m: (g, batch)),
                pl.BlockSpec((blocks, HEAD_DIM, size), lambda g, m: (0, g, 0)),
                pl.BlockSpec((blocks, HEAD_DIM, size), lambda g, m: (0, KV_HEADS + g, 0)),
                pl.BlockSpec((wide, rows), lambda g, m: (g, 0)),
                pl.BlockSpec((wide, rows), lambda g, m: (g, 0)),
                pl.BlockSpec((1, GROUP, rows), lambda g, m: (g, 0, 0)),
            ],
            out_specs=[
                pl.BlockSpec((wide, rows), lambda g, m: (g, 0)),
                pl.BlockSpec((blocks, 2, HEAD_DIM, size), lambda g, m: (0, 0, g, 0)),
            ],
            scratch_shapes=[
                pltpu.VMEM((blocks, size, rows), f32),
                pltpu.VMEM((GROUP, rows, HEAD_DIM), bf16),
                pltpu.VMEM((GROUP, rows, HEAD_DIM), bf16),
                pltpu.VMEM((wide, rows), f32),
                pltpu.VMEM((8, rows), f32),
            ],
        ),
        out_shape=[
            jax.ShapeDtypeStruct((Q_WIDTH, rows), bf16),
            jax.ShapeDtypeStruct((blocks, 2, KV_WIDTH, size), bf16),
        ],
        cost_estimate=pl.CostEstimate(
            flops=10 * HEADS * rows * blocks * size * 128, bytes_accessed=8 * 1024 * 1024,
            transcendentals=HEADS * rows * blocks * size,
        ),
    )(meta, start_row, q_t, window, window, go_t, o_t, lse)


LAYOUT = "yczx"
CTX = ("z", "x")
DOC_ROWS = 16


def after(value, *earlier):
    return lax.optimization_barrier((value, *earlier))[0]


class Transfers:
    def __init__(self, sizes):
        self.sizes = sizes

    def shift(self, value, axis, step):
        size = self.sizes[axis]
        return lax.ppermute(value, axis, [(i, (i + step) % size) for i in range(size)])

    def hop(self, value, axis, step):
        size = self.sizes[axis]
        pairs = [(i, i + step) for i in range(size) if 0 <= i + step < size]
        return lax.ppermute(value, axis, pairs)

    def place(self, pieces, axis, dim):
        size = self.sizes[axis]
        if size == 1:
            return jnp.expand_dims(pieces[0], dim)
        shape = pieces[0].shape
        rank = len(shape) + 1
        index = lax.broadcasted_iota(
            jnp.int32, tuple(size if d == dim else 1 for d in range(rank)), dim
        )
        back = jnp.mod(lax.axis_index(axis) - index, size)
        whole = jnp.broadcast_to(
            jnp.expand_dims(pieces[0], dim), shape[:dim] + (size,) + shape[dim:]
        )
        for k in range(1, size):
            whole = jnp.where(back == k, jnp.expand_dims(pieces[k], dim), whole)
        return whole

    def ring(self, value, axis):
        pieces = [value]
        for _ in range(1, self.sizes[axis]):
            pieces.append(self.shift(pieces[-1], axis, 1))
        return pieces

    def direct(self, value, axis):
        return [value] + [self.shift(value, axis, k) for k in range(1, self.sizes[axis])]

    def total(self, value, axis):
        size, step = self.sizes[axis], 1
        while step < size:
            value = value + lax.ppermute(value, axis, [(i, i ^ step) for i in range(size)])
            step *= 2
        return value

    def gather(self, value, axis, dim):
        return self.place(self.ring(value, axis), axis, dim)

    def take(self, value, axis, dim, step):
        size = self.sizes[axis]
        index = jnp.mod(lax.axis_index(axis) + step, size)
        return lax.dynamic_index_in_dim(value, index, dim, keepdims=False)

    def scatter(self, value, axis, dim):
        total = self.take(value, axis, dim, 0).astype(f32)
        for k in range(1, self.sizes[axis]):
            sent = self.take(value, axis, dim, k).astype(bf16)
            total = total + self.shift(sent, axis, k).astype(f32)
        return total

    def exchange(self, value, axis, dim, out_dim):
        pieces = [self.take(value, axis, dim, 0)]
        for k in range(1, self.sizes[axis]):
            pieces.append(self.shift(self.take(value, axis, dim, k), axis, k))
        return self.place(pieces, axis, out_dim)

    def spread(self, pieces, order):
        value = self.place(pieces, "z", 0)
        have = ["z"]
        for axis in order:
            dim = sum(1 for a in have if LAYOUT.index(a) < LAYOUT.index(axis))
            value = self.gather(value, axis, dim)
            have.append(axis)
        return value

    def scatter_chips(self, value, order):
        have = [axis for axis in LAYOUT if axis in order]
        for number, axis in enumerate(order):
            value = self.scatter(value, axis, have.index(axis))
            if number < len(order) - 1:
                value = value.astype(bf16)
            have.remove(axis)
        return value


def head_forward(lin, gain, cosine, sine):
    scale = lax.rsqrt(jnp.mean(lin * lin, axis=1, keepdims=True) + EPS)
    normal = lin * scale * gain[None, :, None]
    half = HEAD_DIM // 2
    first, second = normal[:, :half], normal[:, half:]
    turned = jnp.concatenate(
        [first * cosine - second * sine, second * cosine + first * sine], axis=1
    )
    return turned, scale


def head_backward(grad, lin, scale, gain, cosine, sine):
    half = HEAD_DIM // 2
    first, second = grad[:, :half], grad[:, half:]
    back = jnp.concatenate(
        [first * cosine + second * sine, second * cosine - first * sine], axis=1
    )
    gain_grad = jnp.sum(back * lin * scale, axis=(0, 2))
    scaled = back * gain[None, :, None]
    lin_grad = scale * scaled - lin * (scale**3) * jnp.mean(scaled * lin, axis=1, keepdims=True)
    return lin_grad, gain_grad


def row_scale(values):
    return lax.rsqrt(jnp.mean(values * values, axis=-1, keepdims=True) + EPS)


def norm_backward(grad, values, scale):
    return scale * grad - values * (scale**3) * jnp.mean(grad * values, axis=-1, keepdims=True)


def per_device(
    sizes, tokens, out_grad, doc_ids, corpus, corpus_weight, attn_gain, w_query, w_key, w_value,
    query_gain, key_gain, w_out, ffn_gain, w_gate, w_up, w_down,
):
    move = Transfers(sizes)
    ys, cs, zs, xs = (sizes[a] for a in LAYOUT)
    batches, local, width = tokens.shape
    both_rows = batches * local
    span = xs * local
    back_groups = -(-(DOC_MOST - 1) // span)
    at_z, at_x = lax.axis_index("z"), lax.axis_index("x")
    ffn_part = w_gate.shape[1] // (ys * cs)
    d_rows = w_gate.shape[0]
    parts = [slice(b * local, (b + 1) * local) for b in range(batches)]

    gain_a = attn_gain.astype(f32)[:, None]
    gain_f = ffn_gain.astype(f32)[:, None]
    w_kv = jnp.concatenate([w_key, w_value], axis=1)
    kv_near = move.direct((w_kv.astype(f32) * gain_a).astype(bf16), "z")
    w_q_low = (w_query.astype(f32) * gain_a).astype(bf16)
    q_near = move.direct(w_q_low, "z")
    w_kv_all = move.spread(kv_near, "xyc").reshape(width, 2 * KV_WIDTH)
    w_q_all = move.spread(q_near, "xyc").reshape(width, Q_WIDTH)
    w_out_all = lax.all_gather(w_out, tuple(LAYOUT), axis=0, tiled=True)

    w_gate_low = (w_gate.astype(f32) * gain_f).astype(bf16).reshape(d_rows, ys, cs, 1, ffn_part)
    w_up_low = (w_up.astype(f32) * gain_f).astype(bf16).reshape(d_rows, ys, cs, 1, ffn_part)
    both = jnp.concatenate([w_gate_low, w_up_low], axis=3).reshape(d_rows, ys, cs, 2 * ffn_part)
    both = move.exchange(both, "c", 2, 0)
    both = move.exchange(both, "y", 2, 0)
    both = lax.all_gather(both, CTX, axis=0)
    w_down_all = lax.all_gather(w_down, CTX, axis=0, tiled=True)
    w_both = both.transpose(1, 2, 0, 3, 4).reshape(width, 2 * ffn_part)

    q_start = back_groups * span + at_x * local
    high = back_groups * xs + at_x + 1

    half_dim = HEAD_DIM // 2
    frequency = jnp.exp(
        jnp.arange(half_dim, dtype=f32) * (-2.0 * math.log(10000.0) / HEAD_DIM)
    )
    positions = (at_z * xs + at_x) * local + jnp.arange(local, dtype=jnp.int32)
    angles = frequency[:, None] * jnp.tile(positions, batches).astype(f32)[None, :]
    cosine, sine = jnp.cos(angles)[None], jnp.sin(angles)[None]
    gain_q, gain_k = query_gain.astype(f32), key_gain.astype(f32)

    tag_range = jnp.arange(TAGS, dtype=jnp.int32)
    grads_out = [
        jnp.sum(jnp.where(tag_range == corpus[b], corpus_weight, 0.0)) * out_grad[b].astype(f32)
        for b in range(batches)
    ]

    def seq_blocks(rows):
        chips = move.ring(rows, "y")
        blocks = list(chips)
        for k in range(1, cs):
            blocks += [move.shift(chip, "c", k) for chip in chips]
        return blocks

    def seq_gather(rows):
        return jnp.concatenate(seq_blocks(rows), axis=0)

    def core_sum(partial):
        blocks = partial.reshape(cs, ys, local, width)
        total = blocks[0].astype(f32)
        for k in range(1, cs):
            total = total + move.shift(blocks[k], "c", -k).astype(f32)
        return [total[0]] + [total[k].astype(bf16) for k in range(1, ys)]

    def chip_sum(rows):
        result = rows[0]
        for k in range(1, ys):
            result = result + move.shift(rows[k], "y", -k).astype(f32)
        return result

    grad_blocks = seq_blocks(
        after(jnp.concatenate(grads_out, axis=0).astype(bf16), w_q_all)
    )
    grads_all = [jnp.concatenate([g[part] for g in grad_blocks], axis=0) for part in parts]

    inputs = after(tokens, *kv_near[1:]).reshape(both_rows, width).astype(f32)
    scale_in = row_scale(inputs)
    normed = (inputs * scale_in).astype(bf16)
    kv_lin = dot(w_kv_all, normed, 0, 1)
    key_lin = kv_lin[:KV_WIDTH].reshape(KV_HEADS, HEAD_DIM, both_rows)
    key_rot, key_scale = head_forward(key_lin, gain_k, cosine, sine)
    kv = jnp.concatenate(
        [
            key_rot.astype(bf16).reshape(KV_WIDTH, both_rows),
            kv_lin[KV_WIDTH:].astype(bf16),
            jnp.broadcast_to(doc_ids.reshape(1, both_rows).astype(bf16), (DOC_ROWS, both_rows)),
        ],
        axis=0,
    )
    hops = [kv]
    for _ in range(back_groups):
        hops.append(move.hop(hops[-1], "z", 1))
    blocks = []
    for group in hops[::-1]:
        blocks += move.direct(group, "x")
    windows = [jnp.stack([block[:, part] for block in blocks]) for part in parts]
    present = at_z + jnp.repeat(jnp.arange(back_groups + 1), xs) >= back_groups
    starts = []
    for b in range(batches):
        docs = jnp.where(present[:, None], windows[b][:, 2 * KV_WIDTH].astype(jnp.int32), -1)
        below = docs.reshape(1, -1) < doc_ids[b][:, None]
        starts.append(jnp.sum(below.astype(jnp.int32), axis=1))

    half = Q_WIDTH // 2
    query_lin = jnp.concatenate(
        [dot(w_q_all[:, :half], normed, 0, 1), dot(w_q_all[:, half:], normed, 0, 1)], axis=0
    ).reshape(HEADS, HEAD_DIM, both_rows)
    query_rot, query_scale = head_forward(query_lin, gain_q, cosine, sine)
    query_t = query_rot.astype(bf16).reshape(Q_WIDTH, both_rows)

    metas, mixed, lses, resids, scale_mids, normed2_all = [], [], [], [], [], []
    for b, part in enumerate(parts):
        meta = jnp.stack([starts[b][0] // local, high, q_start, at_x]).astype(jnp.int32)
        mixed_t, lse = attend_forward(xs, meta, starts[b][:, None], query_t, b, windows[b])
        resid = inputs[part] + dot(mixed_t, w_out_all, 0, 0)
        scale_mid = row_scale(resid)
        normed2_all.append(seq_gather((resid * scale_mid).astype(bf16)))
        metas.append(meta)
        mixed.append(mixed_t)
        lses.append(lse)
        resids.append(resid)
        scale_mids.append(scale_mid)

    hiddens, gate_grads, up_grads, sums = [], [], [], []
    for b in range(batches):
        wide = matmul(normed2_all[b], w_both)
        gate, up = wide[:, :ffn_part], wide[:, ffn_part:]
        sig = jax.nn.sigmoid(gate)
        silu = gate * sig
        hiddens.append((silu * up).astype(bf16))
        grads = after(grads_all[b], *sums[-1][1:]) if sums else grads_all[b]
        grad_hidden = dot(grads, w_down_all, 1, 1)
        grad_gate = (grad_hidden * up * (sig * (1.0 + gate * (1.0 - sig)))).astype(bf16)
        grad_up = (grad_hidden * silu).astype(bf16)
        grad_wide = jnp.concatenate([grad_gate, grad_up], axis=1)
        sums.append(core_sum(dot(grad_wide, w_both, 1, 1).astype(bf16)))
        gate_grads.append(grad_gate)
        up_grads.append(grad_up)

    grad_resids, low_grads = [], []
    for b in range(batches):
        grad_normed2 = chip_sum(sums[b])
        grad_resid = grads_out[b] + norm_backward(grad_normed2, resids[b], scale_mids[b])
        grad_resids.append(grad_resid)
        low_grads.append(grad_resid.astype(bf16))

    def token_sum(lefts, rights):
        total = dot(lefts[0], rights[0], 0, 0)
        for left, right in zip(lefts[1:], rights[1:]):
            total = total + dot(left, right, 0, 0)
        return total.astype(bf16)

    def scatter_columns(lefts, rights):
        value = token_sum(lefts, rights).reshape(ys * cs, zs * xs * d_rows, ffn_part)
        return lax.psum_scatter(value, CTX, scatter_dimension=1, tiled=True)

    gate_sum = scatter_columns(normed2_all, gate_grads)
    up_sum = scatter_columns(normed2_all, [after(g, *sums[-1][1:]) for g in up_grads])
    late = after(hiddens[0], *sums[-1][1:])
    grad_down = lax.psum_scatter(
        token_sum([late] + hiddens[1:], grads_all), CTX, scatter_dimension=0, tiled=True
    ).astype(f32)

    query_grads, groups = [], []
    for b in range(batches):
        grad_mixed_t = dot(w_out_all, low_grads[b], 1, 1).astype(bf16)
        dq_t, dkv = attend_backward(
            xs, metas[b], starts[b][None, :], query_t, b, windows[b], grad_mixed_t, mixed[b],
            lses[b],
        )
        query_grads.append(dq_t)
        groups.append(dkv.reshape(back_groups + 1, xs, 2 * KV_WIDTH, local))

    def split_cores(value, rows):
        value = value.astype(bf16).reshape(ys, cs, zs, xs, rows, -1)
        return move.scatter(value, "c", 1).astype(bf16)

    out_cores = split_cores(
        matmul(jnp.concatenate(mixed, axis=1), jnp.concatenate(low_grads, axis=0)),
        w_out.shape[0],
    )
    query_grad, gq_gain = head_backward(
        jnp.concatenate(query_grads, axis=1).astype(f32).reshape(HEADS, HEAD_DIM, both_rows),
        query_lin, query_scale, gain_q, cosine, sine,
    )
    query_grad = query_grad.astype(bf16).reshape(Q_WIDTH, both_rows)
    q_cores = split_cores(dot(normed, query_grad, 0, 1), d_rows)

    kv_grads = []
    for b in range(batches):
        carried = groups[b][0]
        for k in range(1, back_groups + 1):
            if b == batches - 1 and k == back_groups:
                carried = after(carried, out_cores, q_cores)
            carried = (
                move.hop(carried, "z", -1).astype(f32) + groups[b][k].astype(f32)
            ).astype(bf16)
        total = carried[0].astype(f32)
        for k in range(1, xs):
            total = total + move.shift(carried[k], "x", -k).astype(f32)
        kv_grads.append(total)
    grad_out_w = move.scatter_chips(out_cores, "yxz")
    grad_q_w = move.scatter_chips(q_cores, "xyz")

    kv_sum = jnp.concatenate(kv_grads, axis=1)
    key_grad, gk_gain = head_backward(
        kv_sum[:KV_WIDTH].reshape(KV_HEADS, HEAD_DIM, both_rows), key_lin, key_scale, gain_k,
        cosine, sine,
    )
    kv_grad = jnp.concatenate(
        [key_grad.astype(bf16).reshape(KV_WIDTH, both_rows), kv_sum[KV_WIDTH:].astype(bf16)],
        axis=0,
    )
    grad_kv_w = move.scatter_chips(split_cores(dot(normed, kv_grad, 0, 1), d_rows), "yxz")
    grad_normed = dot(query_grad, w_q_all, 0, 1) + dot(kv_grad, w_kv_all, 0, 1)
    normed_back = norm_backward(grad_normed, inputs, scale_in)
    token_grads = [
        (grad_resids[b] + normed_back[part]).astype(bf16) for b, part in enumerate(parts)
    ]

    outputs = []
    for b in range(batches):
        hidden = after(hiddens[b], low_grads[-1])
        rows = core_sum(matmul(hidden, w_down_all).astype(bf16))
        outputs.append((resids[b] + chip_sum(rows)).astype(bf16))

    both_sum = jnp.concatenate([gate_sum, up_sum], axis=2).reshape(ys, cs, d_rows, -1)
    both_sum = move.exchange(both_sum, "y", 0, 2)
    both_sum = move.exchange(both_sum, "c", 0, 2).astype(f32)
    grad_gate_w = both_sum[..., :ffn_part].reshape(d_rows, -1)
    grad_up_w = both_sum[..., ffn_part:].reshape(d_rows, -1)

    attn_gain_grad = jnp.sum(grad_q_w * w_query.astype(f32), axis=1) + jnp.sum(
        grad_kv_w * w_kv.astype(f32), axis=1
    )
    ffn_gain_grad = jnp.sum(
        grad_gate_w * w_gate.astype(f32) + grad_up_w * w_up.astype(f32), axis=1
    )
    grad_kv_w = grad_kv_w * gain_a
    small = jnp.concatenate([gq_gain, gk_gain])[None, :]
    for axis in LAYOUT:
        small = move.total(small, axis)

    return (
        jnp.stack(outputs),
        jnp.stack(token_grads),
        attn_gain_grad,
        grad_q_w * gain_a,
        grad_kv_w[:, :KV_WIDTH],
        grad_kv_w[:, KV_WIDTH:],
        small[0, :HEAD_DIM],
        small[0, HEAD_DIM:],
        grad_out_w,
        ffn_gain_grad,
        grad_gate_w * gain_f,
        grad_up_w * gain_f,
        grad_down,
    )


def solution(mesh):
    sizes = {"c": 2, "z": Z_CHIPS}
    sizes["y"] = mesh.shape["seq"] // sizes["c"]
    sizes["x"] = mesh.shape["ctx"] // sizes["z"]
    grid = Mesh(mesh.devices.reshape([sizes[a] for a in "yczx"]), ("y", "c", "z", "x"))
    seq, ctx, every = ("y", "c"), ("z", "x"), ("y", "c", "z", "x")
    acts, vector, matrix = P(seq, ctx, None), P(every), P(every, None)
    in_specs = (
        acts, acts, P(seq, ctx), P(seq), P(), vector, matrix, matrix, matrix, P(), P(), matrix,
        vector, matrix, matrix, matrix,
    )
    out_specs = (
        acts, acts, vector, matrix, matrix, matrix, P(), P(), matrix, vector, matrix, matrix,
        matrix,
    )
    return jax.shard_map(
        functools.partial(per_device, sizes), mesh=grid, in_specs=in_specs, out_specs=out_specs,
        check_vma=False,
    )
```

time: 1110 us -> 854 us (0.77)
  waiting for transfers between devices: 476 us -> 357 us
  other arithmetic: 145 us -> 92.2 us
  local copies, waits for them, and re-layouts: 99.9 us -> 58.4 us
  starting transfers between devices: 162 us -> 130 us
  between operations: 8.97 us -> 22 us
  matrix products: 164 us -> 151 us
    ppermute x99 -> x56, waiting for transfers between devices: 476 us -> 244 us  [shift(): lax.ppermute(value, axis, [(i, (i + step) % size) for i in range(size)])]
    ppermute x0 -> x11, waiting for transfers between devices: none -> 112 us  [the longest x6 104 us: hop(): return lax.ppermute(value, axis, pairs)]
    ppermute x99 -> x56, starting transfers between devices: 162 us -> 97.5 us  [shift(): lax.ppermute(value, axis, [(i, (i + step) % size) for i in range(size)])]
    ppermute x0 -> x11, starting transfers between devices: none -> 31.9 us  [the longest x5 16.1 us: total(): lax.ppermute(value, axis, [(i, i ^ step) for i in range(size)])]
    select_n x22 -> x13, other arithmetic: 38.3 us -> 18 us  [place(): whole = jnp.where(back == k, jnp.expand_dims(pieces[k], dim), whole)]
    concatenate x15 -> x6, other arithmetic: 20.3 us -> 3.77 us  [the longest x1 1.57 us: per_device(): jnp.concatenate(grads_out, axis=0).astype(bf16)]
    squeeze x21 -> x13, local copies, waits for them, and re-layouts: 17.5 us -> 3.8 us  [take(): return lax.dynamic_index_in_dim(value, index, dim, keepdims=False)]
    dot_general x32 -> x26, matrix products: 164 us -> 151 us  [dot(): lax.dot_general(left, right, (((left_dim,), (right_dim,)), ((), ())), pre...]
  transfers between devices with their start and end apart: 99 -> 73, of which waited for: 42 -> 32; matrix products, arithmetic and copies ran while one was open for 32% -> 30% of each run, Pallas kernels for 4% -> 4%
where the time goes in v2:
time: 854 us; the launch traced here: 847 us
  waiting for transfers between devices  357 us (42%)
  matrix products  151 us (18%)
  starting transfers between devices  130 us (15%)
  other arithmetic  92.2 us (11%)
  local copies, waits for them, and re-layouts  58.4 us (7%)
  Pallas kernels  35.9 us (4%)
  between operations  22 us (3%)
    ppermute x56, waiting for transfers between devices, shift(): lax.ppermute(value, axis, [(i, (i + step) % size) for i in range(size)])  244 us
    dot_general x26, matrix products, dot(): lax.dot_general(left, right, (((left_dim,), (right_dim,)), ((), ())), pre...  151 us
    ppermute x6, waiting for transfers between devices, hop(): return lax.ppermute(value, axis, pairs)  104 us
    ppermute x56, starting transfers between devices, shift(): lax.ppermute(value, axis, [(i, (i + step) % size) for i in range(size)])  97.5 us
    pallas_call x2, Pallas kernels, attend_backward(): pl.pallas_call(functools.partial(backward_kernel, xs), name='attend_backw...  20.4 us
    unnamed x301, local copies, waits for them, and re-layouts  20.3 us
    select_n x13, other arithmetic, place(): whole = jnp.where(back == k, jnp.expand_dims(pieces[k], dim), whole)  18 us
  transfers between devices with their start and end apart: 73, of which 32 were waited for; matrix products, arithmetic and copies ran while one was open for 30% of the time, Pallas kernels for 4%

profile of v2, /device:TPU:0, one launch (start us, length us, event | category | flops | bytes accessed | tf_op | source)
XLA Modules:
  0.0 846.6 jit_solution(10286437346295100234)
XLA Ops:
  16.6 2.9 collective-permute-start.21
  19.6 12.0 %collective-permute-done.21 = bf16[2,64,1792]{2,1,0:T(8,128)(2,1)S(1)} collective-permute-done((bf16[2,64,1792]{2,1,0:T(8,128)(2,1)S(1)}, bf16[2,64,1792]{2,1,0:T(8,128)(2,1)S(1)}, u32[]{:S(2)}, u32[]{:S(2)}) %collective-permute-start.21) | collective-permute-done | bytes 458784 | tf_op jit(solution)/shard_map/ppermute | solution.py:243
  47.5 6.1 collective-permute-done.3
  55.8 9.2 %collective-permute-done.12 = bf16[64,1280]{1,0:T(8,128)(2,1)S(1)} collective-permute-done((bf16[64,1280]{1,0:T(8,128)(2,1)S(1)}, bf16[64,1280]{1,0:T(8,128)(2,1)S(1)}, u32[]{:S(2)}, u32[]{:S(2)}) %collective-permute-start.12) | collective-permute-done | bytes 163872 | tf_op jit(solution)/shard_map/ppermute | solution.py:243
  66.7 3.6 collective-permute-done.4
  71.8 19.2 %collective-permute-done.14 = bf16[4,64,1280]{2,1,0:T(8,128)(2,1)S(1)} collective-permute-done((bf16[4,64,1280]{2,1,0:T(8,128)(2,1)S(1)}, bf16[4,64,1280]{2,1,0:T(8,128)(2,1)S(1)}, u32[]{:S(2)}, u32[]{:S(2)}) %collective-permute-start.14) | collective-permute-done | bytes 655392 | tf_op jit(solution)/shard_map/ppermute | solution.py:243
  103.2 17.8 %collective-permute-done.6 = bf16[656,512]{1,0:T(8,128)(2,1)} collective-permute-done((bf16[656,512]{1,0:T(8,128)(2,1)S(1)}, bf16[656,512]{1,0:T(8,128)(2,1)}, u32[]{:S(2)}, u32[]{:S(2)}) %collective-permute-start.6) | collective-permute-done | bytes 671776 | tf_op jit(solution)/shard_map/ppermute | solution.py:248
  121.0 7.5 collective-permute-start.7
  130.2 3.2 broadcast_select_fusion.1
  133.4 22.1 %collective-permute-done.7 = bf16[656,512]{1,0:T(8,128)(2,1)} collective-permute-done((bf16[656,512]{1,0:T(8,128)(2,1)}, bf16[656,512]{1,0:T(8,128)(2,1)}, u32[]{:S(2)}, u32[]{:S(2)}) %collective-permute-start.7) | collective-permute-done | bytes 671776 | tf_op jit(solution)/shard_map/ppermute | solution.py:248
  165.6 20.7 %collective-permute-done.8 = bf16[656,512]{1,0:T(8,128)(2,1)S(1)} collective-permute-done((bf16[656,512]{1,0:T(8,128)(2,1)}, bf16[656,512]{1,0:T(8,128)(2,1)S(1)}, u32[]{:S(2)}, u32[]{:S(2)}) %collective-permute-start.8) | collective-permute-done | bytes 671776 | tf_op jit(solution)/shard_map/ppermute | solution.py:243
  187.5 46.9 %collective-permute-done.9 = bf16[656,512]{1,0:T(8,128)(2,1)S(1)} collective-permute-done((bf16[656,512]{1,0:T(8,128)(2,1)}, bf16[656,512]{1,0:T(8,128)(2,1)S(1)}, u32[]{:S(2)}, u32[]{:S(2)}) %collective-permute-start.9) | collective-permute-done | bytes 671776 | tf_op jit(solution)/shard_map/ppermute | solution.py:243
  245.6 3.0 bitcast_select_fusion
  256.0 7.7 attend_forward.2
  264.9 7.8 attend_forward.3
  272.7 7.0 collective-permute-done.22
  279.7 3.2 fusion.122
  282.9 5.2 multiply_reduce_fusion.6
  295.0 19.9 %collective-permute-done.17 = bf16[256,2048]{1,0:T(8,128)(2,1)S(1)} collective-permute-done((bf16[256,2048]{1,0:T(8,128)(2,1)S(1)}, bf16[256,2048]{1,0:T(8,128)(2,1)S(1)}, u32[]{:S(2)}, u32[]{:S(2)}) %collective-permute-start.17) | collective-permute-done | bytes 1048608 | tf_op jit(solution)/shard_map/ppermute | solution.py:243
  314.9 3.1 fusion.123
  318.0 3.1 fusion.124
  321.2 15.8 %collective-permute-done.26 = bf16[256,2048]{1,0:T(8,128)(2,1)} collective-permute-done((bf16[256,2048]{1,0:T(8,128)(2,1)}, bf16[256,2048]{1,0:T(8,128)(2,1)}, u32[]{:S(2)}, u32[]{:S(2)}) %collective-permute-start.26) | collective-permute-done | bytes 1048608 | tf_op jit(solution)/shard_map/ppermute | solution.py:243
  338.0 15.5 %fusion.113 = f32[1024,1792]{1,0:T(8,128)} fusion(bf16[2048,1792]{1,0:T(8,128)(2,1)} %bitcast.450, bf16[256,2048]{1,0:T(8,128)(2,1)} %collective-permute-done.19, bf16[256,2048]{1,0:T(8,128)(2,1)} %copy-done.127, bf16[256,2048]{1,0:T(8,128)(2,1)} %copy-done.125, bf16[256,2048]{1,0:T(8,128)(2,1)} %copy-done.61), kind=kOutput, calls=%fused_computation.357 | convolution fusion | flops 7532969984 | bytes 18874368 | tf_op jit(solution)/shard_map/dot_general | solution.py:32
  353.5 11.8 %multiply_convert_fusion.4 = (bf16[1024,896]{1,0:T(8,128)(2,1)S(1)}, bf16[1024,896]{1,0:T(8,128)(2,1)S(1)}, bf16[1024,896]{1,0:T(8,128)(2,1)}) fusion(f32[1024,1792]{1,0:T(8,128)} %fusion.113, bf16[896,2048]{1,0:T(8,128)(2,1)} %all-gather.8.cloned.1.call-done, bf16[256,2048]{1,0:T(8,128)(2,1)} %get-tuple-element.89, ...), kind=kOutput, calls=%fused_computation.46 | convolution fusion | flops 3788636160 | bytes 20709376 | tf_op jit(solution)/shard_map/dot_general | solution.py:32
  365.4 8.0 convolution_convert_fusion.3
  375.3 11.3 %fusion.112 = f32[1024,1792]{1,0:T(8,128)S(1)} fusion(bf16[2048,1792]{1,0:T(8,128)(2,1)S(1)} %bitcast.453, bf16[256,2048]{1,0:T(8,128)(2,1)} %collective-permute-done.28, bf16[256,2048]{1,0:T(8,128)(2,1)} %collective-permute-done.27, bf16[256,2048]{1,0:T(8,128)(2,1)} %collective-permute-done.26, bf16[256,2048]{1,0:T(8,128)(2,1)} %multiply_convert_fusion.6), kind=kOutput, calls=%fused_computation.356 | convolution fusion | flops 7532969984 | bytes 18874368 | tf_op jit(solution)/shard_map/dot_general | solution.py:32
  390.6 7.2 multiply_convert_fusion.2
  397.8 7.1 fusion.111
  405.0 8.0 add_convert_fusion.2
  413.0 11.4 %convolution_convert_fusion.2 = bf16[1024,2048]{1,0:T(8,128)(2,1)S(1)} fusion(bf16[2048,1792]{1,0:T(8,128)(2,1)} %bitcast.451, bf16[1024,896]{1,0:T(8,128)(2,1)} %get-tuple-element.45, bf16[1024,896]{1,0:T(8,128)(2,1)} %copy-done.135), kind=kOutput, calls=%fused_computation.30 | convolution fusion | flops 7525629952 | bytes 15204352 | tf_op jit(solution)/shard_map/dot_general | solution.py:32
  425.6 3.8 collective-permute-done.29
  433.4 6.5 fusion.110
  439.9 7.9 add_convert_fusion.1
  451.8 5.8 broadcast_select_fusion
  459.4 6.2 fusion.114
  465.5 17.5 %collective-permute-done.35 = bf16[256,2048]{1,0:T(8,128)(2,1)S(1)} collective-permute-done((bf16[256,2048]{1,0:T(8,128)(2,1)S(1)}, bf16[256,2048]{1,0:T(8,128)(2,1)S(1)}, u32[]{:S(2)}, u32[]{:S(2)}) %collective-permute-start.35) | collective-permute-done | bytes 1048608 | tf_op jit(solution)/shard_map/ppermute | solution.py:243
  485.2 7.6 add_convert_fusion
  492.9 15.6 %collective-permute-done.30 = bf16[256,2048]{1,0:T(8,128)(2,1)} collective-permute-done((bf16[256,2048]{1,0:T(8,128)(2,1)}, bf16[256,2048]{1,0:T(8,128)(2,1)}, u32[]{:S(2)}, u32[]{:S(2)}) %collective-permute-start.30) | collective-permute-done | bytes 1048608 | tf_op jit(solution)/shard_map/ppermute | solution.py:243
  510.9 6.3 fusion.115
  517.2 3.1 convolution_convert_fusion.1
  526.9 10.2 %attend_backward.2 = (bf16[1280,256]{1,0:T(8,128)(2,1)}, bf16[6,2,320,256]{3,2,1,0:T(8,128)(2,1)}) custom-call(s32[4]{0:T(128)} %add_add_fusion.meta, s32[1,256]{1,0:T(1,128)} %bitcast.446, bf16[1280,512]{1,0:T(8,128)(2,1)} %bitcast.431, bf16[6,656,256]{2,1,0:T(8,128)(2,1)} %copy-done.82, bf16[6,656,256]{2,1,0:T(8,128)(2,1)} %copy-done.82, ...), custom_call_target="tpu_custom_call" | custom-call | flops 10066329600 | bytes 8388608 | tf_op jit(solution)/shard_map/attend_backward/pallas_call | solution.py:190
  541.2 5.0 fusion.24.go_ref
  546.2 10.2 %attend_backward.3 = (bf16[1280,256]{1,0:T(8,128)(2,1)}, bf16[6,2,320,256]{3,2,1,0:T(8,128)(2,1)}) custom-call(s32[4]{0:T(128)} %add_add_fusion.1.meta, s32[1,256]{1,0:T(1,128)} %bitcast.444, bf16[1280,512]{1,0:T(8,128)(2,1)} %bitcast.432, bf16[6,656,256]{2,1,0:T(8,128)(2,1)} %copy-done.83, bf16[6,656,256]{2,1,0:T(8,128)(2,1)} %copy-done.83, ...), custom_call_target="tpu_custom_call" | custom-call | flops 10066329600 | bytes 8388608 | tf_op jit(solution)/shard_map/attend_backward/pallas_call | solution.py:190
  562.0 4.7 convolution_convert_fusion.5
  568.2 4.7 convolution_convert_fusion.4
  580.1 3.2 convolution_convert_fusion
  583.4 49.5 %collective-permute-done.37 = bf16[2,640,256]{2,1,0:T(8,128)(2,1)S(1)} collective-permute-done((bf16[2,640,256]{2,1,0:T(8,128)(2,1)S(1)}, bf16[2,640,256]{2,1,0:T(8,128)(2,1)S(1)}, u32[]{:S(2)}, u32[]{:S(2)}) %collective-permute-start.37) | collective-permute-done | bytes 655392 | tf_op jit(solution)/shard_map/ppermute | solution.py:248
  633.2 29.9 %collective-permute-start.38 = (bf16[640,256]{1,0:T(8,128)(2,1)S(1)}, bf16[640,256]{1,0:T(8,128)(2,1)S(1)}, u32[]{:S(2)}, u32[]{:S(2)}) collective-permute-start(bf16[640,256]{1,0:T(8,128)(2,1)S(1)} %slice_bitcast_fusion.20), channel_id=1, source_target_pairs={{0,1},{1,0},{2,3},{3,2},{4,5},{5,4},{6,7},{7,6},{8,9},{9,8},{10,11... | collective-permute-start | bytes 983048 | tf_op jit(solution)/shard_map/ppermute | solution.py:243
  665.9 9.9 %collective-permute-done.38 = bf16[640,256]{1,0:T(8,128)(2,1)S(1)} collective-permute-done((bf16[640,256]{1,0:T(8,128)(2,1)S(1)}, bf16[640,256]{1,0:T(8,128)(2,1)S(1)}, u32[]{:S(2)}, u32[]{:S(2)}) %collective-permute-start.38) | collective-permute-done | bytes 327712 | tf_op jit(solution)/shard_map/ppermute | solution.py:243
  678.3 4.2 collective-permute-start.32
  695.6 11.0 %collective-permute-done.32 = bf16[256,2048]{1,0:T(8,128)(2,1)} collective-permute-done((bf16[256,2048]{1,0:T(8,128)(2,1)S(1)}, bf16[256,2048]{1,0:T(8,128)(2,1)}, u32[]{:S(2)}, u32[]{:S(2)}) %collective-permute-start.32) | collective-permute-done | bytes 1048608 | tf_op jit(solution)/shard_map/ppermute | solution.py:243
  708.4 14.7 %collective-permute-done.42 = bf16[2,640,256]{2,1,0:T(8,128)(2,1)S(1)} collective-permute-done((bf16[2,640,256]{2,1,0:T(8,128)(2,1)S(1)}, bf16[2,640,256]{2,1,0:T(8,128)(2,1)S(1)}, u32[]{:S(2)}, u32[]{:S(2)}) %collective-permute-start.42) | collective-permute-done | bytes 655392 | tf_op jit(solution)/shard_map/ppermute | solution.py:248
  724.8 4.1 collective-permute-done.34
  737.2 3.1 convolution_convert_fusion.6
  744.4 3.2 fusion.7
  747.7 5.7 collective-permute-done.55
  754.6 8.2 collective-permute-start.57
  764.3 4.0 collective-permute-start.58
  779.4 10.5 %collective-permute-done.61 = bf16[4,40,2048]{2,1,0:T(8,128)(2,1)S(1)} collective-permute-done((bf16[4,40,2048]{2,1,0:T(8,128)(2,1)S(1)}, bf16[4,40,2048]{2,1,0:T(8,128)(2,1)S(1)}, u32[]{:S(2)}, u32[]{:S(2)}) %collective-permute-start.61) | collective-permute-done | bytes 655392 | tf_op jit(solution)/shard_map/ppermute | solution.py:243
  799.1 7.1 collective-permute-start.47
  806.2 7.9 collective-permute-start.48
  818.2 4.1 collective-permute-done.51
  823.1 3.3 collective-permute-start.54
  836.4 3.1 broadcast_multiply_fusion
  (610 shorter events, 195.9 us)
Async XLA Ops:
  7.2 275.7 %all-gather.4.cloned.1.call-start = ((), (), s32[]{:S(2)}) async-start(), calls=%async_computation.3 | async-start | bytes 5406720 | tf_op jit(solution)/shard_map/all_gather | solution.py:377
  7.9 330.1 %all-gather.6.cloned.1.call-start = ((), (), s32[]{:S(2)}) async-start(), calls=%async_computation.4 | async-start | bytes 8257536 | tf_op jit(solution)/shard_map/all_gather | solution.py:384
  16.6 14.9 %collective-permute-start.21 = (bf16[2,64,1792]{2,1,0:T(8,128)(2,1)S(1)}, bf16[2,64,1792]{2,1,0:T(8,128)(2,1)S(1)}, u32[]{:S(2)}, u32[]{:S(2)}) collective-permute-start(bf16[2,64,1792]{2,1,0:T(8,128)(2,1)S(1)} %get-tuple-element.112), channel_id=1, source_target_pairs={{0,16},{16,0},{1,17},{17,1},{2,18},{18,2},{3,19},{19,3},{4,20},{20... | collective-permute-start | bytes 1376264 | tf_op jit(solution)/shard_map/ppermute | solution.py:243
  32.6 320.9 %all-gather.8.cloned.1.call-start = ((), (), s32[]{:S(2)}) async-start(), calls=%async_computation.5 | async-start | bytes 4128768 | tf_op jit(solution)/shard_map/all_gather | solution.py:385
  32.8 11.9 %collective-permute-start = (bf16[64,640]{1,0:T(8,128)(2,1)S(1)}, bf16[64,640]{1,0:T(8,128)(2,1)S(1)}, u32[]{:S(2)}, u32[]{:S(2)}) collective-permute-start(bf16[64,640]{1,0:T(8,128)(2,1)S(1)} %fusion.87), channel_id=1, source_target_pairs={{0,2},{2,4},{4,6},{6,0},{1,3},{3,5},{5,7},{7,1},{8,10},{10,12},{12... | collective-permute-start | bytes 245768 | tf_op jit(solution)/shard_map/ppermute | solution.py:243
  34.7 10.2 %collective-permute-start.1 = (bf16[64,640]{1,0:T(8,128)(2,1)S(1)}, bf16[64,640]{1,0:T(8,128)(2,1)S(1)}, u32[]{:S(2)}, u32[]{:S(2)}) collective-permute-start(bf16[64,640]{1,0:T(8,128)(2,1)S(1)} %fusion.87), channel_id=1, source_target_pairs={{0,4},{2,6},{4,0},{6,2},{1,5},{3,7},{5,1},{7,3},{8,12},{10,14},{12... | collective-permute-start | bytes 245768 | tf_op jit(solution)/shard_map/ppermute | solution.py:243
  37.3 8.3 collective-permute-start.2
  38.7 17.1 %collective-permute-start.11 = (bf16[64,1280]{1,0:T(8,128)(2,1)S(1)}, bf16[64,1280]{1,0:T(8,128)(2,1)S(1)}, u32[]{:S(2)}, u32[]{:S(2)}) collective-permute-start(bf16[64,1280]{1,0:T(8,128)(2,1)S(1)} %fusion.81), channel_id=1, source_target_pairs={{0,6},{2,0},{4,2},{6,4},{1,7},{3,1},{5,3},{7,5},{8,14},{10,8},{12,... | collective-permute-start | bytes 491528 | tf_op jit(solution)/shard_map/ppermute | solution.py:243
  39.2 25.8 %collective-permute-start.12 = (bf16[64,1280]{1,0:T(8,128)(2,1)S(1)}, bf16[64,1280]{1,0:T(8,128)(2,1)S(1)}, u32[]{:S(2)}, u32[]{:S(2)}) collective-permute-start(bf16[64,1280]{1,0:T(8,128)(2,1)S(1)} %fusion.81), channel_id=1, source_target_pairs={{0,4},{2,6},{4,0},{6,2},{1,5},{3,7},{5,1},{7,3},{8,12},{10,14},{12... | collective-permute-start | bytes 491528 | tf_op jit(solution)/shard_map/ppermute | solution.py:243
  40.9 774.7 %reduce-scatter.4.cloned.1.call-start = ((), (), s32[]{:S(2)}) async-start(), calls=%async_computation.6 | async-start | bytes 4128768 | tf_op jit(solution)/shard_map/reduce_scatter | solution.py:513
  44.7 20.3 %collective-permute-start.13 = (bf16[64,1280]{1,0:T(8,128)(2,1)S(1)}, bf16[64,1280]{1,0:T(8,128)(2,1)S(1)}, u32[]{:S(2)}, u32[]{:S(2)}) collective-permute-start(bf16[64,1280]{1,0:T(8,128)(2,1)S(1)} %fusion.81), channel_id=1, source_target_pairs={{0,2},{2,4},{4,6},{6,0},{1,3},{3,5},{5,7},{7,1},{8,10},{10,12},{12... | collective-permute-start | bytes 491528 | tf_op jit(solution)/shard_map/ppermute | solution.py:243
  45.8 7.9 collective-permute-start.3
  53.8 16.5 %collective-permute-start.4 = (bf16[4,2,64,640]{3,2,1,0:T(8,128)(2,1)S(1)}, bf16[4,2,64,640]{3,2,1,0:T(8,128)(2,1)S(1)}, u32[]{:S(2)}, u32[]{:S(2)}) collective-permute-start(bf16[4,2,64,640]{3,2,1,0:T(8,128)(2,1)S(1)} %broadcast_select_fusion.9), channel_id=1, source_target_pairs={{0,16},{16,0},{1,17},{17,1},{2,18},{18,2},{3,19},{19,3},{4,20},{20... | collective-permute-start | bytes 1966088 | tf_op jit(solution)/shard_map/ppermute | solution.py:243
  65.2 25.7 %collective-permute-start.14 = (bf16[4,64,1280]{2,1,0:T(8,128)(2,1)S(1)}, bf16[4,64,1280]{2,1,0:T(8,128)(2,1)S(1)}, u32[]{:S(2)}, u32[]{:S(2)}) collective-permute-start(bf16[4,64,1280]{2,1,0:T(8,128)(2,1)S(1)} %select_select_fusion), channel_id=1, source_target_pairs={{0,1},{1,0},{2,3},{3,2},{4,5},{5,4},{6,7},{7,6},{8,9},{9,8},{10,11... | collective-permute-start | bytes 1966088 | tf_op jit(solution)/shard_map/ppermute | solution.py:243
  70.6 22.0 %collective-permute-start.5 = (bf16[2,4,2,64,640]{4,3,2,1,0:T(8,128)(2,1)S(1)}, bf16[2,4,2,64,640]{4,3,2,1,0:T(8,128)(2,1)S(1)}, u32[]{:S(2)}, u32[]{:S(2)}) collective-permute-start(bf16[2,4,2,64,640]{4,3,2,1,0:T(8,128)(2,1)S(1)} %broadcast_select_fusion.6), channel_id=1, source_target_pairs={{0,8},{8,0},{1,9},{9,1},{2,10},{10,2},{3,11},{11,3},{4,12},{12,4},... | collective-permute-start | bytes 3932168 | tf_op jit(solution)/shard_map/ppermute | solution.py:243
  91.1 39.1 %collective-permute-start.15 = (bf16[4,2,64,1280]{3,2,1,0:T(8,128)(2,1)S(1)}, bf16[4,2,64,1280]{3,2,1,0:T(8,128)(2,1)}, u32[]{:S(2)}, u32[]{:S(2)}) collective-permute-start(bf16[4,2,64,1280]{3,2,1,0:T(8,128)(2,1)S(1)} %broadcast_select_fusion.5), channel_id=1, source_target_pairs={{0,16},{16,0},{1,17},{17,1},{2,18},{18,2},{3,19},{19,3},{4,20},{20... | collective-permute-start | bytes 3932168 | tf_op jit(solution)/shard_map/ppermute | solution.py:243
  97.7 23.3 %collective-permute-start.6 = (bf16[656,512]{1,0:T(8,128)(2,1)S(1)}, bf16[656,512]{1,0:T(8,128)(2,1)}, u32[]{:S(2)}, u32[]{:S(2)}) collective-permute-start(bf16[656,512]{1,0:T(8,128)(2,1)S(1)} %pad_maximum_fusion.14), channel_id=1, source_target_pairs={{0,2},{2,4},{4,6},{1,3},{3,5},{5,7},{8,10},{10,12},{12,14},{9,11},... | collective-permute-start | bytes 2015240 | tf_op jit(solution)/shard_map/ppermute | solution.py:248
  121.0 34.4 %collective-permute-start.7 = (bf16[656,512]{1,0:T(8,128)(2,1)}, bf16[656,512]{1,0:T(8,128)(2,1)}, u32[]{:S(2)}, u32[]{:S(2)}) collective-permute-start(bf16[656,512]{1,0:T(8,128)(2,1)} %collective-permute-done.6), channel_id=1, source_target_pairs={{0,2},{2,4},{4,6},{1,3},{3,5},{5,7},{8,10},{10,12},{12,14},{9,11},... | collective-permute-start | bytes 2015240 | tf_op jit(solution)/shard_map/ppermute | solution.py:248
  133.4 112.2 %collective-permute-start.16 = (bf16[2,4,2,64,1280]{4,3,2,1,0:T(8,128)(2,1)}, bf16[2,4,2,64,1280]{4,3,2,1,0:T(8,128)(2,1)}, u32[]{:S(2)}, u32[]{:S(2)}) collective-permute-start(bf16[2,4,2,64,1280]{4,3,2,1,0:T(8,128)(2,1)} %broadcast_select_fusion.1), channel_id=1, source_target_pairs={{0,8},{8,0},{1,9},{9,1},{2,10},{10,2},{3,11},{11,3},{4,12},{12,4},... | collective-permute-start | bytes 7864328 | tf_op jit(solution)/shard_map/ppermute | solution.py:243
  155.5 30.8 %collective-permute-start.8 = (bf16[656,512]{1,0:T(8,128)(2,1)}, bf16[656,512]{1,0:T(8,128)(2,1)S(1)}, u32[]{:S(2)}, u32[]{:S(2)}) collective-permute-start(bf16[656,512]{1,0:T(8,128)(2,1)} %collective-permute-done.7), channel_id=1, source_target_pairs={{0,1},{1,0},{2,3},{3,2},{4,5},{5,4},{6,7},{7,6},{8,9},{9,8},{10,11... | collective-permute-start | bytes 2015240 | tf_op jit(solution)/shard_map/ppermute | solution.py:243
  162.4 72.0 %collective-permute-start.10 = (bf16[656,512]{1,0:T(8,128)(2,1)S(1)}, bf16[656,512]{1,0:T(8,128)(2,1)S(1)}, u32[]{:S(2)}, u32[]{:S(2)}) collective-permute-start(bf16[656,512]{1,0:T(8,128)(2,1)S(1)} %copy-done.39), channel_id=1, source_target_pairs={{0,1},{1,0},{2,3},{3,2},{4,5},{5,4},{6,7},{7,6},{8,9},{9,8},{10,11... | collective-permute-start | bytes 2015240 | tf_op jit(solution)/shard_map/ppermute | solution.py:243
  162.4 71.9 %collective-permute-start.9 = (bf16[656,512]{1,0:T(8,128)(2,1)}, bf16[656,512]{1,0:T(8,128)(2,1)S(1)}, u32[]{:S(2)}, u32[]{:S(2)}) collective-permute-start(bf16[656,512]{1,0:T(8,128)(2,1)} %collective-permute-done.6), channel_id=1, source_target_pairs={{0,1},{1,0},{2,3},{3,2},{4,5},{5,4},{6,7},{7,6},{8,9},{9,8},{10,11... | collective-permute-start | bytes 2015240 | tf_op jit(solution)/shard_map/ppermute | solution.py:243
  251.9 27.8 %collective-permute-start.22 = (bf16[512,2048]{1,0:T(8,128)(2,1)S(1)}, bf16[512,2048]{1,0:T(8,128)(2,1)}, u32[]{:S(2)}, u32[]{:S(2)}) collective-permute-start(bf16[512,2048]{1,0:T(8,128)(2,1)S(1)} %copy-done.23), channel_id=1, source_target_pairs={{0,16},{16,0},{1,17},{17,1},{2,18},{18,2},{3,19},{19,3},{4,20},{20... | collective-permute-start | bytes 6291464 | tf_op jit(solution)/shard_map/ppermute | solution.py:243
  252.0 62.9 %collective-permute-start.23 = (bf16[512,2048]{1,0:T(8,128)(2,1)S(1)}, bf16[512,2048]{1,0:T(8,128)(2,1)}, u32[]{:S(2)}, u32[]{:S(2)}) collective-permute-start(bf16[512,2048]{1,0:T(8,128)(2,1)S(1)} %copy-done.23), channel_id=1, source_target_pairs={{0,8},{8,0},{1,9},{9,1},{2,10},{10,2},{3,11},{11,3},{4,12},{12,4},... | collective-permute-start | bytes 6291464 | tf_op jit(solution)/shard_map/ppermute | solution.py:243
  279.7 38.3 %collective-permute-start.24 = (bf16[512,2048]{1,0:T(8,128)(2,1)}, bf16[512,2048]{1,0:T(8,128)(2,1)}, u32[]{:S(2)}, u32[]{:S(2)}) collective-permute-start(bf16[512,2048]{1,0:T(8,128)(2,1)} %collective-permute-done.22), channel_id=1, source_target_pairs={{0,8},{8,0},{1,9},{9,1},{2,10},{10,2},{3,11},{11,3},{4,12},{12,4},... | collective-permute-start | bytes 6291464 | tf_op jit(solution)/shard_map/ppermute | solution.py:243
  288.8 26.1 %collective-permute-start.17 = (bf16[256,2048]{1,0:T(8,128)(2,1)S(1)}, bf16[256,2048]{1,0:T(8,128)(2,1)S(1)}, u32[]{:S(2)}, u32[]{:S(2)}) collective-permute-start(bf16[256,2048]{1,0:T(8,128)(2,1)S(1)} %multiply_convert_fusion.7), channel_id=1, source_target_pairs={{0,16},{16,0},{1,17},{17,1},{2,18},{18,2},{3,19},{19,3},{4,20},{20... | collective-permute-start | bytes 3145736 | tf_op jit(solution)/shard_map/ppermute | solution.py:243
  290.6 46.4 %collective-permute-start.18 = (bf16[256,2048]{1,0:T(8,128)(2,1)S(1)}, bf16[256,2048]{1,0:T(8,128)(2,1)S(1)}, u32[]{:S(2)}, u32[]{:S(2)}) collective-permute-start(bf16[256,2048]{1,0:T(8,128)(2,1)S(1)} %multiply_convert_fusion.7), channel_id=1, source_target_pairs={{0,8},{8,0},{1,9},{9,1},{2,10},{10,2},{3,11},{11,3},{4,12},{12,4},... | collective-permute-start | bytes 3145736 | tf_op jit(solution)/shard_map/ppermute | solution.py:243
  294.3 42.7 %collective-permute-start.26 = (bf16[256,2048]{1,0:T(8,128)(2,1)}, bf16[256,2048]{1,0:T(8,128)(2,1)}, u32[]{:S(2)}, u32[]{:S(2)}) collective-permute-start(bf16[256,2048]{1,0:T(8,128)(2,1)} %multiply_convert_fusion.6), channel_id=1, source_target_pairs={{0,16},{16,0},{1,17},{17,1},{2,18},{18,2},{3,19},{19,3},{4,20},{20... | collective-permute-start | bytes 3145736 | tf_op jit(solution)/shard_map/ppermute | solution.py:243
  314.9 23.1 %collective-permute-start.19 = (bf16[256,2048]{1,0:T(8,128)(2,1)S(1)}, bf16[256,2048]{1,0:T(8,128)(2,1)}, u32[]{:S(2)}, u32[]{:S(2)}) collective-permute-start(bf16[256,2048]{1,0:T(8,128)(2,1)S(1)} %collective-permute-done.17), channel_id=1, source_target_pairs={{0,8},{8,0},{1,9},{9,1},{2,10},{10,2},{3,11},{11,3},{4,12},{12,4},... | collective-permute-start | bytes 3145736 | tf_op jit(solution)/shard_map/ppermute | solution.py:243
  321.1 54.2 %collective-permute-start.27 = (bf16[256,2048]{1,0:T(8,128)(2,1)}, bf16[256,2048]{1,0:T(8,128)(2,1)}, u32[]{:S(2)}, u32[]{:S(2)}) collective-permute-start(bf16[256,2048]{1,0:T(8,128)(2,1)} %multiply_convert_fusion.6), channel_id=1, source_target_pairs={{0,8},{8,0},{1,9},{9,1},{2,10},{10,2},{3,11},{11,3},{4,12},{12,4},... | collective-permute-start | bytes 3145736 | tf_op jit(solution)/shard_map/ppermute | solution.py:243
  337.0 38.3 %collective-permute-start.28 = (bf16[256,2048]{1,0:T(8,128)(2,1)}, bf16[256,2048]{1,0:T(8,128)(2,1)}, u32[]{:S(2)}, u32[]{:S(2)}) collective-permute-start(bf16[256,2048]{1,0:T(8,128)(2,1)} %collective-permute-done.26), channel_id=1, source_target_pairs={{0,8},{8,0},{1,9},{9,1},{2,10},{10,2},{3,11},{11,3},{4,12},{12,4},... | collective-permute-start | bytes 3145736 | tf_op jit(solution)/shard_map/ppermute | solution.py:243
  374.0 12.6 %collective-permute-start.25 = (bf16[2,256,2048]{2,1,0:T(8,128)(2,1)S(1)}, bf16[2,256,2048]{2,1,0:T(8,128)(2,1)S(1)}, u32[]{:S(2)}, u32[]{:S(2)}) collective-permute-start(bf16[2,256,2048]{2,1,0:T(8,128)(2,1)S(1)} %bitcast.427), channel_id=1, source_target_pairs={{0,8},{8,0},{1,9},{9,1},{2,10},{10,2},{3,11},{11,3},{4,12},{12,4},... | collective-permute-start | bytes 6291464 | tf_op jit(solution)/shard_map/ppermute | solution.py:243
  413.0 402.7 %reduce-scatter.6.cloned.1.call-start = ((), (), s32[]{:S(2)}) async-start(), calls=%async_computation.7 | async-start | bytes 4128768 | tf_op jit(solution)/shard_map/reduce_scatter | solution.py:513
  447.8 383.3 %reduce-scatter.8.cloned.1.call-start = ((), (), s32[]{:S(2)}) async-start(), calls=%async_computation.8 | async-start | bytes 4128768 | tf_op jit(solution)/shard_map/reduce_scatter | solution.py:518
  457.6 25.4 %collective-permute-start.35 = (bf16[256,2048]{1,0:T(8,128)(2,1)S(1)}, bf16[256,2048]{1,0:T(8,128)(2,1)S(1)}, u32[]{:S(2)}, u32[]{:S(2)}) collective-permute-start(bf16[256,2048]{1,0:T(8,128)(2,1)S(1)} %copy-done.60), channel_id=1, source_target_pairs={{0,16},{16,0},{1,17},{17,1},{2,18},{18,2},{3,19},{19,3},{4,20},{20... | collective-permute-start | bytes 3145736 | tf_op jit(solution)/shard_map/ppermute | solution.py:243
  483.4 25.0 %collective-permute-start.30 = (bf16[256,2048]{1,0:T(8,128)(2,1)}, bf16[256,2048]{1,0:T(8,128)(2,1)}, u32[]{:S(2)}, u32[]{:S(2)}) collective-permute-start(bf16[256,2048]{1,0:T(8,128)(2,1)} %fusion.49), channel_id=1, source_target_pairs={{0,16},{16,0},{1,17},{17,1},{2,18},{18,2},{3,19},{19,3},{4,20},{20... | collective-permute-start | bytes 3145736 | tf_op jit(solution)/shard_map/ppermute | solution.py:243
  524.4 159.1 %collective-permute-start.40 = (bf16[2,4,2,40,2048]{4,3,1,2,0:T(8,128)(2,1)}, bf16[2,4,2,40,2048]{4,3,1,2,0:T(8,128)(2,1)}, u32[]{:S(2)}, u32[]{:S(2)}) collective-permute-start(bf16[2,4,2,40,2048]{4,3,1,2,0:T(8,128)(2,1)} %bitcast.393), channel_id=1, source_target_pairs={{0,8},{8,0},{1,9},{9,1},{2,10},{10,2},{3,11},{11,3},{4,12},{12,4},... | collective-permute-start | bytes 7864328 | tf_op jit(solution)/shard_map/ppermute | solution.py:243
  539.7 36.0 %collective-permute-start.36 = (bf16[2,640,256]{2,1,0:T(8,128)(2,1)}, bf16[2,640,256]{2,1,0:T(8,128)(2,1)}, u32[]{:S(2)}, u32[]{:S(2)}) collective-permute-start(bf16[2,640,256]{2,1,0:T(8,128)(2,1)} %bitcast.72), channel_id=1, source_target_pairs={{2,0},{4,2},{6,4},{3,1},{5,3},{7,5},{10,8},{12,10},{14,12},{11,9},... | collective-permute-start | bytes 1966088 | tf_op jit(solution)/shard_map/ppermute | solution.py:248
  560.6 103.1 %collective-permute-start.39 = (bf16[2,640,256]{2,1,0:T(8,128)(2,1)}, bf16[2,640,256]{2,1,0:T(8,128)(2,1)S(1)}, u32[]{:S(2)}, u32[]{:S(2)}) collective-permute-start(bf16[2,640,256]{2,1,0:T(8,128)(2,1)} %bitcast.77), channel_id=1, source_target_pairs={{2,0},{4,2},{6,4},{3,1},{5,3},{7,5},{10,8},{12,10},{14,12},{11,9},... | collective-permute-start | bytes 1966088 | tf_op jit(solution)/shard_map/ppermute | solution.py:248
  567.3 108.5 %collective-permute-start.31 = (bf16[2,256,2048]{2,1,0:T(8,128)(2,1)S(1)}, bf16[2,256,2048]{2,1,0:T(8,128)(2,1)}, u32[]{:S(2)}, u32[]{:S(2)}) collective-permute-start(bf16[2,256,2048]{2,1,0:T(8,128)(2,1)S(1)} %bitcast.426), channel_id=1, source_target_pairs={{0,8},{8,0},{1,9},{9,1},{2,10},{10,2},{3,11},{11,3},{4,12},{12,4},... | collective-permute-start | bytes 6291464 | tf_op jit(solution)/shard_map/ppermute | solution.py:243
  573.5 109.0 %collective-permute-start.33 = (bf16[2,256,2048]{2,1,0:T(8,128)(2,1)S(1)}, bf16[2,256,2048]{2,1,0:T(8,128)(2,1)S(1)}, u32[]{:S(2)}, u32[]{:S(2)}) collective-permute-start(bf16[2,256,2048]{2,1,0:T(8,128)(2,1)S(1)} %bitcast.425), channel_id=1, source_target_pairs={{0,8},{8,0},{1,9},{9,1},{2,10},{10,2},{3,11},{11,3},{4,12},{12,4},... | collective-permute-start | bytes 6291464 | tf_op jit(solution)/shard_map/ppermute | solution.py:243
  577.0 55.9 %collective-permute-start.37 = (bf16[2,640,256]{2,1,0:T(8,128)(2,1)S(1)}, bf16[2,640,256]{2,1,0:T(8,128)(2,1)S(1)}, u32[]{:S(2)}, u32[]{:S(2)}) collective-permute-start(bf16[2,640,256]{2,1,0:T(8,128)(2,1)S(1)} %fusion.47), channel_id=1, source_target_pairs={{2,0},{4,2},{6,4},{3,1},{5,3},{7,5},{10,8},{12,10},{14,12},{11,9},... | collective-permute-start | bytes 1966088 | tf_op jit(solution)/shard_map/ppermute | solution.py:248
  633.2 42.6 %collective-permute-start.38 = (bf16[640,256]{1,0:T(8,128)(2,1)S(1)}, bf16[640,256]{1,0:T(8,128)(2,1)S(1)}, u32[]{:S(2)}, u32[]{:S(2)}) collective-permute-start(bf16[640,256]{1,0:T(8,128)(2,1)S(1)} %slice_bitcast_fusion.20), channel_id=1, source_target_pairs={{0,1},{1,0},{2,3},{3,2},{4,5},{5,4},{6,7},{7,6},{8,9},{9,8},{10,11... | collective-permute-start | bytes 983048 | tf_op jit(solution)/shard_map/ppermute | solution.py:243
  664.6 25.2 %collective-permute-start.41 = (bf16[2,4,2,64,1280]{4,3,1,0,2:T(8,128)(2,1)S(1)}, bf16[2,4,2,64,1280]{4,3,1,0,2:T(8,128)(2,1)S(1)}, u32[]{:S(2)}, u32[]{:S(2)}) collective-permute-start(bf16[2,4,2,64,1280]{4,3,1,0,2:T(8,128)(2,1)S(1)} %bitcast.418), channel_id=1, source_target_pairs={{0,8},{8,0},{1,9},{9,1},{2,10},{10,2},{3,11},{11,3},{4,12},{12,4},... | collective-permute-start | bytes 7864328 | tf_op jit(solution)/shard_map/ppermute | solution.py:243
  678.3 28.3 %collective-permute-start.32 = (bf16[256,2048]{1,0:T(8,128)(2,1)S(1)}, bf16[256,2048]{1,0:T(8,128)(2,1)}, u32[]{:S(2)}, u32[]{:S(2)}) collective-permute-start(bf16[256,2048]{1,0:T(8,128)(2,1)S(1)} %fusion.51), channel_id=1, source_target_pairs={{0,16},{16,0},{1,17},{17,1},{2,18},{18,2},{3,19},{19,3},{4,20},{20... | collective-permute-start | bytes 3145736 | tf_op jit(solution)/shard_map/ppermute | solution.py:243
  683.4 45.5 %collective-permute-start.34 = (bf16[256,2048]{1,0:T(8,128)(2,1)S(1)}, bf16[256,2048]{1,0:T(8,128)(2,1)S(1)}, u32[]{:S(2)}, u32[]{:S(2)}) collective-permute-start(bf16[256,2048]{1,0:T(8,128)(2,1)S(1)} %fusion.53), channel_id=1, source_target_pairs={{0,16},{16,0},{1,17},{17,1},{2,18},{18,2},{3,19},{19,3},{4,20},{20... | collective-permute-start | bytes 3145736 | tf_op jit(solution)/shard_map/ppermute | solution.py:243
  688.5 86.0 %collective-permute-start.60 = (bf16[4,2,40,2048]{3,2,0,1:T(8,128)(2,1)}, bf16[4,2,40,2048]{3,2,0,1:T(8,128)(2,1)S(1)}, u32[]{:S(2)}, u32[]{:S(2)}) collective-permute-start(bf16[4,2,40,2048]{3,2,0,1:T(8,128)(2,1)} %dynamic-slice_bitcast_fusion), channel_id=1, source_target_pairs={{0,16},{16,0},{1,17},{17,1},{2,18},{18,2},{3,19},{19,3},{4,20},{20... | collective-permute-start | bytes 3932168 | tf_op jit(solution)/shard_map/ppermute | solution.py:243
  690.6 32.4 %collective-permute-start.42 = (bf16[2,640,256]{2,1,0:T(8,128)(2,1)S(1)}, bf16[2,640,256]{2,1,0:T(8,128)(2,1)S(1)}, u32[]{:S(2)}, u32[]{:S(2)}) collective-permute-start(bf16[2,640,256]{2,1,0:T(8,128)(2,1)S(1)} %fusion.45), channel_id=1, source_target_pairs={{2,0},{4,2},{6,4},{3,1},{5,3},{7,5},{10,8},{12,10},{14,12},{11,9},... | collective-permute-start | bytes 1966088 | tf_op jit(solution)/shard_map/ppermute | solution.py:248
  693.8 83.5 %collective-permute-start.44 = (bf16[2,4,64,1280]{3,2,1,0:T(8,128)(2,1)}, bf16[2,4,64,1280]{3,2,1,0:T(8,128)(2,1)}, u32[]{:S(2)}, u32[]{:S(2)}) collective-permute-start(bf16[2,4,64,1280]{3,2,1,0:T(8,128)(2,1)} %dynamic-slice_bitcast_fusion.1), channel_id=1, source_target_pairs={{0,1},{1,0},{2,3},{3,2},{4,5},{5,4},{6,7},{7,6},{8,9},{9,8},{10,11... | collective-permute-start | bytes 3932168 | tf_op jit(solution)/shard_map/ppermute | solution.py:243
  723.3 9.4 %collective-permute-start.43 = (bf16[640,256]{1,0:T(8,128)(2,1)S(1)}, bf16[640,256]{1,0:T(8,128)(2,1)S(1)}, u32[]{:S(2)}, u32[]{:S(2)}) collective-permute-start(bf16[640,256]{1,0:T(8,128)(2,1)S(1)} %slice_bitcast_fusion.18), channel_id=1, source_target_pairs={{0,1},{1,0},{2,3},{3,2},{4,5},{5,4},{6,7},{7,6},{8,9},{9,8},{10,11... | collective-permute-start | bytes 983048 | tf_op jit(solution)/shard_map/ppermute | solution.py:243
  735.8 17.5 %collective-permute-start.55 = (f32[1,128]{1,0:T(1,128)S(1)}, f32[1,128]{1,0:T(1,128)S(1)}, u32[]{:S(2)}, u32[]{:S(2)}) collective-permute-start(f32[1,128]{1,0:T(1,128)S(1)} %maximum_bitcast_fusion), channel_id=1, source_target_pairs={{0,16},{16,0},{1,17},{17,1},{2,18},{18,2},{3,19},{19,3},{4,20},{20... | collective-permute-start | bytes 1544 | tf_op jit(solution)/shard_map/ppermute | solution.py:279
  740.8 54.9 %collective-permute-start.49 = (bf16[2,4,2,64,640]{4,3,1,2,0:T(8,128)(2,1)S(1)}, bf16[2,4,2,64,640]{4,3,1,2,0:T(8,128)(2,1)S(1)}, u32[]{:S(2)}, u32[]{:S(2)}) collective-permute-start(bf16[2,4,2,64,640]{4,3,1,2,0:T(8,128)(2,1)S(1)} %bitcast.433), channel_id=1, source_target_pairs={{0,8},{8,0},{1,9},{9,1},{2,10},{10,2},{3,11},{11,3},{4,12},{12,4},... | collective-permute-start | bytes 3932168 | tf_op jit(solution)/shard_map/ppermute | solution.py:243
  754.6 9.7 %collective-permute-start.57 = (f32[1,128]{1,0:T(1,128)S(1)}, f32[1,128]{1,0:T(1,128)S(1)}, u32[]{:S(2)}, u32[]{:S(2)}) collective-permute-start(f32[1,128]{1,0:T(1,128)S(1)} %add.628), channel_id=1, source_target_pairs={{0,2},{2,0},{4,6},{6,4},{1,3},{3,1},{5,7},{7,5},{8,10},{10,8},{12,... | collective-permute-start | bytes 1544 | tf_op jit(solution)/shard_map/ppermute | solution.py:279
  775.2 14.7 %collective-permute-start.61 = (bf16[4,40,2048]{2,1,0:T(8,128)(2,1)S(1)}, bf16[4,40,2048]{2,1,0:T(8,128)(2,1)S(1)}, u32[]{:S(2)}, u32[]{:S(2)}) collective-permute-start(bf16[4,40,2048]{2,1,0:T(8,128)(2,1)S(1)} %dynamic-slice_bitcast_fusion.2), channel_id=1, source_target_pairs={{0,1},{1,0},{2,3},{3,2},{4,5},{5,4},{6,7},{7,6},{8,9},{9,8},{10,11... | collective-permute-start | bytes 1966088 | tf_op jit(solution)/shard_map/ppermute | solution.py:243
  779.0 16.6 %collective-permute-start.45 = (bf16[4,64,1280]{2,1,0:T(8,128)(2,1)S(1)}, bf16[4,64,1280]{2,1,0:T(8,128)(2,1)S(1)}, u32[]{:S(2)}, u32[]{:S(2)}) collective-permute-start(bf16[4,64,1280]{2,1,0:T(8,128)(2,1)S(1)} %dynamic-slice_bitcast_fusion.4), channel_id=1, source_target_pairs={{0,16},{16,0},{1,17},{17,1},{2,18},{18,2},{3,19},{19,3},{4,20},{20... | collective-permute-start | bytes 1966088 | tf_op jit(solution)/shard_map/ppermute | solution.py:243
  790.1 9.0 %collective-permute-start.62 = (bf16[40,2048]{1,0:T(8,128)(2,1)S(1)}, bf16[40,2048]{1,0:T(8,128)(2,1)S(1)}, u32[]{:S(2)}, u32[]{:S(2)}) collective-permute-start(bf16[40,2048]{1,0:T(8,128)(2,1)S(1)} %get-tuple-element.132), channel_id=1, source_target_pairs={{0,2},{2,4},{4,6},{6,0},{1,3},{3,5},{5,7},{7,1},{8,10},{10,12},{12... | collective-permute-start | bytes 491528 | tf_op jit(solution)/shard_map/ppermute | solution.py:243
  790.8 15.5 %collective-permute-start.63 = (bf16[40,2048]{1,0:T(8,128)(2,1)S(1)}, bf16[40,2048]{1,0:T(8,128)(2,1)S(1)}, u32[]{:S(2)}, u32[]{:S(2)}) collective-permute-start(bf16[40,2048]{1,0:T(8,128)(2,1)S(1)} %get-tuple-element.134), channel_id=1, source_target_pairs={{0,4},{2,6},{4,0},{6,2},{1,5},{3,7},{5,1},{7,3},{8,12},{10,14},{12... | collective-permute-start | bytes 491528 | tf_op jit(solution)/shard_map/ppermute | solution.py:243
  792.9 21.2 %collective-permute-start.64 = (bf16[40,2048]{1,0:T(8,128)(2,1)S(1)}, bf16[40,2048]{1,0:T(8,128)(2,1)S(1)}, u32[]{:S(2)}, u32[]{:S(2)}) collective-permute-start(bf16[40,2048]{1,0:T(8,128)(2,1)S(1)} %get-tuple-element.133), channel_id=1, source_target_pairs={{0,6},{2,0},{4,2},{6,4},{1,7},{3,1},{5,3},{7,5},{8,14},{10,8},{12,... | collective-permute-start | bytes 491528 | tf_op jit(solution)/shard_map/ppermute | solution.py:243
  796.2 18.7 %collective-permute-start.50 = (bf16[4,2,64,640]{3,2,0,1:T(8,128)(2,1)S(1)}, bf16[4,2,64,640]{3,2,0,1:T(8,128)(2,1)S(1)}, u32[]{:S(2)}, u32[]{:S(2)}) collective-permute-start(bf16[4,2,64,640]{3,2,0,1:T(8,128)(2,1)S(1)} %dynamic-slice_bitcast_fusion.3), channel_id=1, source_target_pairs={{0,16},{16,0},{1,17},{17,1},{2,18},{18,2},{3,19},{19,3},{4,20},{20... | collective-permute-start | bytes 1966088 | tf_op jit(solution)/shard_map/ppermute | solution.py:243
  796.6 20.6 %collective-permute-start.46 = (bf16[64,1280]{1,0:T(8,128)(2,1)S(1)}, bf16[64,1280]{1,0:T(8,128)(2,1)S(1)}, u32[]{:S(2)}, u32[]{:S(2)}) collective-permute-start(bf16[64,1280]{1,0:T(8,128)(2,1)S(1)} %get-tuple-element.135), channel_id=1, source_target_pairs={{0,2},{2,4},{4,6},{6,0},{1,3},{3,5},{5,7},{7,1},{8,10},{10,12},{12... | collective-permute-start | bytes 491528 | tf_op jit(solution)/shard_map/ppermute | solution.py:243
  799.1 18.1 %collective-permute-start.47 = (bf16[64,1280]{1,0:T(8,128)(2,1)S(1)}, bf16[64,1280]{1,0:T(8,128)(2,1)S(1)}, u32[]{:S(2)}, u32[]{:S(2)}) collective-permute-start(bf16[64,1280]{1,0:T(8,128)(2,1)S(1)} %get-tuple-element.137), channel_id=1, source_target_pairs={{0,4},{2,6},{4,0},{6,2},{1,5},{3,7},{5,1},{7,3},{8,12},{10,14},{12... | collective-permute-start | bytes 491528 | tf_op jit(solution)/shard_map/ppermute | solution.py:243
  806.2 11.0 %collective-permute-start.48 = (bf16[64,1280]{1,0:T(8,128)(2,1)S(1)}, bf16[64,1280]{1,0:T(8,128)(2,1)S(1)}, u32[]{:S(2)}, u32[]{:S(2)}) collective-permute-start(bf16[64,1280]{1,0:T(8,128)(2,1)S(1)} %get-tuple-element.136), channel_id=1, source_target_pairs={{0,6},{2,0},{4,2},{6,4},{1,7},{3,1},{5,3},{7,5},{8,14},{10,8},{12,... | collective-permute-start | bytes 491528 | tf_op jit(solution)/shard_map/ppermute | solution.py:243
  815.2 7.1 collective-permute-start.51
  816.9 9.4 %collective-permute-start.65 = (bf16[2,64,1792]{2,1,0:T(8,128)(2,1)S(1)}, bf16[2,64,1792]{2,1,0:T(8,128)(2,1)S(1)}, u32[]{:S(2)}, u32[]{:S(2)}) collective-permute-start(bf16[2,64,1792]{2,1,0:T(8,128)(2,1)S(1)} %get-tuple-element.110), channel_id=1, source_target_pairs={{0,16},{16,0},{1,17},{17,1},{2,18},{18,2},{3,19},{19,3},{4,20},{20... | collective-permute-start | bytes 1376264 | tf_op jit(solution)/shard_map/ppermute | solution.py:243
  (155 other events, 2296.8 us)
Sparse Core Ops, SparseCore 0:
  10.8 84.4 all-gather.3
  98.1 163.8 all-gather.5
  264.2 64.8 all-gather.7
  413.1 99.1 reduce-scatter.3
  515.7 90.4 reduce-scatter.5
  609.7 105.9 reduce-scatter.7

commit v3 on v2

--- a/solution.py
+++ b/solution.py
@@ -24,6 +24,7 @@
 LOG2E = math.log2(math.e)
 MASKED = -1e30
 
+FLAGS = {'wo': 0, 'ybo': 2, 'qg': 0, 'og': 1, 'xq': 0, 'att1': 1, 'ogc': 0, 'gh1': 1, 'dn': 4, 'ou': 5, 'h0': 0, 'ga': 1, 'wg': 0, 'h1': 0, 'up': 1, 's': 0, 'hc': 1, 't': 0, 'oa': 'y', 'qa': 'x', 'w1': 3, 'tl': 3, 'sm': 1, 'bs': 1}
 bf16 = jnp.bfloat16
 f32 = jnp.float32
 
@@ -230,8 +231,12 @@
 DOC_ROWS = 16
 
 
+def opt(name, default=0):
+    return FLAGS.get(name, default)
+
+
 def after(value, *earlier):
-    return lax.optimization_barrier((value, *earlier))[0]
+    return lax.optimization_barrier((value, *earlier))[0] if earlier else value
 
 
 class Transfers:
@@ -301,10 +306,12 @@
             pieces.append(self.shift(self.take(value, axis, dim, k), axis, k))
         return self.place(pieces, axis, out_dim)
 
-    def spread(self, pieces, order):
+    def spread(self, pieces, order, *earlier):
         value = self.place(pieces, "z", 0)
         have = ["z"]
         for axis in order:
+            if earlier and axis == order[-1]:
+                value = after(value, *earlier)
             dim = sum(1 for a in have if LAYOUT.index(a) < LAYOUT.index(axis))
             value = self.gather(value, axis, dim)
             have.append(axis)
@@ -372,15 +379,17 @@
     kv_near = move.direct((w_kv.astype(f32) * gain_a).astype(bf16), "z")
     w_q_low = (w_query.astype(f32) * gain_a).astype(bf16)
     q_near = move.direct(w_q_low, "z")
-    w_kv_all = move.spread(kv_near, "xyc").reshape(width, 2 * KV_WIDTH)
-    w_q_all = move.spread(q_near, "xyc").reshape(width, Q_WIDTH)
-    w_out_all = lax.all_gather(w_out, tuple(LAYOUT), axis=0, tiled=True)
+    kv_x = move.gather(move.place(kv_near, "z", 0), "x", 1)
+    kv_xy = move.gather(kv_x, "y", 0)
+    w_kv_all = move.gather(kv_xy, "c", 1).reshape(width, 2 * KV_WIDTH)
+    if opt("wo"):
+        out_near = move.direct(after(w_out, *(kv_near[1:] if opt("wo") == 1 else [])), "z")
 
     w_gate_low = (w_gate.astype(f32) * gain_f).astype(bf16).reshape(d_rows, ys, cs, 1, ffn_part)
     w_up_low = (w_up.astype(f32) * gain_f).astype(bf16).reshape(d_rows, ys, cs, 1, ffn_part)
     both = jnp.concatenate([w_gate_low, w_up_low], axis=3).reshape(d_rows, ys, cs, 2 * ffn_part)
-    both = move.exchange(both, "c", 2, 0)
-    both = move.exchange(both, "y", 2, 0)
+    both = move.exchange(after(both, *(kv_near[:1] if opt("ybo") else [])), "c", 2, 0)
+    both = move.exchange(after(both, *[[], kv_near[1:], [kv_x], [kv_xy]][opt("ybo")]), "y", 2, 0)
     both = lax.all_gather(both, CTX, axis=0)
     w_down_all = lax.all_gather(w_down, CTX, axis=0, tiled=True)
     w_both = both.transpose(1, 2, 0, 3, 4).reshape(width, 2 * ffn_part)
@@ -403,15 +412,11 @@
         for b in range(batches)
     ]
 
-    def seq_blocks(rows):
-        chips = move.ring(rows, "y")
+    def core_blocks(chips):
         blocks = list(chips)
         for k in range(1, cs):
             blocks += [move.shift(chip, "c", k) for chip in chips]
         return blocks
-
-    def seq_gather(rows):
-        return jnp.concatenate(seq_blocks(rows), axis=0)
 
     def core_sum(partial):
         blocks = partial.reshape(cs, ys, local, width)
@@ -425,11 +430,6 @@
         for k in range(1, ys):
             result = result + move.shift(rows[k], "y", -k).astype(f32)
         return result
-
-    grad_blocks = seq_blocks(
-        after(jnp.concatenate(grads_out, axis=0).astype(bf16), w_q_all)
-    )
-    grads_all = [jnp.concatenate([g[part] for g in grad_blocks], axis=0) for part in parts]
 
     inputs = after(tokens, *kv_near[1:]).reshape(both_rows, width).astype(f32)
     scale_in = row_scale(inputs)
@@ -448,8 +448,31 @@
     hops = [kv]
     for _ in range(back_groups):
         hops.append(move.hop(hops[-1], "z", 1))
+    w_q_all = move.spread(q_near, opt("qord", "xyc"), *([kv] if opt("qg") else [])).reshape(width, Q_WIDTH)
+    if opt("wo"):
+        w_out_all = move.spread(
+            out_near, opt("woord", "xyc"), *([hops[1]] if opt("wog") else [])
+        ).reshape(Q_WIDTH, width)
+    else:
+        w_out_all = lax.all_gather(w_out, tuple(LAYOUT), axis=0, tiled=True)
+    half = Q_WIDTH // 2
+    query_lin = jnp.concatenate(
+        [dot(w_q_all[:, :half], normed, 0, 1), dot(w_q_all[:, half:], normed, 0, 1)], axis=0
+    ).reshape(HEADS, HEAD_DIM, both_rows)
+    query_rot, query_scale = head_forward(query_lin, gain_q, cosine, sine)
+    query_t = query_rot.astype(bf16).reshape(Q_WIDTH, both_rows)
+
+    grad_chips = move.ring(
+        after(
+            jnp.concatenate(grads_out, axis=0).astype(bf16),
+            *([[], [hops[1]], [kv], [w_q_all], [w_kv_all]][opt("og")]),
+        ), "y"
+    )
+
     blocks = []
-    for group in hops[::-1]:
+    for number, group in enumerate(hops[::-1]):
+        if number == 0 and opt("xq"):
+            group = after(group, query_t)
         blocks += move.direct(group, "x")
     windows = [jnp.stack([block[:, part] for block in blocks]) for part in parts]
     present = at_z + jnp.repeat(jnp.arange(back_groups + 1), xs) >= back_groups
@@ -459,39 +482,54 @@
         below = docs.reshape(1, -1) < doc_ids[b][:, None]
         starts.append(jnp.sum(below.astype(jnp.int32), axis=1))
 
-    half = Q_WIDTH // 2
-    query_lin = jnp.concatenate(
-        [dot(w_q_all[:, :half], normed, 0, 1), dot(w_q_all[:, half:], normed, 0, 1)], axis=0
-    ).reshape(HEADS, HEAD_DIM, both_rows)
-    query_rot, query_scale = head_forward(query_lin, gain_q, cosine, sine)
-    query_t = query_rot.astype(bf16).reshape(Q_WIDTH, both_rows)
-
+    if opt("eh") == 2:
+        grad_blocks = core_blocks(grad_chips)
+        grads_all = [jnp.concatenate([g[part] for g in grad_blocks], axis=0) for part in parts]
+        early = [dot(g, w_down_all, 1, 1) for g in grads_all]
     metas, mixed, lses, resids, scale_mids, normed2_all = [], [], [], [], [], []
+    rows, normed2_chips = None, []
     for b, part in enumerate(parts):
         meta = jnp.stack([starts[b][0] // local, high, q_start, at_x]).astype(jnp.int32)
+        if rows is not None and opt("att1"):
+            meta = after(meta, rows, *(early[:1] if opt("eh") == 2 else []))
         mixed_t, lse = attend_forward(xs, meta, starts[b][:, None], query_t, b, windows[b])
         resid = inputs[part] + dot(mixed_t, w_out_all, 0, 0)
         scale_mid = row_scale(resid)
-        normed2_all.append(seq_gather((resid * scale_mid).astype(bf16)))
+        rows = (resid * scale_mid).astype(bf16)
+        normed2_chips.append(move.ring(rows, "y"))
         metas.append(meta)
         mixed.append(mixed_t)
         lses.append(lse)
         resids.append(resid)
         scale_mids.append(scale_mid)
 
+    grad_blocks = grad_blocks if opt("eh") == 2 else core_blocks(
+        [after(chip, *([rows] if opt("ogc") else [])) for chip in grad_chips]
+    )
+    grads_all = [jnp.concatenate([g[part] for g in grad_blocks], axis=0) for part in parts]
+
+    if opt("eh") == 1:
+        early = [dot(g, w_down_all, 1, 1) for g in grads_all]
     hiddens, gate_grads, up_grads, sums = [], [], [], []
     for b in range(batches):
+        chips = normed2_chips[b]
+        if b > 0 and opt("w1"):
+            chips = chips[:1] + [after(chip, [0, wide, grad_gate, partial][opt("w1")]) for chip in chips[1:]]
+        normed2_all.append(jnp.concatenate(core_blocks(chips), axis=0))
         wide = matmul(normed2_all[b], w_both)
         gate, up = wide[:, :ffn_part], wide[:, ffn_part:]
         sig = jax.nn.sigmoid(gate)
         silu = gate * sig
         hiddens.append((silu * up).astype(bf16))
-        grads = after(grads_all[b], *sums[-1][1:]) if sums else grads_all[b]
-        grad_hidden = dot(grads, w_down_all, 1, 1)
+        grads = after(grads_all[b], *sums[-1][1:]) if sums and opt("gh1") else grads_all[b]
+        grad_hidden = early[b] if opt("eh") else dot(grads, w_down_all, 1, 1)
+        if sums and opt("eh") and opt("gh1"):
+            grad_hidden = after(grad_hidden, *sums[-1][1:])
         grad_gate = (grad_hidden * up * (sig * (1.0 + gate * (1.0 - sig)))).astype(bf16)
         grad_up = (grad_hidden * silu).astype(bf16)
         grad_wide = jnp.concatenate([grad_gate, grad_up], axis=1)
-        sums.append(core_sum(dot(grad_wide, w_both, 1, 1).astype(bf16)))
+        partial = dot(grad_wide, w_both, 1, 1).astype(bf16)
+        sums.append(core_sum(partial))
         gate_grads.append(grad_gate)
         up_grads.append(grad_up)
 
@@ -508,35 +546,63 @@
             total = total + dot(left, right, 0, 0)
         return total.astype(bf16)
 
-    def scatter_columns(lefts, rights):
-        value = token_sum(lefts, rights).reshape(ys * cs, zs * xs * d_rows, ffn_part)
+    def scatter_columns(total):
+        value = total.reshape(ys * cs, zs * xs * d_rows, ffn_part)
         return lax.psum_scatter(value, CTX, scatter_dimension=1, tiled=True)
 
-    gate_sum = scatter_columns(normed2_all, gate_grads)
-    up_sum = scatter_columns(normed2_all, [after(g, *sums[-1][1:]) for g in up_grads])
-    late = after(hiddens[0], *sums[-1][1:])
-    grad_down = lax.psum_scatter(
-        token_sum([late] + hiddens[1:], grads_all), CTX, scatter_dimension=0, tiled=True
-    ).astype(f32)
-
-    query_grads, groups = [], []
+    late = [
+        after(hidden, *[[], [partial], sums[-1][1:], [low_grads[0]]][opt("dn") % 4])
+        for hidden in hiddens
+    ]
+    if opt("dn") < 4:
+        down_total = token_sum(late, grads_all)
+        grad_down = lax.psum_scatter(down_total, CTX, scatter_dimension=0, tiled=True).astype(f32)
+    late = [
+        after(hidden, *[[], [partial], sums[-1][1:], [low_grads[0]], low_grads][min(opt("ou"), 4)])
+        for hidden in hiddens
+    ]
+    if opt("ou") < 5:
+        out_rows = [core_sum(matmul(hidden, w_down_all).astype(bf16)) for hidden in late]
+
+    def split_cores(value, rows):
+        value = value.astype(bf16).reshape(ys, cs, zs, xs, rows, -1)
+        return move.scatter(value, "c", 1).astype(bf16)
+
+    query_grads, carried = [], []
+    gate_total, held = None, []
+    if opt("h0") & 1:
+        held += [down_total]
+    if opt("h0") & 2:
+        held += [row for rows in out_rows for row in rows[1:]]
     for b in range(batches):
-        grad_mixed_t = dot(w_out_all, low_grads[b], 1, 1).astype(bf16)
+        low = after(low_grads[b], *held)
+        grad_mixed_t = dot(w_out_all, low, 1, 1).astype(bf16)
         dq_t, dkv = attend_backward(
             xs, metas[b], starts[b][None, :], query_t, b, windows[b], grad_mixed_t, mixed[b],
             lses[b],
         )
         query_grads.append(dq_t)
-        groups.append(dkv.reshape(back_groups + 1, xs, 2 * KV_WIDTH, local))
-
-    def split_cores(value, rows):
-        value = value.astype(bf16).reshape(ys, cs, zs, xs, rows, -1)
-        return move.scatter(value, "c", 1).astype(bf16)
-
-    out_cores = split_cores(
-        matmul(jnp.concatenate(mixed, axis=1), jnp.concatenate(low_grads, axis=0)),
-        w_out.shape[0],
-    )
+        groups = dkv.reshape(back_groups + 1, xs, 2 * KV_WIDTH, local)
+        first = (move.hop(groups[0], "z", -1).astype(f32) + groups[1].astype(f32)).astype(bf16)
+        carried.append([first] + [groups[k] for k in range(2, back_groups + 1)])
+        if gate_total is None:
+            gate_total = token_sum(normed2_all, [after(gate_grads[0], *[[], [dq_t], sums[-1][1:], low_grads, [low_grads[0]] + sums[-1][1:]][opt("ga")])] + gate_grads[1:])
+            out_cores = split_cores(
+                matmul(
+                    jnp.concatenate(mixed, axis=1),
+                    jnp.concatenate([after(low_grads[0], *([dq_t] if opt("wg") else []))] + low_grads[1:], axis=0),
+                ),
+                w_out.shape[0],
+            )
+            held = []
+            if opt("h1") & 1:
+                held += [gate_total]
+            if opt("h1") & 2:
+                held += [out_cores]
+            if opt("h1") & 4:
+                held += [first]
+    gate_sum = scatter_columns(gate_total)
+
     query_grad, gq_gain = head_backward(
         jnp.concatenate(query_grads, axis=1).astype(f32).reshape(HEADS, HEAD_DIM, both_rows),
         query_lin, query_scale, gain_q, cosine, sine,
@@ -544,21 +610,40 @@
     query_grad = query_grad.astype(bf16).reshape(Q_WIDTH, both_rows)
     q_cores = split_cores(dot(normed, query_grad, 0, 1), d_rows)
 
+    up_total = token_sum(normed2_all, [after(up_grads[0], *[[], [query_grads[0]], [query_grads[-1]], [carried[-1][0]], sums[-1][1:]][opt("up")])] + up_grads[1:])
+    up_sum = scatter_columns(up_total)
+    if opt("dn") >= 4:
+        late = [after(hiddens[0], query_grads[opt("dn") - 4])] + hiddens[1:]
+        down_total = token_sum(late, grads_all)
+        grad_down = lax.psum_scatter(down_total, CTX, scatter_dimension=0, tiled=True).astype(f32)
+
+    oa, qa = opt("oa", "x"), opt("qa", "y")
+    out_chips = move.scatter(out_cores, oa, "yzx".index(oa)).astype(bf16)
+    q_chips = move.scatter(q_cores, qa, "yzx".index(qa)).astype(bf16)
     kv_grads = []
+    if opt("ou") == 5:
+        out_rows = [
+            core_sum(matmul(after(hidden, query_grads[0]), w_down_all).astype(bf16)) for hidden in hiddens
+        ]
     for b in range(batches):
-        carried = groups[b][0]
-        for k in range(1, back_groups + 1):
-            if b == batches - 1 and k == back_groups:
-                carried = after(carried, out_cores, q_cores)
-            carried = (
-                move.hop(carried, "z", -1).astype(f32) + groups[b][k].astype(f32)
-            ).astype(bf16)
-        total = carried[0].astype(f32)
+        if b == batches - 1 and opt("hc"):
+            carried[b][0] = after(carried[b][0], *[[], [out_cores, q_cores], [out_cores], [q_cores]][opt("hc")])
+        sent = carried[b][0]
+        for group in carried[b][1:]:
+            sent = (move.hop(sent, "z", -1).astype(f32) + group.astype(f32)).astype(bf16)
+        if b == batches - 1:
+            sent = after(sent, *([up_total] if opt("s") & 1 else []), *([q_cores] if opt("s") & 2 else []))
+        total = sent[0].astype(f32)
         for k in range(1, xs):
-            total = total + move.shift(carried[k], "x", -k).astype(f32)
+            total = total + move.shift(sent[k], "x", -k).astype(f32)
         kv_grads.append(total)
-    grad_out_w = move.scatter_chips(out_cores, "yxz")
-    grad_q_w = move.scatter_chips(q_cores, "xyz")
+    outputs = [
+        (resids[b] + chip_sum(out_rows[b])).astype(bf16) for b in range(batches)
+    ]
+    kv_grads[-1] = after(
+        kv_grads[-1], *([out_chips] if opt("t") & 1 else []), *(outputs if opt("t") & 2 else []),
+        *([q_chips] if opt("t") & 4 else []),
+    )
 
     kv_sum = jnp.concatenate(kv_grads, axis=1)
     key_grad, gk_gain = head_backward(
@@ -569,20 +654,24 @@
         [key_grad.astype(bf16).reshape(KV_WIDTH, both_rows), kv_sum[KV_WIDTH:].astype(bf16)],
         axis=0,
     )
-    grad_kv_w = move.scatter_chips(split_cores(dot(normed, kv_grad, 0, 1), d_rows), "yxz")
+    kv_cores = split_cores(dot(normed, kv_grad, 0, 1), d_rows)
+    if opt("tl") & 1:
+        out_chips = after(out_chips, kv_cores)
+    if opt("tl") & 2:
+        q_chips = after(q_chips, kv_cores)
+    kv_chips = kv_cores
+    grad_out_w = move.scatter_chips(out_chips, "xyz".replace(oa, ""))
+    grad_q_w = move.scatter_chips(q_chips, "xyz".replace(qa, ""))
+    grad_kv_w = move.scatter_chips(kv_chips, opt("kord", "xyz"))
     grad_normed = dot(query_grad, w_q_all, 0, 1) + dot(kv_grad, w_kv_all, 0, 1)
     normed_back = norm_backward(grad_normed, inputs, scale_in)
     token_grads = [
         (grad_resids[b] + normed_back[part]).astype(bf16) for b, part in enumerate(parts)
     ]
 
-    outputs = []
-    for b in range(batches):
-        hidden = after(hiddens[b], low_grads[-1])
-        rows = core_sum(matmul(hidden, w_down_all).astype(bf16))
-        outputs.append((resids[b] + chip_sum(rows)).astype(bf16))
-
     both_sum = jnp.concatenate([gate_sum, up_sum], axis=2).reshape(ys, cs, d_rows, -1)
+    if opt("bs"):
+        both_sum = after(both_sum, kv_cores)
     both_sum = move.exchange(both_sum, "y", 0, 2)
     both_sum = move.exchange(both_sum, "c", 0, 2).astype(f32)
     grad_gate_w = both_sum[..., :ffn_part].reshape(d_rows, -1)
@@ -596,6 +685,8 @@
     )
     grad_kv_w = grad_kv_w * gain_a
     small = jnp.concatenate([gq_gain, gk_gain])[None, :]
+    if opt("sm"):
+        small = after(small, *[[], [kv_cores], [grad_kv_w]][opt("sm")])
     for axis in LAYOUT:
         small = move.total(small, axis)
 

time: 854 us -> 846 us (level)
  waiting for transfers between devices: 357 us -> 311 us
  matrix products: 151 us -> 164 us
  local copies, waits for them, and re-layouts: 58.4 us -> 68.6 us
    ppermute x56, waiting for transfers between devices: 244 us -> 186 us  [shift(): lax.ppermute(value, axis, [(i, (i + step) % size) for i in range(size)])]
    ppermute x6, waiting for transfers between devices: 104 us -> 82.8 us  [hop(): return lax.ppermute(value, axis, pairs)]
    ppermute x5, waiting for transfers between devices: 8.04 us -> 28.2 us  [total(): lax.ppermute(value, axis, [(i, i ^ step) for i in range(size)])]
    dot_general x26, matrix products: 151 us -> 164 us  [dot(): lax.dot_general(left, right, (((left_dim,), (right_dim,)), ((), ())), pre...]
    all_gather x1, waiting for transfers between devices: 0.01 us -> 12.6 us  [per_device(): w_down_all = lax.all_gather(w_down, CTX, axis=0, tiled=True)]
    unnamed x301 -> x269, local copies, waits for them, and re-layouts: 20.3 us -> 20.9 us
  transfers between devices with their start and end apart: 73 -> 73, of which waited for: 32 -> 31; matrix products, arithmetic and copies ran while one was open for 30% -> 31% of each run, Pallas kernels for 4% -> 3%
where the time goes in v3:
time: 846 us; the launch traced here: 835 us
  waiting for transfers between devices  311 us (37%)
  matrix products  164 us (19%)
  starting transfers between devices  138 us (16%)
  other arithmetic  94.9 us (11%)
  local copies, waits for them, and re-layouts  68.6 us (8%)
  Pallas kernels  36.3 us (4%)
  between operations  22.1 us (3%)
    ppermute x56, waiting for transfers between devices, shift(): lax.ppermute(value, axis, [(i, (i + step) % size) for i in range(size)])  186 us
    dot_general x26, matrix products, dot(): lax.dot_general(left, right, (((left_dim,), (right_dim,)), ((), ())), pre...  164 us
    ppermute x56, starting transfers between devices, shift(): lax.ppermute(value, axis, [(i, (i + step) % size) for i in range(size)])  98.2 us
    ppermute x6, waiting for transfers between devices, hop(): return lax.ppermute(value, axis, pairs)  82.8 us
    ppermute x5, waiting for transfers between devices, total(): lax.ppermute(value, axis, [(i, i ^ step) for i in range(size)])  28.2 us
    ppermute x6, starting transfers between devices, hop(): return lax.ppermute(value, axis, pairs)  22.9 us
    unnamed x269, local copies, waits for them, and re-layouts  20.9 us
    pallas_call x2, Pallas kernels, attend_backward(): pl.pallas_call(functools.partial(backward_kernel, xs), name='attend_backw...  20.9 us
  transfers between devices with their start and end apart: 73, of which 31 were waited for; matrix products, arithmetic and copies ran while one was open for 31% of the time, Pallas kernels for 3%

profile of v3, /device:TPU:0, one launch (start us, length us, event | category | flops | bytes accessed | tf_op | source)
XLA Modules:
  0.0 834.7 jit_solution(15012076039298728279)
XLA Ops:
  9.5 3.1 collective-permute-start
  24.8 8.1 collective-permute-done.3
  34.9 12.5 %collective-permute-done.21 = bf16[2,64,1792]{2,1,0:T(8,128)(2,1)S(1)} collective-permute-done((bf16[2,64,1792]{2,1,0:T(8,128)(2,1)S(1)}, bf16[2,64,1792]{2,1,0:T(8,128)(2,1)S(1)}, u32[]{:S(2)}, u32[]{:S(2)}) %collective-permute-start.21) | collective-permute-done | bytes 458784 | tf_op jit(solution)/shard_map/ppermute | solution.py:248
  56.8 9.6 %collective-permute-done.12 = bf16[64,1280]{1,0:T(8,128)(2,1)S(1)} collective-permute-done((bf16[64,1280]{1,0:T(8,128)(2,1)S(1)}, bf16[64,1280]{1,0:T(8,128)(2,1)S(1)}, u32[]{:S(2)}, u32[]{:S(2)}) %collective-permute-start.12) | collective-permute-done | bytes 163872 | tf_op jit(solution)/shard_map/ppermute | solution.py:248
  69.1 5.4 collective-permute-done.4
  75.3 14.9 %collective-permute-done.14 = bf16[4,64,1280]{2,1,0:T(8,128)(2,1)S(1)} collective-permute-done((bf16[4,64,1280]{2,1,0:T(8,128)(2,1)S(1)}, bf16[4,64,1280]{2,1,0:T(8,128)(2,1)S(1)}, u32[]{:S(2)}, u32[]{:S(2)}) %collective-permute-start.14) | collective-permute-done | bytes 655392 | tf_op jit(solution)/shard_map/ppermute | solution.py:248
  97.1 3.4 collective-permute-start.6
  103.7 20.6 %collective-permute-done.6 = bf16[656,512]{1,0:T(8,128)(2,1)S(1)} collective-permute-done((bf16[656,512]{1,0:T(8,128)(2,1)S(1)}, bf16[656,512]{1,0:T(8,128)(2,1)S(1)}, u32[]{:S(2)}, u32[]{:S(2)}) %collective-permute-start.6) | collective-permute-done | bytes 671776 | tf_op jit(solution)/shard_map/ppermute | solution.py:253
  124.3 12.9 %collective-permute-start.7 = (bf16[656,512]{1,0:T(8,128)(2,1)S(1)}, bf16[656,512]{1,0:T(8,128)(2,1)S(1)}, u32[]{:S(2)}, u32[]{:S(2)}) collective-permute-start(bf16[656,512]{1,0:T(8,128)(2,1)S(1)} %collective-permute-done.6), channel_id=1, source_target_pairs={{0,2},{2,4},{4,6},{1,3},{3,5},{5,7},{8,10},{10,12},{12,14},{9,11},... | collective-permute-start | bytes 2015240 | tf_op jit(solution)/shard_map/ppermute | solution.py:253
  142.0 16.2 %collective-permute-done.7 = bf16[656,512]{1,0:T(8,128)(2,1)S(1)} collective-permute-done((bf16[656,512]{1,0:T(8,128)(2,1)S(1)}, bf16[656,512]{1,0:T(8,128)(2,1)S(1)}, u32[]{:S(2)}, u32[]{:S(2)}) %collective-permute-start.7) | collective-permute-done | bytes 671776 | tf_op jit(solution)/shard_map/ppermute | solution.py:253
  158.9 3.1 fusion.121
  163.5 25.5 %collective-permute-done.8 = bf16[656,512]{1,0:T(8,128)(2,1)S(1)} collective-permute-done((bf16[656,512]{1,0:T(8,128)(2,1)S(1)}, bf16[656,512]{1,0:T(8,128)(2,1)S(1)}, u32[]{:S(2)}, u32[]{:S(2)}) %collective-permute-start.8) | collective-permute-done | bytes 671776 | tf_op jit(solution)/shard_map/ppermute | solution.py:248
  189.1 26.2 %collective-permute-done.9 = bf16[656,512]{1,0:T(8,128)(2,1)S(1)} collective-permute-done((bf16[656,512]{1,0:T(8,128)(2,1)S(1)}, bf16[656,512]{1,0:T(8,128)(2,1)S(1)}, u32[]{:S(2)}, u32[]{:S(2)}) %collective-permute-start.9) | collective-permute-done | bytes 671776 | tf_op jit(solution)/shard_map/ppermute | solution.py:248
  238.1 7.7 attend_forward.2
  245.9 2.7 fusion.122
  248.7 5.3 multiply_reduce_fusion.6
  255.4 3.2 fusion.123
  258.6 3.3 fusion.124
  262.3 7.7 attend_forward.3
  270.1 11.2 %collective-permute-done.17 = bf16[256,2048]{1,0:T(8,128)(2,1)} collective-permute-done((bf16[256,2048]{1,0:T(8,128)(2,1)}, bf16[256,2048]{1,0:T(8,128)(2,1)}, u32[]{:S(2)}, u32[]{:S(2)}) %collective-permute-start.17) | collective-permute-done | bytes 1048608 | tf_op jit(solution)/shard_map/ppermute | solution.py:248
  281.3 5.4 multiply_reduce_fusion.4
  289.7 15.4 %fusion.113 = f32[1024,1792]{1,0:T(8,128)} fusion(bf16[2048,1792]{1,0:T(8,128)(2,1)} %bitcast.444, bf16[256,2048]{1,0:T(8,128)(2,1)} %collective-permute-done.19, bf16[256,2048]{1,0:T(8,128)(2,1)} %collective-permute-done.18, bf16[256,2048]{1,0:T(8,128)(2,1)} %collective-permute-done.17, bf16[256,2048]{1,0:T(8,128)(2,1)} %multiply_convert_fusion.7), kind=kOutput, calls=%fused_computation.357 | convolution fusion | flops 7532969984 | bytes 18874368 | tf_op jit(solution)/shard_map/dot_general | solution.py:33
  305.2 12.6 %all-gather.8.cloned.1.call-done = bf16[896,2048]{1,0:T(8,128)(2,1)} async-done(((bf16[112,2048]{1,0:T(8,128)(2,1)}), bf16[896,2048]{1,0:T(8,128)(2,1)}) %all-gather.8.cloned.1.call-update) | async-done | bytes 3670032 | tf_op jit(solution)/shard_map/all_gather | solution.py:394
  317.7 11.8 %multiply_convert_fusion.4 = (bf16[1024,896]{1,0:T(8,128)(2,1)S(1)}, bf16[1024,896]{1,0:T(8,128)(2,1)S(1)}, bf16[1024,896]{1,0:T(8,128)(2,1)}) fusion(f32[1024,1792]{1,0:T(8,128)} %fusion.113, bf16[896,2048]{1,0:T(8,128)(2,1)} %all-gather.8.cloned.1.call-done, bf16[256,2048]{1,0:T(8,128)(2,1)} %get-tuple-element.104, ...), kind=kOutput, calls=%fused_computation.46 | convolution fusion | flops 3788636160 | bytes 20709376 | tf_op jit(solution)/shard_map/dot_general | solution.py:33
  329.6 8.0 convolution_convert_fusion.3
  340.6 13.4 %fusion.112 = f32[1024,1792]{1,0:T(8,128)} fusion(bf16[2048,1792]{1,0:T(8,128)(2,1)S(1)} %bitcast.446, bf16[256,2048]{1,0:T(8,128)(2,1)S(1)} %collective-permute-done.31, bf16[256,2048]{1,0:T(8,128)(2,1)} %collective-permute-done.30, bf16[256,2048]{1,0:T(8,128)(2,1)} %collective-permute-done.29, bf16[256,2048]{1,0:T(8,128)(2,1)} %multiply_convert_fusion.6), kind=kOutput, calls=%fused_computation.356 | convolution fusion | flops 7532969984 | bytes 18874368 | tf_op jit(solution)/shard_map/dot_general | solution.py:33
  357.0 8.8 %multiply_convert_fusion.1 = (bf16[1024,896]{1,0:T(8,128)(2,1)S(1)}, bf16[1024,896]{1,0:T(8,128)(2,1)S(1)}, bf16[1024,896]{1,0:T(8,128)(2,1)}) fusion(f32[1024,1792]{1,0:T(8,128)} %fusion.112, bf16[1024,2048]{1,0:T(8,128)(2,1)S(1)} %pad_maximum_fusion.3, bf16[896,2048]{1,0:T(8,128)(2,1)S(1)} %copy-done.106), kind=kOutput, calls=%fused_computation.41 | convolution fusion | flops 3771858944 | bytes 20709376 | tf_op jit(solution)/shard_map/dot_general | solution.py:33
  365.8 8.4 %convolution_convert_fusion.2 = bf16[1024,2048]{1,0:T(8,128)(2,1)S(1)} fusion(bf16[2048,1792]{1,0:T(8,128)(2,1)S(1)} %bitcast.447, bf16[1024,896]{1,0:T(8,128)(2,1)S(1)} %get-tuple-element.70, bf16[1024,896]{1,0:T(8,128)(2,1)S(1)} %get-tuple-element.69), kind=kOutput, calls=%fused_computation.30 | convolution fusion | flops 7525629952 | bytes 15204352 | tf_op jit(solution)/shard_map/dot_general | solution.py:33
  381.3 3.2 convert_add_fusion.2
  386.2 9.5 %fusion.111 = f32[2048,896]{1,0:T(8,128)} fusion(bf16[1024,896]{1,0:T(8,128)(2,1)S(1)} %copy-done.117, bf16[256,2048]{1,0:T(8,128)(2,1)S(1)} %copy-done.109, bf16[256,2048]{1,0:T(8,128)(2,1)} %collective-permute-done.30, bf16[256,2048]{1,0:T(8,128)(2,1)} %collective-permute-done.29, bf16[256,2048]{1,0:T(8,128)(2,1)} %multiply_convert_fusion.6), kind=kOutput, calls=%fused_computation.355 | convolution fusion | flops 3774873600 | bytes 13369344 | tf_op jit(solution)/shard_map/dot_general | solution.py:33
  395.8 7.8 collective-permute-done.26
  404.1 21.4 %collective-permute-done.35 = bf16[256,2048]{1,0:T(8,128)(2,1)S(1)} collective-permute-done((bf16[256,2048]{1,0:T(8,128)(2,1)S(1)}, bf16[256,2048]{1,0:T(8,128)(2,1)S(1)}, u32[]{:S(2)}, u32[]{:S(2)}) %collective-permute-start.35) | collective-permute-done | bytes 1048608 | tf_op jit(solution)/shard_map/ppermute | solution.py:248
  426.0 5.1 fusion.115
  433.6 10.5 %attend_backward.2 = (bf16[1280,256]{1,0:T(8,128)(2,1)}, bf16[6,2,320,256]{3,2,1,0:T(8,128)(2,1)}) custom-call(s32[4]{0:T(128)} %add_add_fusion.meta, s32[1,256]{1,0:T(1,128)} %bitcast.440, bf16[1280,512]{1,0:T(8,128)(2,1)} %bitcast.426, bf16[6,656,256]{2,1,0:T(8,128)(2,1)} %copy-done.78, bf16[6,656,256]{2,1,0:T(8,128)(2,1)} %copy-done.78, ...), custom_call_target="tpu_custom_call" | custom-call | flops 10066329600 | bytes 8388608 | tf_op jit(solution)/shard_map/attend_backward/pallas_call | solution.py:191
  444.1 10.8 %add_convert_fusion.2 = bf16[2048,896]{1,0:T(8,128)(2,1)} fusion(f32[2048,896]{1,0:T(8,128)} %fusion.111, bf16[1024,896]{1,0:T(8,128)(2,1)S(1)} %copy-done.121, bf16[256,2048]{1,0:T(8,128)(2,1)} %collective-permute-done.19, bf16[256,2048]{1,0:T(8,128)(2,1)} %collective-permute-done.18, bf16[256,2048]{1,0:T(8,128)(2,1)} %collective-permute-done.17, ...), kind=kOutput, calls=%fused_computation.4 | convolution fusion | flops 3778543616 | bytes 17039360 | tf_op jit(solution)/shard_map/dot_general | solution.py:33
  459.3 4.8 broadcast_select_fusion
  464.2 9.5 %fusion.110 = f32[2048,896]{1,0:T(8,128)} fusion(bf16[1024,896]{1,0:T(8,128)(2,1)S(1)} %copy-done.115, bf16[256,2048]{1,0:T(8,128)(2,1)S(1)} %copy-done.110, bf16[256,2048]{1,0:T(8,128)(2,1)} %collective-permute-done.30, bf16[256,2048]{1,0:T(8,128)(2,1)} %collective-permute-done.29, bf16[256,2048]{1,0:T(8,128)(2,1)} %multiply_convert_fusion.6), kind=kOutput, calls=%fused_computation.354 | convolution fusion | flops 3774873600 | bytes 13369344 | tf_op jit(solution)/shard_map/dot_general | solution.py:33
  473.8 6.1 fusion.114
  485.2 10.4 %attend_backward.3 = (bf16[1280,256]{1,0:T(8,128)(2,1)}, bf16[6,2,320,256]{3,2,1,0:T(8,128)(2,1)}) custom-call(s32[4]{0:T(128)} %add_add_fusion.1.meta, s32[1,256]{1,0:T(1,128)} %bitcast.438, bf16[1280,512]{1,0:T(8,128)(2,1)} %bitcast.427, bf16[6,656,256]{2,1,0:T(8,128)(2,1)} %copy-done.79, bf16[6,656,256]{2,1,0:T(8,128)(2,1)} %copy-done.79, ...), custom_call_target="tpu_custom_call" | custom-call | flops 10066329600 | bytes 8388608 | tf_op jit(solution)/shard_map/attend_backward/pallas_call | solution.py:191
  501.3 11.1 %add_convert_fusion.1 = bf16[2048,896]{1,0:T(8,128)(2,1)} fusion(f32[2048,896]{1,0:T(8,128)} %fusion.110, bf16[1024,896]{1,0:T(8,128)(2,1)S(1)} %copy-done.119, bf16[256,2048]{1,0:T(8,128)(2,1)} %collective-permute-done.19, bf16[256,2048]{1,0:T(8,128)(2,1)} %collective-permute-done.18, bf16[256,2048]{1,0:T(8,128)(2,1)} %collective-permute-done.17, ...), kind=kOutput, calls=%fused_computation.3 | convolution fusion | flops 3778543616 | bytes 17039360 | tf_op jit(solution)/shard_map/dot_general | solution.py:33
  513.2 2.8 subtract_convert_fusion
  516.0 3.2 convolution_convert_fusion
  526.4 4.7 convolution_convert_fusion.5
  534.1 5.8 add_convert_fusion
  539.9 7.2 convolution_convert_fusion.4
  552.7 3.1 convolution_convert_fusion.1
  555.9 34.2 %collective-permute-done.37 = bf16[2,640,256]{2,1,0:T(8,128)(2,1)S(1)} collective-permute-done((bf16[2,640,256]{2,1,0:T(8,128)(2,1)S(1)}, bf16[2,640,256]{2,1,0:T(8,128)(2,1)S(1)}, u32[]{:S(2)}, u32[]{:S(2)}) %collective-permute-start.37) | collective-permute-done | bytes 655392 | tf_op jit(solution)/shard_map/ppermute | solution.py:253
  591.0 10.5 %collective-permute-start.38 = (bf16[640,256]{1,0:T(8,128)(2,1)}, bf16[640,256]{1,0:T(8,128)(2,1)}, u32[]{:S(2)}, u32[]{:S(2)}) collective-permute-start(bf16[640,256]{1,0:T(8,128)(2,1)} %slice_bitcast_fusion.20), channel_id=1, source_target_pairs={{0,1},{1,0},{2,3},{3,2},{4,5},{5,4},{6,7},{7,6},{8,9},{9,8},{10,11... | collective-permute-start | bytes 983048 | tf_op jit(solution)/shard_map/ppermute | solution.py:248
  613.7 8.9 %collective-permute-start.28 = (bf16[256,2048]{1,0:T(8,128)(2,1)S(1)}, bf16[256,2048]{1,0:T(8,128)(2,1)S(1)}, u32[]{:S(2)}, u32[]{:S(2)}) collective-permute-start(bf16[256,2048]{1,0:T(8,128)(2,1)S(1)} %fusion.50), channel_id=1, source_target_pairs={{0,16},{16,0},{1,17},{17,1},{2,18},{18,2},{3,19},{19,3},{4,20},{20... | collective-permute-start | bytes 3145736 | tf_op jit(solution)/shard_map/ppermute | solution.py:248
  635.6 11.0 %collective-permute-done.28 = bf16[256,2048]{1,0:T(8,128)(2,1)S(1)} collective-permute-done((bf16[256,2048]{1,0:T(8,128)(2,1)S(1)}, bf16[256,2048]{1,0:T(8,128)(2,1)S(1)}, u32[]{:S(2)}, u32[]{:S(2)}) %collective-permute-start.28) | collective-permute-done | bytes 1048608 | tf_op jit(solution)/shard_map/ppermute | solution.py:248
  647.2 11.8 %collective-permute-done.42 = bf16[2,640,256]{2,1,0:T(8,128)(2,1)S(1)} collective-permute-done((bf16[2,640,256]{2,1,0:T(8,128)(2,1)S(1)}, bf16[2,640,256]{2,1,0:T(8,128)(2,1)S(1)}, u32[]{:S(2)}, u32[]{:S(2)}) %collective-permute-start.42) | collective-permute-done | bytes 655392 | tf_op jit(solution)/shard_map/ppermute | solution.py:253
  661.8 7.3 collective-permute-done.33
  671.2 13.0 %collective-permute-done.43 = bf16[640,256]{1,0:T(8,128)(2,1)S(1)} collective-permute-done((bf16[640,256]{1,0:T(8,128)(2,1)S(1)}, bf16[640,256]{1,0:T(8,128)(2,1)S(1)}, u32[]{:S(2)}, u32[]{:S(2)}) %collective-permute-start.43) | collective-permute-done | bytes 327712 | tf_op jit(solution)/shard_map/ppermute | solution.py:248
  693.8 3.1 fusion.7
  701.9 3.1 pad_maximum_fusion.8
  712.0 6.9 collective-permute-start.57
  720.7 6.8 collective-permute-start.58
  730.9 26.1 %collective-permute-done.59 = f32[1,128]{1,0:T(1,128)S(1)} collective-permute-done((f32[1,128]{1,0:T(1,128)S(1)}, f32[1,128]{1,0:T(1,128)S(1)}, u32[]{:S(2)}, u32[]{:S(2)}) %collective-permute-start.59) | collective-permute-done | bytes 544 | tf_op jit(solution)/shard_map/ppermute | solution.py:284
  760.1 5.5 collective-permute-start.63
  768.7 2.8 collective-permute-done.62
  771.5 13.6 %collective-permute-start.48 = (bf16[64,1280]{1,0:T(8,128)(2,1)S(1)}, bf16[64,1280]{1,0:T(8,128)(2,1)S(1)}, u32[]{:S(2)}, u32[]{:S(2)}) collective-permute-start(bf16[64,1280]{1,0:T(8,128)(2,1)S(1)} %get-tuple-element.151), channel_id=1, source_target_pairs={{0,4},{2,6},{4,0},{6,2},{1,5},{3,7},{5,1},{7,3},{8,12},{10,14},{12... | collective-permute-start | bytes 491528 | tf_op jit(solution)/shard_map/ppermute | solution.py:248
  785.1 16.3 %collective-permute-start.49 = (bf16[64,1280]{1,0:T(8,128)(2,1)S(1)}, bf16[64,1280]{1,0:T(8,128)(2,1)S(1)}, u32[]{:S(2)}, u32[]{:S(2)}) collective-permute-start(bf16[64,1280]{1,0:T(8,128)(2,1)S(1)} %get-tuple-element.150), channel_id=1, source_target_pairs={{0,6},{2,0},{4,2},{6,4},{1,7},{3,1},{5,3},{7,5},{8,14},{10,8},{12,... | collective-permute-start | bytes 491528 | tf_op jit(solution)/shard_map/ppermute | solution.py:248
  806.6 3.5 collective-permute-start.52
  824.3 3.1 broadcast_multiply_fusion
  (579 shorter events, 201.4 us)
Async XLA Ops:
  7.2 241.5 %all-gather.4.cloned.1.call-start = ((), (), s32[]{:S(2)}) async-start(), calls=%async_computation.3 | async-start | bytes 5406720 | tf_op jit(solution)/shard_map/all_gather | solution.py:457
  7.9 281.8 %all-gather.6.cloned.1.call-start = ((), (), s32[]{:S(2)}) async-start(), calls=%async_computation.4 | async-start | bytes 8257536 | tf_op jit(solution)/shard_map/all_gather | solution.py:393
  9.5 13.3 %collective-permute-start = (bf16[64,640]{1,0:T(8,128)(2,1)S(1)}, bf16[64,640]{1,0:T(8,128)(2,1)S(1)}, u32[]{:S(2)}, u32[]{:S(2)}) collective-permute-start(bf16[64,640]{1,0:T(8,128)(2,1)S(1)} %fusion.87), channel_id=1, source_target_pairs={{0,2},{2,4},{4,6},{6,0},{1,3},{3,5},{5,7},{7,1},{8,10},{10,12},{12... | collective-permute-start | bytes 245768 | tf_op jit(solution)/shard_map/ppermute | solution.py:248
  12.6 10.2 %collective-permute-start.1 = (bf16[64,640]{1,0:T(8,128)(2,1)S(1)}, bf16[64,640]{1,0:T(8,128)(2,1)S(1)}, u32[]{:S(2)}, u32[]{:S(2)}) collective-permute-start(bf16[64,640]{1,0:T(8,128)(2,1)S(1)} %fusion.87), channel_id=1, source_target_pairs={{0,4},{2,6},{4,0},{6,2},{1,5},{3,7},{5,1},{7,3},{8,12},{10,14},{12... | collective-permute-start | bytes 245768 | tf_op jit(solution)/shard_map/ppermute | solution.py:248
  23.0 9.9 %collective-permute-start.3 = (bf16[4,64,640]{2,1,0:T(8,128)(2,1)S(1)}, bf16[4,64,640]{2,1,0:T(8,128)(2,1)S(1)}, u32[]{:S(2)}, u32[]{:S(2)}) collective-permute-start(bf16[4,64,640]{2,1,0:T(8,128)(2,1)S(1)} %select_select_fusion.1), channel_id=1, source_target_pairs={{0,1},{1,0},{2,3},{3,2},{4,5},{5,4},{6,7},{7,6},{8,9},{9,8},{10,11... | collective-permute-start | bytes 983048 | tf_op jit(solution)/shard_map/ppermute | solution.py:248
  24.6 8.4 %collective-permute-start.20 = (bf16[64,2,1792]{2,0,1:T(8,128)(2,1)S(1)}, bf16[64,2,1792]{2,0,1:T(8,128)(2,1)S(1)}, u32[]{:S(2)}, u32[]{:S(2)}) collective-permute-start(bf16[64,2,1792]{2,0,1:T(8,128)(2,1)S(1)} %get-tuple-element.128), channel_id=1, source_target_pairs={{0,8},{8,0},{1,9},{9,1},{2,10},{10,2},{3,11},{11,3},{4,12},{12,4},... | collective-permute-start | bytes 1376264 | tf_op jit(solution)/shard_map/ppermute | solution.py:248
  33.3 14.1 %collective-permute-start.21 = (bf16[2,64,1792]{2,1,0:T(8,128)(2,1)S(1)}, bf16[2,64,1792]{2,1,0:T(8,128)(2,1)S(1)}, u32[]{:S(2)}, u32[]{:S(2)}) collective-permute-start(bf16[2,64,1792]{2,1,0:T(8,128)(2,1)S(1)} %get-tuple-element.126), channel_id=1, source_target_pairs={{0,16},{16,0},{1,17},{17,1},{2,18},{18,2},{3,19},{19,3},{4,20},{20... | collective-permute-start | bytes 1376264 | tf_op jit(solution)/shard_map/ppermute | solution.py:248
  48.6 269.2 %all-gather.8.cloned.1.call-start = ((), (), s32[]{:S(2)}) async-start(), calls=%async_computation.5 | async-start | bytes 4128768 | tf_op jit(solution)/shard_map/all_gather | solution.py:394
  48.8 8.0 collective-permute-start.11
  48.8 17.5 %collective-permute-start.12 = (bf16[64,1280]{1,0:T(8,128)(2,1)S(1)}, bf16[64,1280]{1,0:T(8,128)(2,1)S(1)}, u32[]{:S(2)}, u32[]{:S(2)}) collective-permute-start(bf16[64,1280]{1,0:T(8,128)(2,1)S(1)} %fusion.81), channel_id=1, source_target_pairs={{0,4},{2,6},{4,0},{6,2},{1,5},{3,7},{5,1},{7,3},{8,12},{10,14},{12... | collective-permute-start | bytes 491528 | tf_op jit(solution)/shard_map/ppermute | solution.py:248
  51.5 14.9 %collective-permute-start.13 = (bf16[64,1280]{1,0:T(8,128)(2,1)S(1)}, bf16[64,1280]{1,0:T(8,128)(2,1)}, u32[]{:S(2)}, u32[]{:S(2)}) collective-permute-start(bf16[64,1280]{1,0:T(8,128)(2,1)S(1)} %fusion.81), channel_id=1, source_target_pairs={{0,2},{2,4},{4,6},{6,0},{1,3},{3,5},{5,7},{7,1},{8,10},{10,12},{12... | collective-permute-start | bytes 491528 | tf_op jit(solution)/shard_map/ppermute | solution.py:248
  51.5 750.7 %reduce-scatter.4.cloned.1.call-start = ((), (), s32[]{:S(2)}) async-start(), calls=%async_computation.6 | async-start | bytes 4128768 | tf_op jit(solution)/shard_map/reduce_scatter | solution.py:551
  54.9 19.6 %collective-permute-start.4 = (bf16[4,2,64,640]{3,2,1,0:T(8,128)(2,1)S(1)}, bf16[4,2,64,640]{3,2,1,0:T(8,128)(2,1)S(1)}, u32[]{:S(2)}, u32[]{:S(2)}) collective-permute-start(bf16[4,2,64,640]{3,2,1,0:T(8,128)(2,1)S(1)} %broadcast_select_fusion.9), channel_id=1, source_target_pairs={{0,16},{16,0},{1,17},{17,1},{2,18},{18,2},{3,19},{19,3},{4,20},{20... | collective-permute-start | bytes 1966088 | tf_op jit(solution)/shard_map/ppermute | solution.py:248
  67.5 22.7 %collective-permute-start.14 = (bf16[4,64,1280]{2,1,0:T(8,128)(2,1)S(1)}, bf16[4,64,1280]{2,1,0:T(8,128)(2,1)S(1)}, u32[]{:S(2)}, u32[]{:S(2)}) collective-permute-start(bf16[4,64,1280]{2,1,0:T(8,128)(2,1)S(1)} %select_select_fusion), channel_id=1, source_target_pairs={{0,1},{1,0},{2,3},{3,2},{4,5},{5,4},{6,7},{7,6},{8,9},{9,8},{10,11... | collective-permute-start | bytes 1966088 | tf_op jit(solution)/shard_map/ppermute | solution.py:248
  74.8 17.1 %collective-permute-start.5 = (bf16[2,4,2,64,640]{4,3,2,1,0:T(8,128)(2,1)S(1)}, bf16[2,4,2,64,640]{4,3,2,1,0:T(8,128)(2,1)S(1)}, u32[]{:S(2)}, u32[]{:S(2)}) collective-permute-start(bf16[2,4,2,64,640]{4,3,2,1,0:T(8,128)(2,1)S(1)} %broadcast_select_fusion.6), channel_id=1, source_target_pairs={{0,8},{8,0},{1,9},{9,1},{2,10},{10,2},{3,11},{11,3},{4,12},{12,4},... | collective-permute-start | bytes 3932168 | tf_op jit(solution)/shard_map/ppermute | solution.py:248
  90.4 51.1 %collective-permute-start.15 = (bf16[4,2,64,1280]{3,2,1,0:T(8,128)(2,1)S(1)}, bf16[4,2,64,1280]{3,2,1,0:T(8,128)(2,1)S(1)}, u32[]{:S(2)}, u32[]{:S(2)}) collective-permute-start(bf16[4,2,64,1280]{3,2,1,0:T(8,128)(2,1)S(1)} %broadcast_select_fusion.5), channel_id=1, source_target_pairs={{0,16},{16,0},{1,17},{17,1},{2,18},{18,2},{3,19},{19,3},{4,20},{20... | collective-permute-start | bytes 3932168 | tf_op jit(solution)/shard_map/ppermute | solution.py:248
  97.1 27.2 %collective-permute-start.6 = (bf16[656,512]{1,0:T(8,128)(2,1)S(1)}, bf16[656,512]{1,0:T(8,128)(2,1)S(1)}, u32[]{:S(2)}, u32[]{:S(2)}) collective-permute-start(bf16[656,512]{1,0:T(8,128)(2,1)S(1)} %pad_maximum_fusion.14), channel_id=1, source_target_pairs={{0,2},{2,4},{4,6},{1,3},{3,5},{5,7},{8,10},{10,12},{12,14},{9,11},... | collective-permute-start | bytes 2015240 | tf_op jit(solution)/shard_map/ppermute | solution.py:253
  124.3 34.0 %collective-permute-start.7 = (bf16[656,512]{1,0:T(8,128)(2,1)S(1)}, bf16[656,512]{1,0:T(8,128)(2,1)S(1)}, u32[]{:S(2)}, u32[]{:S(2)}) collective-permute-start(bf16[656,512]{1,0:T(8,128)(2,1)S(1)} %collective-permute-done.6), channel_id=1, source_target_pairs={{0,2},{2,4},{4,6},{1,3},{3,5},{5,7},{8,10},{10,12},{12,14},{9,11},... | collective-permute-start | bytes 2015240 | tf_op jit(solution)/shard_map/ppermute | solution.py:253
  141.8 86.7 %collective-permute-start.16 = (bf16[2,4,2,64,1280]{4,3,2,1,0:T(8,128)(2,1)S(1)}, bf16[2,4,2,64,1280]{4,3,2,1,0:T(8,128)(2,1)}, u32[]{:S(2)}, u32[]{:S(2)}) collective-permute-start(bf16[2,4,2,64,1280]{4,3,2,1,0:T(8,128)(2,1)S(1)} %broadcast_select_fusion.1), channel_id=1, source_target_pairs={{0,8},{8,0},{1,9},{9,1},{2,10},{10,2},{3,11},{11,3},{4,12},{12,4},... | collective-permute-start | bytes 7864328 | tf_op jit(solution)/shard_map/ppermute | solution.py:248
  141.9 73.5 %collective-permute-start.10 = (bf16[656,512]{1,0:T(8,128)(2,1)S(1)}, bf16[656,512]{1,0:T(8,128)(2,1)S(1)}, u32[]{:S(2)}, u32[]{:S(2)}) collective-permute-start(bf16[656,512]{1,0:T(8,128)(2,1)S(1)} %pad_maximum_fusion.14), channel_id=1, source_target_pairs={{0,1},{1,0},{2,3},{3,2},{4,5},{5,4},{6,7},{7,6},{8,9},{9,8},{10,11... | collective-permute-start | bytes 2015240 | tf_op jit(solution)/shard_map/ppermute | solution.py:248
  142.0 103.9 %collective-permute-start.22 = (bf16[512,2048]{1,0:T(8,128)(2,1)}, bf16[512,2048]{1,0:T(8,128)(2,1)}, u32[]{:S(2)}, u32[]{:S(2)}) collective-permute-start(bf16[512,2048]{1,0:T(8,128)(2,1)} %pad_maximum_fusion.6), channel_id=1, source_target_pairs={{0,16},{16,0},{1,17},{17,1},{2,18},{18,2},{3,19},{19,3},{4,20},{20... | collective-permute-start | bytes 6291464 | tf_op jit(solution)/shard_map/ppermute | solution.py:248
  158.3 30.7 %collective-permute-start.8 = (bf16[656,512]{1,0:T(8,128)(2,1)S(1)}, bf16[656,512]{1,0:T(8,128)(2,1)S(1)}, u32[]{:S(2)}, u32[]{:S(2)}) collective-permute-start(bf16[656,512]{1,0:T(8,128)(2,1)S(1)} %collective-permute-done.7), channel_id=1, source_target_pairs={{0,1},{1,0},{2,3},{3,2},{4,5},{5,4},{6,7},{7,6},{8,9},{9,8},{10,11... | collective-permute-start | bytes 2015240 | tf_op jit(solution)/shard_map/ppermute | solution.py:248
  162.0 53.3 %collective-permute-start.9 = (bf16[656,512]{1,0:T(8,128)(2,1)S(1)}, bf16[656,512]{1,0:T(8,128)(2,1)S(1)}, u32[]{:S(2)}, u32[]{:S(2)}) collective-permute-start(bf16[656,512]{1,0:T(8,128)(2,1)S(1)} %collective-permute-done.6), channel_id=1, source_target_pairs={{0,1},{1,0},{2,3},{3,2},{4,5},{5,4},{6,7},{7,6},{8,9},{9,8},{10,11... | collective-permute-start | bytes 2015240 | tf_op jit(solution)/shard_map/ppermute | solution.py:248
  189.0 66.4 %collective-permute-start.23 = (bf16[512,2048]{1,0:T(8,128)(2,1)}, bf16[512,2048]{1,0:T(8,128)(2,1)}, u32[]{:S(2)}, u32[]{:S(2)}) collective-permute-start(bf16[512,2048]{1,0:T(8,128)(2,1)} %pad_maximum_fusion.6), channel_id=1, source_target_pairs={{0,8},{8,0},{1,9},{9,1},{2,10},{10,2},{3,11},{11,3},{4,12},{12,4},... | collective-permute-start | bytes 6291464 | tf_op jit(solution)/shard_map/ppermute | solution.py:248
  245.9 12.7 %collective-permute-start.24 = (bf16[512,2048]{1,0:T(8,128)(2,1)}, bf16[512,2048]{1,0:T(8,128)(2,1)}, u32[]{:S(2)}, u32[]{:S(2)}) collective-permute-start(bf16[512,2048]{1,0:T(8,128)(2,1)} %collective-permute-done.22), channel_id=1, source_target_pairs={{0,8},{8,0},{1,9},{9,1},{2,10},{10,2},{3,11},{11,3},{4,12},{12,4},... | collective-permute-start | bytes 6291464 | tf_op jit(solution)/shard_map/ppermute | solution.py:248
  255.4 25.9 %collective-permute-start.17 = (bf16[256,2048]{1,0:T(8,128)(2,1)}, bf16[256,2048]{1,0:T(8,128)(2,1)}, u32[]{:S(2)}, u32[]{:S(2)}) collective-permute-start(bf16[256,2048]{1,0:T(8,128)(2,1)} %multiply_convert_fusion.7), channel_id=1, source_target_pairs={{0,16},{16,0},{1,17},{17,1},{2,18},{18,2},{3,19},{19,3},{4,20},{20... | collective-permute-start | bytes 3145736 | tf_op jit(solution)/shard_map/ppermute | solution.py:248
  261.8 27.9 %collective-permute-start.18 = (bf16[256,2048]{1,0:T(8,128)(2,1)}, bf16[256,2048]{1,0:T(8,128)(2,1)}, u32[]{:S(2)}, u32[]{:S(2)}) collective-permute-start(bf16[256,2048]{1,0:T(8,128)(2,1)} %multiply_convert_fusion.7), channel_id=1, source_target_pairs={{0,8},{8,0},{1,9},{9,1},{2,10},{10,2},{3,11},{11,3},{4,12},{12,4},... | collective-permute-start | bytes 3145736 | tf_op jit(solution)/shard_map/ppermute | solution.py:248
  281.2 8.5 %collective-permute-start.19 = (bf16[256,2048]{1,0:T(8,128)(2,1)}, bf16[256,2048]{1,0:T(8,128)(2,1)}, u32[]{:S(2)}, u32[]{:S(2)}) collective-permute-start(bf16[256,2048]{1,0:T(8,128)(2,1)} %collective-permute-done.17), channel_id=1, source_target_pairs={{0,8},{8,0},{1,9},{9,1},{2,10},{10,2},{3,11},{11,3},{4,12},{12,4},... | collective-permute-start | bytes 3145736 | tf_op jit(solution)/shard_map/ppermute | solution.py:248
  289.2 48.4 %collective-permute-start.29 = (bf16[256,2048]{1,0:T(8,128)(2,1)}, bf16[256,2048]{1,0:T(8,128)(2,1)}, u32[]{:S(2)}, u32[]{:S(2)}) collective-permute-start(bf16[256,2048]{1,0:T(8,128)(2,1)} %multiply_convert_fusion.6), channel_id=1, source_target_pairs={{0,16},{16,0},{1,17},{17,1},{2,18},{18,2},{3,19},{19,3},{4,20},{20... | collective-permute-start | bytes 3145736 | tf_op jit(solution)/shard_map/ppermute | solution.py:248
  289.2 50.8 %collective-permute-start.30 = (bf16[256,2048]{1,0:T(8,128)(2,1)}, bf16[256,2048]{1,0:T(8,128)(2,1)}, u32[]{:S(2)}, u32[]{:S(2)}) collective-permute-start(bf16[256,2048]{1,0:T(8,128)(2,1)} %multiply_convert_fusion.6), channel_id=1, source_target_pairs={{0,8},{8,0},{1,9},{9,1},{2,10},{10,2},{3,11},{11,3},{4,12},{12,4},... | collective-permute-start | bytes 3145736 | tf_op jit(solution)/shard_map/ppermute | solution.py:248
  338.3 15.7 %collective-permute-start.25 = (bf16[2,256,2048]{2,1,0:T(8,128)(2,1)S(1)}, bf16[2,256,2048]{2,1,0:T(8,128)(2,1)S(1)}, u32[]{:S(2)}, u32[]{:S(2)}) collective-permute-start(bf16[2,256,2048]{2,1,0:T(8,128)(2,1)S(1)} %bitcast.423), channel_id=1, source_target_pairs={{0,8},{8,0},{1,9},{9,1},{2,10},{10,2},{3,11},{11,3},{4,12},{12,4},... | collective-permute-start | bytes 6291464 | tf_op jit(solution)/shard_map/ppermute | solution.py:248
  377.6 26.0 %collective-permute-start.26 = (bf16[256,2048]{1,0:T(8,128)(2,1)S(1)}, bf16[256,2048]{1,0:T(8,128)(2,1)S(1)}, u32[]{:S(2)}, u32[]{:S(2)}) collective-permute-start(bf16[256,2048]{1,0:T(8,128)(2,1)S(1)} %fusion.48), channel_id=1, source_target_pairs={{0,16},{16,0},{1,17},{17,1},{2,18},{18,2},{3,19},{19,3},{4,20},{20... | collective-permute-start | bytes 3145736 | tf_op jit(solution)/shard_map/ppermute | solution.py:248
  384.6 40.9 %collective-permute-start.35 = (bf16[256,2048]{1,0:T(8,128)(2,1)S(1)}, bf16[256,2048]{1,0:T(8,128)(2,1)S(1)}, u32[]{:S(2)}, u32[]{:S(2)}) collective-permute-start(bf16[256,2048]{1,0:T(8,128)(2,1)S(1)} %fusion.53), channel_id=1, source_target_pairs={{0,16},{16,0},{1,17},{17,1},{2,18},{18,2},{3,19},{19,3},{4,20},{20... | collective-permute-start | bytes 3145736 | tf_op jit(solution)/shard_map/ppermute | solution.py:248
  455.0 347.2 %reduce-scatter.6.cloned.1.call-start = ((), (), s32[]{:S(2)}) async-start(), calls=%async_computation.7 | async-start | bytes 4128768 | tf_op jit(solution)/shard_map/reduce_scatter | solution.py:551
  481.2 65.8 %collective-permute-start.36 = (bf16[2,640,256]{2,1,0:T(8,128)(2,1)}, bf16[2,640,256]{2,1,0:T(8,128)(2,1)}, u32[]{:S(2)}, u32[]{:S(2)}) collective-permute-start(bf16[2,640,256]{2,1,0:T(8,128)(2,1)} %bitcast.72), channel_id=1, source_target_pairs={{2,0},{4,2},{6,4},{3,1},{5,3},{7,5},{10,8},{12,10},{14,12},{11,9},... | collective-permute-start | bytes 1966088 | tf_op jit(solution)/shard_map/ppermute | solution.py:253
  512.4 306.6 %reduce-scatter.8.cloned.1.call-start = ((), (), s32[]{:S(2)}) async-start(), calls=%async_computation.8 | async-start | bytes 4128768 | tf_op jit(solution)/shard_map/reduce_scatter | solution.py:618
  522.8 103.9 %collective-permute-start.41 = (bf16[2,4,2,64,1280]{4,3,1,0,2:T(8,128)(2,1)}, bf16[2,4,2,64,1280]{4,3,1,0,2:T(8,128)(2,1)}, u32[]{:S(2)}, u32[]{:S(2)}) collective-permute-start(bf16[2,4,2,64,1280]{4,3,1,0,2:T(8,128)(2,1)} %bitcast.390), channel_id=1, source_target_pairs={{0,8},{8,0},{1,9},{9,1},{2,10},{10,2},{3,11},{11,3},{4,12},{12,4},... | collective-permute-start | bytes 7864328 | tf_op jit(solution)/shard_map/ppermute | solution.py:248
  524.8 80.8 %collective-permute-start.39 = (bf16[2,640,256]{2,1,0:T(8,128)(2,1)}, bf16[2,640,256]{2,1,0:T(8,128)(2,1)}, u32[]{:S(2)}, u32[]{:S(2)}) collective-permute-start(bf16[2,640,256]{2,1,0:T(8,128)(2,1)} %bitcast.77), channel_id=1, source_target_pairs={{2,0},{4,2},{6,4},{3,1},{5,3},{7,5},{10,8},{12,10},{14,12},{11,9},... | collective-permute-start | bytes 1966088 | tf_op jit(solution)/shard_map/ppermute | solution.py:253
  533.0 78.2 %collective-permute-start.27 = (bf16[2,256,2048]{2,1,0:T(8,128)(2,1)}, bf16[2,256,2048]{2,1,0:T(8,128)(2,1)}, u32[]{:S(2)}, u32[]{:S(2)}) collective-permute-start(bf16[2,256,2048]{2,1,0:T(8,128)(2,1)} %bitcast.41), channel_id=1, source_target_pairs={{0,8},{8,0},{1,9},{9,1},{2,10},{10,2},{3,11},{11,3},{4,12},{12,4},... | collective-permute-start | bytes 6291464 | tf_op jit(solution)/shard_map/ppermute | solution.py:248
  548.4 41.6 %collective-permute-start.37 = (bf16[2,640,256]{2,1,0:T(8,128)(2,1)S(1)}, bf16[2,640,256]{2,1,0:T(8,128)(2,1)S(1)}, u32[]{:S(2)}, u32[]{:S(2)}) collective-permute-start(bf16[2,640,256]{2,1,0:T(8,128)(2,1)S(1)} %fusion.47), channel_id=1, source_target_pairs={{2,0},{4,2},{6,4},{3,1},{5,3},{7,5},{10,8},{12,10},{14,12},{11,9},... | collective-permute-start | bytes 1966088 | tf_op jit(solution)/shard_map/ppermute | solution.py:253
  552.7 70.0 %collective-permute-start.32 = (bf16[2,256,2048]{2,1,0:T(8,128)(2,1)}, bf16[2,256,2048]{2,1,0:T(8,128)(2,1)}, u32[]{:S(2)}, u32[]{:S(2)}) collective-permute-start(bf16[2,256,2048]{2,1,0:T(8,128)(2,1)} %bitcast.57), channel_id=1, source_target_pairs={{0,8},{8,0},{1,9},{9,1},{2,10},{10,2},{3,11},{11,3},{4,12},{12,4},... | collective-permute-start | bytes 6291464 | tf_op jit(solution)/shard_map/ppermute | solution.py:248
  591.0 19.1 %collective-permute-start.38 = (bf16[640,256]{1,0:T(8,128)(2,1)}, bf16[640,256]{1,0:T(8,128)(2,1)}, u32[]{:S(2)}, u32[]{:S(2)}) collective-permute-start(bf16[640,256]{1,0:T(8,128)(2,1)} %slice_bitcast_fusion.20), channel_id=1, source_target_pairs={{0,1},{1,0},{2,3},{3,2},{4,5},{5,4},{6,7},{7,6},{8,9},{9,8},{10,11... | collective-permute-start | bytes 983048 | tf_op jit(solution)/shard_map/ppermute | solution.py:248
  605.6 23.9 %collective-permute-start.40 = (bf16[2,4,2,40,2048]{4,3,1,2,0:T(8,128)(2,1)}, bf16[2,4,2,40,2048]{4,3,1,2,0:T(8,128)(2,1)S(1)}, u32[]{:S(2)}, u32[]{:S(2)}) collective-permute-start(bf16[2,4,2,40,2048]{4,3,1,2,0:T(8,128)(2,1)} %bitcast.416), channel_id=1, source_target_pairs={{0,8},{8,0},{1,9},{9,1},{2,10},{10,2},{3,11},{11,3},{4,12},{12,4},... | collective-permute-start | bytes 7864328 | tf_op jit(solution)/shard_map/ppermute | solution.py:248
  613.7 32.9 %collective-permute-start.28 = (bf16[256,2048]{1,0:T(8,128)(2,1)S(1)}, bf16[256,2048]{1,0:T(8,128)(2,1)S(1)}, u32[]{:S(2)}, u32[]{:S(2)}) collective-permute-start(bf16[256,2048]{1,0:T(8,128)(2,1)S(1)} %fusion.50), channel_id=1, source_target_pairs={{0,16},{16,0},{1,17},{17,1},{2,18},{18,2},{3,19},{19,3},{4,20},{20... | collective-permute-start | bytes 3145736 | tf_op jit(solution)/shard_map/ppermute | solution.py:248
  625.3 43.8 %collective-permute-start.33 = (bf16[256,2048]{1,0:T(8,128)(2,1)S(1)}, bf16[256,2048]{1,0:T(8,128)(2,1)S(1)}, u32[]{:S(2)}, u32[]{:S(2)}) collective-permute-start(bf16[256,2048]{1,0:T(8,128)(2,1)S(1)} %fusion.52), channel_id=1, source_target_pairs={{0,16},{16,0},{1,17},{17,1},{2,18},{18,2},{3,19},{19,3},{4,20},{20... | collective-permute-start | bytes 3145736 | tf_op jit(solution)/shard_map/ppermute | solution.py:248
  630.7 28.2 %collective-permute-start.42 = (bf16[2,640,256]{2,1,0:T(8,128)(2,1)S(1)}, bf16[2,640,256]{2,1,0:T(8,128)(2,1)S(1)}, u32[]{:S(2)}, u32[]{:S(2)}) collective-permute-start(bf16[2,640,256]{2,1,0:T(8,128)(2,1)S(1)} %fusion.45), channel_id=1, source_target_pairs={{2,0},{4,2},{6,4},{3,1},{5,3},{7,5},{10,8},{12,10},{14,12},{11,9},... | collective-permute-start | bytes 1966088 | tf_op jit(solution)/shard_map/ppermute | solution.py:253
  633.7 74.5 %collective-permute-start.60 = (bf16[4,2,40,2048]{3,2,0,1:T(8,128)(2,1)}, bf16[4,2,40,2048]{3,2,0,1:T(8,128)(2,1)}, u32[]{:S(2)}, u32[]{:S(2)}) collective-permute-start(bf16[4,2,40,2048]{3,2,0,1:T(8,128)(2,1)} %dynamic-slice_bitcast_fusion), channel_id=1, source_target_pairs={{0,16},{16,0},{1,17},{17,1},{2,18},{18,2},{3,19},{19,3},{4,20},{20... | collective-permute-start | bytes 3932168 | tf_op jit(solution)/shard_map/ppermute | solution.py:248
  635.6 83.2 %collective-permute-start.44 = (bf16[2,4,64,1280]{3,2,1,0:T(8,128)(2,1)}, bf16[2,4,64,1280]{3,2,1,0:T(8,128)(2,1)}, u32[]{:S(2)}, u32[]{:S(2)}) collective-permute-start(bf16[2,4,64,1280]{3,2,1,0:T(8,128)(2,1)} %dynamic-slice_bitcast_fusion.1), channel_id=1, source_target_pairs={{0,1},{1,0},{2,3},{3,2},{4,5},{5,4},{6,7},{7,6},{8,9},{9,8},{10,11... | collective-permute-start | bytes 3932168 | tf_op jit(solution)/shard_map/ppermute | solution.py:248
  659.2 24.9 %collective-permute-start.43 = (bf16[640,256]{1,0:T(8,128)(2,1)S(1)}, bf16[640,256]{1,0:T(8,128)(2,1)S(1)}, u32[]{:S(2)}, u32[]{:S(2)}) collective-permute-start(bf16[640,256]{1,0:T(8,128)(2,1)S(1)} %slice_bitcast_fusion.18), channel_id=1, source_target_pairs={{0,1},{1,0},{2,3},{3,2},{4,5},{5,4},{6,7},{7,6},{8,9},{9,8},{10,11... | collective-permute-start | bytes 983048 | tf_op jit(solution)/shard_map/ppermute | solution.py:248
  691.0 14.0 %collective-permute-start.45 = (bf16[2,4,2,64,640]{4,3,1,0,2:T(8,128)(2,1)}, bf16[2,4,2,64,640]{4,3,1,0,2:T(8,128)(2,1)}, u32[]{:S(2)}, u32[]{:S(2)}) collective-permute-start(bf16[2,4,2,64,640]{4,3,1,0,2:T(8,128)(2,1)} %bitcast.392), channel_id=1, source_target_pairs={{0,8},{8,0},{1,9},{9,1},{2,10},{10,2},{3,11},{11,3},{4,12},{12,4},... | collective-permute-start | bytes 3932168 | tf_op jit(solution)/shard_map/ppermute | solution.py:248
  710.9 46.7 %collective-permute-start.61 = (bf16[4,40,2048]{2,1,0:T(8,128)(2,1)S(1)}, bf16[4,40,2048]{2,1,0:T(8,128)(2,1)S(1)}, u32[]{:S(2)}, u32[]{:S(2)}) collective-permute-start(bf16[4,40,2048]{2,1,0:T(8,128)(2,1)S(1)} %dynamic-slice_bitcast_fusion.2), channel_id=1, source_target_pairs={{0,1},{1,0},{2,3},{3,2},{4,5},{5,4},{6,7},{7,6},{8,9},{9,8},{10,11... | collective-permute-start | bytes 1966088 | tf_op jit(solution)/shard_map/ppermute | solution.py:248
  712.0 8.7 %collective-permute-start.57 = (f32[1,128]{1,0:T(1,128)S(1)}, f32[1,128]{1,0:T(1,128)S(1)}, u32[]{:S(2)}, u32[]{:S(2)}) collective-permute-start(f32[1,128]{1,0:T(1,128)S(1)} %add.628), channel_id=1, source_target_pairs={{0,2},{2,0},{4,6},{6,4},{1,3},{3,1},{5,7},{7,5},{8,10},{10,8},{12,... | collective-permute-start | bytes 1544 | tf_op jit(solution)/shard_map/ppermute | solution.py:284
  720.7 8.3 collective-permute-start.58
  727.5 39.4 %collective-permute-start.50 = (bf16[2,4,64,640]{3,2,1,0:T(8,128)(2,1)S(1)}, bf16[2,4,64,640]{3,2,1,0:T(8,128)(2,1)S(1)}, u32[]{:S(2)}, u32[]{:S(2)}) collective-permute-start(bf16[2,4,64,640]{3,2,1,0:T(8,128)(2,1)S(1)} %dynamic-slice_bitcast_fusion.3), channel_id=1, source_target_pairs={{0,1},{1,0},{2,3},{3,2},{4,5},{5,4},{6,7},{7,6},{8,9},{9,8},{10,11... | collective-permute-start | bytes 1966088 | tf_op jit(solution)/shard_map/ppermute | solution.py:248
  729.0 28.0 %collective-permute-start.59 = (f32[1,128]{1,0:T(1,128)S(1)}, f32[1,128]{1,0:T(1,128)S(1)}, u32[]{:S(2)}, u32[]{:S(2)}) collective-permute-start(f32[1,128]{1,0:T(1,128)S(1)} %add.630), channel_id=1, source_target_pairs={{0,1},{1,0},{2,3},{3,2},{4,5},{5,4},{6,7},{7,6},{8,9},{9,8},{10,11... | collective-permute-start | bytes 1544 | tf_op jit(solution)/shard_map/ppermute | solution.py:284
  730.2 37.4 %collective-permute-start.46 = (bf16[4,64,1280]{2,1,0:T(8,128)(2,1)S(1)}, bf16[4,64,1280]{2,1,0:T(8,128)(2,1)S(1)}, u32[]{:S(2)}, u32[]{:S(2)}) collective-permute-start(bf16[4,64,1280]{2,1,0:T(8,128)(2,1)S(1)} %dynamic-slice_bitcast_fusion.4), channel_id=1, source_target_pairs={{0,16},{16,0},{1,17},{17,1},{2,18},{18,2},{3,19},{19,3},{4,20},{20... | collective-permute-start | bytes 1966088 | tf_op jit(solution)/shard_map/ppermute | solution.py:248
  757.8 13.7 %collective-permute-start.62 = (bf16[40,2048]{1,0:T(8,128)(2,1)S(1)}, bf16[40,2048]{1,0:T(8,128)(2,1)S(1)}, u32[]{:S(2)}, u32[]{:S(2)}) collective-permute-start(bf16[40,2048]{1,0:T(8,128)(2,1)S(1)} %get-tuple-element.146), channel_id=1, source_target_pairs={{0,2},{2,4},{4,6},{6,0},{1,3},{3,5},{5,7},{7,1},{8,10},{10,12},{12... | collective-permute-start | bytes 491528 | tf_op jit(solution)/shard_map/ppermute | solution.py:248
  760.1 25.0 %collective-permute-start.63 = (bf16[40,2048]{1,0:T(8,128)(2,1)S(1)}, bf16[40,2048]{1,0:T(8,128)(2,1)S(1)}, u32[]{:S(2)}, u32[]{:S(2)}) collective-permute-start(bf16[40,2048]{1,0:T(8,128)(2,1)S(1)} %get-tuple-element.148), channel_id=1, source_target_pairs={{0,4},{2,6},{4,0},{6,2},{1,5},{3,7},{5,1},{7,3},{8,12},{10,14},{12... | collective-permute-start | bytes 491528 | tf_op jit(solution)/shard_map/ppermute | solution.py:248
  765.7 35.7 %collective-permute-start.64 = (bf16[40,2048]{1,0:T(8,128)(2,1)S(1)}, bf16[40,2048]{1,0:T(8,128)(2,1)S(1)}, u32[]{:S(2)}, u32[]{:S(2)}) collective-permute-start(bf16[40,2048]{1,0:T(8,128)(2,1)S(1)} %get-tuple-element.147), channel_id=1, source_target_pairs={{0,6},{2,0},{4,2},{6,4},{1,7},{3,1},{5,3},{7,5},{8,14},{10,8},{12,... | collective-permute-start | bytes 491528 | tf_op jit(solution)/shard_map/ppermute | solution.py:248
  767.1 39.3 %collective-permute-start.51 = (bf16[4,64,640]{2,1,0:T(8,128)(2,1)S(1)}, bf16[4,64,640]{2,1,0:T(8,128)(2,1)S(1)}, u32[]{:S(2)}, u32[]{:S(2)}) collective-permute-start(bf16[4,64,640]{2,1,0:T(8,128)(2,1)S(1)} %dynamic-slice_bitcast_fusion.13), channel_id=1, source_target_pairs={{0,16},{16,0},{1,17},{17,1},{2,18},{18,2},{3,19},{19,3},{4,20},{20... | collective-permute-start | bytes 983048 | tf_op jit(solution)/shard_map/ppermute | solution.py:248
  767.9 35.9 %collective-permute-start.47 = (bf16[64,1280]{1,0:T(8,128)(2,1)S(1)}, bf16[64,1280]{1,0:T(8,128)(2,1)S(1)}, u32[]{:S(2)}, u32[]{:S(2)}) collective-permute-start(bf16[64,1280]{1,0:T(8,128)(2,1)S(1)} %get-tuple-element.149), channel_id=1, source_target_pairs={{0,2},{2,4},{4,6},{6,0},{1,3},{3,5},{5,7},{7,1},{8,10},{10,12},{12... | collective-permute-start | bytes 491528 | tf_op jit(solution)/shard_map/ppermute | solution.py:248
  771.5 33.4 %collective-permute-start.48 = (bf16[64,1280]{1,0:T(8,128)(2,1)S(1)}, bf16[64,1280]{1,0:T(8,128)(2,1)S(1)}, u32[]{:S(2)}, u32[]{:S(2)}) collective-permute-start(bf16[64,1280]{1,0:T(8,128)(2,1)S(1)} %get-tuple-element.151), channel_id=1, source_target_pairs={{0,4},{2,6},{4,0},{6,2},{1,5},{3,7},{5,1},{7,3},{8,12},{10,14},{12... | collective-permute-start | bytes 491528 | tf_op jit(solution)/shard_map/ppermute | solution.py:248
  785.1 20.4 %collective-permute-start.49 = (bf16[64,1280]{1,0:T(8,128)(2,1)S(1)}, bf16[64,1280]{1,0:T(8,128)(2,1)S(1)}, u32[]{:S(2)}, u32[]{:S(2)}) collective-permute-start(bf16[64,1280]{1,0:T(8,128)(2,1)S(1)} %get-tuple-element.150), channel_id=1, source_target_pairs={{0,6},{2,0},{4,2},{6,4},{1,7},{3,1},{5,3},{7,5},{8,14},{10,8},{12,... | collective-permute-start | bytes 491528 | tf_op jit(solution)/shard_map/ppermute | solution.py:248
  803.5 9.0 %collective-permute-start.65 = (bf16[2,64,1792]{2,1,0:T(8,128)(2,1)S(1)}, bf16[2,64,1792]{2,1,0:T(8,128)(2,1)S(1)}, u32[]{:S(2)}, u32[]{:S(2)}) collective-permute-start(bf16[2,64,1792]{2,1,0:T(8,128)(2,1)S(1)} %get-tuple-element.124), channel_id=1, source_target_pairs={{0,16},{16,0},{1,17},{17,1},{2,18},{18,2},{3,19},{19,3},{4,20},{20... | collective-permute-start | bytes 1376264 | tf_op jit(solution)/shard_map/ppermute | solution.py:248
  (139 other events, 2252.3 us)
Sparse Core Ops, SparseCore 0:
  10.8 82.4 all-gather.3
  96.1 156.5 all-gather.5
  254.8 62.8 all-gather.7
  455.1 122.1 reduce-scatter.3
  580.8 108.5 reduce-scatter.5
  692.9 109.9 reduce-scatter.7

commit v4 on v2

--- a/solution.py
+++ b/solution.py
@@ -372,15 +372,14 @@
     kv_near = move.direct((w_kv.astype(f32) * gain_a).astype(bf16), "z")
     w_q_low = (w_query.astype(f32) * gain_a).astype(bf16)
     q_near = move.direct(w_q_low, "z")
-    w_kv_all = move.spread(kv_near, "xyc").reshape(width, 2 * KV_WIDTH)
-    w_q_all = move.spread(q_near, "xyc").reshape(width, Q_WIDTH)
-    w_out_all = lax.all_gather(w_out, tuple(LAYOUT), axis=0, tiled=True)
+    kv_x = move.gather(move.place(kv_near, "z", 0), "x", 1)
+    w_kv_all = move.gather(move.gather(kv_x, "y", 0), "c", 1).reshape(width, 2 * KV_WIDTH)
 
     w_gate_low = (w_gate.astype(f32) * gain_f).astype(bf16).reshape(d_rows, ys, cs, 1, ffn_part)
     w_up_low = (w_up.astype(f32) * gain_f).astype(bf16).reshape(d_rows, ys, cs, 1, ffn_part)
     both = jnp.concatenate([w_gate_low, w_up_low], axis=3).reshape(d_rows, ys, cs, 2 * ffn_part)
-    both = move.exchange(both, "c", 2, 0)
-    both = move.exchange(both, "y", 2, 0)
+    both = move.exchange(after(both, kv_near[0]), "c", 2, 0)
+    both = move.exchange(after(both, kv_x), "y", 2, 0)
     both = lax.all_gather(both, CTX, axis=0)
     w_down_all = lax.all_gather(w_down, CTX, axis=0, tiled=True)
     w_both = both.transpose(1, 2, 0, 3, 4).reshape(width, 2 * ffn_part)
@@ -403,15 +402,11 @@
         for b in range(batches)
     ]
 
-    def seq_blocks(rows):
-        chips = move.ring(rows, "y")
+    def core_blocks(chips):
         blocks = list(chips)
         for k in range(1, cs):
             blocks += [move.shift(chip, "c", k) for chip in chips]
         return blocks
-
-    def seq_gather(rows):
-        return jnp.concatenate(seq_blocks(rows), axis=0)
 
     def core_sum(partial):
         blocks = partial.reshape(cs, ys, local, width)
@@ -425,11 +420,6 @@
         for k in range(1, ys):
             result = result + move.shift(rows[k], "y", -k).astype(f32)
         return result
-
-    grad_blocks = seq_blocks(
-        after(jnp.concatenate(grads_out, axis=0).astype(bf16), w_q_all)
-    )
-    grads_all = [jnp.concatenate([g[part] for g in grad_blocks], axis=0) for part in parts]
 
     inputs = after(tokens, *kv_near[1:]).reshape(both_rows, width).astype(f32)
     scale_in = row_scale(inputs)
@@ -448,6 +438,19 @@
     hops = [kv]
     for _ in range(back_groups):
         hops.append(move.hop(hops[-1], "z", 1))
+    w_q_all = move.spread(q_near, "xyc").reshape(width, Q_WIDTH)
+    w_out_all = lax.all_gather(w_out, tuple(LAYOUT), axis=0, tiled=True)
+    half = Q_WIDTH // 2
+    query_lin = jnp.concatenate(
+        [dot(w_q_all[:, :half], normed, 0, 1), dot(w_q_all[:, half:], normed, 0, 1)], axis=0
+    ).reshape(HEADS, HEAD_DIM, both_rows)
+    query_rot, query_scale = head_forward(query_lin, gain_q, cosine, sine)
+    query_t = query_rot.astype(bf16).reshape(Q_WIDTH, both_rows)
+
+    grad_chips = move.ring(
+        after(jnp.concatenate(grads_out, axis=0).astype(bf16), hops[1]), "y"
+    )
+
     blocks = []
     for group in hops[::-1]:
         blocks += move.direct(group, "x")
@@ -459,39 +462,47 @@
         below = docs.reshape(1, -1) < doc_ids[b][:, None]
         starts.append(jnp.sum(below.astype(jnp.int32), axis=1))
 
-    half = Q_WIDTH // 2
-    query_lin = jnp.concatenate(
-        [dot(w_q_all[:, :half], normed, 0, 1), dot(w_q_all[:, half:], normed, 0, 1)], axis=0
-    ).reshape(HEADS, HEAD_DIM, both_rows)
-    query_rot, query_scale = head_forward(query_lin, gain_q, cosine, sine)
-    query_t = query_rot.astype(bf16).reshape(Q_WIDTH, both_rows)
-
     metas, mixed, lses, resids, scale_mids, normed2_all = [], [], [], [], [], []
+    rows, normed2_chips = None, []
     for b, part in enumerate(parts):
         meta = jnp.stack([starts[b][0] // local, high, q_start, at_x]).astype(jnp.int32)
+        if rows is not None:
+            meta = after(meta, rows)
         mixed_t, lse = attend_forward(xs, meta, starts[b][:, None], query_t, b, windows[b])
         resid = inputs[part] + dot(mixed_t, w_out_all, 0, 0)
         scale_mid = row_scale(resid)
-        normed2_all.append(seq_gather((resid * scale_mid).astype(bf16)))
+        rows = (resid * scale_mid).astype(bf16)
+        normed2_chips.append(move.ring(rows, "y"))
         metas.append(meta)
         mixed.append(mixed_t)
         lses.append(lse)
         resids.append(resid)
         scale_mids.append(scale_mid)
 
+    grad_blocks = core_blocks(grad_chips)
+    grads_all = [jnp.concatenate([g[part] for g in grad_blocks], axis=0) for part in parts]
+
+    hidden_grads = [dot(grads, w_down_all, 1, 1) for grads in grads_all]
+
     hiddens, gate_grads, up_grads, sums = [], [], [], []
     for b in range(batches):
+        chips = normed2_chips[b]
+        if b > 0:
+            chips = chips[:1] + [after(chip, partial) for chip in chips[1:]]
+        normed2_all.append(jnp.concatenate(core_blocks(chips), axis=0))
         wide = matmul(normed2_all[b], w_both)
         gate, up = wide[:, :ffn_part], wide[:, ffn_part:]
         sig = jax.nn.sigmoid(gate)
         silu = gate * sig
         hiddens.append((silu * up).astype(bf16))
-        grads = after(grads_all[b], *sums[-1][1:]) if sums else grads_all[b]
-        grad_hidden = dot(grads, w_down_all, 1, 1)
+        grad_hidden = hidden_grads[b]
+        if b > 0:
+            grad_hidden = after(grad_hidden, *sums[-1][1:])
         grad_gate = (grad_hidden * up * (sig * (1.0 + gate * (1.0 - sig)))).astype(bf16)
         grad_up = (grad_hidden * silu).astype(bf16)
         grad_wide = jnp.concatenate([grad_gate, grad_up], axis=1)
-        sums.append(core_sum(dot(grad_wide, w_both, 1, 1).astype(bf16)))
+        partial = dot(grad_wide, w_both, 1, 1).astype(bf16)
+        sums.append(core_sum(partial))
         gate_grads.append(grad_gate)
         up_grads.append(grad_up)
 
@@ -508,18 +519,18 @@
             total = total + dot(left, right, 0, 0)
         return total.astype(bf16)
 
-    def scatter_columns(lefts, rights):
-        value = token_sum(lefts, rights).reshape(ys * cs, zs * xs * d_rows, ffn_part)
+    def scatter_columns(total):
+        value = total.reshape(ys * cs, zs * xs * d_rows, ffn_part)
         return lax.psum_scatter(value, CTX, scatter_dimension=1, tiled=True)
 
-    gate_sum = scatter_columns(normed2_all, gate_grads)
-    up_sum = scatter_columns(normed2_all, [after(g, *sums[-1][1:]) for g in up_grads])
-    late = after(hiddens[0], *sums[-1][1:])
-    grad_down = lax.psum_scatter(
-        token_sum([late] + hiddens[1:], grads_all), CTX, scatter_dimension=0, tiled=True
-    ).astype(f32)
-
-    query_grads, groups = [], []
+    down_total = token_sum([after(hidden, partial) for hidden in hiddens], grads_all)
+    grad_down = lax.psum_scatter(down_total, CTX, scatter_dimension=0, tiled=True).astype(f32)
+
+    def split_cores(value, rows):
+        value = value.astype(bf16).reshape(ys, cs, zs, xs, rows, -1)
+        return move.scatter(value, "c", 1).astype(bf16)
+
+    query_grads, carried = [], []
     for b in range(batches):
         grad_mixed_t = dot(w_out_all, low_grads[b], 1, 1).astype(bf16)
         dq_t, dkv = attend_backward(
@@ -527,16 +538,17 @@
             lses[b],
         )
         query_grads.append(dq_t)
-        groups.append(dkv.reshape(back_groups + 1, xs, 2 * KV_WIDTH, local))
-
-    def split_cores(value, rows):
-        value = value.astype(bf16).reshape(ys, cs, zs, xs, rows, -1)
-        return move.scatter(value, "c", 1).astype(bf16)
-
+        groups = dkv.reshape(back_groups + 1, xs, 2 * KV_WIDTH, local)
+        first = (move.hop(groups[0], "z", -1).astype(f32) + groups[1].astype(f32)).astype(bf16)
+        carried.append([first] + [groups[k] for k in range(2, back_groups + 1)])
+
+    held = query_grads[0]
     out_cores = split_cores(
-        matmul(jnp.concatenate(mixed, axis=1), jnp.concatenate(low_grads, axis=0)),
-        w_out.shape[0],
-    )
+        matmul(jnp.concatenate(mixed, axis=1), jnp.concatenate(low_grads, axis=0)), w_out.shape[0]
+    )
+    gate_total = token_sum(normed2_all, [after(gate_grads[0], held)] + gate_grads[1:])
+    gate_sum = scatter_columns(gate_total)
+
     query_grad, gq_gain = head_backward(
         jnp.concatenate(query_grads, axis=1).astype(f32).reshape(HEADS, HEAD_DIM, both_rows),
         query_lin, query_scale, gain_q, cosine, sine,
@@ -544,21 +556,28 @@
     query_grad = query_grad.astype(bf16).reshape(Q_WIDTH, both_rows)
     q_cores = split_cores(dot(normed, query_grad, 0, 1), d_rows)
 
+    up_total = token_sum(normed2_all, [after(up_grads[0], held)] + up_grads[1:])
+    up_sum = scatter_columns(up_total)
+
+    out_chips = move.scatter(out_cores, "y", 0).astype(bf16)
+    q_chips = move.scatter(q_cores, "x", 2).astype(bf16)
+    out_rows = [
+        core_sum(matmul(after(hidden, held), w_down_all).astype(bf16)) for hidden in hiddens
+    ]
     kv_grads = []
     for b in range(batches):
-        carried = groups[b][0]
-        for k in range(1, back_groups + 1):
-            if b == batches - 1 and k == back_groups:
-                carried = after(carried, out_cores, q_cores)
-            carried = (
-                move.hop(carried, "z", -1).astype(f32) + groups[b][k].astype(f32)
-            ).astype(bf16)
-        total = carried[0].astype(f32)
+        sent = carried[b][0]
+        if b == batches - 1:
+            sent = after(sent, out_cores, q_cores)
+        for group in carried[b][1:]:
+            sent = (move.hop(sent, "z", -1).astype(f32) + group.astype(f32)).astype(bf16)
+        total = sent[0].astype(f32)
         for k in range(1, xs):
-            total = total + move.shift(carried[k], "x", -k).astype(f32)
+            total = total + move.shift(sent[k], "x", -k).astype(f32)
         kv_grads.append(total)
-    grad_out_w = move.scatter_chips(out_cores, "yxz")
-    grad_q_w = move.scatter_chips(q_cores, "xyz")
+    outputs = [
+        (resids[b] + chip_sum(out_rows[b])).astype(bf16) for b in range(batches)
+    ]
 
     kv_sum = jnp.concatenate(kv_grads, axis=1)
     key_grad, gk_gain = head_backward(
@@ -569,21 +588,18 @@
         [key_grad.astype(bf16).reshape(KV_WIDTH, both_rows), kv_sum[KV_WIDTH:].astype(bf16)],
         axis=0,
     )
-    grad_kv_w = move.scatter_chips(split_cores(dot(normed, kv_grad, 0, 1), d_rows), "yxz")
+    kv_cores = split_cores(dot(normed, kv_grad, 0, 1), d_rows)
+    grad_out_w = move.scatter_chips(after(out_chips, kv_cores), "xz")
+    grad_q_w = move.scatter_chips(after(q_chips, kv_cores), "yz")
+    grad_kv_w = move.scatter_chips(kv_cores, "xyz")
     grad_normed = dot(query_grad, w_q_all, 0, 1) + dot(kv_grad, w_kv_all, 0, 1)
     normed_back = norm_backward(grad_normed, inputs, scale_in)
     token_grads = [
         (grad_resids[b] + normed_back[part]).astype(bf16) for b, part in enumerate(parts)
     ]
 
-    outputs = []
-    for b in range(batches):
-        hidden = after(hiddens[b], low_grads[-1])
-        rows = core_sum(matmul(hidden, w_down_all).astype(bf16))
-        outputs.append((resids[b] + chip_sum(rows)).astype(bf16))
-
     both_sum = jnp.concatenate([gate_sum, up_sum], axis=2).reshape(ys, cs, d_rows, -1)
-    both_sum = move.exchange(both_sum, "y", 0, 2)
+    both_sum = move.exchange(after(both_sum, kv_cores), "y", 0, 2)
     both_sum = move.exchange(both_sum, "c", 0, 2).astype(f32)
     grad_gate_w = both_sum[..., :ffn_part].reshape(d_rows, -1)
     grad_up_w = both_sum[..., ffn_part:].reshape(d_rows, -1)
@@ -595,7 +611,7 @@
         grad_gate_w * w_gate.astype(f32) + grad_up_w * w_up.astype(f32), axis=1
     )
     grad_kv_w = grad_kv_w * gain_a
-    small = jnp.concatenate([gq_gain, gk_gain])[None, :]
+    small = after(jnp.concatenate([gq_gain, gk_gain])[None, :], kv_cores)
     for axis in LAYOUT:
         small = move.total(small, axis)
 

time: 854 us -> 812 us (0.951)
  waiting for transfers between devices: 357 us -> 286 us
  matrix products: 151 us -> 164 us
  local copies, waits for them, and re-layouts: 58.4 us -> 70.3 us
  other arithmetic: 92.2 us -> 103 us
    ppermute x56, waiting for transfers between devices: 244 us -> 148 us  [shift(): lax.ppermute(value, axis, [(i, (i + step) % size) for i in range(size)])]
    ppermute x5, waiting for transfers between devices: 8.04 us -> 22.8 us  [total(): lax.ppermute(value, axis, [(i, i ^ step) for i in range(size)])]
    all_gather x1, waiting for transfers between devices: 0.01 us -> 13.4 us  [per_device(): w_down_all = lax.all_gather(w_down, CTX, axis=0, tiled=True)]
    dot_general x26, matrix products: 151 us -> 164 us  [dot(): lax.dot_general(left, right, (((left_dim,), (right_dim,)), ((), ())), pre...]
    ppermute x56, starting transfers between devices: 97.5 us -> 87.2 us  [shift(): lax.ppermute(value, axis, [(i, (i + step) % size) for i in range(size)])]
    unnamed x301 -> x255, local copies, waits for them, and re-layouts: 20.3 us -> 16.9 us
  transfers between devices with their start and end apart: 73 -> 73, of which waited for: 32 -> 24; matrix products, arithmetic and copies ran while one was open for 30% -> 39% of each run, Pallas kernels for 4% -> 5%
where the time goes in v4:
time: 812 us; the launch traced here: 804 us
  waiting for transfers between devices  286 us (35%)
  matrix products  164 us (20%)
  starting transfers between devices  122 us (15%)
  other arithmetic  103 us (13%)
  local copies, waits for them, and re-layouts  70.3 us (9%)
  Pallas kernels  36.2 us (4%)
  between operations  22 us (3%)
    dot_general x26, matrix products, dot(): lax.dot_general(left, right, (((left_dim,), (right_dim,)), ((), ())), pre...  164 us
    ppermute x56, waiting for transfers between devices, shift(): lax.ppermute(value, axis, [(i, (i + step) % size) for i in range(size)])  148 us
    ppermute x6, waiting for transfers between devices, hop(): return lax.ppermute(value, axis, pairs)  101 us
    ppermute x56, starting transfers between devices, shift(): lax.ppermute(value, axis, [(i, (i + step) % size) for i in range(size)])  87.2 us
    ppermute x5, waiting for transfers between devices, total(): lax.ppermute(value, axis, [(i, i ^ step) for i in range(size)])  22.8 us
    ppermute x6, starting transfers between devices, hop(): return lax.ppermute(value, axis, pairs)  21.2 us
    pallas_call x2, Pallas kernels, attend_backward(): pl.pallas_call(functools.partial(backward_kernel, xs), name='attend_backw...  20.6 us
    unnamed x255, local copies, waits for them, and re-layouts  16.9 us
  transfers between devices with their start and end apart: 73, of which 24 were waited for; matrix products, arithmetic and copies ran while one was open for 39% of the time, Pallas kernels for 5%

profile of v4, /device:TPU:0, one launch (start us, length us, event | category | flops | bytes accessed | tf_op | source)
XLA Modules:
  0.0 803.6 jit_solution(12277245582160120815)
XLA Ops:
  9.5 3.1 collective-permute-start
  24.8 8.1 %collective-permute-done.3 = bf16[4,64,640]{2,1,0:T(8,128)(2,1)S(1)} collective-permute-done((bf16[4,64,640]{2,1,0:T(8,128)(2,1)S(1)}, bf16[4,64,640]{2,1,0:T(8,128)(2,1)S(1)}, u32[]{:S(2)}, u32[]{:S(2)}) %collective-permute-start.3) | collective-permute-done | bytes 327712 | tf_op jit(solution)/shard_map/ppermute | solution.py:243
  34.9 12.5 %collective-permute-done.21 = bf16[2,64,1792]{2,1,0:T(8,128)(2,1)S(1)} collective-permute-done((bf16[2,64,1792]{2,1,0:T(8,128)(2,1)S(1)}, bf16[2,64,1792]{2,1,0:T(8,128)(2,1)S(1)}, u32[]{:S(2)}, u32[]{:S(2)}) %collective-permute-start.21) | collective-permute-done | bytes 458784 | tf_op jit(solution)/shard_map/ppermute | solution.py:243
  60.8 5.6 collective-permute-done.12
  69.1 13.0 %collective-permute-done.4 = bf16[4,2,64,640]{3,2,1,0:T(8,128)(2,1)S(1)} collective-permute-done((bf16[4,2,64,640]{3,2,1,0:T(8,128)(2,1)S(1)}, bf16[4,2,64,640]{3,2,1,0:T(8,128)(2,1)S(1)}, u32[]{:S(2)}, u32[]{:S(2)}) %collective-permute-start.4) | collective-permute-done | bytes 655392 | tf_op jit(solution)/shard_map/ppermute | solution.py:243
  82.8 7.4 collective-permute-done.14
  95.7 3.9 collective-permute-start.6
  101.3 20.1 %collective-permute-done.6 = bf16[656,512]{1,0:T(8,128)(2,1)S(1)} collective-permute-done((bf16[656,512]{1,0:T(8,128)(2,1)S(1)}, bf16[656,512]{1,0:T(8,128)(2,1)S(1)}, u32[]{:S(2)}, u32[]{:S(2)}) %collective-permute-start.6) | collective-permute-done | bytes 671776 | tf_op jit(solution)/shard_map/ppermute | solution.py:248
  121.5 11.0 %collective-permute-start.7 = (bf16[656,512]{1,0:T(8,128)(2,1)S(1)}, bf16[656,512]{1,0:T(8,128)(2,1)S(1)}, u32[]{:S(2)}, u32[]{:S(2)}) collective-permute-start(bf16[656,512]{1,0:T(8,128)(2,1)S(1)} %collective-permute-done.6), channel_id=1, source_target_pairs={{0,2},{2,4},{4,6},{1,3},{3,5},{5,7},{8,10},{10,12},{12,14},{9,11},... | collective-permute-start | bytes 2015240 | tf_op jit(solution)/shard_map/ppermute | solution.py:248
  138.0 18.9 %collective-permute-done.7 = bf16[656,512]{1,0:T(8,128)(2,1)S(1)} collective-permute-done((bf16[656,512]{1,0:T(8,128)(2,1)S(1)}, bf16[656,512]{1,0:T(8,128)(2,1)S(1)}, u32[]{:S(2)}, u32[]{:S(2)}) %collective-permute-start.7) | collective-permute-done | bytes 671776 | tf_op jit(solution)/shard_map/ppermute | solution.py:248
  157.5 3.2 fusion.124
  162.1 24.6 %collective-permute-done.8 = bf16[656,512]{1,0:T(8,128)(2,1)S(1)} collective-permute-done((bf16[656,512]{1,0:T(8,128)(2,1)S(1)}, bf16[656,512]{1,0:T(8,128)(2,1)S(1)}, u32[]{:S(2)}, u32[]{:S(2)}) %collective-permute-start.8) | collective-permute-done | bytes 671776 | tf_op jit(solution)/shard_map/ppermute | solution.py:243
  186.8 22.5 %collective-permute-done.9 = bf16[656,512]{1,0:T(8,128)(2,1)S(1)} collective-permute-done((bf16[656,512]{1,0:T(8,128)(2,1)S(1)}, bf16[656,512]{1,0:T(8,128)(2,1)S(1)}, u32[]{:S(2)}, u32[]{:S(2)}) %collective-permute-start.9) | collective-permute-done | bytes 671776 | tf_op jit(solution)/shard_map/ppermute | solution.py:243
  232.3 4.6 broadcast_select_fusion
  237.0 7.7 attend_forward.2
  244.8 3.2 fusion.125
  248.0 4.8 multiply_reduce_fusion.6
  253.7 3.5 fusion.126
  257.2 3.2 fusion.127
  260.8 7.9 attend_forward.3
  268.7 10.5 %collective-permute-done.17 = bf16[256,2048]{1,0:T(8,128)(2,1)} collective-permute-done((bf16[256,2048]{1,0:T(8,128)(2,1)S(1)}, bf16[256,2048]{1,0:T(8,128)(2,1)}, u32[]{:S(2)}, u32[]{:S(2)}) %collective-permute-start.17) | collective-permute-done | bytes 1048608 | tf_op jit(solution)/shard_map/ppermute | solution.py:243
  279.3 5.4 multiply_reduce_fusion.4
  287.7 15.0 %fusion.117 = f32[1024,1792]{1,0:T(8,128)} fusion(bf16[2048,1792]{1,0:T(8,128)(2,1)} %bitcast.441, bf16[256,2048]{1,0:T(8,128)(2,1)} %collective-permute-done.19, bf16[256,2048]{1,0:T(8,128)(2,1)} %collective-permute-done.18, bf16[256,2048]{1,0:T(8,128)(2,1)} %collective-permute-done.17, bf16[256,2048]{1,0:T(8,128)(2,1)S(1)} %multiply_convert_fusion.7), kind=kOutput, calls=%fused_computation.361 | convolution fusion | flops 7532969984 | bytes 18874368 | tf_op jit(solution)/shard_map/dot_general | solution.py:32
  302.7 13.4 %all-gather.8.cloned.1.call-done = bf16[896,2048]{1,0:T(8,128)(2,1)} async-done(((bf16[112,2048]{1,0:T(8,128)(2,1)}), bf16[896,2048]{1,0:T(8,128)(2,1)}) %all-gather.8.cloned.1.call-update) | async-done | bytes 3670032 | tf_op jit(solution)/shard_map/all_gather | solution.py:384
  316.1 11.8 %multiply_convert_fusion.4 = (bf16[1024,896]{1,0:T(8,128)(2,1)S(1)}, bf16[1024,896]{1,0:T(8,128)(2,1)S(1)}, bf16[1024,896]{1,0:T(8,128)(2,1)}) fusion(f32[1024,1792]{1,0:T(8,128)} %fusion.117, bf16[896,2048]{1,0:T(8,128)(2,1)} %all-gather.8.cloned.1.call-done, bf16[256,2048]{1,0:T(8,128)(2,1)} %get-tuple-element.108, ...), kind=kOutput, calls=%fused_computation.46 | convolution fusion | flops 3788636160 | bytes 20709376 | tf_op jit(solution)/shard_map/dot_general | solution.py:32
  329.8 8.4 %convolution_convert_fusion.3 = bf16[1024,2048]{1,0:T(8,128)(2,1)S(1)} fusion(bf16[2048,1792]{1,0:T(8,128)(2,1)S(1)} %bitcast.444, bf16[1024,896]{1,0:T(8,128)(2,1)S(1)} %get-tuple-element.61, bf16[1024,896]{1,0:T(8,128)(2,1)S(1)} %get-tuple-element.60), kind=kOutput, calls=%fused_computation.31 | convolution fusion | flops 7525629952 | bytes 15204352 | tf_op jit(solution)/shard_map/dot_general | solution.py:32
  340.4 6.6 fusion.62
  347.0 12.1 %fusion.116 = f32[1024,1792]{1,0:T(8,128)S(1)} fusion(bf16[2048,1792]{1,0:T(8,128)(2,1)} %bitcast.442, bf16[256,2048]{1,0:T(8,128)(2,1)S(1)} %collective-permute-done.31, bf16[256,2048]{1,0:T(8,128)(2,1)} %collective-permute-done.30, bf16[256,2048]{1,0:T(8,128)(2,1)} %collective-permute-done.29, bf16[256,2048]{1,0:T(8,128)(2,1)} %multiply_convert_fusion.6), kind=kOutput, calls=%fused_computation.360 | convolution fusion | flops 7532969984 | bytes 18874368 | tf_op jit(solution)/shard_map/dot_general | solution.py:32
  366.7 12.0 %convolution_convert_fusion.2 = bf16[1024,2048]{1,0:T(8,128)(2,1)S(1)} fusion(bf16[2048,1792]{1,0:T(8,128)(2,1)} %bitcast.443, bf16[1024,896]{1,0:T(8,128)(2,1)S(1)} %get-tuple-element.74, bf16[1024,896]{1,0:T(8,128)(2,1)S(1)} %get-tuple-element.73), kind=kOutput, calls=%fused_computation.30 | convolution fusion | flops 7525629952 | bytes 15204352 | tf_op jit(solution)/shard_map/dot_general | solution.py:32
  381.3 6.1 fusion.61
  387.5 7.6 add_convert_fusion
  395.2 10.4 %fusion.115 = f32[2048,896]{1,0:T(8,128)} fusion(bf16[1024,896]{1,0:T(8,128)(2,1)} %copy-done.46, bf16[256,2048]{1,0:T(8,128)(2,1)} %copy-done.108, bf16[256,2048]{1,0:T(8,128)(2,1)} %collective-permute-done.30, bf16[256,2048]{1,0:T(8,128)(2,1)} %collective-permute-done.29, bf16[256,2048]{1,0:T(8,128)(2,1)} %multiply_convert_fusion.6), kind=kOutput, calls=%fused_computation.359 | convolution fusion | flops 3774873600 | bytes 13369344 | tf_op jit(solution)/shard_map/dot_general | solution.py:32
  408.9 9.8 %fusion.114 = f32[2048,896]{1,0:T(8,128)} fusion(bf16[1024,896]{1,0:T(8,128)(2,1)S(1)} %copy-done.45, bf16[256,2048]{1,0:T(8,128)(2,1)S(1)} %copy-done.109, bf16[256,2048]{1,0:T(8,128)(2,1)} %collective-permute-done.30, bf16[256,2048]{1,0:T(8,128)(2,1)} %collective-permute-done.29, bf16[256,2048]{1,0:T(8,128)(2,1)} %multiply_convert_fusion.6), kind=kOutput, calls=%fused_computation.358 | convolution fusion | flops 3774873600 | bytes 13369344 | tf_op jit(solution)/shard_map/dot_general | solution.py:32
  419.2 14.6 %collective-permute-done.35 = bf16[256,2048]{1,0:T(8,128)(2,1)S(1)} collective-permute-done((bf16[256,2048]{1,0:T(8,128)(2,1)S(1)}, bf16[256,2048]{1,0:T(8,128)(2,1)S(1)}, u32[]{:S(2)}, u32[]{:S(2)}) %collective-permute-start.35) | collective-permute-done | bytes 1048608 | tf_op jit(solution)/shard_map/ppermute | solution.py:243
  434.4 5.1 fusion.118
  441.9 10.2 %attend_backward.2 = (bf16[1280,256]{1,0:T(8,128)(2,1)}, bf16[6,2,320,256]{3,2,1,0:T(8,128)(2,1)}) custom-call(s32[4]{0:T(128)} %add_add_fusion.meta, s32[1,256]{1,0:T(1,128)} %bitcast.437, bf16[1280,512]{1,0:T(8,128)(2,1)} %bitcast.423, bf16[6,656,256]{2,1,0:T(8,128)(2,1)} %copy-done.81, bf16[6,656,256]{2,1,0:T(8,128)(2,1)} %copy-done.81, ...), custom_call_target="tpu_custom_call" | custom-call | flops 10066329600 | bytes 8388608 | tf_op jit(solution)/shard_map/attend_backward/pallas_call | solution.py:190
  452.1 2.9 fusion.128
  456.3 5.1 fusion.24.go_ref
  461.5 10.3 %attend_backward.3 = (bf16[1280,256]{1,0:T(8,128)(2,1)}, bf16[6,2,320,256]{3,2,1,0:T(8,128)(2,1)}) custom-call(s32[4]{0:T(128)} %add_add_fusion.1.meta, s32[1,256]{1,0:T(1,128)} %bitcast.435, bf16[1280,512]{1,0:T(8,128)(2,1)} %bitcast.424, bf16[6,656,256]{2,1,0:T(8,128)(2,1)} %copy-done.82, bf16[6,656,256]{2,1,0:T(8,128)(2,1)} %copy-done.82, ...), custom_call_target="tpu_custom_call" | custom-call | flops 10066329600 | bytes 8388608 | tf_op jit(solution)/shard_map/attend_backward/pallas_call | solution.py:190
  476.1 10.5 %add_convert_fusion.2 = bf16[2048,896]{1,0:T(8,128)(2,1)} fusion(f32[2048,896]{1,0:T(8,128)} %fusion.115, bf16[1024,896]{1,0:T(8,128)(2,1)S(1)} %copy-done.116, bf16[256,2048]{1,0:T(8,128)(2,1)} %collective-permute-done.19, bf16[256,2048]{1,0:T(8,128)(2,1)} %collective-permute-done.18, bf16[256,2048]{1,0:T(8,128)(2,1)} %collective-permute-done.17, ...), kind=kOutput, calls=%fused_computation.4 | convolution fusion | flops 3778543616 | bytes 17039360 | tf_op jit(solution)/shard_map/dot_general | solution.py:32
  492.6 3.2 convolution_convert_fusion
  502.7 4.7 convolution_convert_fusion.5
  510.2 4.7 convolution_convert_fusion.4
  520.3 8.5 %add_convert_fusion.1 = bf16[2048,896]{1,0:T(8,128)(2,1)} fusion(f32[2048,896]{1,0:T(8,128)S(1)} %bitcast.446, bf16[1024,896]{1,0:T(8,128)(2,1)S(1)} %copy-done.114, bf16[256,2048]{1,0:T(8,128)(2,1)} %collective-permute-done.19, bf16[256,2048]{1,0:T(8,128)(2,1)} %collective-permute-done.18, bf16[256,2048]{1,0:T(8,128)(2,1)} %collective-permute-done.17, ...), kind=kOutput, calls=%fused_computation.3 | convolution fusion | flops 3778543616 | bytes 17039360 | tf_op jit(solution)/shard_map/dot_general | solution.py:32
  528.8 3.1 convolution_convert_fusion.1
  532.0 41.3 %collective-permute-done.37 = bf16[2,640,256]{2,1,0:T(8,128)(2,1)S(1)} collective-permute-done((bf16[2,640,256]{2,1,0:T(8,128)(2,1)S(1)}, bf16[2,640,256]{2,1,0:T(8,128)(2,1)S(1)}, u32[]{:S(2)}, u32[]{:S(2)}) %collective-permute-start.37) | collective-permute-done | bytes 655392 | tf_op jit(solution)/shard_map/ppermute | solution.py:248
  574.3 19.6 %collective-permute-start.38 = (bf16[640,256]{1,0:T(8,128)(2,1)}, bf16[640,256]{1,0:T(8,128)(2,1)}, u32[]{:S(2)}, u32[]{:S(2)}) collective-permute-start(bf16[640,256]{1,0:T(8,128)(2,1)} %slice_bitcast_fusion.20), channel_id=1, source_target_pairs={{0,1},{1,0},{2,3},{3,2},{4,5},{5,4},{6,7},{7,6},{8,9},{9,8},{10,11... | collective-permute-start | bytes 983048 | tf_op jit(solution)/shard_map/ppermute | solution.py:243
  599.6 5.3 collective-permute-done.38
  624.2 10.4 %collective-permute-done.28 = bf16[256,2048]{1,0:T(8,128)(2,1)S(1)} collective-permute-done((bf16[256,2048]{1,0:T(8,128)(2,1)S(1)}, bf16[256,2048]{1,0:T(8,128)(2,1)S(1)}, u32[]{:S(2)}, u32[]{:S(2)}) %collective-permute-start.28) | collective-permute-done | bytes 1048608 | tf_op jit(solution)/shard_map/ppermute | solution.py:243
  635.1 20.5 %collective-permute-done.42 = bf16[2,640,256]{2,1,0:T(8,128)(2,1)S(1)} collective-permute-done((bf16[2,640,256]{2,1,0:T(8,128)(2,1)S(1)}, bf16[2,640,256]{2,1,0:T(8,128)(2,1)S(1)}, u32[]{:S(2)}, u32[]{:S(2)}) %collective-permute-start.42) | collective-permute-done | bytes 655392 | tf_op jit(solution)/shard_map/ppermute | solution.py:248
  659.5 5.5 collective-permute-done.43
  674.9 3.1 fusion.7
  678.0 2.8 fusion.6
  681.2 4.3 fusion.54
  687.3 2.9 fusion.21
  696.6 5.2 collective-permute-start.57
  706.7 4.5 collective-permute-start.58
  716.1 22.4 %collective-permute-done.59 = f32[1,128]{1,0:T(1,128)S(1)} collective-permute-done((f32[1,128]{1,0:T(1,128)S(1)}, f32[1,128]{1,0:T(1,128)S(1)}, u32[]{:S(2)}, u32[]{:S(2)}) %collective-permute-start.59) | collective-permute-done | bytes 544 | tf_op jit(solution)/shard_map/ppermute | solution.py:279
  741.1 5.4 collective-permute-start.63
  751.5 2.9 collective-permute-done.62
  754.4 7.0 collective-permute-start.48
  761.9 7.5 collective-permute-start.49
  778.0 4.1 collective-permute-start.52
  793.5 3.1 broadcast_multiply_fusion
  (564 shorter events, 202.6 us)
Async XLA Ops:
  7.2 240.8 %all-gather.4.cloned.1.call-start = ((), (), s32[]{:S(2)}) async-start(), calls=%async_computation.3 | async-start | bytes 5406720 | tf_op jit(solution)/shard_map/all_gather | solution.py:442
  7.9 279.8 %all-gather.6.cloned.1.call-start = ((), (), s32[]{:S(2)}) async-start(), calls=%async_computation.4 | async-start | bytes 8257536 | tf_op jit(solution)/shard_map/all_gather | solution.py:383
  9.5 13.3 %collective-permute-start = (bf16[64,640]{1,0:T(8,128)(2,1)S(1)}, bf16[64,640]{1,0:T(8,128)(2,1)S(1)}, u32[]{:S(2)}, u32[]{:S(2)}) collective-permute-start(bf16[64,640]{1,0:T(8,128)(2,1)S(1)} %fusion.89), channel_id=1, source_target_pairs={{0,2},{2,4},{4,6},{6,0},{1,3},{3,5},{5,7},{7,1},{8,10},{10,12},{12... | collective-permute-start | bytes 245768 | tf_op jit(solution)/shard_map/ppermute | solution.py:243
  12.6 10.2 %collective-permute-start.1 = (bf16[64,640]{1,0:T(8,128)(2,1)S(1)}, bf16[64,640]{1,0:T(8,128)(2,1)S(1)}, u32[]{:S(2)}, u32[]{:S(2)}) collective-permute-start(bf16[64,640]{1,0:T(8,128)(2,1)S(1)} %fusion.89), channel_id=1, source_target_pairs={{0,4},{2,6},{4,0},{6,2},{1,5},{3,7},{5,1},{7,3},{8,12},{10,14},{12... | collective-permute-start | bytes 245768 | tf_op jit(solution)/shard_map/ppermute | solution.py:243
  23.0 9.9 %collective-permute-start.3 = (bf16[4,64,640]{2,1,0:T(8,128)(2,1)S(1)}, bf16[4,64,640]{2,1,0:T(8,128)(2,1)S(1)}, u32[]{:S(2)}, u32[]{:S(2)}) collective-permute-start(bf16[4,64,640]{2,1,0:T(8,128)(2,1)S(1)} %select_select_fusion.1), channel_id=1, source_target_pairs={{0,1},{1,0},{2,3},{3,2},{4,5},{5,4},{6,7},{7,6},{8,9},{9,8},{10,11... | collective-permute-start | bytes 983048 | tf_op jit(solution)/shard_map/ppermute | solution.py:243
  33.3 14.1 %collective-permute-start.21 = (bf16[2,64,1792]{2,1,0:T(8,128)(2,1)S(1)}, bf16[2,64,1792]{2,1,0:T(8,128)(2,1)S(1)}, u32[]{:S(2)}, u32[]{:S(2)}) collective-permute-start(bf16[2,64,1792]{2,1,0:T(8,128)(2,1)S(1)} %get-tuple-element.130), channel_id=1, source_target_pairs={{0,16},{16,0},{1,17},{17,1},{2,18},{18,2},{3,19},{19,3},{4,20},{20... | collective-permute-start | bytes 1376264 | tf_op jit(solution)/shard_map/ppermute | solution.py:243
  48.6 267.6 %all-gather.8.cloned.1.call-start = ((), (), s32[]{:S(2)}) async-start(), calls=%async_computation.5 | async-start | bytes 4128768 | tf_op jit(solution)/shard_map/all_gather | solution.py:384
  48.8 12.0 %collective-permute-start.11 = (bf16[64,1280]{1,0:T(8,128)(2,1)S(1)}, bf16[64,1280]{1,0:T(8,128)(2,1)S(1)}, u32[]{:S(2)}, u32[]{:S(2)}) collective-permute-start(bf16[64,1280]{1,0:T(8,128)(2,1)S(1)} %fusion.83), channel_id=1, source_target_pairs={{0,6},{2,0},{4,2},{6,4},{1,7},{3,1},{5,3},{7,5},{8,14},{10,8},{12,... | collective-permute-start | bytes 491528 | tf_op jit(solution)/shard_map/ppermute | solution.py:243
  48.8 17.5 %collective-permute-start.12 = (bf16[64,1280]{1,0:T(8,128)(2,1)S(1)}, bf16[64,1280]{1,0:T(8,128)(2,1)S(1)}, u32[]{:S(2)}, u32[]{:S(2)}) collective-permute-start(bf16[64,1280]{1,0:T(8,128)(2,1)S(1)} %fusion.83), channel_id=1, source_target_pairs={{0,4},{2,6},{4,0},{6,2},{1,5},{3,7},{5,1},{7,3},{8,12},{10,14},{12... | collective-permute-start | bytes 491528 | tf_op jit(solution)/shard_map/ppermute | solution.py:243
  51.5 14.9 %collective-permute-start.13 = (bf16[64,1280]{1,0:T(8,128)(2,1)S(1)}, bf16[64,1280]{1,0:T(8,128)(2,1)}, u32[]{:S(2)}, u32[]{:S(2)}) collective-permute-start(bf16[64,1280]{1,0:T(8,128)(2,1)S(1)} %fusion.83), channel_id=1, source_target_pairs={{0,2},{2,4},{4,6},{6,0},{1,3},{3,5},{5,7},{7,1},{8,10},{10,12},{12... | collective-permute-start | bytes 491528 | tf_op jit(solution)/shard_map/ppermute | solution.py:243
  51.5 653.1 %reduce-scatter.8.cloned.1.call-start = ((), (), s32[]{:S(2)}) async-start(), calls=%async_computation.8 | async-start | bytes 4128768 | tf_op jit(solution)/shard_map/reduce_scatter | solution.py:527
  58.9 23.1 %collective-permute-start.4 = (bf16[4,2,64,640]{3,2,1,0:T(8,128)(2,1)S(1)}, bf16[4,2,64,640]{3,2,1,0:T(8,128)(2,1)S(1)}, u32[]{:S(2)}, u32[]{:S(2)}) collective-permute-start(bf16[4,2,64,640]{3,2,1,0:T(8,128)(2,1)S(1)} %broadcast_select_fusion.9), channel_id=1, source_target_pairs={{0,16},{16,0},{1,17},{17,1},{2,18},{18,2},{3,19},{19,3},{4,20},{20... | collective-permute-start | bytes 1966088 | tf_op jit(solution)/shard_map/ppermute | solution.py:243
  67.5 22.7 %collective-permute-start.14 = (bf16[4,64,1280]{2,1,0:T(8,128)(2,1)S(1)}, bf16[4,64,1280]{2,1,0:T(8,128)(2,1)S(1)}, u32[]{:S(2)}, u32[]{:S(2)}) collective-permute-start(bf16[4,64,1280]{2,1,0:T(8,128)(2,1)S(1)} %select_select_fusion), channel_id=1, source_target_pairs={{0,1},{1,0},{2,3},{3,2},{4,5},{5,4},{6,7},{7,6},{8,9},{9,8},{10,11... | collective-permute-start | bytes 1966088 | tf_op jit(solution)/shard_map/ppermute | solution.py:243
  82.3 9.6 %collective-permute-start.5 = (bf16[2,4,2,64,640]{4,3,2,1,0:T(8,128)(2,1)S(1)}, bf16[2,4,2,64,640]{4,3,2,1,0:T(8,128)(2,1)S(1)}, u32[]{:S(2)}, u32[]{:S(2)}) collective-permute-start(bf16[2,4,2,64,640]{4,3,2,1,0:T(8,128)(2,1)S(1)} %broadcast_select_fusion.6), channel_id=1, source_target_pairs={{0,8},{8,0},{1,9},{9,1},{2,10},{10,2},{3,11},{11,3},{4,12},{12,4},... | collective-permute-start | bytes 3932168 | tf_op jit(solution)/shard_map/ppermute | solution.py:243
  90.4 45.3 %collective-permute-start.15 = (bf16[4,2,64,1280]{3,2,1,0:T(8,128)(2,1)S(1)}, bf16[4,2,64,1280]{3,2,1,0:T(8,128)(2,1)S(1)}, u32[]{:S(2)}, u32[]{:S(2)}) collective-permute-start(bf16[4,2,64,1280]{3,2,1,0:T(8,128)(2,1)S(1)} %broadcast_select_fusion.5), channel_id=1, source_target_pairs={{0,16},{16,0},{1,17},{17,1},{2,18},{18,2},{3,19},{19,3},{4,20},{20... | collective-permute-start | bytes 3932168 | tf_op jit(solution)/shard_map/ppermute | solution.py:243
  95.7 25.8 %collective-permute-start.6 = (bf16[656,512]{1,0:T(8,128)(2,1)S(1)}, bf16[656,512]{1,0:T(8,128)(2,1)S(1)}, u32[]{:S(2)}, u32[]{:S(2)}) collective-permute-start(bf16[656,512]{1,0:T(8,128)(2,1)S(1)} %pad_maximum_fusion.16), channel_id=1, source_target_pairs={{0,2},{2,4},{4,6},{1,3},{3,5},{5,7},{8,10},{10,12},{12,14},{9,11},... | collective-permute-start | bytes 2015240 | tf_op jit(solution)/shard_map/ppermute | solution.py:248
  121.5 35.4 %collective-permute-start.7 = (bf16[656,512]{1,0:T(8,128)(2,1)S(1)}, bf16[656,512]{1,0:T(8,128)(2,1)S(1)}, u32[]{:S(2)}, u32[]{:S(2)}) collective-permute-start(bf16[656,512]{1,0:T(8,128)(2,1)S(1)} %collective-permute-done.6), channel_id=1, source_target_pairs={{0,2},{2,4},{4,6},{1,3},{3,5},{5,7},{8,10},{10,12},{12,14},{9,11},... | collective-permute-start | bytes 2015240 | tf_op jit(solution)/shard_map/ppermute | solution.py:248
  136.0 86.7 %collective-permute-start.16 = (bf16[2,4,2,64,1280]{4,3,2,1,0:T(8,128)(2,1)S(1)}, bf16[2,4,2,64,1280]{4,3,2,1,0:T(8,128)(2,1)}, u32[]{:S(2)}, u32[]{:S(2)}) collective-permute-start(bf16[2,4,2,64,1280]{4,3,2,1,0:T(8,128)(2,1)S(1)} %broadcast_select_fusion.1), channel_id=1, source_target_pairs={{0,8},{8,0},{1,9},{9,1},{2,10},{10,2},{3,11},{11,3},{4,12},{12,4},... | collective-permute-start | bytes 7864328 | tf_op jit(solution)/shard_map/ppermute | solution.py:243
  136.1 73.4 %collective-permute-start.10 = (bf16[656,512]{1,0:T(8,128)(2,1)S(1)}, bf16[656,512]{1,0:T(8,128)(2,1)S(1)}, u32[]{:S(2)}, u32[]{:S(2)}) collective-permute-start(bf16[656,512]{1,0:T(8,128)(2,1)S(1)} %pad_maximum_fusion.16), channel_id=1, source_target_pairs={{0,1},{1,0},{2,3},{3,2},{4,5},{5,4},{6,7},{7,6},{8,9},{9,8},{10,11... | collective-permute-start | bytes 2015240 | tf_op jit(solution)/shard_map/ppermute | solution.py:243
  138.0 106.7 %collective-permute-start.22 = (bf16[512,2048]{1,0:T(8,128)(2,1)}, bf16[512,2048]{1,0:T(8,128)(2,1)}, u32[]{:S(2)}, u32[]{:S(2)}) collective-permute-start(bf16[512,2048]{1,0:T(8,128)(2,1)} %pad_maximum_fusion.6), channel_id=1, source_target_pairs={{0,16},{16,0},{1,17},{17,1},{2,18},{18,2},{3,19},{19,3},{4,20},{20... | collective-permute-start | bytes 6291464 | tf_op jit(solution)/shard_map/ppermute | solution.py:243
  156.9 29.8 %collective-permute-start.8 = (bf16[656,512]{1,0:T(8,128)(2,1)S(1)}, bf16[656,512]{1,0:T(8,128)(2,1)S(1)}, u32[]{:S(2)}, u32[]{:S(2)}) collective-permute-start(bf16[656,512]{1,0:T(8,128)(2,1)S(1)} %collective-permute-done.7), channel_id=1, source_target_pairs={{0,1},{1,0},{2,3},{3,2},{4,5},{5,4},{6,7},{7,6},{8,9},{9,8},{10,11... | collective-permute-start | bytes 2015240 | tf_op jit(solution)/shard_map/ppermute | solution.py:243
  160.7 48.7 %collective-permute-start.9 = (bf16[656,512]{1,0:T(8,128)(2,1)S(1)}, bf16[656,512]{1,0:T(8,128)(2,1)S(1)}, u32[]{:S(2)}, u32[]{:S(2)}) collective-permute-start(bf16[656,512]{1,0:T(8,128)(2,1)S(1)} %collective-permute-done.6), channel_id=1, source_target_pairs={{0,1},{1,0},{2,3},{3,2},{4,5},{5,4},{6,7},{7,6},{8,9},{9,8},{10,11... | collective-permute-start | bytes 2015240 | tf_op jit(solution)/shard_map/ppermute | solution.py:243
  186.7 66.9 %collective-permute-start.23 = (bf16[512,2048]{1,0:T(8,128)(2,1)}, bf16[512,2048]{1,0:T(8,128)(2,1)}, u32[]{:S(2)}, u32[]{:S(2)}) collective-permute-start(bf16[512,2048]{1,0:T(8,128)(2,1)} %pad_maximum_fusion.6), channel_id=1, source_target_pairs={{0,8},{8,0},{1,9},{9,1},{2,10},{10,2},{3,11},{11,3},{4,12},{12,4},... | collective-permute-start | bytes 6291464 | tf_op jit(solution)/shard_map/ppermute | solution.py:243
  244.7 12.5 %collective-permute-start.24 = (bf16[512,2048]{1,0:T(8,128)(2,1)}, bf16[512,2048]{1,0:T(8,128)(2,1)}, u32[]{:S(2)}, u32[]{:S(2)}) collective-permute-start(bf16[512,2048]{1,0:T(8,128)(2,1)} %collective-permute-done.22), channel_id=1, source_target_pairs={{0,8},{8,0},{1,9},{9,1},{2,10},{10,2},{3,11},{11,3},{4,12},{12,4},... | collective-permute-start | bytes 6291464 | tf_op jit(solution)/shard_map/ppermute | solution.py:243
  253.6 25.7 %collective-permute-start.17 = (bf16[256,2048]{1,0:T(8,128)(2,1)S(1)}, bf16[256,2048]{1,0:T(8,128)(2,1)}, u32[]{:S(2)}, u32[]{:S(2)}) collective-permute-start(bf16[256,2048]{1,0:T(8,128)(2,1)S(1)} %multiply_convert_fusion.7), channel_id=1, source_target_pairs={{0,16},{16,0},{1,17},{17,1},{2,18},{18,2},{3,19},{19,3},{4,20},{20... | collective-permute-start | bytes 3145736 | tf_op jit(solution)/shard_map/ppermute | solution.py:243
  260.4 27.3 %collective-permute-start.18 = (bf16[256,2048]{1,0:T(8,128)(2,1)S(1)}, bf16[256,2048]{1,0:T(8,128)(2,1)}, u32[]{:S(2)}, u32[]{:S(2)}) collective-permute-start(bf16[256,2048]{1,0:T(8,128)(2,1)S(1)} %multiply_convert_fusion.7), channel_id=1, source_target_pairs={{0,8},{8,0},{1,9},{9,1},{2,10},{10,2},{3,11},{11,3},{4,12},{12,4},... | collective-permute-start | bytes 3145736 | tf_op jit(solution)/shard_map/ppermute | solution.py:243
  287.2 51.0 %collective-permute-start.29 = (bf16[256,2048]{1,0:T(8,128)(2,1)}, bf16[256,2048]{1,0:T(8,128)(2,1)}, u32[]{:S(2)}, u32[]{:S(2)}) collective-permute-start(bf16[256,2048]{1,0:T(8,128)(2,1)} %multiply_convert_fusion.6), channel_id=1, source_target_pairs={{0,16},{16,0},{1,17},{17,1},{2,18},{18,2},{3,19},{19,3},{4,20},{20... | collective-permute-start | bytes 3145736 | tf_op jit(solution)/shard_map/ppermute | solution.py:243
  287.2 59.7 %collective-permute-start.30 = (bf16[256,2048]{1,0:T(8,128)(2,1)}, bf16[256,2048]{1,0:T(8,128)(2,1)}, u32[]{:S(2)}, u32[]{:S(2)}) collective-permute-start(bf16[256,2048]{1,0:T(8,128)(2,1)} %multiply_convert_fusion.6), channel_id=1, source_target_pairs={{0,8},{8,0},{1,9},{9,1},{2,10},{10,2},{3,11},{11,3},{4,12},{12,4},... | collective-permute-start | bytes 3145736 | tf_op jit(solution)/shard_map/ppermute | solution.py:243
  338.2 8.7 %collective-permute-start.31 = (bf16[256,2048]{1,0:T(8,128)(2,1)}, bf16[256,2048]{1,0:T(8,128)(2,1)S(1)}, u32[]{:S(2)}, u32[]{:S(2)}) collective-permute-start(bf16[256,2048]{1,0:T(8,128)(2,1)} %collective-permute-done.29), channel_id=1, source_target_pairs={{0,8},{8,0},{1,9},{9,1},{2,10},{10,2},{3,11},{11,3},{4,12},{12,4},... | collective-permute-start | bytes 3145736 | tf_op jit(solution)/shard_map/ppermute | solution.py:243
  338.9 20.2 %collective-permute-start.25 = (bf16[2,256,2048]{2,1,0:T(8,128)(2,1)S(1)}, bf16[2,256,2048]{2,1,0:T(8,128)(2,1)S(1)}, u32[]{:S(2)}, u32[]{:S(2)}) collective-permute-start(bf16[2,256,2048]{2,1,0:T(8,128)(2,1)S(1)} %bitcast.420), channel_id=1, source_target_pairs={{0,8},{8,0},{1,9},{9,1},{2,10},{10,2},{3,11},{11,3},{4,12},{12,4},... | collective-permute-start | bytes 6291464 | tf_op jit(solution)/shard_map/ppermute | solution.py:243
  363.1 55.7 %collective-permute-start.26 = (bf16[256,2048]{1,0:T(8,128)(2,1)}, bf16[256,2048]{1,0:T(8,128)(2,1)S(1)}, u32[]{:S(2)}, u32[]{:S(2)}) collective-permute-start(bf16[256,2048]{1,0:T(8,128)(2,1)} %fusion.48), channel_id=1, source_target_pairs={{0,16},{16,0},{1,17},{17,1},{2,18},{18,2},{3,19},{19,3},{4,20},{20... | collective-permute-start | bytes 3145736 | tf_op jit(solution)/shard_map/ppermute | solution.py:243
  387.4 18.1 %collective-permute-start.34 = (bf16[2,256,2048]{2,1,0:T(8,128)(2,1)}, bf16[2,256,2048]{2,1,0:T(8,128)(2,1)}, u32[]{:S(2)}, u32[]{:S(2)}) collective-permute-start(bf16[2,256,2048]{2,1,0:T(8,128)(2,1)} %bitcast.64), channel_id=1, source_target_pairs={{0,8},{8,0},{1,9},{9,1},{2,10},{10,2},{3,11},{11,3},{4,12},{12,4},... | collective-permute-start | bytes 6291464 | tf_op jit(solution)/shard_map/ppermute | solution.py:243
  395.1 375.1 %reduce-scatter.4.cloned.1.call-start = ((), (), s32[]{:S(2)}) async-start(), calls=%async_computation.6 | async-start | bytes 4128768 | tf_op jit(solution)/shard_map/reduce_scatter | solution.py:524
  408.2 25.6 %collective-permute-start.35 = (bf16[256,2048]{1,0:T(8,128)(2,1)S(1)}, bf16[256,2048]{1,0:T(8,128)(2,1)S(1)}, u32[]{:S(2)}, u32[]{:S(2)}) collective-permute-start(bf16[256,2048]{1,0:T(8,128)(2,1)S(1)} %fusion.53), channel_id=1, source_target_pairs={{0,16},{16,0},{1,17},{17,1},{2,18},{18,2},{3,19},{19,3},{4,20},{20... | collective-permute-start | bytes 3145736 | tf_op jit(solution)/shard_map/ppermute | solution.py:243
  455.0 62.1 %collective-permute-start.36 = (bf16[2,640,256]{2,1,0:T(8,128)(2,1)}, bf16[2,640,256]{2,1,0:T(8,128)(2,1)}, u32[]{:S(2)}, u32[]{:S(2)}) collective-permute-start(bf16[2,640,256]{2,1,0:T(8,128)(2,1)} %bitcast.72), channel_id=1, source_target_pairs={{2,0},{4,2},{6,4},{3,1},{5,3},{7,5},{10,8},{12,10},{14,12},{11,9},... | collective-permute-start | bytes 1966088 | tf_op jit(solution)/shard_map/ppermute | solution.py:248
  486.7 283.5 %reduce-scatter.6.cloned.1.call-start = ((), (), s32[]{:S(2)}) async-start(), calls=%async_computation.7 | async-start | bytes 4128768 | tf_op jit(solution)/shard_map/reduce_scatter | solution.py:524
  499.4 113.9 %collective-permute-start.41 = (bf16[2,4,2,64,1280]{4,3,1,0,2:T(8,128)(2,1)}, bf16[2,4,2,64,1280]{4,3,1,0,2:T(8,128)(2,1)}, u32[]{:S(2)}, u32[]{:S(2)}) collective-permute-start(bf16[2,4,2,64,1280]{4,3,1,0,2:T(8,128)(2,1)} %bitcast.389), channel_id=1, source_target_pairs={{0,8},{8,0},{1,9},{9,1},{2,10},{10,2},{3,11},{11,3},{4,12},{12,4},... | collective-permute-start | bytes 7864328 | tf_op jit(solution)/shard_map/ppermute | solution.py:243
  501.4 96.5 %collective-permute-start.39 = (bf16[2,640,256]{2,1,0:T(8,128)(2,1)}, bf16[2,640,256]{2,1,0:T(8,128)(2,1)}, u32[]{:S(2)}, u32[]{:S(2)}) collective-permute-start(bf16[2,640,256]{2,1,0:T(8,128)(2,1)} %bitcast.77), channel_id=1, source_target_pairs={{2,0},{4,2},{6,4},{3,1},{5,3},{7,5},{10,8},{12,10},{14,12},{11,9},... | collective-permute-start | bytes 1966088 | tf_op jit(solution)/shard_map/ppermute | solution.py:248
  510.1 95.8 %collective-permute-start.27 = (bf16[2,256,2048]{2,1,0:T(8,128)(2,1)}, bf16[2,256,2048]{2,1,0:T(8,128)(2,1)}, u32[]{:S(2)}, u32[]{:S(2)}) collective-permute-start(bf16[2,256,2048]{2,1,0:T(8,128)(2,1)} %bitcast.41), channel_id=1, source_target_pairs={{0,8},{8,0},{1,9},{9,1},{2,10},{10,2},{3,11},{11,3},{4,12},{12,4},... | collective-permute-start | bytes 6291464 | tf_op jit(solution)/shard_map/ppermute | solution.py:243
  516.7 91.9 %collective-permute-start.32 = (bf16[2,256,2048]{2,1,0:T(8,128)(2,1)}, bf16[2,256,2048]{2,1,0:T(8,128)(2,1)}, u32[]{:S(2)}, u32[]{:S(2)}) collective-permute-start(bf16[2,256,2048]{2,1,0:T(8,128)(2,1)} %bitcast.57), channel_id=1, source_target_pairs={{0,8},{8,0},{1,9},{9,1},{2,10},{10,2},{3,11},{11,3},{4,12},{12,4},... | collective-permute-start | bytes 6291464 | tf_op jit(solution)/shard_map/ppermute | solution.py:243
  518.5 54.8 %collective-permute-start.37 = (bf16[2,640,256]{2,1,0:T(8,128)(2,1)S(1)}, bf16[2,640,256]{2,1,0:T(8,128)(2,1)S(1)}, u32[]{:S(2)}, u32[]{:S(2)}) collective-permute-start(bf16[2,640,256]{2,1,0:T(8,128)(2,1)S(1)} %fusion.47), channel_id=1, source_target_pairs={{2,0},{4,2},{6,4},{3,1},{5,3},{7,5},{10,8},{12,10},{14,12},{11,9},... | collective-permute-start | bytes 1966088 | tf_op jit(solution)/shard_map/ppermute | solution.py:248
  574.3 30.7 %collective-permute-start.38 = (bf16[640,256]{1,0:T(8,128)(2,1)}, bf16[640,256]{1,0:T(8,128)(2,1)}, u32[]{:S(2)}, u32[]{:S(2)}) collective-permute-start(bf16[640,256]{1,0:T(8,128)(2,1)} %slice_bitcast_fusion.20), channel_id=1, source_target_pairs={{0,1},{1,0},{2,3},{3,2},{4,5},{5,4},{6,7},{7,6},{8,9},{9,8},{10,11... | collective-permute-start | bytes 983048 | tf_op jit(solution)/shard_map/ppermute | solution.py:243
  597.9 18.1 %collective-permute-start.40 = (bf16[2,4,2,40,2048]{4,3,1,2,0:T(8,128)(2,1)}, bf16[2,4,2,40,2048]{4,3,1,2,0:T(8,128)(2,1)S(1)}, u32[]{:S(2)}, u32[]{:S(2)}) collective-permute-start(bf16[2,4,2,40,2048]{4,3,1,2,0:T(8,128)(2,1)} %bitcast.413), channel_id=1, source_target_pairs={{0,8},{8,0},{1,9},{9,1},{2,10},{10,2},{3,11},{11,3},{4,12},{12,4},... | collective-permute-start | bytes 7864328 | tf_op jit(solution)/shard_map/ppermute | solution.py:243
  608.5 26.1 %collective-permute-start.28 = (bf16[256,2048]{1,0:T(8,128)(2,1)S(1)}, bf16[256,2048]{1,0:T(8,128)(2,1)S(1)}, u32[]{:S(2)}, u32[]{:S(2)}) collective-permute-start(bf16[256,2048]{1,0:T(8,128)(2,1)S(1)} %fusion.50), channel_id=1, source_target_pairs={{0,16},{16,0},{1,17},{17,1},{2,18},{18,2},{3,19},{19,3},{4,20},{20... | collective-permute-start | bytes 3145736 | tf_op jit(solution)/shard_map/ppermute | solution.py:243
  611.3 46.2 %collective-permute-start.33 = (bf16[256,2048]{1,0:T(8,128)(2,1)S(1)}, bf16[256,2048]{1,0:T(8,128)(2,1)S(1)}, u32[]{:S(2)}, u32[]{:S(2)}) collective-permute-start(bf16[256,2048]{1,0:T(8,128)(2,1)S(1)} %fusion.52), channel_id=1, source_target_pairs={{0,16},{16,0},{1,17},{17,1},{2,18},{18,2},{3,19},{19,3},{4,20},{20... | collective-permute-start | bytes 3145736 | tf_op jit(solution)/shard_map/ppermute | solution.py:243
  617.3 38.3 %collective-permute-start.42 = (bf16[2,640,256]{2,1,0:T(8,128)(2,1)S(1)}, bf16[2,640,256]{2,1,0:T(8,128)(2,1)S(1)}, u32[]{:S(2)}, u32[]{:S(2)}) collective-permute-start(bf16[2,640,256]{2,1,0:T(8,128)(2,1)S(1)} %fusion.45), channel_id=1, source_target_pairs={{2,0},{4,2},{6,4},{3,1},{5,3},{7,5},{10,8},{12,10},{14,12},{11,9},... | collective-permute-start | bytes 1966088 | tf_op jit(solution)/shard_map/ppermute | solution.py:248
  620.5 71.2 %collective-permute-start.60 = (bf16[4,2,40,2048]{3,2,0,1:T(8,128)(2,1)}, bf16[4,2,40,2048]{3,2,0,1:T(8,128)(2,1)}, u32[]{:S(2)}, u32[]{:S(2)}) collective-permute-start(bf16[4,2,40,2048]{3,2,0,1:T(8,128)(2,1)} %dynamic-slice_bitcast_fusion), channel_id=1, source_target_pairs={{0,16},{16,0},{1,17},{17,1},{2,18},{18,2},{3,19},{19,3},{4,20},{20... | collective-permute-start | bytes 3932168 | tf_op jit(solution)/shard_map/ppermute | solution.py:243
  621.7 80.1 %collective-permute-start.44 = (bf16[2,4,64,1280]{3,2,1,0:T(8,128)(2,1)}, bf16[2,4,64,1280]{3,2,1,0:T(8,128)(2,1)}, u32[]{:S(2)}, u32[]{:S(2)}) collective-permute-start(bf16[2,4,64,1280]{3,2,1,0:T(8,128)(2,1)} %dynamic-slice_bitcast_fusion.1), channel_id=1, source_target_pairs={{0,1},{1,0},{2,3},{3,2},{4,5},{5,4},{6,7},{7,6},{8,9},{9,8},{10,11... | collective-permute-start | bytes 3932168 | tf_op jit(solution)/shard_map/ppermute | solution.py:243
  655.9 9.0 %collective-permute-start.43 = (bf16[640,256]{1,0:T(8,128)(2,1)S(1)}, bf16[640,256]{1,0:T(8,128)(2,1)S(1)}, u32[]{:S(2)}, u32[]{:S(2)}) collective-permute-start(bf16[640,256]{1,0:T(8,128)(2,1)S(1)} %slice_bitcast_fusion.18), channel_id=1, source_target_pairs={{0,1},{1,0},{2,3},{3,2},{4,5},{5,4},{6,7},{7,6},{8,9},{9,8},{10,11... | collective-permute-start | bytes 983048 | tf_op jit(solution)/shard_map/ppermute | solution.py:243
  671.9 15.2 %collective-permute-start.45 = (bf16[2,4,2,64,640]{4,3,1,0,2:T(8,128)(2,1)}, bf16[2,4,2,64,640]{4,3,1,0,2:T(8,128)(2,1)}, u32[]{:S(2)}, u32[]{:S(2)}) collective-permute-start(bf16[2,4,2,64,640]{4,3,1,0,2:T(8,128)(2,1)} %bitcast.391), channel_id=1, source_target_pairs={{0,8},{8,0},{1,9},{9,1},{2,10},{10,2},{3,11},{11,3},{4,12},{12,4},... | collective-permute-start | bytes 3932168 | tf_op jit(solution)/shard_map/ppermute | solution.py:243
  694.9 44.2 %collective-permute-start.61 = (bf16[4,40,2048]{2,1,0:T(8,128)(2,1)}, bf16[4,40,2048]{2,1,0:T(8,128)(2,1)S(1)}, u32[]{:S(2)}, u32[]{:S(2)}) collective-permute-start(bf16[4,40,2048]{2,1,0:T(8,128)(2,1)} %dynamic-slice_bitcast_fusion.2), channel_id=1, source_target_pairs={{0,1},{1,0},{2,3},{3,2},{4,5},{5,4},{6,7},{7,6},{8,9},{9,8},{10,11... | collective-permute-start | bytes 1966088 | tf_op jit(solution)/shard_map/ppermute | solution.py:243
  696.6 10.1 %collective-permute-start.57 = (f32[1,128]{1,0:T(1,128)S(1)}, f32[1,128]{1,0:T(1,128)S(1)}, u32[]{:S(2)}, u32[]{:S(2)}) collective-permute-start(f32[1,128]{1,0:T(1,128)S(1)} %add.628), channel_id=1, source_target_pairs={{0,2},{2,0},{4,6},{6,4},{1,3},{3,1},{5,7},{7,5},{8,10},{10,8},{12,... | collective-permute-start | bytes 1544 | tf_op jit(solution)/shard_map/ppermute | solution.py:279
  712.4 34.9 %collective-permute-start.50 = (bf16[2,4,64,640]{3,2,1,0:T(8,128)(2,1)S(1)}, bf16[2,4,64,640]{3,2,1,0:T(8,128)(2,1)S(1)}, u32[]{:S(2)}, u32[]{:S(2)}) collective-permute-start(bf16[2,4,64,640]{3,2,1,0:T(8,128)(2,1)S(1)} %dynamic-slice_bitcast_fusion.3), channel_id=1, source_target_pairs={{0,1},{1,0},{2,3},{3,2},{4,5},{5,4},{6,7},{7,6},{8,9},{9,8},{10,11... | collective-permute-start | bytes 1966088 | tf_op jit(solution)/shard_map/ppermute | solution.py:243
  712.8 25.7 %collective-permute-start.59 = (f32[1,128]{1,0:T(1,128)S(1)}, f32[1,128]{1,0:T(1,128)S(1)}, u32[]{:S(2)}, u32[]{:S(2)}) collective-permute-start(f32[1,128]{1,0:T(1,128)S(1)} %add.630), channel_id=1, source_target_pairs={{0,1},{1,0},{2,3},{3,2},{4,5},{5,4},{6,7},{7,6},{8,9},{9,8},{10,11... | collective-permute-start | bytes 1544 | tf_op jit(solution)/shard_map/ppermute | solution.py:279
  714.5 34.7 %collective-permute-start.46 = (bf16[4,64,1280]{2,1,0:T(8,128)(2,1)S(1)}, bf16[4,64,1280]{2,1,0:T(8,128)(2,1)S(1)}, u32[]{:S(2)}, u32[]{:S(2)}) collective-permute-start(bf16[4,64,1280]{2,1,0:T(8,128)(2,1)S(1)} %dynamic-slice_bitcast_fusion.4), channel_id=1, source_target_pairs={{0,16},{16,0},{1,17},{17,1},{2,18},{18,2},{3,19},{19,3},{4,20},{20... | collective-permute-start | bytes 1966088 | tf_op jit(solution)/shard_map/ppermute | solution.py:243
  739.4 15.0 %collective-permute-start.62 = (bf16[40,2048]{1,0:T(8,128)(2,1)S(1)}, bf16[40,2048]{1,0:T(8,128)(2,1)S(1)}, u32[]{:S(2)}, u32[]{:S(2)}) collective-permute-start(bf16[40,2048]{1,0:T(8,128)(2,1)S(1)} %get-tuple-element.150), channel_id=1, source_target_pairs={{0,2},{2,4},{4,6},{6,0},{1,3},{3,5},{5,7},{7,1},{8,10},{10,12},{12... | collective-permute-start | bytes 491528 | tf_op jit(solution)/shard_map/ppermute | solution.py:243
  741.1 20.8 %collective-permute-start.63 = (bf16[40,2048]{1,0:T(8,128)(2,1)S(1)}, bf16[40,2048]{1,0:T(8,128)(2,1)S(1)}, u32[]{:S(2)}, u32[]{:S(2)}) collective-permute-start(bf16[40,2048]{1,0:T(8,128)(2,1)S(1)} %get-tuple-element.152), channel_id=1, source_target_pairs={{0,4},{2,6},{4,0},{6,2},{1,5},{3,7},{5,1},{7,3},{8,12},{10,14},{12... | collective-permute-start | bytes 491528 | tf_op jit(solution)/shard_map/ppermute | solution.py:243
  746.6 22.8 %collective-permute-start.64 = (bf16[40,2048]{1,0:T(8,128)(2,1)S(1)}, bf16[40,2048]{1,0:T(8,128)(2,1)S(1)}, u32[]{:S(2)}, u32[]{:S(2)}) collective-permute-start(bf16[40,2048]{1,0:T(8,128)(2,1)S(1)} %get-tuple-element.151), channel_id=1, source_target_pairs={{0,6},{2,0},{4,2},{6,4},{1,7},{3,1},{5,3},{7,5},{8,14},{10,8},{12,... | collective-permute-start | bytes 491528 | tf_op jit(solution)/shard_map/ppermute | solution.py:243
  747.5 30.3 %collective-permute-start.51 = (bf16[4,64,640]{2,1,0:T(8,128)(2,1)S(1)}, bf16[4,64,640]{2,1,0:T(8,128)(2,1)S(1)}, u32[]{:S(2)}, u32[]{:S(2)}) collective-permute-start(bf16[4,64,640]{2,1,0:T(8,128)(2,1)S(1)} %dynamic-slice_bitcast_fusion.13), channel_id=1, source_target_pairs={{0,16},{16,0},{1,17},{17,1},{2,18},{18,2},{3,19},{19,3},{4,20},{20... | collective-permute-start | bytes 983048 | tf_op jit(solution)/shard_map/ppermute | solution.py:243
  750.2 23.1 %collective-permute-start.47 = (bf16[64,1280]{1,0:T(8,128)(2,1)}, bf16[64,1280]{1,0:T(8,128)(2,1)S(1)}, u32[]{:S(2)}, u32[]{:S(2)}) collective-permute-start(bf16[64,1280]{1,0:T(8,128)(2,1)} %get-tuple-element.153), channel_id=1, source_target_pairs={{0,2},{2,4},{4,6},{6,0},{1,3},{3,5},{5,7},{7,1},{8,10},{10,12},{12... | collective-permute-start | bytes 491528 | tf_op jit(solution)/shard_map/ppermute | solution.py:243
  754.4 21.5 %collective-permute-start.48 = (bf16[64,1280]{1,0:T(8,128)(2,1)}, bf16[64,1280]{1,0:T(8,128)(2,1)S(1)}, u32[]{:S(2)}, u32[]{:S(2)}) collective-permute-start(bf16[64,1280]{1,0:T(8,128)(2,1)} %get-tuple-element.155), channel_id=1, source_target_pairs={{0,4},{2,6},{4,0},{6,2},{1,5},{3,7},{5,1},{7,3},{8,12},{10,14},{12... | collective-permute-start | bytes 491528 | tf_op jit(solution)/shard_map/ppermute | solution.py:243
  761.9 14.0 %collective-permute-start.49 = (bf16[64,1280]{1,0:T(8,128)(2,1)}, bf16[64,1280]{1,0:T(8,128)(2,1)}, u32[]{:S(2)}, u32[]{:S(2)}) collective-permute-start(bf16[64,1280]{1,0:T(8,128)(2,1)} %get-tuple-element.154), channel_id=1, source_target_pairs={{0,6},{2,0},{4,2},{6,4},{1,7},{3,1},{5,3},{7,5},{8,14},{10,8},{12,... | collective-permute-start | bytes 491528 | tf_op jit(solution)/shard_map/ppermute | solution.py:243
  771.5 13.1 %collective-permute-start.65 = (bf16[2,64,1792]{2,1,0:T(8,128)(2,1)S(1)}, bf16[2,64,1792]{2,1,0:T(8,128)(2,1)S(1)}, u32[]{:S(2)}, u32[]{:S(2)}) collective-permute-start(bf16[2,64,1792]{2,1,0:T(8,128)(2,1)S(1)} %get-tuple-element.128), channel_id=1, source_target_pairs={{0,16},{16,0},{1,17},{17,1},{2,18},{18,2},{3,19},{19,3},{4,20},{20... | collective-permute-start | bytes 1376264 | tf_op jit(solution)/shard_map/ppermute | solution.py:243
  778.0 8.7 %collective-permute-start.52 = (bf16[64,640]{1,0:T(8,128)(2,1)S(1)}, bf16[64,640]{1,0:T(8,128)(2,1)S(1)}, u32[]{:S(2)}, u32[]{:S(2)}) collective-permute-start(bf16[64,640]{1,0:T(8,128)(2,1)S(1)} %get-tuple-element.160), channel_id=1, source_target_pairs={{0,2},{2,4},{4,6},{6,0},{1,3},{3,5},{5,7},{7,1},{8,10},{10,12},{12... | collective-permute-start | bytes 245768 | tf_op jit(solution)/shard_map/ppermute | solution.py:243
  (132 other events, 2103.3 us)
Sparse Core Ops, SparseCore 0:
  10.8 82.4 all-gather.3
  96.1 154.6 all-gather.5
  253.0 63.1 all-gather.7
  395.2 83.1 reduce-scatter.7
  486.8 163.7 reduce-scatter.3
  654.0 107.6 reduce-scatter.5

commit v5 on v4

--- a/solution.py
+++ b/solution.py
@@ -559,8 +559,8 @@
     up_total = token_sum(normed2_all, [after(up_grads[0], held)] + up_grads[1:])
     up_sum = scatter_columns(up_total)
 
-    out_chips = move.scatter(out_cores, "y", 0).astype(bf16)
-    q_chips = move.scatter(q_cores, "x", 2).astype(bf16)
+    out_chips = move.scatter(out_cores, "x", 2).astype(bf16)
+    q_chips = move.scatter(q_cores, "y", 0).astype(bf16)
     out_rows = [
         core_sum(matmul(after(hidden, held), w_down_all).astype(bf16)) for hidden in hiddens
     ]
@@ -589,9 +589,9 @@
         axis=0,
     )
     kv_cores = split_cores(dot(normed, kv_grad, 0, 1), d_rows)
-    grad_out_w = move.scatter_chips(after(out_chips, kv_cores), "xz")
-    grad_q_w = move.scatter_chips(after(q_chips, kv_cores), "yz")
-    grad_kv_w = move.scatter_chips(kv_cores, "xyz")
+    grad_out_w = move.scatter_chips(after(out_chips, kv_cores), "yz")
+    grad_q_w = move.scatter_chips(after(q_chips, kv_cores), "xz")
+    grad_kv_w = move.scatter_chips(kv_cores, "yxz")
     grad_normed = dot(query_grad, w_q_all, 0, 1) + dot(kv_grad, w_kv_all, 0, 1)
     normed_back = norm_backward(grad_normed, inputs, scale_in)
     token_grads = [
@@ -612,7 +612,7 @@
     )
     grad_kv_w = grad_kv_w * gain_a
     small = after(jnp.concatenate([gq_gain, gk_gain])[None, :], kv_cores)
-    for axis in LAYOUT:
+    for axis in "xyzc":
         small = move.total(small, axis)
 
     return (

time: 812 us -> 797 us (0.982)
  starting transfers between devices: 122 us -> 101 us
    ppermute x5, waiting for transfers between devices: 22.8 us -> 1.5 us  [total(): lax.ppermute(value, axis, [(i, i ^ step) for i in range(size)])]
    ppermute x56, waiting for transfers between devices: 148 us -> 166 us  [shift(): lax.ppermute(value, axis, [(i, (i + step) % size) for i in range(size)])]
    ppermute x56, starting transfers between devices: 87.2 us -> 74.1 us  [shift(): lax.ppermute(value, axis, [(i, (i + step) % size) for i in range(size)])]
  transfers between devices with their start and end apart: 73 -> 73, of which waited for: 24 -> 27; matrix products, arithmetic and copies ran while one was open for 39% -> 40% of each run, Pallas kernels for 5% -> 5%
where the time goes in v5:
time: 797 us; the launch traced here: 783 us
  waiting for transfers between devices  285 us (36%)
  matrix products  164 us (21%)
  other arithmetic  103 us (13%)
  starting transfers between devices  101 us (13%)
  local copies, waits for them, and re-layouts  70.3 us (9%)
  Pallas kernels  36.2 us (5%)
  between operations  22 us (3%)
    ppermute x56, waiting for transfers between devices, shift(): lax.ppermute(value, axis, [(i, (i + step) % size) for i in range(size)])  166 us
    dot_general x26, matrix products, dot(): lax.dot_general(left, right, (((left_dim,), (right_dim,)), ((), ())), pre...  164 us
    ppermute x6, waiting for transfers between devices, hop(): return lax.ppermute(value, axis, pairs)  104 us
    ppermute x56, starting transfers between devices, shift(): lax.ppermute(value, axis, [(i, (i + step) % size) for i in range(size)])  74.1 us
    ppermute x6, starting transfers between devices, hop(): return lax.ppermute(value, axis, pairs)  21.2 us
    pallas_call x2, Pallas kernels, attend_backward(): pl.pallas_call(functools.partial(backward_kernel, xs), name='attend_backw...  20.5 us
    unnamed x255, local copies, waits for them, and re-layouts  16.7 us
  transfers between devices with their start and end apart: 73, of which 27 were waited for; matrix products, arithmetic and copies ran while one was open for 40% of the time, Pallas kernels for 5%

profile of v5, /device:TPU:0, one launch (start us, length us, event | category | flops | bytes accessed | tf_op | source)
XLA Modules:
  0.0 782.5 jit_solution(6724693483546223097)
XLA Ops:
  9.5 3.1 collective-permute-start
  24.8 8.1 %collective-permute-done.3 = bf16[4,64,640]{2,1,0:T(8,128)(2,1)S(1)} collective-permute-done((bf16[4,64,640]{2,1,0:T(8,128)(2,1)S(1)}, bf16[4,64,640]{2,1,0:T(8,128)(2,1)S(1)}, u32[]{:S(2)}, u32[]{:S(2)}) %collective-permute-start.3) | collective-permute-done | bytes 327712 | tf_op jit(solution)/shard_map/ppermute | solution.py:243
  34.9 12.5 %collective-permute-done.21 = bf16[2,64,1792]{2,1,0:T(8,128)(2,1)S(1)} collective-permute-done((bf16[2,64,1792]{2,1,0:T(8,128)(2,1)S(1)}, bf16[2,64,1792]{2,1,0:T(8,128)(2,1)S(1)}, u32[]{:S(2)}, u32[]{:S(2)}) %collective-permute-start.21) | collective-permute-done | bytes 458784 | tf_op jit(solution)/shard_map/ppermute | solution.py:243
  60.8 5.6 collective-permute-done.12
  69.1 13.0 %collective-permute-done.4 = bf16[4,2,64,640]{3,2,1,0:T(8,128)(2,1)S(1)} collective-permute-done((bf16[4,2,64,640]{3,2,1,0:T(8,128)(2,1)S(1)}, bf16[4,2,64,640]{3,2,1,0:T(8,128)(2,1)S(1)}, u32[]{:S(2)}, u32[]{:S(2)}) %collective-permute-start.4) | collective-permute-done | bytes 655392 | tf_op jit(solution)/shard_map/ppermute | solution.py:243
  82.8 7.4 collective-permute-done.14
  95.7 3.9 collective-permute-start.6
  101.3 20.1 %collective-permute-done.6 = bf16[656,512]{1,0:T(8,128)(2,1)S(1)} collective-permute-done((bf16[656,512]{1,0:T(8,128)(2,1)S(1)}, bf16[656,512]{1,0:T(8,128)(2,1)S(1)}, u32[]{:S(2)}, u32[]{:S(2)}) %collective-permute-start.6) | collective-permute-done | bytes 671776 | tf_op jit(solution)/shard_map/ppermute | solution.py:248
  121.5 11.0 %collective-permute-start.7 = (bf16[656,512]{1,0:T(8,128)(2,1)S(1)}, bf16[656,512]{1,0:T(8,128)(2,1)S(1)}, u32[]{:S(2)}, u32[]{:S(2)}) collective-permute-start(bf16[656,512]{1,0:T(8,128)(2,1)S(1)} %collective-permute-done.6), channel_id=1, source_target_pairs={{0,2},{2,4},{4,6},{1,3},{3,5},{5,7},{8,10},{10,12},{12,14},{9,11},... | collective-permute-start | bytes 2015240 | tf_op jit(solution)/shard_map/ppermute | solution.py:248
  138.0 18.9 %collective-permute-done.7 = bf16[656,512]{1,0:T(8,128)(2,1)S(1)} collective-permute-done((bf16[656,512]{1,0:T(8,128)(2,1)S(1)}, bf16[656,512]{1,0:T(8,128)(2,1)S(1)}, u32[]{:S(2)}, u32[]{:S(2)}) %collective-permute-start.7) | collective-permute-done | bytes 671776 | tf_op jit(solution)/shard_map/ppermute | solution.py:248
  157.5 3.2 fusion.124
  162.1 24.6 %collective-permute-done.8 = bf16[656,512]{1,0:T(8,128)(2,1)S(1)} collective-permute-done((bf16[656,512]{1,0:T(8,128)(2,1)S(1)}, bf16[656,512]{1,0:T(8,128)(2,1)S(1)}, u32[]{:S(2)}, u32[]{:S(2)}) %collective-permute-start.8) | collective-permute-done | bytes 671776 | tf_op jit(solution)/shard_map/ppermute | solution.py:243
  186.8 22.5 %collective-permute-done.9 = bf16[656,512]{1,0:T(8,128)(2,1)S(1)} collective-permute-done((bf16[656,512]{1,0:T(8,128)(2,1)S(1)}, bf16[656,512]{1,0:T(8,128)(2,1)S(1)}, u32[]{:S(2)}, u32[]{:S(2)}) %collective-permute-start.9) | collective-permute-done | bytes 671776 | tf_op jit(solution)/shard_map/ppermute | solution.py:243
  232.3 4.6 broadcast_select_fusion
  237.0 7.7 attend_forward.2
  244.8 3.2 fusion.125
  248.0 4.8 multiply_reduce_fusion.6
  253.7 3.5 fusion.126
  257.2 3.2 fusion.127
  260.8 7.9 %attend_forward.3 = (bf16[1280,256]{1,0:T(8,128)(2,1)}, f32[5,4,256]{2,1,0:T(4,128)}) custom-call(s32[4]{0:T(128)} %add_add_fusion.1.meta, s32[256,1]{1,0:T(8,128)} %copy.59.start_ref, bf16[1280,512]{1,0:T(8,128)(2,1)} %bitcast.422, bf16[6,656,256]{2,1,0:T(8,128)(2,1)} %copy-done.82, bf16[6,656,256]{2,1,0:T(8,128)(2,1)} %copy-done.82), custom_call_target="tpu_custom_call" | custom-call | flops 4026531840 | bytes 4194304 | tf_op jit(solution)/shard_map/attend_forward/pallas_call | solution.py:153
  268.7 10.5 %collective-permute-done.17 = bf16[256,2048]{1,0:T(8,128)(2,1)} collective-permute-done((bf16[256,2048]{1,0:T(8,128)(2,1)S(1)}, bf16[256,2048]{1,0:T(8,128)(2,1)}, u32[]{:S(2)}, u32[]{:S(2)}) %collective-permute-start.17) | collective-permute-done | bytes 1048608 | tf_op jit(solution)/shard_map/ppermute | solution.py:243
  279.3 5.4 multiply_reduce_fusion.4
  287.7 15.0 %fusion.117 = f32[1024,1792]{1,0:T(8,128)} fusion(bf16[2048,1792]{1,0:T(8,128)(2,1)} %bitcast.441, bf16[256,2048]{1,0:T(8,128)(2,1)} %collective-permute-done.19, bf16[256,2048]{1,0:T(8,128)(2,1)} %collective-permute-done.18, bf16[256,2048]{1,0:T(8,128)(2,1)} %collective-permute-done.17, bf16[256,2048]{1,0:T(8,128)(2,1)S(1)} %multiply_convert_fusion.7), kind=kOutput, calls=%fused_computation.361 | convolution fusion | flops 7532969984 | bytes 18874368 | tf_op jit(solution)/shard_map/dot_general | solution.py:32
  302.7 13.4 %all-gather.8.cloned.1.call-done = bf16[896,2048]{1,0:T(8,128)(2,1)} async-done(((bf16[112,2048]{1,0:T(8,128)(2,1)}), bf16[896,2048]{1,0:T(8,128)(2,1)}) %all-gather.8.cloned.1.call-update) | async-done | bytes 3670032 | tf_op jit(solution)/shard_map/all_gather | solution.py:384
  316.1 11.8 %multiply_convert_fusion.4 = (bf16[1024,896]{1,0:T(8,128)(2,1)S(1)}, bf16[1024,896]{1,0:T(8,128)(2,1)S(1)}, bf16[1024,896]{1,0:T(8,128)(2,1)}) fusion(f32[1024,1792]{1,0:T(8,128)} %fusion.117, bf16[896,2048]{1,0:T(8,128)(2,1)} %all-gather.8.cloned.1.call-done, bf16[256,2048]{1,0:T(8,128)(2,1)} %get-tuple-element.108, ...), kind=kOutput, calls=%fused_computation.46 | convolution fusion | flops 3788636160 | bytes 20709376 | tf_op jit(solution)/shard_map/dot_general | solution.py:32
  329.8 8.4 %convolution_convert_fusion.3 = bf16[1024,2048]{1,0:T(8,128)(2,1)S(1)} fusion(bf16[2048,1792]{1,0:T(8,128)(2,1)S(1)} %bitcast.444, bf16[1024,896]{1,0:T(8,128)(2,1)S(1)} %get-tuple-element.61, bf16[1024,896]{1,0:T(8,128)(2,1)S(1)} %get-tuple-element.60), kind=kOutput, calls=%fused_computation.31 | convolution fusion | flops 7525629952 | bytes 15204352 | tf_op jit(solution)/shard_map/dot_general | solution.py:32
  340.4 6.6 fusion.62
  346.9 12.1 %fusion.116 = f32[1024,1792]{1,0:T(8,128)S(1)} fusion(bf16[2048,1792]{1,0:T(8,128)(2,1)} %bitcast.442, bf16[256,2048]{1,0:T(8,128)(2,1)S(1)} %collective-permute-done.31, bf16[256,2048]{1,0:T(8,128)(2,1)} %collective-permute-done.30, bf16[256,2048]{1,0:T(8,128)(2,1)} %collective-permute-done.29, bf16[256,2048]{1,0:T(8,128)(2,1)} %multiply_convert_fusion.6), kind=kOutput, calls=%fused_computation.360 | convolution fusion | flops 7532969984 | bytes 18874368 | tf_op jit(solution)/shard_map/dot_general | solution.py:32
  366.7 12.0 %convolution_convert_fusion.2 = bf16[1024,2048]{1,0:T(8,128)(2,1)S(1)} fusion(bf16[2048,1792]{1,0:T(8,128)(2,1)} %bitcast.443, bf16[1024,896]{1,0:T(8,128)(2,1)S(1)} %get-tuple-element.74, bf16[1024,896]{1,0:T(8,128)(2,1)S(1)} %get-tuple-element.73), kind=kOutput, calls=%fused_computation.30 | convolution fusion | flops 7525629952 | bytes 15204352 | tf_op jit(solution)/shard_map/dot_general | solution.py:32
  381.3 6.1 fusion.61
  387.5 7.6 add_convert_fusion
  395.2 10.4 %fusion.115 = f32[2048,896]{1,0:T(8,128)} fusion(bf16[1024,896]{1,0:T(8,128)(2,1)} %copy-done.46, bf16[256,2048]{1,0:T(8,128)(2,1)} %copy-done.108, bf16[256,2048]{1,0:T(8,128)(2,1)} %collective-permute-done.30, bf16[256,2048]{1,0:T(8,128)(2,1)} %collective-permute-done.29, bf16[256,2048]{1,0:T(8,128)(2,1)} %multiply_convert_fusion.6), kind=kOutput, calls=%fused_computation.359 | convolution fusion | flops 3774873600 | bytes 13369344 | tf_op jit(solution)/shard_map/dot_general | solution.py:32
  408.9 9.8 %fusion.114 = f32[2048,896]{1,0:T(8,128)} fusion(bf16[1024,896]{1,0:T(8,128)(2,1)S(1)} %copy-done.45, bf16[256,2048]{1,0:T(8,128)(2,1)S(1)} %copy-done.109, bf16[256,2048]{1,0:T(8,128)(2,1)} %collective-permute-done.30, bf16[256,2048]{1,0:T(8,128)(2,1)} %collective-permute-done.29, bf16[256,2048]{1,0:T(8,128)(2,1)} %multiply_convert_fusion.6), kind=kOutput, calls=%fused_computation.358 | convolution fusion | flops 3774873600 | bytes 13369344 | tf_op jit(solution)/shard_map/dot_general | solution.py:32
  419.2 14.6 %collective-permute-done.35 = bf16[256,2048]{1,0:T(8,128)(2,1)S(1)} collective-permute-done((bf16[256,2048]{1,0:T(8,128)(2,1)S(1)}, bf16[256,2048]{1,0:T(8,128)(2,1)S(1)}, u32[]{:S(2)}, u32[]{:S(2)}) %collective-permute-start.35) | collective-permute-done | bytes 1048608 | tf_op jit(solution)/shard_map/ppermute | solution.py:243
  434.3 5.1 fusion.118
  441.9 10.2 %attend_backward.2 = (bf16[1280,256]{1,0:T(8,128)(2,1)}, bf16[6,2,320,256]{3,2,1,0:T(8,128)(2,1)}) custom-call(s32[4]{0:T(128)} %add_add_fusion.meta, s32[1,256]{1,0:T(1,128)} %bitcast.437, bf16[1280,512]{1,0:T(8,128)(2,1)} %bitcast.423, bf16[6,656,256]{2,1,0:T(8,128)(2,1)} %copy-done.81, bf16[6,656,256]{2,1,0:T(8,128)(2,1)} %copy-done.81, ...), custom_call_target="tpu_custom_call" | custom-call | flops 10066329600 | bytes 8388608 | tf_op jit(solution)/shard_map/attend_backward/pallas_call | solution.py:190
  452.1 2.9 fusion.128
  456.3 5.2 fusion.24.go_ref
  461.5 10.3 %attend_backward.3 = (bf16[1280,256]{1,0:T(8,128)(2,1)}, bf16[6,2,320,256]{3,2,1,0:T(8,128)(2,1)}) custom-call(s32[4]{0:T(128)} %add_add_fusion.1.meta, s32[1,256]{1,0:T(1,128)} %bitcast.435, bf16[1280,512]{1,0:T(8,128)(2,1)} %bitcast.424, bf16[6,656,256]{2,1,0:T(8,128)(2,1)} %copy-done.82, bf16[6,656,256]{2,1,0:T(8,128)(2,1)} %copy-done.82, ...), custom_call_target="tpu_custom_call" | custom-call | flops 10066329600 | bytes 8388608 | tf_op jit(solution)/shard_map/attend_backward/pallas_call | solution.py:190
  476.1 10.5 %add_convert_fusion.2 = bf16[2048,896]{1,0:T(8,128)(2,1)} fusion(f32[2048,896]{1,0:T(8,128)} %fusion.115, bf16[1024,896]{1,0:T(8,128)(2,1)S(1)} %copy-done.116, bf16[256,2048]{1,0:T(8,128)(2,1)} %collective-permute-done.19, bf16[256,2048]{1,0:T(8,128)(2,1)} %collective-permute-done.18, bf16[256,2048]{1,0:T(8,128)(2,1)} %collective-permute-done.17, ...), kind=kOutput, calls=%fused_computation.4 | convolution fusion | flops 3778543616 | bytes 17039360 | tf_op jit(solution)/shard_map/dot_general | solution.py:32
  492.6 3.2 convolution_convert_fusion
  502.7 4.7 convolution_convert_fusion.5
  510.1 4.7 convolution_convert_fusion.4
  520.3 8.5 %add_convert_fusion.1 = bf16[2048,896]{1,0:T(8,128)(2,1)} fusion(f32[2048,896]{1,0:T(8,128)S(1)} %bitcast.446, bf16[1024,896]{1,0:T(8,128)(2,1)S(1)} %copy-done.114, bf16[256,2048]{1,0:T(8,128)(2,1)} %collective-permute-done.19, bf16[256,2048]{1,0:T(8,128)(2,1)} %collective-permute-done.18, bf16[256,2048]{1,0:T(8,128)(2,1)} %collective-permute-done.17, ...), kind=kOutput, calls=%fused_computation.3 | convolution fusion | flops 3778543616 | bytes 17039360 | tf_op jit(solution)/shard_map/dot_general | solution.py:32
  528.8 3.1 convolution_convert_fusion.1
  531.9 54.6 %collective-permute-done.37 = bf16[2,640,256]{2,1,0:T(8,128)(2,1)S(1)} collective-permute-done((bf16[2,640,256]{2,1,0:T(8,128)(2,1)S(1)}, bf16[2,640,256]{2,1,0:T(8,128)(2,1)S(1)}, u32[]{:S(2)}, u32[]{:S(2)}) %collective-permute-start.37) | collective-permute-done | bytes 655392 | tf_op jit(solution)/shard_map/ppermute | solution.py:248
  587.6 6.6 collective-permute-start.38
  599.9 6.8 collective-permute-done.38
  615.2 3.0 fusion
  625.5 10.9 %collective-permute-done.28 = bf16[256,2048]{1,0:T(8,128)(2,1)S(1)} collective-permute-done((bf16[256,2048]{1,0:T(8,128)(2,1)S(1)}, bf16[256,2048]{1,0:T(8,128)(2,1)S(1)}, u32[]{:S(2)}, u32[]{:S(2)}) %collective-permute-start.28) | collective-permute-done | bytes 1048608 | tf_op jit(solution)/shard_map/ppermute | solution.py:243
  637.0 10.1 %collective-permute-done.42 = bf16[2,640,256]{2,1,0:T(8,128)(2,1)S(1)} collective-permute-done((bf16[2,640,256]{2,1,0:T(8,128)(2,1)S(1)}, bf16[2,640,256]{2,1,0:T(8,128)(2,1)S(1)}, u32[]{:S(2)}, u32[]{:S(2)}) %collective-permute-start.42) | collective-permute-done | bytes 655392 | tf_op jit(solution)/shard_map/ppermute | solution.py:248
  648.9 10.0 %collective-permute-done.33 = bf16[256,2048]{1,0:T(8,128)(2,1)S(1)} collective-permute-done((bf16[256,2048]{1,0:T(8,128)(2,1)S(1)}, bf16[256,2048]{1,0:T(8,128)(2,1)S(1)}, u32[]{:S(2)}, u32[]{:S(2)}) %collective-permute-start.33) | collective-permute-done | bytes 1048608 | tf_op jit(solution)/shard_map/ppermute | solution.py:243
  660.9 2.9 collective-permute-done.43
  673.6 3.1 fusion.7
  676.7 2.8 fusion.6
  680.0 4.2 fusion.54
  686.0 3.0 fusion.21
  699.6 2.7 fusion.22
  718.6 6.0 collective-permute-done.50
  725.8 5.9 collective-permute-done.46
  732.7 4.6 collective-permute-start.48
  737.3 13.6 %collective-permute-start.49 = (bf16[64,1280]{1,0:T(8,128)(2,1)}, bf16[64,1280]{1,0:T(8,128)(2,1)}, u32[]{:S(2)}, u32[]{:S(2)}) collective-permute-start(bf16[64,1280]{1,0:T(8,128)(2,1)} %get-tuple-element.154), channel_id=1, source_target_pairs={{0,6},{2,0},{4,2},{6,4},{1,7},{3,1},{5,3},{7,5},{8,14},{10,8},{12,... | collective-permute-start | bytes 491528 | tf_op jit(solution)/shard_map/ppermute | solution.py:243
  757.4 3.0 collective-permute-start.52
  772.4 3.1 broadcast_multiply_fusion
  (564 shorter events, 202.5 us)
Async XLA Ops:
  7.2 240.8 %all-gather.4.cloned.1.call-start = ((), (), s32[]{:S(2)}) async-start(), calls=%async_computation.3 | async-start | bytes 5406720 | tf_op jit(solution)/shard_map/all_gather | solution.py:442
  7.9 279.8 %all-gather.6.cloned.1.call-start = ((), (), s32[]{:S(2)}) async-start(), calls=%async_computation.4 | async-start | bytes 8257536 | tf_op jit(solution)/shard_map/all_gather | solution.py:383
  9.5 13.3 %collective-permute-start = (bf16[64,640]{1,0:T(8,128)(2,1)S(1)}, bf16[64,640]{1,0:T(8,128)(2,1)S(1)}, u32[]{:S(2)}, u32[]{:S(2)}) collective-permute-start(bf16[64,640]{1,0:T(8,128)(2,1)S(1)} %fusion.89), channel_id=1, source_target_pairs={{0,2},{2,4},{4,6},{6,0},{1,3},{3,5},{5,7},{7,1},{8,10},{10,12},{12... | collective-permute-start | bytes 245768 | tf_op jit(solution)/shard_map/ppermute | solution.py:243
  12.6 10.2 %collective-permute-start.1 = (bf16[64,640]{1,0:T(8,128)(2,1)S(1)}, bf16[64,640]{1,0:T(8,128)(2,1)S(1)}, u32[]{:S(2)}, u32[]{:S(2)}) collective-permute-start(bf16[64,640]{1,0:T(8,128)(2,1)S(1)} %fusion.89), channel_id=1, source_target_pairs={{0,4},{2,6},{4,0},{6,2},{1,5},{3,7},{5,1},{7,3},{8,12},{10,14},{12... | collective-permute-start | bytes 245768 | tf_op jit(solution)/shard_map/ppermute | solution.py:243
  23.0 9.9 %collective-permute-start.3 = (bf16[4,64,640]{2,1,0:T(8,128)(2,1)S(1)}, bf16[4,64,640]{2,1,0:T(8,128)(2,1)S(1)}, u32[]{:S(2)}, u32[]{:S(2)}) collective-permute-start(bf16[4,64,640]{2,1,0:T(8,128)(2,1)S(1)} %select_select_fusion.1), channel_id=1, source_target_pairs={{0,1},{1,0},{2,3},{3,2},{4,5},{5,4},{6,7},{7,6},{8,9},{9,8},{10,11... | collective-permute-start | bytes 983048 | tf_op jit(solution)/shard_map/ppermute | solution.py:243
  24.6 8.4 %collective-permute-start.20 = (bf16[64,2,1792]{2,0,1:T(8,128)(2,1)S(1)}, bf16[64,2,1792]{2,0,1:T(8,128)(2,1)S(1)}, u32[]{:S(2)}, u32[]{:S(2)}) collective-permute-start(bf16[64,2,1792]{2,0,1:T(8,128)(2,1)S(1)} %get-tuple-element.132), channel_id=1, source_target_pairs={{0,8},{8,0},{1,9},{9,1},{2,10},{10,2},{3,11},{11,3},{4,12},{12,4},... | collective-permute-start | bytes 1376264 | tf_op jit(solution)/shard_map/ppermute | solution.py:243
  33.3 14.1 %collective-permute-start.21 = (bf16[2,64,1792]{2,1,0:T(8,128)(2,1)S(1)}, bf16[2,64,1792]{2,1,0:T(8,128)(2,1)S(1)}, u32[]{:S(2)}, u32[]{:S(2)}) collective-permute-start(bf16[2,64,1792]{2,1,0:T(8,128)(2,1)S(1)} %get-tuple-element.130), channel_id=1, source_target_pairs={{0,16},{16,0},{1,17},{17,1},{2,18},{18,2},{3,19},{19,3},{4,20},{20... | collective-permute-start | bytes 1376264 | tf_op jit(solution)/shard_map/ppermute | solution.py:243
  48.6 267.5 %all-gather.8.cloned.1.call-start = ((), (), s32[]{:S(2)}) async-start(), calls=%async_computation.5 | async-start | bytes 4128768 | tf_op jit(solution)/shard_map/all_gather | solution.py:384
  48.8 12.0 %collective-permute-start.11 = (bf16[64,1280]{1,0:T(8,128)(2,1)S(1)}, bf16[64,1280]{1,0:T(8,128)(2,1)S(1)}, u32[]{:S(2)}, u32[]{:S(2)}) collective-permute-start(bf16[64,1280]{1,0:T(8,128)(2,1)S(1)} %fusion.83), channel_id=1, source_target_pairs={{0,6},{2,0},{4,2},{6,4},{1,7},{3,1},{5,3},{7,5},{8,14},{10,8},{12,... | collective-permute-start | bytes 491528 | tf_op jit(solution)/shard_map/ppermute | solution.py:243
  48.8 17.5 %collective-permute-start.12 = (bf16[64,1280]{1,0:T(8,128)(2,1)S(1)}, bf16[64,1280]{1,0:T(8,128)(2,1)S(1)}, u32[]{:S(2)}, u32[]{:S(2)}) collective-permute-start(bf16[64,1280]{1,0:T(8,128)(2,1)S(1)} %fusion.83), channel_id=1, source_target_pairs={{0,4},{2,6},{4,0},{6,2},{1,5},{3,7},{5,1},{7,3},{8,12},{10,14},{12... | collective-permute-start | bytes 491528 | tf_op jit(solution)/shard_map/ppermute | solution.py:243
  51.5 14.9 %collective-permute-start.13 = (bf16[64,1280]{1,0:T(8,128)(2,1)S(1)}, bf16[64,1280]{1,0:T(8,128)(2,1)}, u32[]{:S(2)}, u32[]{:S(2)}) collective-permute-start(bf16[64,1280]{1,0:T(8,128)(2,1)S(1)} %fusion.83), channel_id=1, source_target_pairs={{0,2},{2,4},{4,6},{6,0},{1,3},{3,5},{5,7},{7,1},{8,10},{10,12},{12... | collective-permute-start | bytes 491528 | tf_op jit(solution)/shard_map/ppermute | solution.py:243
  51.5 650.8 %reduce-scatter.8.cloned.1.call-start = ((), (), s32[]{:S(2)}) async-start(), calls=%async_computation.8 | async-start | bytes 4128768 | tf_op jit(solution)/shard_map/reduce_scatter | solution.py:527
  58.9 23.1 %collective-permute-start.4 = (bf16[4,2,64,640]{3,2,1,0:T(8,128)(2,1)S(1)}, bf16[4,2,64,640]{3,2,1,0:T(8,128)(2,1)S(1)}, u32[]{:S(2)}, u32[]{:S(2)}) collective-permute-start(bf16[4,2,64,640]{3,2,1,0:T(8,128)(2,1)S(1)} %broadcast_select_fusion.9), channel_id=1, source_target_pairs={{0,16},{16,0},{1,17},{17,1},{2,18},{18,2},{3,19},{19,3},{4,20},{20... | collective-permute-start | bytes 1966088 | tf_op jit(solution)/shard_map/ppermute | solution.py:243
  67.5 22.7 %collective-permute-start.14 = (bf16[4,64,1280]{2,1,0:T(8,128)(2,1)S(1)}, bf16[4,64,1280]{2,1,0:T(8,128)(2,1)S(1)}, u32[]{:S(2)}, u32[]{:S(2)}) collective-permute-start(bf16[4,64,1280]{2,1,0:T(8,128)(2,1)S(1)} %select_select_fusion), channel_id=1, source_target_pairs={{0,1},{1,0},{2,3},{3,2},{4,5},{5,4},{6,7},{7,6},{8,9},{9,8},{10,11... | collective-permute-start | bytes 1966088 | tf_op jit(solution)/shard_map/ppermute | solution.py:243
  82.3 9.6 %collective-permute-start.5 = (bf16[2,4,2,64,640]{4,3,2,1,0:T(8,128)(2,1)S(1)}, bf16[2,4,2,64,640]{4,3,2,1,0:T(8,128)(2,1)S(1)}, u32[]{:S(2)}, u32[]{:S(2)}) collective-permute-start(bf16[2,4,2,64,640]{4,3,2,1,0:T(8,128)(2,1)S(1)} %broadcast_select_fusion.6), channel_id=1, source_target_pairs={{0,8},{8,0},{1,9},{9,1},{2,10},{10,2},{3,11},{11,3},{4,12},{12,4},... | collective-permute-start | bytes 3932168 | tf_op jit(solution)/shard_map/ppermute | solution.py:243
  90.4 45.3 %collective-permute-start.15 = (bf16[4,2,64,1280]{3,2,1,0:T(8,128)(2,1)S(1)}, bf16[4,2,64,1280]{3,2,1,0:T(8,128)(2,1)S(1)}, u32[]{:S(2)}, u32[]{:S(2)}) collective-permute-start(bf16[4,2,64,1280]{3,2,1,0:T(8,128)(2,1)S(1)} %broadcast_select_fusion.5), channel_id=1, source_target_pairs={{0,16},{16,0},{1,17},{17,1},{2,18},{18,2},{3,19},{19,3},{4,20},{20... | collective-permute-start | bytes 3932168 | tf_op jit(solution)/shard_map/ppermute | solution.py:243
  95.7 25.8 %collective-permute-start.6 = (bf16[656,512]{1,0:T(8,128)(2,1)S(1)}, bf16[656,512]{1,0:T(8,128)(2,1)S(1)}, u32[]{:S(2)}, u32[]{:S(2)}) collective-permute-start(bf16[656,512]{1,0:T(8,128)(2,1)S(1)} %pad_maximum_fusion.16), channel_id=1, source_target_pairs={{0,2},{2,4},{4,6},{1,3},{3,5},{5,7},{8,10},{10,12},{12,14},{9,11},... | collective-permute-start | bytes 2015240 | tf_op jit(solution)/shard_map/ppermute | solution.py:248
  121.5 35.4 %collective-permute-start.7 = (bf16[656,512]{1,0:T(8,128)(2,1)S(1)}, bf16[656,512]{1,0:T(8,128)(2,1)S(1)}, u32[]{:S(2)}, u32[]{:S(2)}) collective-permute-start(bf16[656,512]{1,0:T(8,128)(2,1)S(1)} %collective-permute-done.6), channel_id=1, source_target_pairs={{0,2},{2,4},{4,6},{1,3},{3,5},{5,7},{8,10},{10,12},{12,14},{9,11},... | collective-permute-start | bytes 2015240 | tf_op jit(solution)/shard_map/ppermute | solution.py:248
  136.0 86.7 %collective-permute-start.16 = (bf16[2,4,2,64,1280]{4,3,2,1,0:T(8,128)(2,1)S(1)}, bf16[2,4,2,64,1280]{4,3,2,1,0:T(8,128)(2,1)}, u32[]{:S(2)}, u32[]{:S(2)}) collective-permute-start(bf16[2,4,2,64,1280]{4,3,2,1,0:T(8,128)(2,1)S(1)} %broadcast_select_fusion.1), channel_id=1, source_target_pairs={{0,8},{8,0},{1,9},{9,1},{2,10},{10,2},{3,11},{11,3},{4,12},{12,4},... | collective-permute-start | bytes 7864328 | tf_op jit(solution)/shard_map/ppermute | solution.py:243
  136.1 73.4 %collective-permute-start.10 = (bf16[656,512]{1,0:T(8,128)(2,1)S(1)}, bf16[656,512]{1,0:T(8,128)(2,1)S(1)}, u32[]{:S(2)}, u32[]{:S(2)}) collective-permute-start(bf16[656,512]{1,0:T(8,128)(2,1)S(1)} %pad_maximum_fusion.16), channel_id=1, source_target_pairs={{0,1},{1,0},{2,3},{3,2},{4,5},{5,4},{6,7},{7,6},{8,9},{9,8},{10,11... | collective-permute-start | bytes 2015240 | tf_op jit(solution)/shard_map/ppermute | solution.py:243
  138.0 106.7 %collective-permute-start.22 = (bf16[512,2048]{1,0:T(8,128)(2,1)}, bf16[512,2048]{1,0:T(8,128)(2,1)}, u32[]{:S(2)}, u32[]{:S(2)}) collective-permute-start(bf16[512,2048]{1,0:T(8,128)(2,1)} %pad_maximum_fusion.6), channel_id=1, source_target_pairs={{0,16},{16,0},{1,17},{17,1},{2,18},{18,2},{3,19},{19,3},{4,20},{20... | collective-permute-start | bytes 6291464 | tf_op jit(solution)/shard_map/ppermute | solution.py:243
  156.9 29.8 %collective-permute-start.8 = (bf16[656,512]{1,0:T(8,128)(2,1)S(1)}, bf16[656,512]{1,0:T(8,128)(2,1)S(1)}, u32[]{:S(2)}, u32[]{:S(2)}) collective-permute-start(bf16[656,512]{1,0:T(8,128)(2,1)S(1)} %collective-permute-done.7), channel_id=1, source_target_pairs={{0,1},{1,0},{2,3},{3,2},{4,5},{5,4},{6,7},{7,6},{8,9},{9,8},{10,11... | collective-permute-start | bytes 2015240 | tf_op jit(solution)/shard_map/ppermute | solution.py:243
  160.7 48.7 %collective-permute-start.9 = (bf16[656,512]{1,0:T(8,128)(2,1)S(1)}, bf16[656,512]{1,0:T(8,128)(2,1)S(1)}, u32[]{:S(2)}, u32[]{:S(2)}) collective-permute-start(bf16[656,512]{1,0:T(8,128)(2,1)S(1)} %collective-permute-done.6), channel_id=1, source_target_pairs={{0,1},{1,0},{2,3},{3,2},{4,5},{5,4},{6,7},{7,6},{8,9},{9,8},{10,11... | collective-permute-start | bytes 2015240 | tf_op jit(solution)/shard_map/ppermute | solution.py:243
  186.7 66.9 %collective-permute-start.23 = (bf16[512,2048]{1,0:T(8,128)(2,1)}, bf16[512,2048]{1,0:T(8,128)(2,1)}, u32[]{:S(2)}, u32[]{:S(2)}) collective-permute-start(bf16[512,2048]{1,0:T(8,128)(2,1)} %pad_maximum_fusion.6), channel_id=1, source_target_pairs={{0,8},{8,0},{1,9},{9,1},{2,10},{10,2},{3,11},{11,3},{4,12},{12,4},... | collective-permute-start | bytes 6291464 | tf_op jit(solution)/shard_map/ppermute | solution.py:243
  244.7 12.5 %collective-permute-start.24 = (bf16[512,2048]{1,0:T(8,128)(2,1)}, bf16[512,2048]{1,0:T(8,128)(2,1)}, u32[]{:S(2)}, u32[]{:S(2)}) collective-permute-start(bf16[512,2048]{1,0:T(8,128)(2,1)} %collective-permute-done.22), channel_id=1, source_target_pairs={{0,8},{8,0},{1,9},{9,1},{2,10},{10,2},{3,11},{11,3},{4,12},{12,4},... | collective-permute-start | bytes 6291464 | tf_op jit(solution)/shard_map/ppermute | solution.py:243
  253.6 25.7 %collective-permute-start.17 = (bf16[256,2048]{1,0:T(8,128)(2,1)S(1)}, bf16[256,2048]{1,0:T(8,128)(2,1)}, u32[]{:S(2)}, u32[]{:S(2)}) collective-permute-start(bf16[256,2048]{1,0:T(8,128)(2,1)S(1)} %multiply_convert_fusion.7), channel_id=1, source_target_pairs={{0,16},{16,0},{1,17},{17,1},{2,18},{18,2},{3,19},{19,3},{4,20},{20... | collective-permute-start | bytes 3145736 | tf_op jit(solution)/shard_map/ppermute | solution.py:243
  260.4 27.3 %collective-permute-start.18 = (bf16[256,2048]{1,0:T(8,128)(2,1)S(1)}, bf16[256,2048]{1,0:T(8,128)(2,1)}, u32[]{:S(2)}, u32[]{:S(2)}) collective-permute-start(bf16[256,2048]{1,0:T(8,128)(2,1)S(1)} %multiply_convert_fusion.7), channel_id=1, source_target_pairs={{0,8},{8,0},{1,9},{9,1},{2,10},{10,2},{3,11},{11,3},{4,12},{12,4},... | collective-permute-start | bytes 3145736 | tf_op jit(solution)/shard_map/ppermute | solution.py:243
  279.3 8.5 %collective-permute-start.19 = (bf16[256,2048]{1,0:T(8,128)(2,1)}, bf16[256,2048]{1,0:T(8,128)(2,1)}, u32[]{:S(2)}, u32[]{:S(2)}) collective-permute-start(bf16[256,2048]{1,0:T(8,128)(2,1)} %collective-permute-done.17), channel_id=1, source_target_pairs={{0,8},{8,0},{1,9},{9,1},{2,10},{10,2},{3,11},{11,3},{4,12},{12,4},... | collective-permute-start | bytes 3145736 | tf_op jit(solution)/shard_map/ppermute | solution.py:243
  287.2 51.0 %collective-permute-start.29 = (bf16[256,2048]{1,0:T(8,128)(2,1)}, bf16[256,2048]{1,0:T(8,128)(2,1)}, u32[]{:S(2)}, u32[]{:S(2)}) collective-permute-start(bf16[256,2048]{1,0:T(8,128)(2,1)} %multiply_convert_fusion.6), channel_id=1, source_target_pairs={{0,16},{16,0},{1,17},{17,1},{2,18},{18,2},{3,19},{19,3},{4,20},{20... | collective-permute-start | bytes 3145736 | tf_op jit(solution)/shard_map/ppermute | solution.py:243
  287.2 59.7 %collective-permute-start.30 = (bf16[256,2048]{1,0:T(8,128)(2,1)}, bf16[256,2048]{1,0:T(8,128)(2,1)}, u32[]{:S(2)}, u32[]{:S(2)}) collective-permute-start(bf16[256,2048]{1,0:T(8,128)(2,1)} %multiply_convert_fusion.6), channel_id=1, source_target_pairs={{0,8},{8,0},{1,9},{9,1},{2,10},{10,2},{3,11},{11,3},{4,12},{12,4},... | collective-permute-start | bytes 3145736 | tf_op jit(solution)/shard_map/ppermute | solution.py:243
  338.2 8.7 %collective-permute-start.31 = (bf16[256,2048]{1,0:T(8,128)(2,1)}, bf16[256,2048]{1,0:T(8,128)(2,1)S(1)}, u32[]{:S(2)}, u32[]{:S(2)}) collective-permute-start(bf16[256,2048]{1,0:T(8,128)(2,1)} %collective-permute-done.29), channel_id=1, source_target_pairs={{0,8},{8,0},{1,9},{9,1},{2,10},{10,2},{3,11},{11,3},{4,12},{12,4},... | collective-permute-start | bytes 3145736 | tf_op jit(solution)/shard_map/ppermute | solution.py:243
  338.9 20.2 %collective-permute-start.25 = (bf16[2,256,2048]{2,1,0:T(8,128)(2,1)S(1)}, bf16[2,256,2048]{2,1,0:T(8,128)(2,1)S(1)}, u32[]{:S(2)}, u32[]{:S(2)}) collective-permute-start(bf16[2,256,2048]{2,1,0:T(8,128)(2,1)S(1)} %bitcast.420), channel_id=1, source_target_pairs={{0,8},{8,0},{1,9},{9,1},{2,10},{10,2},{3,11},{11,3},{4,12},{12,4},... | collective-permute-start | bytes 6291464 | tf_op jit(solution)/shard_map/ppermute | solution.py:243
  363.1 55.6 %collective-permute-start.26 = (bf16[256,2048]{1,0:T(8,128)(2,1)}, bf16[256,2048]{1,0:T(8,128)(2,1)S(1)}, u32[]{:S(2)}, u32[]{:S(2)}) collective-permute-start(bf16[256,2048]{1,0:T(8,128)(2,1)} %fusion.48), channel_id=1, source_target_pairs={{0,16},{16,0},{1,17},{17,1},{2,18},{18,2},{3,19},{19,3},{4,20},{20... | collective-permute-start | bytes 3145736 | tf_op jit(solution)/shard_map/ppermute | solution.py:243
  387.4 18.1 %collective-permute-start.34 = (bf16[2,256,2048]{2,1,0:T(8,128)(2,1)}, bf16[2,256,2048]{2,1,0:T(8,128)(2,1)}, u32[]{:S(2)}, u32[]{:S(2)}) collective-permute-start(bf16[2,256,2048]{2,1,0:T(8,128)(2,1)} %bitcast.64), channel_id=1, source_target_pairs={{0,8},{8,0},{1,9},{9,1},{2,10},{10,2},{3,11},{11,3},{4,12},{12,4},... | collective-permute-start | bytes 6291464 | tf_op jit(solution)/shard_map/ppermute | solution.py:243
  395.1 356.6 %reduce-scatter.4.cloned.1.call-start = ((), (), s32[]{:S(2)}) async-start(), calls=%async_computation.6 | async-start | bytes 4128768 | tf_op jit(solution)/shard_map/reduce_scatter | solution.py:524
  408.2 25.6 %collective-permute-start.35 = (bf16[256,2048]{1,0:T(8,128)(2,1)S(1)}, bf16[256,2048]{1,0:T(8,128)(2,1)S(1)}, u32[]{:S(2)}, u32[]{:S(2)}) collective-permute-start(bf16[256,2048]{1,0:T(8,128)(2,1)S(1)} %fusion.53), channel_id=1, source_target_pairs={{0,16},{16,0},{1,17},{17,1},{2,18},{18,2},{3,19},{19,3},{4,20},{20... | collective-permute-start | bytes 3145736 | tf_op jit(solution)/shard_map/ppermute | solution.py:243
  455.0 62.2 %collective-permute-start.36 = (bf16[2,640,256]{2,1,0:T(8,128)(2,1)}, bf16[2,640,256]{2,1,0:T(8,128)(2,1)}, u32[]{:S(2)}, u32[]{:S(2)}) collective-permute-start(bf16[2,640,256]{2,1,0:T(8,128)(2,1)} %bitcast.72), channel_id=1, source_target_pairs={{2,0},{4,2},{6,4},{3,1},{5,3},{7,5},{10,8},{12,10},{14,12},{11,9},... | collective-permute-start | bytes 1966088 | tf_op jit(solution)/shard_map/ppermute | solution.py:248
  486.6 265.1 %reduce-scatter.6.cloned.1.call-start = ((), (), s32[]{:S(2)}) async-start(), calls=%async_computation.7 | async-start | bytes 4128768 | tf_op jit(solution)/shard_map/reduce_scatter | solution.py:524
  499.4 115.8 %collective-permute-start.41 = (bf16[2,4,2,64,1280]{4,3,1,2,0:T(8,128)(2,1)}, bf16[2,4,2,64,1280]{4,3,1,2,0:T(8,128)(2,1)}, u32[]{:S(2)}, u32[]{:S(2)}) collective-permute-start(bf16[2,4,2,64,1280]{4,3,1,2,0:T(8,128)(2,1)} %bitcast.389), channel_id=1, source_target_pairs={{0,8},{8,0},{1,9},{9,1},{2,10},{10,2},{3,11},{11,3},{4,12},{12,4},... | collective-permute-start | bytes 7864328 | tf_op jit(solution)/shard_map/ppermute | solution.py:243
  501.4 96.8 %collective-permute-start.39 = (bf16[2,640,256]{2,1,0:T(8,128)(2,1)}, bf16[2,640,256]{2,1,0:T(8,128)(2,1)}, u32[]{:S(2)}, u32[]{:S(2)}) collective-permute-start(bf16[2,640,256]{2,1,0:T(8,128)(2,1)} %bitcast.77), channel_id=1, source_target_pairs={{2,0},{4,2},{6,4},{3,1},{5,3},{7,5},{10,8},{12,10},{14,12},{11,9},... | collective-permute-start | bytes 1966088 | tf_op jit(solution)/shard_map/ppermute | solution.py:248
  510.1 97.7 %collective-permute-start.27 = (bf16[2,256,2048]{2,1,0:T(8,128)(2,1)}, bf16[2,256,2048]{2,1,0:T(8,128)(2,1)}, u32[]{:S(2)}, u32[]{:S(2)}) collective-permute-start(bf16[2,256,2048]{2,1,0:T(8,128)(2,1)} %bitcast.41), channel_id=1, source_target_pairs={{0,8},{8,0},{1,9},{9,1},{2,10},{10,2},{3,11},{11,3},{4,12},{12,4},... | collective-permute-start | bytes 6291464 | tf_op jit(solution)/shard_map/ppermute | solution.py:243
  516.6 93.8 %collective-permute-start.32 = (bf16[2,256,2048]{2,1,0:T(8,128)(2,1)}, bf16[2,256,2048]{2,1,0:T(8,128)(2,1)}, u32[]{:S(2)}, u32[]{:S(2)}) collective-permute-start(bf16[2,256,2048]{2,1,0:T(8,128)(2,1)} %bitcast.57), channel_id=1, source_target_pairs={{0,8},{8,0},{1,9},{9,1},{2,10},{10,2},{3,11},{11,3},{4,12},{12,4},... | collective-permute-start | bytes 6291464 | tf_op jit(solution)/shard_map/ppermute | solution.py:243
  518.4 68.1 %collective-permute-start.37 = (bf16[2,640,256]{2,1,0:T(8,128)(2,1)S(1)}, bf16[2,640,256]{2,1,0:T(8,128)(2,1)S(1)}, u32[]{:S(2)}, u32[]{:S(2)}) collective-permute-start(bf16[2,640,256]{2,1,0:T(8,128)(2,1)S(1)} %fusion.47), channel_id=1, source_target_pairs={{2,0},{4,2},{6,4},{3,1},{5,3},{7,5},{10,8},{12,10},{14,12},{11,9},... | collective-permute-start | bytes 1966088 | tf_op jit(solution)/shard_map/ppermute | solution.py:248
  587.6 19.2 %collective-permute-start.38 = (bf16[640,256]{1,0:T(8,128)(2,1)}, bf16[640,256]{1,0:T(8,128)(2,1)}, u32[]{:S(2)}, u32[]{:S(2)}) collective-permute-start(bf16[640,256]{1,0:T(8,128)(2,1)} %slice_bitcast_fusion.20), channel_id=1, source_target_pairs={{0,1},{1,0},{2,3},{3,2},{4,5},{5,4},{6,7},{7,6},{8,9},{9,8},{10,11... | collective-permute-start | bytes 983048 | tf_op jit(solution)/shard_map/ppermute | solution.py:243
  598.3 19.9 %collective-permute-start.40 = (bf16[2,4,2,40,2048]{4,3,1,0,2:T(8,128)(2,1)}, bf16[2,4,2,40,2048]{4,3,1,0,2:T(8,128)(2,1)S(1)}, u32[]{:S(2)}, u32[]{:S(2)}) collective-permute-start(bf16[2,4,2,40,2048]{4,3,1,0,2:T(8,128)(2,1)} %bitcast.413), channel_id=1, source_target_pairs={{0,8},{8,0},{1,9},{9,1},{2,10},{10,2},{3,11},{11,3},{4,12},{12,4},... | collective-permute-start | bytes 7864328 | tf_op jit(solution)/shard_map/ppermute | solution.py:243
  610.3 26.1 %collective-permute-start.28 = (bf16[256,2048]{1,0:T(8,128)(2,1)S(1)}, bf16[256,2048]{1,0:T(8,128)(2,1)S(1)}, u32[]{:S(2)}, u32[]{:S(2)}) collective-permute-start(bf16[256,2048]{1,0:T(8,128)(2,1)S(1)} %fusion.50), channel_id=1, source_target_pairs={{0,16},{16,0},{1,17},{17,1},{2,18},{18,2},{3,19},{19,3},{4,20},{20... | collective-permute-start | bytes 3145736 | tf_op jit(solution)/shard_map/ppermute | solution.py:243
  613.1 45.8 %collective-permute-start.33 = (bf16[256,2048]{1,0:T(8,128)(2,1)S(1)}, bf16[256,2048]{1,0:T(8,128)(2,1)S(1)}, u32[]{:S(2)}, u32[]{:S(2)}) collective-permute-start(bf16[256,2048]{1,0:T(8,128)(2,1)S(1)} %fusion.52), channel_id=1, source_target_pairs={{0,16},{16,0},{1,17},{17,1},{2,18},{18,2},{3,19},{19,3},{4,20},{20... | collective-permute-start | bytes 3145736 | tf_op jit(solution)/shard_map/ppermute | solution.py:243
  619.4 27.6 %collective-permute-start.42 = (bf16[2,640,256]{2,1,0:T(8,128)(2,1)S(1)}, bf16[2,640,256]{2,1,0:T(8,128)(2,1)S(1)}, u32[]{:S(2)}, u32[]{:S(2)}) collective-permute-start(bf16[2,640,256]{2,1,0:T(8,128)(2,1)S(1)} %fusion.45), channel_id=1, source_target_pairs={{2,0},{4,2},{6,4},{3,1},{5,3},{7,5},{10,8},{12,10},{14,12},{11,9},... | collective-permute-start | bytes 1966088 | tf_op jit(solution)/shard_map/ppermute | solution.py:248
  623.8 67.7 %collective-permute-start.60 = (bf16[2,4,40,2048]{3,2,1,0:T(8,128)(2,1)}, bf16[2,4,40,2048]{3,2,1,0:T(8,128)(2,1)}, u32[]{:S(2)}, u32[]{:S(2)}) collective-permute-start(bf16[2,4,40,2048]{3,2,1,0:T(8,128)(2,1)} %dynamic-slice_bitcast_fusion), channel_id=1, source_target_pairs={{0,1},{1,0},{2,3},{3,2},{4,5},{5,4},{6,7},{7,6},{8,9},{9,8},{10,11... | collective-permute-start | bytes 3932168 | tf_op jit(solution)/shard_map/ppermute | solution.py:243
  625.5 74.1 %collective-permute-start.44 = (bf16[4,2,64,1280]{3,2,0,1:T(8,128)(2,1)}, bf16[4,2,64,1280]{3,2,0,1:T(8,128)(2,1)}, u32[]{:S(2)}, u32[]{:S(2)}) collective-permute-start(bf16[4,2,64,1280]{3,2,0,1:T(8,128)(2,1)} %dynamic-slice_bitcast_fusion.1), channel_id=1, source_target_pairs={{0,16},{16,0},{1,17},{17,1},{2,18},{18,2},{3,19},{19,3},{4,20},{20... | collective-permute-start | bytes 3932168 | tf_op jit(solution)/shard_map/ppermute | solution.py:243
  647.3 16.5 %collective-permute-start.43 = (bf16[640,256]{1,0:T(8,128)(2,1)S(1)}, bf16[640,256]{1,0:T(8,128)(2,1)S(1)}, u32[]{:S(2)}, u32[]{:S(2)}) collective-permute-start(bf16[640,256]{1,0:T(8,128)(2,1)S(1)} %slice_bitcast_fusion.18), channel_id=1, source_target_pairs={{0,1},{1,0},{2,3},{3,2},{4,5},{5,4},{6,7},{7,6},{8,9},{9,8},{10,11... | collective-permute-start | bytes 983048 | tf_op jit(solution)/shard_map/ppermute | solution.py:243
  670.6 15.0 %collective-permute-start.45 = (bf16[2,4,2,64,640]{4,3,1,2,0:T(8,128)(2,1)}, bf16[2,4,2,64,640]{4,3,1,2,0:T(8,128)(2,1)}, u32[]{:S(2)}, u32[]{:S(2)}) collective-permute-start(bf16[2,4,2,64,640]{4,3,1,2,0:T(8,128)(2,1)} %bitcast.391), channel_id=1, source_target_pairs={{0,8},{8,0},{1,9},{9,1},{2,10},{10,2},{3,11},{11,3},{4,12},{12,4},... | collective-permute-start | bytes 3932168 | tf_op jit(solution)/shard_map/ppermute | solution.py:243
  694.5 17.8 %collective-permute-start.61 = (bf16[4,40,2048]{2,1,0:T(8,128)(2,1)}, bf16[4,40,2048]{2,1,0:T(8,128)(2,1)S(1)}, u32[]{:S(2)}, u32[]{:S(2)}) collective-permute-start(bf16[4,40,2048]{2,1,0:T(8,128)(2,1)} %dynamic-slice_bitcast_fusion.2), channel_id=1, source_target_pairs={{0,16},{16,0},{1,17},{17,1},{2,18},{18,2},{3,19},{19,3},{4,20},{20... | collective-permute-start | bytes 1966088 | tf_op jit(solution)/shard_map/ppermute | solution.py:243
  706.2 18.4 %collective-permute-start.50 = (bf16[4,2,64,640]{3,2,0,1:T(8,128)(2,1)S(1)}, bf16[4,2,64,640]{3,2,0,1:T(8,128)(2,1)S(1)}, u32[]{:S(2)}, u32[]{:S(2)}) collective-permute-start(bf16[4,2,64,640]{3,2,0,1:T(8,128)(2,1)S(1)} %dynamic-slice_bitcast_fusion.3), channel_id=1, source_target_pairs={{0,16},{16,0},{1,17},{17,1},{2,18},{18,2},{3,19},{19,3},{4,20},{20... | collective-permute-start | bytes 1966088 | tf_op jit(solution)/shard_map/ppermute | solution.py:243
  709.1 22.6 %collective-permute-start.46 = (bf16[4,64,1280]{2,1,0:T(8,128)(2,1)S(1)}, bf16[4,64,1280]{2,1,0:T(8,128)(2,1)S(1)}, u32[]{:S(2)}, u32[]{:S(2)}) collective-permute-start(bf16[4,64,1280]{2,1,0:T(8,128)(2,1)S(1)} %dynamic-slice_bitcast_fusion.4), channel_id=1, source_target_pairs={{0,1},{1,0},{2,3},{3,2},{4,5},{5,4},{6,7},{7,6},{8,9},{9,8},{10,11... | collective-permute-start | bytes 1966088 | tf_op jit(solution)/shard_map/ppermute | solution.py:243
  712.6 20.1 %collective-permute-start.62 = (bf16[40,2048]{1,0:T(8,128)(2,1)S(1)}, bf16[40,2048]{1,0:T(8,128)(2,1)S(1)}, u32[]{:S(2)}, u32[]{:S(2)}) collective-permute-start(bf16[40,2048]{1,0:T(8,128)(2,1)S(1)} %get-tuple-element.150), channel_id=1, source_target_pairs={{0,2},{2,4},{4,6},{6,0},{1,3},{3,5},{5,7},{7,1},{8,10},{10,12},{12... | collective-permute-start | bytes 491528 | tf_op jit(solution)/shard_map/ppermute | solution.py:243
  715.2 22.1 %collective-permute-start.63 = (bf16[40,2048]{1,0:T(8,128)(2,1)S(1)}, bf16[40,2048]{1,0:T(8,128)(2,1)S(1)}, u32[]{:S(2)}, u32[]{:S(2)}) collective-permute-start(bf16[40,2048]{1,0:T(8,128)(2,1)S(1)} %get-tuple-element.152), channel_id=1, source_target_pairs={{0,4},{2,6},{4,0},{6,2},{1,5},{3,7},{5,1},{7,3},{8,12},{10,14},{12... | collective-permute-start | bytes 491528 | tf_op jit(solution)/shard_map/ppermute | solution.py:243
  717.4 33.5 %collective-permute-start.64 = (bf16[40,2048]{1,0:T(8,128)(2,1)S(1)}, bf16[40,2048]{1,0:T(8,128)(2,1)S(1)}, u32[]{:S(2)}, u32[]{:S(2)}) collective-permute-start(bf16[40,2048]{1,0:T(8,128)(2,1)S(1)} %get-tuple-element.151), channel_id=1, source_target_pairs={{0,6},{2,0},{4,2},{6,4},{1,7},{3,1},{5,3},{7,5},{8,14},{10,8},{12,... | collective-permute-start | bytes 491528 | tf_op jit(solution)/shard_map/ppermute | solution.py:243
  724.8 32.4 %collective-permute-start.51 = (bf16[4,64,640]{2,1,0:T(8,128)(2,1)S(1)}, bf16[4,64,640]{2,1,0:T(8,128)(2,1)S(1)}, u32[]{:S(2)}, u32[]{:S(2)}) collective-permute-start(bf16[4,64,640]{2,1,0:T(8,128)(2,1)S(1)} %dynamic-slice_bitcast_fusion.13), channel_id=1, source_target_pairs={{0,1},{1,0},{2,3},{3,2},{4,5},{5,4},{6,7},{7,6},{8,9},{9,8},{10,11... | collective-permute-start | bytes 983048 | tf_op jit(solution)/shard_map/ppermute | solution.py:243
  732.7 22.1 %collective-permute-start.47 = (bf16[64,1280]{1,0:T(8,128)(2,1)}, bf16[64,1280]{1,0:T(8,128)(2,1)S(1)}, u32[]{:S(2)}, u32[]{:S(2)}) collective-permute-start(bf16[64,1280]{1,0:T(8,128)(2,1)} %get-tuple-element.153), channel_id=1, source_target_pairs={{0,2},{2,4},{4,6},{6,0},{1,3},{3,5},{5,7},{7,1},{8,10},{10,12},{12... | collective-permute-start | bytes 491528 | tf_op jit(solution)/shard_map/ppermute | solution.py:243
  732.7 22.1 %collective-permute-start.48 = (bf16[64,1280]{1,0:T(8,128)(2,1)}, bf16[64,1280]{1,0:T(8,128)(2,1)S(1)}, u32[]{:S(2)}, u32[]{:S(2)}) collective-permute-start(bf16[64,1280]{1,0:T(8,128)(2,1)} %get-tuple-element.155), channel_id=1, source_target_pairs={{0,4},{2,6},{4,0},{6,2},{1,5},{3,7},{5,1},{7,3},{8,12},{10,14},{12... | collective-permute-start | bytes 491528 | tf_op jit(solution)/shard_map/ppermute | solution.py:243
  737.3 18.0 %collective-permute-start.49 = (bf16[64,1280]{1,0:T(8,128)(2,1)}, bf16[64,1280]{1,0:T(8,128)(2,1)}, u32[]{:S(2)}, u32[]{:S(2)}) collective-permute-start(bf16[64,1280]{1,0:T(8,128)(2,1)} %get-tuple-element.154), channel_id=1, source_target_pairs={{0,6},{2,0},{4,2},{6,4},{1,7},{3,1},{5,3},{7,5},{8,14},{10,8},{12,... | collective-permute-start | bytes 491528 | tf_op jit(solution)/shard_map/ppermute | solution.py:243
  753.0 12.2 %collective-permute-start.65 = (bf16[2,64,1792]{2,1,0:T(8,128)(2,1)S(1)}, bf16[2,64,1792]{2,1,0:T(8,128)(2,1)S(1)}, u32[]{:S(2)}, u32[]{:S(2)}) collective-permute-start(bf16[2,64,1792]{2,1,0:T(8,128)(2,1)S(1)} %get-tuple-element.128), channel_id=1, source_target_pairs={{0,16},{16,0},{1,17},{17,1},{2,18},{18,2},{3,19},{19,3},{4,20},{20... | collective-permute-start | bytes 1376264 | tf_op jit(solution)/shard_map/ppermute | solution.py:243
  757.4 9.9 %collective-permute-start.52 = (bf16[64,640]{1,0:T(8,128)(2,1)S(1)}, bf16[64,640]{1,0:T(8,128)(2,1)S(1)}, u32[]{:S(2)}, u32[]{:S(2)}) collective-permute-start(bf16[64,640]{1,0:T(8,128)(2,1)S(1)} %get-tuple-element.160), channel_id=1, source_target_pairs={{0,2},{2,4},{4,6},{6,0},{1,3},{3,5},{5,7},{7,1},{8,10},{10,12},{12... | collective-permute-start | bytes 245768 | tf_op jit(solution)/shard_map/ppermute | solution.py:243
  (132 other events, 2049.6 us)
Sparse Core Ops, SparseCore 0:
  10.8 82.4 all-gather.3
  96.1 154.6 all-gather.5
  253.0 63.0 all-gather.7
  395.2 84.8 reduce-scatter.7
  486.8 153.8 reduce-scatter.3
  644.2 107.1 reduce-scatter.5

commit v6 on v5

--- a/solution.py
+++ b/solution.py
@@ -532,12 +532,15 @@
 
     query_grads, carried = [], []
     for b in range(batches):
-        grad_mixed_t = dot(w_out_all, low_grads[b], 1, 1).astype(bf16)
+        low = after(low_grads[b], gate_total) if b > 0 else low_grads[b]
+        grad_mixed_t = dot(w_out_all, low, 1, 1).astype(bf16)
         dq_t, dkv = attend_backward(
             xs, metas[b], starts[b][None, :], query_t, b, windows[b], grad_mixed_t, mixed[b],
             lses[b],
         )
         query_grads.append(dq_t)
+        if b == 0:
+            gate_total = token_sum(normed2_all, [after(gate_grads[0], dq_t)] + gate_grads[1:])
         groups = dkv.reshape(back_groups + 1, xs, 2 * KV_WIDTH, local)
         first = (move.hop(groups[0], "z", -1).astype(f32) + groups[1].astype(f32)).astype(bf16)
         carried.append([first] + [groups[k] for k in range(2, back_groups + 1)])
@@ -546,7 +549,6 @@
     out_cores = split_cores(
         matmul(jnp.concatenate(mixed, axis=1), jnp.concatenate(low_grads, axis=0)), w_out.shape[0]
     )
-    gate_total = token_sum(normed2_all, [after(gate_grads[0], held)] + gate_grads[1:])
     gate_sum = scatter_columns(gate_total)
 
     query_grad, gq_gain = head_backward(

time: 797 us -> 791 us (level)
    ppermute x56, waiting for transfers between devices: 166 us -> 155 us  [shift(): lax.ppermute(value, axis, [(i, (i + step) % size) for i in range(size)])]
    unnamed x255 -> x241, local copies, waits for them, and re-layouts: 16.7 us -> 15.2 us
  transfers between devices with their start and end apart: 73 -> 73, of which waited for: 27 -> 26; matrix products, arithmetic and copies ran while one was open for 40% -> 40% of each run, Pallas kernels for 5% -> 5%
where the time goes in v6:
time: 791 us; the launch traced here: 780 us
  waiting for transfers between devices  282 us (36%)
  matrix products  165 us (21%)
  starting transfers between devices  108 us (14%)
  other arithmetic  98.4 us (12%)
  local copies, waits for them, and re-layouts  68.3 us (9%)
  Pallas kernels  36.4 us (5%)
  between operations  22.1 us (3%)
    dot_general x26, matrix products, dot(): lax.dot_general(left, right, (((left_dim,), (right_dim,)), ((), ())), pre...  165 us
    ppermute x56, waiting for transfers between devices, shift(): lax.ppermute(value, axis, [(i, (i + step) % size) for i in range(size)])  155 us
    ppermute x6, waiting for transfers between devices, hop(): return lax.ppermute(value, axis, pairs)  110 us
    ppermute x56, starting transfers between devices, shift(): lax.ppermute(value, axis, [(i, (i + step) % size) for i in range(size)])  75.2 us
    ppermute x6, starting transfers between devices, hop(): return lax.ppermute(value, axis, pairs)  20.8 us
    pallas_call x2, Pallas kernels, attend_backward(): pl.pallas_call(functools.partial(backward_kernel, xs), name='attend_backw...  20.6 us
    pallas_call x2, Pallas kernels, attend_forward(): pl.pallas_call(functools.partial(forward_kernel, xs), name='attend_forwar...  15.9 us
  transfers between devices with their start and end apart: 73, of which 26 were waited for; matrix products, arithmetic and copies ran while one was open for 40% of the time, Pallas kernels for 5%

profile of v6, /device:TPU:0, one launch (start us, length us, event | category | flops | bytes accessed | tf_op | source)
XLA Modules:
  0.0 780.0 jit_solution(18122437484024872721)
XLA Ops:
  9.5 3.1 collective-permute-start
  12.6 2.6 collective-permute-start.1
  24.8 8.1 %collective-permute-done.3 = bf16[4,64,640]{2,1,0:T(8,128)(2,1)S(1)} collective-permute-done((bf16[4,64,640]{2,1,0:T(8,128)(2,1)S(1)}, bf16[4,64,640]{2,1,0:T(8,128)(2,1)S(1)}, u32[]{:S(2)}, u32[]{:S(2)}) %collective-permute-start.3) | collective-permute-done | bytes 327712 | tf_op jit(solution)/shard_map/ppermute | solution.py:243
  34.9 12.5 %collective-permute-done.21 = bf16[2,64,1792]{2,1,0:T(8,128)(2,1)S(1)} collective-permute-done((bf16[2,64,1792]{2,1,0:T(8,128)(2,1)S(1)}, bf16[2,64,1792]{2,1,0:T(8,128)(2,1)S(1)}, u32[]{:S(2)}, u32[]{:S(2)}) %collective-permute-start.21) | collective-permute-done | bytes 458784 | tf_op jit(solution)/shard_map/ppermute | solution.py:243
  48.8 2.6 collective-permute-start.12
  60.7 5.7 collective-permute-done.12
  69.1 12.9 %collective-permute-done.4 = bf16[4,2,64,640]{3,2,1,0:T(8,128)(2,1)S(1)} collective-permute-done((bf16[4,2,64,640]{3,2,1,0:T(8,128)(2,1)S(1)}, bf16[4,2,64,640]{3,2,1,0:T(8,128)(2,1)S(1)}, u32[]{:S(2)}, u32[]{:S(2)}) %collective-permute-start.4) | collective-permute-done | bytes 655392 | tf_op jit(solution)/shard_map/ppermute | solution.py:243
  82.7 7.5 collective-permute-done.14
  95.6 3.6 collective-permute-start.6
  101.0 20.3 %collective-permute-done.6 = bf16[656,512]{1,0:T(8,128)(2,1)S(1)} collective-permute-done((bf16[656,512]{1,0:T(8,128)(2,1)S(1)}, bf16[656,512]{1,0:T(8,128)(2,1)S(1)}, u32[]{:S(2)}, u32[]{:S(2)}) %collective-permute-start.6) | collective-permute-done | bytes 671776 | tf_op jit(solution)/shard_map/ppermute | solution.py:248
  121.4 11.1 %collective-permute-start.7 = (bf16[656,512]{1,0:T(8,128)(2,1)S(1)}, bf16[656,512]{1,0:T(8,128)(2,1)S(1)}, u32[]{:S(2)}, u32[]{:S(2)}) collective-permute-start(bf16[656,512]{1,0:T(8,128)(2,1)S(1)} %collective-permute-done.6), channel_id=1, source_target_pairs={{0,2},{2,4},{4,6},{1,3},{3,5},{5,7},{8,10},{10,12},{12,14},{9,11},... | collective-permute-start | bytes 2015240 | tf_op jit(solution)/shard_map/ppermute | solution.py:248
  138.0 18.8 %collective-permute-done.7 = bf16[656,512]{1,0:T(8,128)(2,1)S(1)} collective-permute-done((bf16[656,512]{1,0:T(8,128)(2,1)S(1)}, bf16[656,512]{1,0:T(8,128)(2,1)S(1)}, u32[]{:S(2)}, u32[]{:S(2)}) %collective-permute-start.7) | collective-permute-done | bytes 671776 | tf_op jit(solution)/shard_map/ppermute | solution.py:248
  157.4 3.1 fusion.124
  162.0 24.7 %collective-permute-done.8 = bf16[656,512]{1,0:T(8,128)(2,1)S(1)} collective-permute-done((bf16[656,512]{1,0:T(8,128)(2,1)S(1)}, bf16[656,512]{1,0:T(8,128)(2,1)S(1)}, u32[]{:S(2)}, u32[]{:S(2)}) %collective-permute-start.8) | collective-permute-done | bytes 671776 | tf_op jit(solution)/shard_map/ppermute | solution.py:243
  186.8 22.3 %collective-permute-done.9 = bf16[656,512]{1,0:T(8,128)(2,1)S(1)} collective-permute-done((bf16[656,512]{1,0:T(8,128)(2,1)S(1)}, bf16[656,512]{1,0:T(8,128)(2,1)S(1)}, u32[]{:S(2)}, u32[]{:S(2)}) %collective-permute-start.9) | collective-permute-done | bytes 671776 | tf_op jit(solution)/shard_map/ppermute | solution.py:243
  232.1 4.6 broadcast_select_fusion
  236.8 7.7 attend_forward.2
  244.6 3.2 fusion.125
  247.8 4.8 multiply_reduce_fusion.6
  253.5 3.4 fusion.126
  256.9 3.3 fusion.127
  260.6 8.1 %attend_forward.3 = (bf16[1280,256]{1,0:T(8,128)(2,1)}, f32[5,4,256]{2,1,0:T(4,128)}) custom-call(s32[4]{0:T(128)} %add_add_fusion.1.meta, s32[256,1]{1,0:T(8,128)} %copy.59.start_ref, bf16[1280,512]{1,0:T(8,128)(2,1)} %bitcast.422, bf16[6,656,256]{2,1,0:T(8,128)(2,1)} %copy-done.75, bf16[6,656,256]{2,1,0:T(8,128)(2,1)} %copy-done.75), custom_call_target="tpu_custom_call" | custom-call | flops 4026531840 | bytes 4194304 | tf_op jit(solution)/shard_map/attend_forward/pallas_call | solution.py:153
  268.7 10.4 %collective-permute-done.17 = bf16[256,2048]{1,0:T(8,128)(2,1)} collective-permute-done((bf16[256,2048]{1,0:T(8,128)(2,1)S(1)}, bf16[256,2048]{1,0:T(8,128)(2,1)}, u32[]{:S(2)}, u32[]{:S(2)}) %collective-permute-start.17) | collective-permute-done | bytes 1048608 | tf_op jit(solution)/shard_map/ppermute | solution.py:243
  279.0 5.4 multiply_reduce_fusion.4
  287.5 14.9 %fusion.117 = f32[1024,1792]{1,0:T(8,128)} fusion(bf16[2048,1792]{1,0:T(8,128)(2,1)} %bitcast.441, bf16[256,2048]{1,0:T(8,128)(2,1)} %collective-permute-done.19, bf16[256,2048]{1,0:T(8,128)(2,1)} %collective-permute-done.18, bf16[256,2048]{1,0:T(8,128)(2,1)} %collective-permute-done.17, bf16[256,2048]{1,0:T(8,128)(2,1)S(1)} %multiply_convert_fusion.7), kind=kOutput, calls=%fused_computation.361 | convolution fusion | flops 7532969984 | bytes 18874368 | tf_op jit(solution)/shard_map/dot_general | solution.py:32
  302.4 13.7 %all-gather.8.cloned.1.call-done = bf16[896,2048]{1,0:T(8,128)(2,1)} async-done(((bf16[112,2048]{1,0:T(8,128)(2,1)}), bf16[896,2048]{1,0:T(8,128)(2,1)}) %all-gather.8.cloned.1.call-update) | async-done | bytes 3670032 | tf_op jit(solution)/shard_map/all_gather | solution.py:384
  316.1 11.8 %multiply_convert_fusion.4 = (bf16[1024,896]{1,0:T(8,128)(2,1)S(1)}, bf16[1024,896]{1,0:T(8,128)(2,1)S(1)}, bf16[1024,896]{1,0:T(8,128)(2,1)}) fusion(f32[1024,1792]{1,0:T(8,128)} %fusion.117, bf16[896,2048]{1,0:T(8,128)(2,1)} %all-gather.8.cloned.1.call-done, bf16[256,2048]{1,0:T(8,128)(2,1)} %get-tuple-element.110, ...), kind=kOutput, calls=%fused_computation.46 | convolution fusion | flops 3788636160 | bytes 20709376 | tf_op jit(solution)/shard_map/dot_general | solution.py:32
  329.7 8.2 %convolution_convert_fusion.3 = bf16[1024,2048]{1,0:T(8,128)(2,1)S(1)} fusion(bf16[2048,1792]{1,0:T(8,128)(2,1)S(1)} %bitcast.444, bf16[1024,896]{1,0:T(8,128)(2,1)S(1)} %get-tuple-element.63, bf16[1024,896]{1,0:T(8,128)(2,1)S(1)} %get-tuple-element.53), kind=kOutput, calls=%fused_computation.31 | convolution fusion | flops 7525629952 | bytes 15204352 | tf_op jit(solution)/shard_map/dot_general | solution.py:32
  340.0 6.6 fusion.62
  346.6 12.1 %fusion.116 = f32[1024,1792]{1,0:T(8,128)S(1)} fusion(bf16[2048,1792]{1,0:T(8,128)(2,1)} %bitcast.442, bf16[256,2048]{1,0:T(8,128)(2,1)S(1)} %collective-permute-done.31, bf16[256,2048]{1,0:T(8,128)(2,1)} %collective-permute-done.30, bf16[256,2048]{1,0:T(8,128)(2,1)} %collective-permute-done.29, bf16[256,2048]{1,0:T(8,128)(2,1)} %multiply_convert_fusion.6), kind=kOutput, calls=%fused_computation.360 | convolution fusion | flops 7532969984 | bytes 18874368 | tf_op jit(solution)/shard_map/dot_general | solution.py:32
  366.5 12.0 %convolution_convert_fusion.2 = bf16[1024,2048]{1,0:T(8,128)(2,1)S(1)} fusion(bf16[2048,1792]{1,0:T(8,128)(2,1)} %bitcast.443, bf16[1024,896]{1,0:T(8,128)(2,1)S(1)} %get-tuple-element.76, bf16[1024,896]{1,0:T(8,128)(2,1)S(1)} %get-tuple-element.75), kind=kOutput, calls=%fused_computation.30 | convolution fusion | flops 7525629952 | bytes 15204352 | tf_op jit(solution)/shard_map/dot_general | solution.py:32
  381.2 6.1 fusion.61
  387.4 7.7 add_convert_fusion
  395.1 10.5 %fusion.114 = f32[2048,896]{1,0:T(8,128)} fusion(bf16[1024,896]{1,0:T(8,128)(2,1)} %copy-done.41, bf16[256,2048]{1,0:T(8,128)(2,1)} %copy-done.101, bf16[256,2048]{1,0:T(8,128)(2,1)} %collective-permute-done.30, bf16[256,2048]{1,0:T(8,128)(2,1)} %collective-permute-done.29, bf16[256,2048]{1,0:T(8,128)(2,1)} %multiply_convert_fusion.6), kind=kOutput, calls=%fused_computation.358 | convolution fusion | flops 3774873600 | bytes 13369344 | tf_op jit(solution)/shard_map/dot_general | solution.py:32
  408.9 9.8 %fusion.115 = f32[2048,896]{1,0:T(8,128)} fusion(bf16[1024,896]{1,0:T(8,128)(2,1)S(1)} %copy-done.40, bf16[256,2048]{1,0:T(8,128)(2,1)S(1)} %copy-done.102, bf16[256,2048]{1,0:T(8,128)(2,1)} %collective-permute-done.30, bf16[256,2048]{1,0:T(8,128)(2,1)} %collective-permute-done.29, bf16[256,2048]{1,0:T(8,128)(2,1)} %multiply_convert_fusion.6), kind=kOutput, calls=%fused_computation.359 | convolution fusion | flops 3774873600 | bytes 13369344 | tf_op jit(solution)/shard_map/dot_general | solution.py:32
  419.2 14.6 %collective-permute-done.35 = bf16[256,2048]{1,0:T(8,128)(2,1)S(1)} collective-permute-done((bf16[256,2048]{1,0:T(8,128)(2,1)S(1)}, bf16[256,2048]{1,0:T(8,128)(2,1)S(1)}, u32[]{:S(2)}, u32[]{:S(2)}) %collective-permute-start.35) | collective-permute-done | bytes 1048608 | tf_op jit(solution)/shard_map/ppermute | solution.py:243
  434.4 4.8 fusion.118
  441.6 10.2 %attend_backward.2 = (bf16[1280,256]{1,0:T(8,128)(2,1)}, bf16[6,2,320,256]{3,2,1,0:T(8,128)(2,1)}) custom-call(s32[4]{0:T(128)} %add_add_fusion.meta, s32[1,256]{1,0:T(1,128)} %bitcast.437, bf16[1280,512]{1,0:T(8,128)(2,1)} %bitcast.423, bf16[6,656,256]{2,1,0:T(8,128)(2,1)} %copy-done.74, bf16[6,656,256]{2,1,0:T(8,128)(2,1)} %copy-done.74, ...), custom_call_target="tpu_custom_call" | custom-call | flops 10066329600 | bytes 8388608 | tf_op jit(solution)/shard_map/attend_backward/pallas_call | solution.py:190
  451.9 2.8 fusion.128
  456.3 11.6 %add_convert_fusion.2 = bf16[2048,896]{1,0:T(8,128)(2,1)} fusion(f32[2048,896]{1,0:T(8,128)} %fusion.115, bf16[1024,896]{1,0:T(8,128)(2,1)S(1)} %copy-done.109, bf16[256,2048]{1,0:T(8,128)(2,1)} %collective-permute-done.19, bf16[256,2048]{1,0:T(8,128)(2,1)} %collective-permute-done.18, bf16[256,2048]{1,0:T(8,128)(2,1)} %collective-permute-done.17, ...), kind=kOutput, calls=%fused_computation.4 | convolution fusion | flops 3778543616 | bytes 17039360 | tf_op jit(solution)/shard_map/dot_general | solution.py:32
  467.9 8.6 %add_convert_fusion.1 = bf16[2048,896]{1,0:T(8,128)(2,1)} fusion(f32[2048,896]{1,0:T(8,128)S(1)} %bitcast.446, bf16[1024,896]{1,0:T(8,128)(2,1)S(1)} %copy-done.107, bf16[256,2048]{1,0:T(8,128)(2,1)} %collective-permute-done.19, bf16[256,2048]{1,0:T(8,128)(2,1)} %collective-permute-done.18, bf16[256,2048]{1,0:T(8,128)(2,1)} %collective-permute-done.17, ...), kind=kOutput, calls=%fused_computation.3 | convolution fusion | flops 3778543616 | bytes 17039360 | tf_op jit(solution)/shard_map/dot_general | solution.py:32
  477.0 5.2 fusion.24.go_ref
  482.2 10.3 %attend_backward.3 = (bf16[1280,256]{1,0:T(8,128)(2,1)}, bf16[6,2,320,256]{3,2,1,0:T(8,128)(2,1)}) custom-call(s32[4]{0:T(128)} %add_add_fusion.1.meta, s32[1,256]{1,0:T(1,128)} %bitcast.435, bf16[1280,512]{1,0:T(8,128)(2,1)} %bitcast.424, bf16[6,656,256]{2,1,0:T(8,128)(2,1)} %copy-done.75, bf16[6,656,256]{2,1,0:T(8,128)(2,1)} %copy-done.75, ...), custom_call_target="tpu_custom_call" | custom-call | flops 10066329600 | bytes 8388608 | tf_op jit(solution)/shard_map/attend_backward/pallas_call | solution.py:190
  498.6 3.2 convolution_convert_fusion
  509.0 4.7 convolution_convert_fusion.5
  516.2 4.7 convolution_convert_fusion.4
  527.0 3.1 convolution_convert_fusion.1
  530.1 37.3 %collective-permute-done.37 = bf16[2,640,256]{2,1,0:T(8,128)(2,1)S(1)} collective-permute-done((bf16[2,640,256]{2,1,0:T(8,128)(2,1)S(1)}, bf16[2,640,256]{2,1,0:T(8,128)(2,1)S(1)}, u32[]{:S(2)}, u32[]{:S(2)}) %collective-permute-start.37) | collective-permute-done | bytes 655392 | tf_op jit(solution)/shard_map/ppermute | solution.py:248
  575.8 2.8 collective-permute-done.38
  582.2 18.3 %collective-permute-start.28 = (bf16[256,2048]{1,0:T(8,128)(2,1)S(1)}, bf16[256,2048]{1,0:T(8,128)(2,1)S(1)}, u32[]{:S(2)}, u32[]{:S(2)}) collective-permute-start(bf16[256,2048]{1,0:T(8,128)(2,1)S(1)} %fusion.50), channel_id=1, source_target_pairs={{0,16},{16,0},{1,17},{17,1},{2,18},{18,2},{3,19},{19,3},{4,20},{20... | collective-permute-start | bytes 3145736 | tf_op jit(solution)/shard_map/ppermute | solution.py:243
  604.6 2.7 fusion
  614.7 9.8 %collective-permute-done.28 = bf16[256,2048]{1,0:T(8,128)(2,1)S(1)} collective-permute-done((bf16[256,2048]{1,0:T(8,128)(2,1)S(1)}, bf16[256,2048]{1,0:T(8,128)(2,1)S(1)}, u32[]{:S(2)}, u32[]{:S(2)}) %collective-permute-start.28) | collective-permute-done | bytes 1048608 | tf_op jit(solution)/shard_map/ppermute | solution.py:243
  625.1 33.2 %collective-permute-done.42 = bf16[2,640,256]{2,1,0:T(8,128)(2,1)S(1)} collective-permute-done((bf16[2,640,256]{2,1,0:T(8,128)(2,1)S(1)}, bf16[2,640,256]{2,1,0:T(8,128)(2,1)S(1)}, u32[]{:S(2)}, u32[]{:S(2)}) %collective-permute-start.42) | collective-permute-done | bytes 655392 | tf_op jit(solution)/shard_map/ppermute | solution.py:248
  662.0 10.7 %collective-permute-done.43 = bf16[640,256]{1,0:T(8,128)(2,1)S(1)} collective-permute-done((bf16[640,256]{1,0:T(8,128)(2,1)S(1)}, bf16[640,256]{1,0:T(8,128)(2,1)S(1)}, u32[]{:S(2)}, u32[]{:S(2)}) %collective-permute-start.43) | collective-permute-done | bytes 327712 | tf_op jit(solution)/shard_map/ppermute | solution.py:243
  681.4 3.2 fusion.7
  684.6 2.8 fusion.6
  687.8 3.6 fusion.54
  692.9 2.9 fusion.21
  703.2 7.5 collective-permute-start.57
  721.0 5.4 collective-permute-start.62
  732.3 4.4 collective-permute-done.46
  747.3 4.8 collective-permute-done.48
  754.2 3.6 collective-permute-start.52
  769.6 3.1 broadcast_multiply_fusion
  (550 shorter events, 194.5 us)
Async XLA Ops:
  7.2 240.6 %all-gather.4.cloned.1.call-start = ((), (), s32[]{:S(2)}) async-start(), calls=%async_computation.3 | async-start | bytes 5406720 | tf_op jit(solution)/shard_map/all_gather | solution.py:442
  7.9 279.6 %all-gather.6.cloned.1.call-start = ((), (), s32[]{:S(2)}) async-start(), calls=%async_computation.4 | async-start | bytes 8257536 | tf_op jit(solution)/shard_map/all_gather | solution.py:383
  9.5 13.3 %collective-permute-start = (bf16[64,640]{1,0:T(8,128)(2,1)S(1)}, bf16[64,640]{1,0:T(8,128)(2,1)S(1)}, u32[]{:S(2)}, u32[]{:S(2)}) collective-permute-start(bf16[64,640]{1,0:T(8,128)(2,1)S(1)} %fusion.89), channel_id=1, source_target_pairs={{0,2},{2,4},{4,6},{6,0},{1,3},{3,5},{5,7},{7,1},{8,10},{10,12},{12... | collective-permute-start | bytes 245768 | tf_op jit(solution)/shard_map/ppermute | solution.py:243
  12.6 10.2 %collective-permute-start.1 = (bf16[64,640]{1,0:T(8,128)(2,1)S(1)}, bf16[64,640]{1,0:T(8,128)(2,1)S(1)}, u32[]{:S(2)}, u32[]{:S(2)}) collective-permute-start(bf16[64,640]{1,0:T(8,128)(2,1)S(1)} %fusion.89), channel_id=1, source_target_pairs={{0,4},{2,6},{4,0},{6,2},{1,5},{3,7},{5,1},{7,3},{8,12},{10,14},{12... | collective-permute-start | bytes 245768 | tf_op jit(solution)/shard_map/ppermute | solution.py:243
  23.0 9.9 %collective-permute-start.3 = (bf16[4,64,640]{2,1,0:T(8,128)(2,1)S(1)}, bf16[4,64,640]{2,1,0:T(8,128)(2,1)S(1)}, u32[]{:S(2)}, u32[]{:S(2)}) collective-permute-start(bf16[4,64,640]{2,1,0:T(8,128)(2,1)S(1)} %select_select_fusion.1), channel_id=1, source_target_pairs={{0,1},{1,0},{2,3},{3,2},{4,5},{5,4},{6,7},{7,6},{8,9},{9,8},{10,11... | collective-permute-start | bytes 983048 | tf_op jit(solution)/shard_map/ppermute | solution.py:243
  24.6 8.4 %collective-permute-start.20 = (bf16[64,2,1792]{2,0,1:T(8,128)(2,1)S(1)}, bf16[64,2,1792]{2,0,1:T(8,128)(2,1)S(1)}, u32[]{:S(2)}, u32[]{:S(2)}) collective-permute-start(bf16[64,2,1792]{2,0,1:T(8,128)(2,1)S(1)} %get-tuple-element.134), channel_id=1, source_target_pairs={{0,8},{8,0},{1,9},{9,1},{2,10},{10,2},{3,11},{11,3},{4,12},{12,4},... | collective-permute-start | bytes 1376264 | tf_op jit(solution)/shard_map/ppermute | solution.py:243
  33.3 14.1 %collective-permute-start.21 = (bf16[2,64,1792]{2,1,0:T(8,128)(2,1)S(1)}, bf16[2,64,1792]{2,1,0:T(8,128)(2,1)S(1)}, u32[]{:S(2)}, u32[]{:S(2)}) collective-permute-start(bf16[2,64,1792]{2,1,0:T(8,128)(2,1)S(1)} %get-tuple-element.132), channel_id=1, source_target_pairs={{0,16},{16,0},{1,17},{17,1},{2,18},{18,2},{3,19},{19,3},{4,20},{20... | collective-permute-start | bytes 1376264 | tf_op jit(solution)/shard_map/ppermute | solution.py:243
  48.6 267.5 %all-gather.8.cloned.1.call-start = ((), (), s32[]{:S(2)}) async-start(), calls=%async_computation.5 | async-start | bytes 4128768 | tf_op jit(solution)/shard_map/all_gather | solution.py:384
  48.8 11.9 %collective-permute-start.11 = (bf16[64,1280]{1,0:T(8,128)(2,1)S(1)}, bf16[64,1280]{1,0:T(8,128)(2,1)S(1)}, u32[]{:S(2)}, u32[]{:S(2)}) collective-permute-start(bf16[64,1280]{1,0:T(8,128)(2,1)S(1)} %fusion.83), channel_id=1, source_target_pairs={{0,6},{2,0},{4,2},{6,4},{1,7},{3,1},{5,3},{7,5},{8,14},{10,8},{12,... | collective-permute-start | bytes 491528 | tf_op jit(solution)/shard_map/ppermute | solution.py:243
  48.8 17.5 %collective-permute-start.12 = (bf16[64,1280]{1,0:T(8,128)(2,1)S(1)}, bf16[64,1280]{1,0:T(8,128)(2,1)S(1)}, u32[]{:S(2)}, u32[]{:S(2)}) collective-permute-start(bf16[64,1280]{1,0:T(8,128)(2,1)S(1)} %fusion.83), channel_id=1, source_target_pairs={{0,4},{2,6},{4,0},{6,2},{1,5},{3,7},{5,1},{7,3},{8,12},{10,14},{12... | collective-permute-start | bytes 491528 | tf_op jit(solution)/shard_map/ppermute | solution.py:243
  51.5 14.9 %collective-permute-start.13 = (bf16[64,1280]{1,0:T(8,128)(2,1)S(1)}, bf16[64,1280]{1,0:T(8,128)(2,1)}, u32[]{:S(2)}, u32[]{:S(2)}) collective-permute-start(bf16[64,1280]{1,0:T(8,128)(2,1)S(1)} %fusion.83), channel_id=1, source_target_pairs={{0,2},{2,4},{4,6},{6,0},{1,3},{3,5},{5,7},{7,1},{8,10},{10,12},{12... | collective-permute-start | bytes 491528 | tf_op jit(solution)/shard_map/ppermute | solution.py:243
  51.5 660.9 %reduce-scatter.8.cloned.1.call-start = ((), (), s32[]{:S(2)}) async-start(), calls=%async_computation.8 | async-start | bytes 4128768 | tf_op jit(solution)/shard_map/reduce_scatter | solution.py:527
  58.8 23.1 %collective-permute-start.4 = (bf16[4,2,64,640]{3,2,1,0:T(8,128)(2,1)S(1)}, bf16[4,2,64,640]{3,2,1,0:T(8,128)(2,1)S(1)}, u32[]{:S(2)}, u32[]{:S(2)}) collective-permute-start(bf16[4,2,64,640]{3,2,1,0:T(8,128)(2,1)S(1)} %broadcast_select_fusion.9), channel_id=1, source_target_pairs={{0,16},{16,0},{1,17},{17,1},{2,18},{18,2},{3,19},{19,3},{4,20},{20... | collective-permute-start | bytes 1966088 | tf_op jit(solution)/shard_map/ppermute | solution.py:243
  67.5 22.7 %collective-permute-start.14 = (bf16[4,64,1280]{2,1,0:T(8,128)(2,1)S(1)}, bf16[4,64,1280]{2,1,0:T(8,128)(2,1)S(1)}, u32[]{:S(2)}, u32[]{:S(2)}) collective-permute-start(bf16[4,64,1280]{2,1,0:T(8,128)(2,1)S(1)} %select_select_fusion), channel_id=1, source_target_pairs={{0,1},{1,0},{2,3},{3,2},{4,5},{5,4},{6,7},{7,6},{8,9},{9,8},{10,11... | collective-permute-start | bytes 1966088 | tf_op jit(solution)/shard_map/ppermute | solution.py:243
  82.2 9.7 %collective-permute-start.5 = (bf16[2,4,2,64,640]{4,3,2,1,0:T(8,128)(2,1)S(1)}, bf16[2,4,2,64,640]{4,3,2,1,0:T(8,128)(2,1)S(1)}, u32[]{:S(2)}, u32[]{:S(2)}) collective-permute-start(bf16[2,4,2,64,640]{4,3,2,1,0:T(8,128)(2,1)S(1)} %broadcast_select_fusion.6), channel_id=1, source_target_pairs={{0,8},{8,0},{1,9},{9,1},{2,10},{10,2},{3,11},{11,3},{4,12},{12,4},... | collective-permute-start | bytes 3932168 | tf_op jit(solution)/shard_map/ppermute | solution.py:243
  90.4 45.3 %collective-permute-start.15 = (bf16[4,2,64,1280]{3,2,1,0:T(8,128)(2,1)S(1)}, bf16[4,2,64,1280]{3,2,1,0:T(8,128)(2,1)S(1)}, u32[]{:S(2)}, u32[]{:S(2)}) collective-permute-start(bf16[4,2,64,1280]{3,2,1,0:T(8,128)(2,1)S(1)} %broadcast_select_fusion.5), channel_id=1, source_target_pairs={{0,16},{16,0},{1,17},{17,1},{2,18},{18,2},{3,19},{19,3},{4,20},{20... | collective-permute-start | bytes 3932168 | tf_op jit(solution)/shard_map/ppermute | solution.py:243
  95.6 25.8 %collective-permute-start.6 = (bf16[656,512]{1,0:T(8,128)(2,1)S(1)}, bf16[656,512]{1,0:T(8,128)(2,1)S(1)}, u32[]{:S(2)}, u32[]{:S(2)}) collective-permute-start(bf16[656,512]{1,0:T(8,128)(2,1)S(1)} %pad_maximum_fusion.16), channel_id=1, source_target_pairs={{0,2},{2,4},{4,6},{1,3},{3,5},{5,7},{8,10},{10,12},{12,14},{9,11},... | collective-permute-start | bytes 2015240 | tf_op jit(solution)/shard_map/ppermute | solution.py:248
  121.4 35.4 %collective-permute-start.7 = (bf16[656,512]{1,0:T(8,128)(2,1)S(1)}, bf16[656,512]{1,0:T(8,128)(2,1)S(1)}, u32[]{:S(2)}, u32[]{:S(2)}) collective-permute-start(bf16[656,512]{1,0:T(8,128)(2,1)S(1)} %collective-permute-done.6), channel_id=1, source_target_pairs={{0,2},{2,4},{4,6},{1,3},{3,5},{5,7},{8,10},{10,12},{12,14},{9,11},... | collective-permute-start | bytes 2015240 | tf_op jit(solution)/shard_map/ppermute | solution.py:248
  136.0 86.4 %collective-permute-start.16 = (bf16[2,4,2,64,1280]{4,3,2,1,0:T(8,128)(2,1)S(1)}, bf16[2,4,2,64,1280]{4,3,2,1,0:T(8,128)(2,1)}, u32[]{:S(2)}, u32[]{:S(2)}) collective-permute-start(bf16[2,4,2,64,1280]{4,3,2,1,0:T(8,128)(2,1)S(1)} %broadcast_select_fusion.1), channel_id=1, source_target_pairs={{0,8},{8,0},{1,9},{9,1},{2,10},{10,2},{3,11},{11,3},{4,12},{12,4},... | collective-permute-start | bytes 7864328 | tf_op jit(solution)/shard_map/ppermute | solution.py:243
  136.1 73.0 %collective-permute-start.10 = (bf16[656,512]{1,0:T(8,128)(2,1)S(1)}, bf16[656,512]{1,0:T(8,128)(2,1)S(1)}, u32[]{:S(2)}, u32[]{:S(2)}) collective-permute-start(bf16[656,512]{1,0:T(8,128)(2,1)S(1)} %pad_maximum_fusion.16), channel_id=1, source_target_pairs={{0,1},{1,0},{2,3},{3,2},{4,5},{5,4},{6,7},{7,6},{8,9},{9,8},{10,11... | collective-permute-start | bytes 2015240 | tf_op jit(solution)/shard_map/ppermute | solution.py:243
  138.0 106.5 %collective-permute-start.22 = (bf16[512,2048]{1,0:T(8,128)(2,1)}, bf16[512,2048]{1,0:T(8,128)(2,1)}, u32[]{:S(2)}, u32[]{:S(2)}) collective-permute-start(bf16[512,2048]{1,0:T(8,128)(2,1)} %pad_maximum_fusion.6), channel_id=1, source_target_pairs={{0,16},{16,0},{1,17},{17,1},{2,18},{18,2},{3,19},{19,3},{4,20},{20... | collective-permute-start | bytes 6291464 | tf_op jit(solution)/shard_map/ppermute | solution.py:243
  156.8 29.8 %collective-permute-start.8 = (bf16[656,512]{1,0:T(8,128)(2,1)S(1)}, bf16[656,512]{1,0:T(8,128)(2,1)S(1)}, u32[]{:S(2)}, u32[]{:S(2)}) collective-permute-start(bf16[656,512]{1,0:T(8,128)(2,1)S(1)} %collective-permute-done.7), channel_id=1, source_target_pairs={{0,1},{1,0},{2,3},{3,2},{4,5},{5,4},{6,7},{7,6},{8,9},{9,8},{10,11... | collective-permute-start | bytes 2015240 | tf_op jit(solution)/shard_map/ppermute | solution.py:243
  160.5 48.5 %collective-permute-start.9 = (bf16[656,512]{1,0:T(8,128)(2,1)S(1)}, bf16[656,512]{1,0:T(8,128)(2,1)S(1)}, u32[]{:S(2)}, u32[]{:S(2)}) collective-permute-start(bf16[656,512]{1,0:T(8,128)(2,1)S(1)} %collective-permute-done.6), channel_id=1, source_target_pairs={{0,1},{1,0},{2,3},{3,2},{4,5},{5,4},{6,7},{7,6},{8,9},{9,8},{10,11... | collective-permute-start | bytes 2015240 | tf_op jit(solution)/shard_map/ppermute | solution.py:243
  186.7 66.8 %collective-permute-start.23 = (bf16[512,2048]{1,0:T(8,128)(2,1)}, bf16[512,2048]{1,0:T(8,128)(2,1)}, u32[]{:S(2)}, u32[]{:S(2)}) collective-permute-start(bf16[512,2048]{1,0:T(8,128)(2,1)} %pad_maximum_fusion.6), channel_id=1, source_target_pairs={{0,8},{8,0},{1,9},{9,1},{2,10},{10,2},{3,11},{11,3},{4,12},{12,4},... | collective-permute-start | bytes 6291464 | tf_op jit(solution)/shard_map/ppermute | solution.py:243
  244.5 12.3 %collective-permute-start.24 = (bf16[512,2048]{1,0:T(8,128)(2,1)}, bf16[512,2048]{1,0:T(8,128)(2,1)}, u32[]{:S(2)}, u32[]{:S(2)}) collective-permute-start(bf16[512,2048]{1,0:T(8,128)(2,1)} %collective-permute-done.22), channel_id=1, source_target_pairs={{0,8},{8,0},{1,9},{9,1},{2,10},{10,2},{3,11},{11,3},{4,12},{12,4},... | collective-permute-start | bytes 6291464 | tf_op jit(solution)/shard_map/ppermute | solution.py:243
  253.4 25.7 %collective-permute-start.17 = (bf16[256,2048]{1,0:T(8,128)(2,1)S(1)}, bf16[256,2048]{1,0:T(8,128)(2,1)}, u32[]{:S(2)}, u32[]{:S(2)}) collective-permute-start(bf16[256,2048]{1,0:T(8,128)(2,1)S(1)} %multiply_convert_fusion.7), channel_id=1, source_target_pairs={{0,16},{16,0},{1,17},{17,1},{2,18},{18,2},{3,19},{19,3},{4,20},{20... | collective-permute-start | bytes 3145736 | tf_op jit(solution)/shard_map/ppermute | solution.py:243
  260.1 27.4 %collective-permute-start.18 = (bf16[256,2048]{1,0:T(8,128)(2,1)S(1)}, bf16[256,2048]{1,0:T(8,128)(2,1)}, u32[]{:S(2)}, u32[]{:S(2)}) collective-permute-start(bf16[256,2048]{1,0:T(8,128)(2,1)S(1)} %multiply_convert_fusion.7), channel_id=1, source_target_pairs={{0,8},{8,0},{1,9},{9,1},{2,10},{10,2},{3,11},{11,3},{4,12},{12,4},... | collective-permute-start | bytes 3145736 | tf_op jit(solution)/shard_map/ppermute | solution.py:243
  279.0 8.4 %collective-permute-start.19 = (bf16[256,2048]{1,0:T(8,128)(2,1)}, bf16[256,2048]{1,0:T(8,128)(2,1)}, u32[]{:S(2)}, u32[]{:S(2)}) collective-permute-start(bf16[256,2048]{1,0:T(8,128)(2,1)} %collective-permute-done.17), channel_id=1, source_target_pairs={{0,8},{8,0},{1,9},{9,1},{2,10},{10,2},{3,11},{11,3},{4,12},{12,4},... | collective-permute-start | bytes 3145736 | tf_op jit(solution)/shard_map/ppermute | solution.py:243
  287.0 50.9 %collective-permute-start.29 = (bf16[256,2048]{1,0:T(8,128)(2,1)}, bf16[256,2048]{1,0:T(8,128)(2,1)}, u32[]{:S(2)}, u32[]{:S(2)}) collective-permute-start(bf16[256,2048]{1,0:T(8,128)(2,1)} %multiply_convert_fusion.6), channel_id=1, source_target_pairs={{0,16},{16,0},{1,17},{17,1},{2,18},{18,2},{3,19},{19,3},{4,20},{20... | collective-permute-start | bytes 3145736 | tf_op jit(solution)/shard_map/ppermute | solution.py:243
  287.0 59.6 %collective-permute-start.30 = (bf16[256,2048]{1,0:T(8,128)(2,1)}, bf16[256,2048]{1,0:T(8,128)(2,1)}, u32[]{:S(2)}, u32[]{:S(2)}) collective-permute-start(bf16[256,2048]{1,0:T(8,128)(2,1)} %multiply_convert_fusion.6), channel_id=1, source_target_pairs={{0,8},{8,0},{1,9},{9,1},{2,10},{10,2},{3,11},{11,3},{4,12},{12,4},... | collective-permute-start | bytes 3145736 | tf_op jit(solution)/shard_map/ppermute | solution.py:243
  337.9 8.7 %collective-permute-start.31 = (bf16[256,2048]{1,0:T(8,128)(2,1)}, bf16[256,2048]{1,0:T(8,128)(2,1)S(1)}, u32[]{:S(2)}, u32[]{:S(2)}) collective-permute-start(bf16[256,2048]{1,0:T(8,128)(2,1)} %collective-permute-done.29), channel_id=1, source_target_pairs={{0,8},{8,0},{1,9},{9,1},{2,10},{10,2},{3,11},{11,3},{4,12},{12,4},... | collective-permute-start | bytes 3145736 | tf_op jit(solution)/shard_map/ppermute | solution.py:243
  338.6 20.2 %collective-permute-start.25 = (bf16[2,256,2048]{2,1,0:T(8,128)(2,1)S(1)}, bf16[2,256,2048]{2,1,0:T(8,128)(2,1)S(1)}, u32[]{:S(2)}, u32[]{:S(2)}) collective-permute-start(bf16[2,256,2048]{2,1,0:T(8,128)(2,1)S(1)} %bitcast.420), channel_id=1, source_target_pairs={{0,8},{8,0},{1,9},{9,1},{2,10},{10,2},{3,11},{11,3},{4,12},{12,4},... | collective-permute-start | bytes 6291464 | tf_op jit(solution)/shard_map/ppermute | solution.py:243
  362.8 55.9 %collective-permute-start.26 = (bf16[256,2048]{1,0:T(8,128)(2,1)}, bf16[256,2048]{1,0:T(8,128)(2,1)S(1)}, u32[]{:S(2)}, u32[]{:S(2)}) collective-permute-start(bf16[256,2048]{1,0:T(8,128)(2,1)} %fusion.48), channel_id=1, source_target_pairs={{0,16},{16,0},{1,17},{17,1},{2,18},{18,2},{3,19},{19,3},{4,20},{20... | collective-permute-start | bytes 3145736 | tf_op jit(solution)/shard_map/ppermute | solution.py:243
  387.3 18.3 %collective-permute-start.34 = (bf16[2,256,2048]{2,1,0:T(8,128)(2,1)}, bf16[2,256,2048]{2,1,0:T(8,128)(2,1)}, u32[]{:S(2)}, u32[]{:S(2)}) collective-permute-start(bf16[2,256,2048]{2,1,0:T(8,128)(2,1)} %bitcast.64), channel_id=1, source_target_pairs={{0,8},{8,0},{1,9},{9,1},{2,10},{10,2},{3,11},{11,3},{4,12},{12,4},... | collective-permute-start | bytes 6291464 | tf_op jit(solution)/shard_map/ppermute | solution.py:243
  395.0 349.1 %reduce-scatter.6.cloned.1.call-start = ((), (), s32[]{:S(2)}) async-start(), calls=%async_computation.7 | async-start | bytes 4128768 | tf_op jit(solution)/shard_map/reduce_scatter | solution.py:524
  408.3 25.6 %collective-permute-start.35 = (bf16[256,2048]{1,0:T(8,128)(2,1)S(1)}, bf16[256,2048]{1,0:T(8,128)(2,1)S(1)}, u32[]{:S(2)}, u32[]{:S(2)}) collective-permute-start(bf16[256,2048]{1,0:T(8,128)(2,1)S(1)} %fusion.53), channel_id=1, source_target_pairs={{0,16},{16,0},{1,17},{17,1},{2,18},{18,2},{3,19},{19,3},{4,20},{20... | collective-permute-start | bytes 3145736 | tf_op jit(solution)/shard_map/ppermute | solution.py:243
  454.7 66.2 %collective-permute-start.36 = (bf16[2,640,256]{2,1,0:T(8,128)(2,1)}, bf16[2,640,256]{2,1,0:T(8,128)(2,1)}, u32[]{:S(2)}, u32[]{:S(2)}) collective-permute-start(bf16[2,640,256]{2,1,0:T(8,128)(2,1)} %bitcast.72), channel_id=1, source_target_pairs={{2,0},{4,2},{6,4},{3,1},{5,3},{7,5},{10,8},{12,10},{14,12},{11,9},... | collective-permute-start | bytes 1966088 | tf_op jit(solution)/shard_map/ppermute | solution.py:248
  476.5 267.6 %reduce-scatter.4.cloned.1.call-start = ((), (), s32[]{:S(2)}) async-start(), calls=%async_computation.6 | async-start | bytes 4128768 | tf_op jit(solution)/shard_map/reduce_scatter | solution.py:524
  505.6 99.0 %collective-permute-start.41 = (bf16[2,4,2,64,1280]{4,3,1,2,0:T(8,128)(2,1)}, bf16[2,4,2,64,1280]{4,3,1,2,0:T(8,128)(2,1)}, u32[]{:S(2)}, u32[]{:S(2)}) collective-permute-start(bf16[2,4,2,64,1280]{4,3,1,2,0:T(8,128)(2,1)} %bitcast.389), channel_id=1, source_target_pairs={{0,8},{8,0},{1,9},{9,1},{2,10},{10,2},{3,11},{11,3},{4,12},{12,4},... | collective-permute-start | bytes 7864328 | tf_op jit(solution)/shard_map/ppermute | solution.py:243
  507.5 66.6 %collective-permute-start.39 = (bf16[2,640,256]{2,1,0:T(8,128)(2,1)}, bf16[2,640,256]{2,1,0:T(8,128)(2,1)}, u32[]{:S(2)}, u32[]{:S(2)}) collective-permute-start(bf16[2,640,256]{2,1,0:T(8,128)(2,1)} %bitcast.77), channel_id=1, source_target_pairs={{2,0},{4,2},{6,4},{3,1},{5,3},{7,5},{10,8},{12,10},{14,12},{11,9},... | collective-permute-start | bytes 1966088 | tf_op jit(solution)/shard_map/ppermute | solution.py:248
  516.2 63.4 %collective-permute-start.27 = (bf16[2,256,2048]{2,1,0:T(8,128)(2,1)}, bf16[2,256,2048]{2,1,0:T(8,128)(2,1)}, u32[]{:S(2)}, u32[]{:S(2)}) collective-permute-start(bf16[2,256,2048]{2,1,0:T(8,128)(2,1)} %bitcast.41), channel_id=1, source_target_pairs={{0,8},{8,0},{1,9},{9,1},{2,10},{10,2},{3,11},{11,3},{4,12},{12,4},... | collective-permute-start | bytes 6291464 | tf_op jit(solution)/shard_map/ppermute | solution.py:243
  522.2 45.2 %collective-permute-start.37 = (bf16[2,640,256]{2,1,0:T(8,128)(2,1)S(1)}, bf16[2,640,256]{2,1,0:T(8,128)(2,1)S(1)}, u32[]{:S(2)}, u32[]{:S(2)}) collective-permute-start(bf16[2,640,256]{2,1,0:T(8,128)(2,1)S(1)} %fusion.47), channel_id=1, source_target_pairs={{2,0},{4,2},{6,4},{3,1},{5,3},{7,5},{10,8},{12,10},{14,12},{11,9},... | collective-permute-start | bytes 1966088 | tf_op jit(solution)/shard_map/ppermute | solution.py:248
  526.5 74.1 %collective-permute-start.32 = (bf16[2,256,2048]{2,1,0:T(8,128)(2,1)}, bf16[2,256,2048]{2,1,0:T(8,128)(2,1)}, u32[]{:S(2)}, u32[]{:S(2)}) collective-permute-start(bf16[2,256,2048]{2,1,0:T(8,128)(2,1)} %bitcast.57), channel_id=1, source_target_pairs={{0,8},{8,0},{1,9},{9,1},{2,10},{10,2},{3,11},{11,3},{4,12},{12,4},... | collective-permute-start | bytes 6291464 | tf_op jit(solution)/shard_map/ppermute | solution.py:243
  568.5 10.1 %collective-permute-start.38 = (bf16[640,256]{1,0:T(8,128)(2,1)}, bf16[640,256]{1,0:T(8,128)(2,1)}, u32[]{:S(2)}, u32[]{:S(2)}) collective-permute-start(bf16[640,256]{1,0:T(8,128)(2,1)} %slice_bitcast_fusion.20), channel_id=1, source_target_pairs={{0,1},{1,0},{2,3},{3,2},{4,5},{5,4},{6,7},{7,6},{8,9},{9,8},{10,11... | collective-permute-start | bytes 983048 | tf_op jit(solution)/shard_map/ppermute | solution.py:243
  574.2 33.2 %collective-permute-start.40 = (bf16[2,4,2,40,2048]{4,3,1,0,2:T(8,128)(2,1)}, bf16[2,4,2,40,2048]{4,3,1,0,2:T(8,128)(2,1)S(1)}, u32[]{:S(2)}, u32[]{:S(2)}) collective-permute-start(bf16[2,4,2,40,2048]{4,3,1,0,2:T(8,128)(2,1)} %bitcast.413), channel_id=1, source_target_pairs={{0,8},{8,0},{1,9},{9,1},{2,10},{10,2},{3,11},{11,3},{4,12},{12,4},... | collective-permute-start | bytes 7864328 | tf_op jit(solution)/shard_map/ppermute | solution.py:243
  582.2 42.3 %collective-permute-start.28 = (bf16[256,2048]{1,0:T(8,128)(2,1)S(1)}, bf16[256,2048]{1,0:T(8,128)(2,1)S(1)}, u32[]{:S(2)}, u32[]{:S(2)}) collective-permute-start(bf16[256,2048]{1,0:T(8,128)(2,1)S(1)} %fusion.50), channel_id=1, source_target_pairs={{0,16},{16,0},{1,17},{17,1},{2,18},{18,2},{3,19},{19,3},{4,20},{20... | collective-permute-start | bytes 3145736 | tf_op jit(solution)/shard_map/ppermute | solution.py:243
  603.2 56.8 %collective-permute-start.33 = (bf16[256,2048]{1,0:T(8,128)(2,1)S(1)}, bf16[256,2048]{1,0:T(8,128)(2,1)S(1)}, u32[]{:S(2)}, u32[]{:S(2)}) collective-permute-start(bf16[256,2048]{1,0:T(8,128)(2,1)S(1)} %fusion.52), channel_id=1, source_target_pairs={{0,16},{16,0},{1,17},{17,1},{2,18},{18,2},{3,19},{19,3},{4,20},{20... | collective-permute-start | bytes 3145736 | tf_op jit(solution)/shard_map/ppermute | solution.py:243
  608.6 49.7 %collective-permute-start.42 = (bf16[2,640,256]{2,1,0:T(8,128)(2,1)S(1)}, bf16[2,640,256]{2,1,0:T(8,128)(2,1)S(1)}, u32[]{:S(2)}, u32[]{:S(2)}) collective-permute-start(bf16[2,640,256]{2,1,0:T(8,128)(2,1)S(1)} %fusion.45), channel_id=1, source_target_pairs={{2,0},{4,2},{6,4},{3,1},{5,3},{7,5},{10,8},{12,10},{14,12},{11,9},... | collective-permute-start | bytes 1966088 | tf_op jit(solution)/shard_map/ppermute | solution.py:248
  612.3 84.1 %collective-permute-start.60 = (bf16[2,4,40,2048]{3,2,1,0:T(8,128)(2,1)}, bf16[2,4,40,2048]{3,2,1,0:T(8,128)(2,1)}, u32[]{:S(2)}, u32[]{:S(2)}) collective-permute-start(bf16[2,4,40,2048]{3,2,1,0:T(8,128)(2,1)} %dynamic-slice_bitcast_fusion), channel_id=1, source_target_pairs={{0,1},{1,0},{2,3},{3,2},{4,5},{5,4},{6,7},{7,6},{8,9},{9,8},{10,11... | collective-permute-start | bytes 3932168 | tf_op jit(solution)/shard_map/ppermute | solution.py:243
  614.1 96.7 %collective-permute-start.44 = (bf16[4,2,64,1280]{3,2,0,1:T(8,128)(2,1)}, bf16[4,2,64,1280]{3,2,0,1:T(8,128)(2,1)}, u32[]{:S(2)}, u32[]{:S(2)}) collective-permute-start(bf16[4,2,64,1280]{3,2,0,1:T(8,128)(2,1)} %dynamic-slice_bitcast_fusion.1), channel_id=1, source_target_pairs={{0,16},{16,0},{1,17},{17,1},{2,18},{18,2},{3,19},{19,3},{4,20},{20... | collective-permute-start | bytes 3932168 | tf_op jit(solution)/shard_map/ppermute | solution.py:243
  658.6 14.1 %collective-permute-start.43 = (bf16[640,256]{1,0:T(8,128)(2,1)S(1)}, bf16[640,256]{1,0:T(8,128)(2,1)S(1)}, u32[]{:S(2)}, u32[]{:S(2)}) collective-permute-start(bf16[640,256]{1,0:T(8,128)(2,1)S(1)} %slice_bitcast_fusion.18), channel_id=1, source_target_pairs={{0,1},{1,0},{2,3},{3,2},{4,5},{5,4},{6,7},{7,6},{8,9},{9,8},{10,11... | collective-permute-start | bytes 983048 | tf_op jit(solution)/shard_map/ppermute | solution.py:243
  678.4 14.6 %collective-permute-start.45 = (bf16[2,4,2,64,640]{4,3,1,2,0:T(8,128)(2,1)}, bf16[2,4,2,64,640]{4,3,1,2,0:T(8,128)(2,1)}, u32[]{:S(2)}, u32[]{:S(2)}) collective-permute-start(bf16[2,4,2,64,640]{4,3,1,2,0:T(8,128)(2,1)} %bitcast.391), channel_id=1, source_target_pairs={{0,8},{8,0},{1,9},{9,1},{2,10},{10,2},{3,11},{11,3},{4,12},{12,4},... | collective-permute-start | bytes 3932168 | tf_op jit(solution)/shard_map/ppermute | solution.py:243
  701.9 18.8 %collective-permute-start.61 = (bf16[4,40,2048]{2,1,0:T(8,128)(2,1)}, bf16[4,40,2048]{2,1,0:T(8,128)(2,1)S(1)}, u32[]{:S(2)}, u32[]{:S(2)}) collective-permute-start(bf16[4,40,2048]{2,1,0:T(8,128)(2,1)} %dynamic-slice_bitcast_fusion.2), channel_id=1, source_target_pairs={{0,16},{16,0},{1,17},{17,1},{2,18},{18,2},{3,19},{19,3},{4,20},{20... | collective-permute-start | bytes 1966088 | tf_op jit(solution)/shard_map/ppermute | solution.py:243
  703.2 11.2 %collective-permute-start.57 = (f32[1,128]{1,0:T(1,128)S(1)}, f32[1,128]{1,0:T(1,128)S(1)}, u32[]{:S(2)}, u32[]{:S(2)}) collective-permute-start(f32[1,128]{1,0:T(1,128)S(1)} %add.629), channel_id=1, source_target_pairs={{0,2},{2,0},{4,6},{6,4},{1,3},{3,1},{5,7},{7,5},{8,10},{10,8},{12,... | collective-permute-start | bytes 1544 | tf_op jit(solution)/shard_map/ppermute | solution.py:279
  717.1 14.2 %collective-permute-start.50 = (bf16[4,2,64,640]{3,2,0,1:T(8,128)(2,1)S(1)}, bf16[4,2,64,640]{3,2,0,1:T(8,128)(2,1)S(1)}, u32[]{:S(2)}, u32[]{:S(2)}) collective-permute-start(bf16[4,2,64,640]{3,2,0,1:T(8,128)(2,1)S(1)} %dynamic-slice_bitcast_fusion.3), channel_id=1, source_target_pairs={{0,16},{16,0},{1,17},{17,1},{2,18},{18,2},{3,19},{19,3},{4,20},{20... | collective-permute-start | bytes 1966088 | tf_op jit(solution)/shard_map/ppermute | solution.py:243
  719.0 17.7 %collective-permute-start.46 = (bf16[4,64,1280]{2,1,0:T(8,128)(2,1)S(1)}, bf16[4,64,1280]{2,1,0:T(8,128)(2,1)S(1)}, u32[]{:S(2)}, u32[]{:S(2)}) collective-permute-start(bf16[4,64,1280]{2,1,0:T(8,128)(2,1)S(1)} %dynamic-slice_bitcast_fusion.4), channel_id=1, source_target_pairs={{0,1},{1,0},{2,3},{3,2},{4,5},{5,4},{6,7},{7,6},{8,9},{9,8},{10,11... | collective-permute-start | bytes 1966088 | tf_op jit(solution)/shard_map/ppermute | solution.py:243
  721.0 18.8 %collective-permute-start.62 = (bf16[40,2048]{1,0:T(8,128)(2,1)S(1)}, bf16[40,2048]{1,0:T(8,128)(2,1)S(1)}, u32[]{:S(2)}, u32[]{:S(2)}) collective-permute-start(bf16[40,2048]{1,0:T(8,128)(2,1)S(1)} %get-tuple-element.152), channel_id=1, source_target_pairs={{0,2},{2,4},{4,6},{6,0},{1,3},{3,5},{5,7},{7,1},{8,10},{10,12},{12... | collective-permute-start | bytes 491528 | tf_op jit(solution)/shard_map/ppermute | solution.py:243
  726.4 15.7 %collective-permute-start.63 = (bf16[40,2048]{1,0:T(8,128)(2,1)S(1)}, bf16[40,2048]{1,0:T(8,128)(2,1)S(1)}, u32[]{:S(2)}, u32[]{:S(2)}) collective-permute-start(bf16[40,2048]{1,0:T(8,128)(2,1)S(1)} %get-tuple-element.154), channel_id=1, source_target_pairs={{0,4},{2,6},{4,0},{6,2},{1,5},{3,7},{5,1},{7,3},{8,12},{10,14},{12... | collective-permute-start | bytes 491528 | tf_op jit(solution)/shard_map/ppermute | solution.py:243
  728.9 14.5 %collective-permute-start.64 = (bf16[40,2048]{1,0:T(8,128)(2,1)S(1)}, bf16[40,2048]{1,0:T(8,128)(2,1)S(1)}, u32[]{:S(2)}, u32[]{:S(2)}) collective-permute-start(bf16[40,2048]{1,0:T(8,128)(2,1)S(1)} %get-tuple-element.153), channel_id=1, source_target_pairs={{0,6},{2,0},{4,2},{6,4},{1,7},{3,1},{5,3},{7,5},{8,14},{10,8},{12,... | collective-permute-start | bytes 491528 | tf_op jit(solution)/shard_map/ppermute | solution.py:243
  731.5 22.5 %collective-permute-start.51 = (bf16[4,64,640]{2,1,0:T(8,128)(2,1)S(1)}, bf16[4,64,640]{2,1,0:T(8,128)(2,1)S(1)}, u32[]{:S(2)}, u32[]{:S(2)}) collective-permute-start(bf16[4,64,640]{2,1,0:T(8,128)(2,1)S(1)} %dynamic-slice_bitcast_fusion.13), channel_id=1, source_target_pairs={{0,1},{1,0},{2,3},{3,2},{4,5},{5,4},{6,7},{7,6},{8,9},{9,8},{10,11... | collective-permute-start | bytes 983048 | tf_op jit(solution)/shard_map/ppermute | solution.py:243
  737.7 9.6 %collective-permute-start.47 = (bf16[64,1280]{1,0:T(8,128)(2,1)}, bf16[64,1280]{1,0:T(8,128)(2,1)S(1)}, u32[]{:S(2)}, u32[]{:S(2)}) collective-permute-start(bf16[64,1280]{1,0:T(8,128)(2,1)} %get-tuple-element.155), channel_id=1, source_target_pairs={{0,2},{2,4},{4,6},{6,0},{1,3},{3,5},{5,7},{7,1},{8,10},{10,12},{12... | collective-permute-start | bytes 491528 | tf_op jit(solution)/shard_map/ppermute | solution.py:243
  739.8 12.4 %collective-permute-start.48 = (bf16[64,1280]{1,0:T(8,128)(2,1)}, bf16[64,1280]{1,0:T(8,128)(2,1)S(1)}, u32[]{:S(2)}, u32[]{:S(2)}) collective-permute-start(bf16[64,1280]{1,0:T(8,128)(2,1)} %get-tuple-element.157), channel_id=1, source_target_pairs={{0,4},{2,6},{4,0},{6,2},{1,5},{3,7},{5,1},{7,3},{8,12},{10,14},{12... | collective-permute-start | bytes 491528 | tf_op jit(solution)/shard_map/ppermute | solution.py:243
  742.1 10.0 %collective-permute-start.49 = (bf16[64,1280]{1,0:T(8,128)(2,1)}, bf16[64,1280]{1,0:T(8,128)(2,1)}, u32[]{:S(2)}, u32[]{:S(2)}) collective-permute-start(bf16[64,1280]{1,0:T(8,128)(2,1)} %get-tuple-element.156), channel_id=1, source_target_pairs={{0,6},{2,0},{4,2},{6,4},{1,7},{3,1},{5,3},{7,5},{8,14},{10,8},{12,... | collective-permute-start | bytes 491528 | tf_op jit(solution)/shard_map/ppermute | solution.py:243
  745.5 14.7 %collective-permute-start.65 = (bf16[2,64,1792]{2,1,0:T(8,128)(2,1)S(1)}, bf16[2,64,1792]{2,1,0:T(8,128)(2,1)S(1)}, u32[]{:S(2)}, u32[]{:S(2)}) collective-permute-start(bf16[2,64,1792]{2,1,0:T(8,128)(2,1)S(1)} %get-tuple-element.130), channel_id=1, source_target_pairs={{0,16},{16,0},{1,17},{17,1},{2,18},{18,2},{3,19},{19,3},{4,20},{20... | collective-permute-start | bytes 1376264 | tf_op jit(solution)/shard_map/ppermute | solution.py:243
  (125 other events, 1811.2 us)
Sparse Core Ops, SparseCore 0:
  10.8 82.4 all-gather.3
  96.1 154.7 all-gather.5
  253.0 63.0 all-gather.7
  395.2 86.2 reduce-scatter.7
  485.0 105.7 reduce-scatter.5
  594.3 112.4 reduce-scatter.3
